TPU v7x, 128 devices: a whole 4x4x4 slice. The times are simulated.
128 devices in a mesh: row: 16 (over x, y), col: 4 (over z), layer: 2 (over core).
Axes of the slice: x: 4, y: 4, z: 4, core: 2. Of those that a mesh axis runs over, the one named last changes fastest.
Arguments:
- density: float32 [4096, 4096], P('row', ('col', 'layer')), may hold values from -2 to 2
- masks: int32 [6, 64, 64], replicated, may hold values from 0 to 1, as said below
- branch: int32 [5], replicated, may hold values from 0 to 1, as said below
- perm: int32 [64], replicated, may hold values from 0 to 63, each once
Outputs:
- purified: float32 [4096, 4096], P('row', ('col', 'layer'))
Inputs may be any that keep to these rules, and one draw needn't show every extreme that they name: masks are symmetric in their last two dimensions, every diagonal block is occupied, and block (i, j) of masks[s] is occupied only where the cyclic distance between i and j is at most 6 + s. `branch`: both values occur among the steps. `perm`: a permutation of 0..63.
All inputs are finite; a program needn't handle non-finite values.
Results may differ from a plain program's by a relative error of at most 0.0003.
Values sent between devices are 32-bit elements; how exact they have to be, the bound alone decides.
No kernel may reach another device: no remote copies, remote signals or barrier semaphores. Data moves between devices by JAX's collectives and lax.ppermute only.
A program may use at most 64 MiB of HBM per device.

v0:
```python
import jax
import jax.numpy as jnp
from jax import lax
from jax.sharding import PartitionSpec as P

BS = 64
STEPS = 5


def expand(block_mask):
    grown = jnp.repeat(block_mask, BS, axis=0)
    return jnp.repeat(grown, BS, axis=1).astype(jnp.float32)


def shards(density, masks, branch, perm):
    rows_here = density.shape[0]
    cols_here = density.shape[1]
    row_blocks = rows_here // BS
    col_blocks = cols_here // BS
    row_start = lax.axis_index("row") * row_blocks
    col_start = lax.axis_index(("col", "layer")) * col_blocks
    row_ids = lax.dynamic_slice_in_dim(perm, row_start, row_blocks)
    col_ids = lax.dynamic_slice_in_dim(perm, col_start, col_blocks)
    local_masks = jnp.take(jnp.take(masks, row_ids, axis=1), col_ids, axis=2)
    current = density * expand(local_masks[0])
    for step in range(STEPS):
        panel = lax.all_gather(current, ("col", "layer"), axis=1, tiled=True)
        square = jnp.dot(
            panel,
            lax.all_gather(current, "row", axis=0, tiled=True),
            preferred_element_type=jnp.float32,
            precision=lax.Precision.HIGHEST,
        )
        picked = jnp.where(branch[step] == 1, 2.0 * current - square, square)
        current = picked * expand(local_masks[step + 1])
    return current


def solution(mesh):
    return jax.shard_map(
        shards,
        mesh=mesh,
        in_specs=(P("row", ("col", "layer")), P(), P(), P()),
        out_specs=P("row", ("col", "layer")),
        check_vma=False,
    )
```

profile of v0, /device:TPU:1, one launch (start us, length us, event | category | flops | bytes accessed | tf_op | source)
XLA Modules:
  0.0 603.6 jit_solution(2125554987655784131)
XLA Ops:
  6.5 0.8 compare_and_fusion
  7.5 0.6 gather_fusion
  8.3 0.7 compare_and_fusion.1
  9.0 0.6 gather_fusion.1
  10.0 0.2 copy.27
  10.2 1.9 mul.45
  12.2 0.7 all-gather.13.cloned.1.call-update
  13.3 0.2 copy.29
  13.5 1.5 fusion.11
  15.5 32.8 %all-gather.11.cloned.1.call-done = f32[256,4096]{1,0:T(8,128)} async-done(((f32[256,512]{1,0:T(8,128)}), f32[256,4096]{1,0:T(8,128)}) %all-gather.11.cloned.1.call-update) | async-done | bytes 4194320 | tf_op jit(solution)/shard_map/all_gather | solution.py:27
  48.3 72.2 %all-gather.13.cloned.1.call-done = f32[4096,512]{1,0:T(8,128)} async-done(((f32[256,512]{1,0:T(8,128)}), f32[4096,512]{1,0:T(8,128)}) %all-gather.13.cloned.1.call-update) | async-done | bytes 8388624 | tf_op jit(solution)/shard_map/all_gather | solution.py:30
  120.5 11.5 %fusion = f32[256,512]{1,0:T(8,128)} fusion(f32[256,512]{1,0:T(8,128)S(1)} %copy.29, f32[256,512]{1,0:T(8,128)} %mul.45, pred[]{:T(512)} %bitcast.4, f32[256,4096]{1,0:T(8,128)} %all-gather.11.cloned.1.call-done, f32[4096,512]{1,0:T(8,128)} %all-gather.13.cloned.1.call-done), kind=kOutput, calls=%fused_computation.7 | convolution fusion | flops 6442975232 | bytes 14155777 | tf_op jit(solution)/shard_map/dot_general | solution.py:28
  132.0 0.5 all-gather.17.cloned.1.call-update
  132.9 0.2 copy.31
  133.8 30.8 %all-gather.15.cloned.1.call-done = f32[256,4096]{1,0:T(8,128)} async-done(((f32[256,512]{1,0:T(8,128)}), f32[256,4096]{1,0:T(8,128)}) %all-gather.15.cloned.1.call-update) | async-done | bytes 4194320 | tf_op jit(solution)/shard_map/all_gather | solution.py:27
  164.6 72.0 %all-gather.17.cloned.1.call-done = f32[4096,512]{1,0:T(8,128)} async-done(((f32[256,512]{1,0:T(8,128)}), f32[4096,512]{1,0:T(8,128)}) %all-gather.17.cloned.1.call-update) | async-done | bytes 8388624 | tf_op jit(solution)/shard_map/all_gather | solution.py:30
  236.6 11.5 %fusion.1 = f32[256,512]{1,0:T(8,128)} fusion(f32[256,512]{1,0:T(8,128)S(1)} %copy.31, f32[256,512]{1,0:T(8,128)} %fusion, pred[]{:T(512)} %bitcast.3, f32[256,4096]{1,0:T(8,128)} %all-gather.15.cloned.1.call-done, f32[4096,512]{1,0:T(8,128)} %all-gather.17.cloned.1.call-done), kind=kOutput, calls=%fused_computation.8 | convolution fusion | flops 6442975232 | bytes 14155777 | tf_op jit(solution)/shard_map/dot_general | solution.py:28
  248.2 0.5 all-gather.21.cloned.1.call-update
  248.7 0.2 all-gather.23.cloned.1.call-start
  249.2 0.2 copy.33
  250.1 30.7 %all-gather.19.cloned.1.call-done = f32[256,4096]{1,0:T(8,128)} async-done(((f32[256,512]{1,0:T(8,128)}), f32[256,4096]{1,0:T(8,128)}) %all-gather.19.cloned.1.call-update) | async-done | bytes 4194320 | tf_op jit(solution)/shard_map/all_gather | solution.py:27
  280.8 72.0 %all-gather.21.cloned.1.call-done = f32[4096,512]{1,0:T(8,128)} async-done(((f32[256,512]{1,0:T(8,128)}), f32[4096,512]{1,0:T(8,128)}) %all-gather.21.cloned.1.call-update) | async-done | bytes 8388624 | tf_op jit(solution)/shard_map/all_gather | solution.py:30
  352.8 11.5 %fusion.2 = f32[256,512]{1,0:T(8,128)} fusion(f32[256,512]{1,0:T(8,128)S(1)} %copy.33, f32[256,512]{1,0:T(8,128)} %fusion.1, pred[]{:T(512)} %bitcast.2, f32[256,4096]{1,0:T(8,128)} %all-gather.19.cloned.1.call-done, f32[4096,512]{1,0:T(8,128)} %all-gather.21.cloned.1.call-done), kind=kOutput, calls=%fused_computation.9 | convolution fusion | flops 6442975232 | bytes 14155777 | tf_op jit(solution)/shard_map/dot_general | solution.py:28
  364.4 0.7 all-gather.25.cloned.1.call-update
  366.2 30.7 %all-gather.23.cloned.1.call-done = f32[256,4096]{1,0:T(8,128)} async-done(((f32[256,512]{1,0:T(8,128)}), f32[256,4096]{1,0:T(8,128)}) %all-gather.23.cloned.1.call-update) | async-done | bytes 4194320 | tf_op jit(solution)/shard_map/all_gather | solution.py:27
  397.0 72.2 %all-gather.25.cloned.1.call-done = f32[4096,512]{1,0:T(8,128)} async-done(((f32[256,512]{1,0:T(8,128)}), f32[4096,512]{1,0:T(8,128)}) %all-gather.25.cloned.1.call-update) | async-done | bytes 8388624 | tf_op jit(solution)/shard_map/all_gather | solution.py:30
  469.1 11.5 %fusion.3 = f32[256,512]{1,0:T(8,128)} fusion(f32[256,512]{1,0:T(8,128)S(1)} %copy.35, f32[256,512]{1,0:T(8,128)} %fusion.2, pred[]{:T(512)} %bitcast.1, f32[256,4096]{1,0:T(8,128)} %all-gather.23.cloned.1.call-done, f32[4096,512]{1,0:T(8,128)} %all-gather.25.cloned.1.call-done), kind=kOutput, calls=%fused_computation.10 | convolution fusion | flops 6442975232 | bytes 14155777 | tf_op jit(solution)/shard_map/dot_general | solution.py:28
  480.6 0.3 all-gather.29.cloned.1.call-start
  480.9 0.3 all-gather.29.cloned.1.call-update
  482.4 30.8 %all-gather.27.cloned.1.call-done = f32[256,4096]{1,0:T(8,128)} async-done(((f32[256,512]{1,0:T(8,128)}), f32[256,4096]{1,0:T(8,128)}) %all-gather.27.cloned.1.call-update) | async-done | bytes 4194320 | tf_op jit(solution)/shard_map/all_gather | solution.py:27
  513.2 72.0 %all-gather.29.cloned.1.call-done = f32[4096,512]{1,0:T(8,128)} async-done(((f32[256,512]{1,0:T(8,128)}), f32[4096,512]{1,0:T(8,128)}) %all-gather.29.cloned.1.call-update) | async-done | bytes 8388624 | tf_op jit(solution)/shard_map/all_gather | solution.py:30
  585.3 11.5 %fusion.4 = f32[256,512]{1,0:T(8,128)} fusion(f32[256,512]{1,0:T(8,128)S(1)} %copy.37, f32[256,512]{1,0:T(8,128)} %fusion.3, pred[]{:T(512)} %bitcast, f32[256,4096]{1,0:T(8,128)} %all-gather.27.cloned.1.call-done, f32[4096,512]{1,0:T(8,128)} %all-gather.29.cloned.1.call-done), kind=kOutput, calls=%fused_computation.11 | convolution fusion | flops 6442975232 | bytes 14155777 | tf_op jit(solution)/shard_map/dot_general | solution.py:28
  (50 shorter events, 3.0 us)
Async XLA Ops:
  6.5 0.9 copy-start
  6.5 41.8 %all-gather.11.cloned.1.call-start = ((), (), s32[]{:S(2)}) async-start(), calls=%async_computation | async-start | bytes 4718592 | tf_op jit(solution)/shard_map/all_gather | solution.py:27
  12.2 108.3 %all-gather.13.cloned.1.call-start = ((), (), s32[]{:S(2)}) async-start(), calls=%async_computation.1 | async-start | bytes 8912896 | tf_op jit(solution)/shard_map/all_gather | solution.py:30
  12.9 151.7 %all-gather.15.cloned.1.call-start = ((), (), s32[]{:S(2)}) async-start(), calls=%async_computation.2 | async-start | bytes 4718592 | tf_op jit(solution)/shard_map/all_gather | solution.py:27
  132.0 104.7 %all-gather.17.cloned.1.call-start = ((), (), s32[]{:S(2)}) async-start(), calls=%async_computation.3 | async-start | bytes 8912896 | tf_op jit(solution)/shard_map/all_gather | solution.py:30
  132.6 148.2 %all-gather.19.cloned.1.call-start = ((), (), s32[]{:S(2)}) async-start(), calls=%async_computation.4 | async-start | bytes 4718592 | tf_op jit(solution)/shard_map/all_gather | solution.py:27
  248.1 104.7 %all-gather.21.cloned.1.call-start = ((), (), s32[]{:S(2)}) async-start(), calls=%async_computation.5 | async-start | bytes 8912896 | tf_op jit(solution)/shard_map/all_gather | solution.py:30
  248.7 148.3 %all-gather.23.cloned.1.call-start = ((), (), s32[]{:S(2)}) async-start(), calls=%async_computation.6 | async-start | bytes 4718592 | tf_op jit(solution)/shard_map/all_gather | solution.py:27
  364.3 104.8 %all-gather.25.cloned.1.call-start = ((), (), s32[]{:S(2)}) async-start(), calls=%async_computation.7 | async-start | bytes 8912896 | tf_op jit(solution)/shard_map/all_gather | solution.py:30
  365.1 148.2 %all-gather.27.cloned.1.call-start = ((), (), s32[]{:S(2)}) async-start(), calls=%async_computation.8 | async-start | bytes 4718592 | tf_op jit(solution)/shard_map/all_gather | solution.py:27
  480.6 116.1 %copy-start.1 = (s32[6,64,64]{2,1,0:T(8,128)S(1)}, s32[6,64,64]{2,1,0:T(8,128)}, u32[]{:S(2)}) copy-start(s32[6,64,64]{2,1,0:T(8,128)} %param.5) | copy-start | bytes 294916
  480.6 104.6 %all-gather.29.cloned.1.call-start = ((), (), s32[]{:S(2)}) async-start(), calls=%async_computation.9 | async-start | bytes 8912896 | tf_op jit(solution)/shard_map/all_gather | solution.py:30
Sparse Core Ops, SparseCore 0:
  12.3 35.9 all-gather.10
  50.5 69.9 all-gather.12
  132.1 32.4 all-gather.14
  166.6 69.9 all-gather.16
  248.3 32.5 all-gather.18
  282.8 69.9 all-gather.20
  364.4 32.4 all-gather.22
  399.1 69.9 all-gather.24
  480.7 32.4 all-gather.26
  515.2 69.9 all-gather.28
where the time goes:
time: 604 us
  waiting for transfers between devices  519 us (86%)
  matrix products  57.3 us (9%)
  between operations  16.9 us (3%)
    all_gather x5, waiting for transfers between devices, shards(): lax.all_gather(current, 'row', axis=0, tiled=True)  360 us
    all_gather x5, waiting for transfers between devices, shards(): panel = lax.all_gather(current, ('col', 'layer'), axis=1, tiled=True)  156 us
    dot_general x5, matrix products, shards(): jnp.dot(panel, lax.all_gather(current, 'row', axis=0, tiled=True), prefer...  57.3 us
  transfers between devices with their start and end apart: 10, of which 10 were waited for; matrix products, arithmetic and copies ran while one was open for 1% of the time, Pallas kernels for 0%

commit v1 on v0

v1 whole, which is shorter than its diff:
```python
import jax
import jax.numpy as jnp
from jax import lax
from jax.experimental import pallas as pl
from jax.experimental.pallas import tpu as pltpu
from jax.sharding import PartitionSpec as P

STEPS = 5
BAND = 6
NB = 64
GROUP = ("col", "layer")
PERM, INV, BRANCH, BITS, PLACE = 0, 64, 128, 136, 136 + 6 * 128
F32, BF16 = jnp.float32, jnp.bfloat16


def ring_xy(pos):
    a, b = pos // 2, pos % 2
    return (a, b) if a < 4 else (7 - a, 3 - b)


RING = [ring_xy(p)[0] * 4 + ring_xy(p)[1] for p in range(16)]


def ring_shift(value, k):
    return lax.ppermute(value, "row", [(RING[p], RING[(p + k) % 16]) for p in range(16)])


def xy_shift(value, dx, dy):
    return lax.ppermute(
        value, "row", [(i, ((i // 4 + dx) % 4) * 4 + (i % 4 + dy) % 4) for i in range(16)]
    )


def z_swap(value, k):
    return lax.ppermute(value, "col", [(i, i ^ k) for i in range(4)])


def core_swap(value):
    return lax.ppermute(value, "layer", [(0, 1), (1, 0)])


def low_half():
    return lax.broadcasted_iota(jnp.int32, (8, 128), 1) < 64


def swap_halves(tile):
    return pltpu.roll(tile, 64, 1)


def bit(tab, s, i, j):
    word = tab[BITS + s * 128 + i * 2 + lax.shift_right_logical(j, 5)]
    return lax.shift_right_logical(word, j & 31) & 1


def shifted(tiles, d, count):
    n = len(tiles)
    get = lambda seq, t: seq[t] if 0 <= t < n else None
    if d % 2 == 0:
        return [get(tiles, m - d // 2) for m in range(count)]
    q = (d - 1) // 2
    low = low_half()
    turned = [swap_halves(t) for t in tiles]
    out = []
    for m in range(count):
        a, b = get(turned, m - q - 1), get(turned, m - q)
        if a is None and b is None:
            out.append(None)
        else:
            zero = jnp.zeros((8, 128), F32)
            out.append(jnp.where(low, zero if a is None else a, zero if b is None else b))
    return out


def store_split(hi_ref, lo_ref, row, first, second):
    zero = jnp.zeros((8, 128), F32)
    for m, (a, b) in enumerate(zip(first, second)):
        both = jnp.concatenate([zero if a is None else a, zero if b is None else b], axis=0)
        hi = both.astype(BF16)
        hi_ref[row : row + 16, m * 128 : (m + 1) * 128] = hi
        lo_ref[row : row + 16, m * 128 : (m + 1) * 128] = (both - hi.astype(F32)).astype(BF16)


def tdot(a, b):
    return lax.dot_general(a, b, (((0,), (0,)), ((), ())), preferred_element_type=F32)


def product(hi_ref, lo_ref, start, width):
    xh = hi_ref[:, start : start + width]
    xl = lo_ref[:, start : start + width]
    zh = hi_ref[...]
    return tdot(xh, zh) + tdot(xh, lo_ref[...]) + tdot(xl, zh)


def call(kernel, outs, tab, args, scratch=(), anyspace=False):
    space = pl.ANY if anyspace else pltpu.VMEM
    return pl.pallas_call(
        kernel,
        out_shape=[jax.ShapeDtypeStruct(o, F32) for o in outs],
        in_specs=[pl.BlockSpec(memory_space=pltpu.SMEM)]
        + [pl.BlockSpec(memory_space=space)] * len(args),
        out_specs=[pl.BlockSpec(memory_space=pltpu.VMEM)] * len(outs),
        scratch_shapes=list(scratch),
        compiler_params=pltpu.CompilerParams(vmem_limit_bytes=48 * 1024 * 1024),
    )(tab, *args)


def split_kernel(tab, d_ref, out_ref):
    for c in range(8):
        for e in range(4):
            rows = d_ref[e * 64 + c * 8 : e * 64 + c * 8 + 8, :]
            for t in range(4):
                out_ref[c, e, t] = rows[:, t * 128 : (t + 1) * 128]


def compact_kernel(tab, x_ref, a_ref, b_ref):
    low = low_half()
    row0 = tab[PLACE] * 4
    for e in range(4):
        i = tab[PERM + row0 + e]
        out_ref = a_ref if e < 2 else b_ref
        halves = []
        for t in range(2 * BAND + 2):
            if t > 2 * BAND:
                halves.append(jnp.zeros((8, 128), F32))
                continue
            j = (i + t - BAND) & 63
            sj = tab[INV + j]
            tile = x_ref[sj >> 3, e, (sj & 7) >> 1]
            tile = jnp.where((sj & 1) == (t & 1), tile, swap_halves(tile))
            halves.append(jnp.where(bit(tab, 0, i, j) == 1, tile, 0.0))
        for t in range(BAND + 1):
            out_ref[e % 2, t] = jnp.where(low, halves[2 * t], halves[2 * t + 1])


def gather_rows(half_a, half_b):
    stack_a = jnp.stack([half_a] + [xy_shift(half_a, k, 0) for k in (1, 2, 3)])
    stack_b = jnp.stack([half_b] + [xy_shift(half_b, 0, k) for k in (1, 2, 3)])
    all_a = [stack_a] + [xy_shift(stack_a, 0, k) for k in (1, 2, 3)]
    all_b = [stack_b] + [xy_shift(stack_b, k, 0) for k in (1, 2, 3)]
    return all_a + all_b


def fetch(refs, g_ref, sem):
    copies = [pltpu.make_async_copy(refs[n], g_ref.at[n], sem.at[n]) for n in range(8)]
    for copy in copies:
        copy.start()
    for copy in copies:
        copy.wait()


def seat(tab, r, e):
    dx = (tab[PLACE + 2] - (r >> 2)) & 3
    dy = (tab[PLACE + 3] - (r & 3)) & 3
    first = e < 2
    return jnp.where(first, dy, 4 + dx), jnp.where(first, dx, dy), e & 1


def write_slabs(tab, p_ref, own_ref, oth_ref, e, base, d, tiles):
    h = tab[PLACE + 4]
    low = low_half()
    for zz in range(4):
        for ref, core in ((own_ref, h), (oth_ref, 1 - h)):
            rows = p_ref[base + 2 * zz + core]
            if d % 2 == 0:
                for m in range(tiles):
                    at = (d // 2 + m) * 128
                    ref[zz, e, m] = rows[:, at : at + 128]
            else:
                q = d // 2
                turned = []
                for m in range(tiles + 1):
                    at = (q + m) * 128
                    if at < rows.shape[1]:
                        turned.append(swap_halves(rows[:, at : at + 128]))
                    else:
                        turned.append(jnp.zeros((8, 128), F32))
                for m in range(tiles):
                    ref[zz, e, m] = jnp.where(low, turned[m], turned[m + 1])


def geometry(w):
    left = w + 1 + (w + 1) % 2
    return left, (left + 4 + w + 1 + 1) // 2


def step_body(tab, strips, w, own_ref, oth_ref, hi_ref, lo_ref, p_ref):
    left, count = geometry(w)
    nk = 4 + 2 * w
    for a in range(0, nk, 2):
        pair = []
        for b in (a, a + 1):
            pair.append(shifted(strips(b), left - 2 * w + b, count))
        store_split(hi_ref, lo_ref, a * 8, pair[0], pair[1])
    p_ref[...] = product(hi_ref, lo_ref, left * 64, 256).reshape(32, 8, count * 128)
    for e in range(4):
        write_slabs(tab, p_ref, own_ref, oth_ref, e, e * 8, left - (w + 1) + e, w + 2)


def first_step_kernel(tab, *refs):
    ins, (own_ref, oth_ref, cur_ref, hi_ref, lo_ref, p_ref, g_ref, sem) = refs[:8], refs[8:]
    fetch(ins, g_ref, sem)
    w = BAND
    base = tab[PLACE + 5] * 4 + 64 - w

    def strips(b):
        sk = tab[INV + ((base + b) & 63)]
        u, v, e = seat(tab, sk >> 2, sk & 3)
        strip = g_ref[u, v, e]
        if w <= b < w + 4:
            cur_ref[b - w] = strip
        return [strip[t] for t in range(w + 1)]

    step_body(tab, strips, w, own_ref, oth_ref, hi_ref, lo_ref, p_ref)


def step_kernel(w, reach, tab, *refs):
    n = 1 + 2 * len(reach)
    ins, (own_ref, oth_ref, hi_ref, lo_ref, p_ref) = refs[:n], refs[n:]

    def strips(b):
        off = b - w
        if 0 <= off < 4:
            ref, row = ins[0], off
        elif off < 0:
            d = (-off + 3) // 4
            ref, row = ins[2 * d - 1], off + 4 * (d - 1) + reach[d - 1]
        else:
            d = off // 4
            ref, row = ins[2 * d], off - 4 * d
        return [ref[row, t] for t in range(w + 1)]

    step_body(tab, strips, w, own_ref, oth_ref, hi_ref, lo_ref, p_ref)


def reach_of(w):
    return [min(4, w - 4 * d) for d in range((w + 3) // 4)]


def last_step_kernel(tab, *refs):
    ins, (own_ref, oth_ref, cur_ref, hi_ref, lo_ref, p_ref, g_ref, sem) = refs[:8], refs[8:]
    fetch(ins, g_ref, sem)
    w = BAND + STEPS - 1
    row0 = tab[PLACE] * 4
    left, count = w + 2, w + 2
    for e in range(4):
        i = tab[PERM + row0 + e]

        def strips(b):
            k = (i + b - w) & 63
            pos = k >> 2
            a, odd = pos >> 1, pos & 1
            r = jnp.where(a < 4, a * 4 + odd, (7 - a) * 4 + 3 - odd)
            u, v, ee = seat(tab, r, k & 3)
            strip = g_ref[u, v, ee]
            if b == w:
                cur_ref[e] = strip
            return [strip[t] for t in range(w + 1)]

        for a in range(0, 2 * w + 2, 2):
            one = shifted(strips(a), left - 2 * w + a, count)
            two = [None] * count
            if a + 1 <= 2 * w:
                two = shifted(strips(a + 1), left - 2 * w + a + 1, count)
            store_split(hi_ref, lo_ref, a * 8, one, two)
        p_ref[...] = product(hi_ref, lo_ref, left * 64, 64).reshape(8, 8, count * 128)
        write_slabs(tab, p_ref, own_ref, oth_ref, e, 0, 0, count)


def pair_kernel(tab, own_ref, got_ref, *outs):
    z = tab[PLACE + 6]
    for k in range(4):
        outs[k][...] = own_ref[z ^ k] + got_ref[z ^ k]


def polynomial(tab, step, cur, square):
    return jnp.where(tab[BRANCH + step] == 1, 2.0 * cur - square, square)


def close_kernel(step, cuts, tab, p0, p1, p2, p3, *refs):
    w = BAND + step
    if step == 0:
        cur_ref, refs = refs[0], refs[1:]
    else:
        cur_ref, refs = refs[0], refs[1:]
    low = low_half()
    i0 = tab[PLACE + 5] * 4
    for e in range(4):
        i = i0 + e
        turned = [swap_halves(cur_ref[e, t]) for t in range(w + 1)]
        zero = jnp.zeros((8, 128), F32)
        for m in range(w + 2):
            before = turned[m - 1] if m >= 1 else zero
            after = turned[m] if m <= w else zero
            cur = jnp.where(low, before, after)
            square = (p0[e, m] + p1[e, m]) + (p2[e, m] + p3[e, m])
            one = bit(tab, step + 1, i, (i + 2 * m + 63 - w) & 63)
            two = 0
            if 2 * m + 1 <= 2 * w + 2:
                two = bit(tab, step + 1, i, (i + 2 * m + 64 - w) & 63)
            keep = jnp.where(low, one, two) == 1
            value = jnp.where(keep, polynomial(tab, step, cur, square), 0.0)
            for ref, (lo, hi) in zip(refs, cuts):
                if lo <= e < hi:
                    ref[e - lo, m] = value


def finish_kernel(tab, p0, p1, p2, p3, cur_ref, y_ref):
    w = BAND + STEPS - 1
    low = low_half()
    row0 = tab[PLACE] * 4
    y_ref[...] = jnp.zeros_like(y_ref)
    for e in range(4):
        i = tab[PERM + row0 + e]
        for m in range(w + 2):
            cur = cur_ref[e, m - 1] if 1 <= m <= w + 1 else jnp.zeros((8, 128), F32)
            square = (p0[e, m] + p1[e, m]) + (p2[e, m] + p3[e, m])
            value = polynomial(tab, STEPS - 1, cur, square)
            turned = swap_halves(value)
            for half in (0, 1):
                v = 2 * m + half
                if v == 0:
                    continue
                j = (i + v + 64 - (w + 2)) & 63
                sj = tab[INV + j]
                odd = sj & 1
                piece = jnp.where(odd == half, value, turned)
                piece = jnp.where(bit(tab, STEPS, i, j) == 1, piece, 0.0)
                side = jnp.where(low, 0, 1) == odd
                c, t = sj >> 3, (sj & 7) >> 1
                y_ref[c, e, t] = jnp.where(side, piece, y_ref[c, e, t])


def join_kernel(tab, y_ref, out_ref):
    for c in range(8):
        for e in range(4):
            for t in range(4):
                out_ref[e * 64 + c * 8 : e * 64 + c * 8 + 8, t * 128 : (t + 1) * 128] = y_ref[c, e, t]


def tables(masks, branch, perm):
    r = lax.axis_index("row")
    z = lax.axis_index("col")
    h = lax.axis_index("layer")
    ids = jnp.arange(64, dtype=jnp.int32)
    inverse = jnp.sum(jnp.where(perm[:, None] == ids[None, :], ids[:, None], 0), axis=0)
    shifts = jnp.arange(32, dtype=jnp.int32)
    bits = jnp.sum(masks.reshape(6, 64, 2, 32) << shifts, axis=-1, dtype=jnp.int32)
    pos = jnp.sum(jnp.where(jnp.asarray(RING) == r, jnp.arange(16), 0))
    place = jnp.stack([r, z * 2 + h, r // 4, r % 4, h, pos, z, z]).astype(jnp.int32)
    return jnp.concatenate(
        [perm, inverse.astype(jnp.int32), branch, jnp.zeros((3,), jnp.int32), bits.reshape(-1), place]
    )


def reduce_group(tab, own, oth, tiles):
    got = core_swap(oth)
    parts = call(pair_kernel, [(4, tiles, 8, 128)] * 4, tab, [own, got])
    return [parts[0]] + [z_swap(parts[k], k) for k in (1, 2, 3)]


def exchange(value):
    return lax.all_to_all(value, GROUP, 0, 0, tiled=True)


def shards(density, masks, branch, perm):
    tab = tables(masks, branch, perm)
    (split,) = call(split_kernel, [(8, 4, 4, 8, 128)], tab, [density])
    split = exchange(split)
    halves = call(compact_kernel, [(2, BAND + 1, 8, 128)] * 2, tab, [split])
    gathered = gather_rows(*halves)
    for step in range(STEPS - 1):
        w = BAND + step
        left, count = geometry(w)
        rows = (4 + 2 * w) * 8
        part = (4, 4, w + 2, 8, 128)
        scratch = [
            pltpu.VMEM((rows, count * 128), BF16),
            pltpu.VMEM((rows, count * 128), BF16),
            pltpu.VMEM((32, 8, count * 128), F32),
        ]
        if step == 0:
            scratch += [pltpu.VMEM((8, 4, 2, w + 1, 8, 128), F32), pltpu.SemaphoreType.DMA((8,))]
            own, oth, cur = call(
                first_step_kernel, [part, part, (4, w + 1, 8, 128)], tab, gathered, scratch, True
            )
        else:
            reach = reach_of(w)
            kernel = lambda *refs, w=w, reach=reach: step_kernel(w, reach, *refs)
            own, oth = call(kernel, [part, part], tab, around, scratch)
        parts = reduce_group(tab, own, oth, w + 2)
        if step < STEPS - 2:
            reach = reach_of(w + 1)
            cuts = [(0, 4)]
            for n in reach:
                for cut in ((4 - n, 4), (0, n)):
                    if cut not in cuts:
                        cuts.append(cut)
        else:
            cuts = [(0, 2), (2, 4)]
        kernel = lambda *refs, step=step, cuts=cuts: close_kernel(step, cuts, *refs)
        shapes = [(hi - lo, w + 2, 8, 128) for lo, hi in cuts]
        pieces = call(kernel, shapes, tab, parts + [cur])
        if step < STEPS - 2:
            cur = pieces[0]
            around = [cur]
            for d, n in enumerate(reach):
                around.append(ring_shift(pieces[cuts.index((4 - n, 4))], d + 1))
                around.append(ring_shift(pieces[cuts.index((0, n))], -(d + 1)))
        else:
            gathered = gather_rows(*pieces)
    w = BAND + STEPS - 1
    part = (4, 4, w + 2, 8, 128)
    scratch = [
        pltpu.VMEM(((2 * w + 2) * 8, (w + 2) * 128), BF16),
        pltpu.VMEM(((2 * w + 2) * 8, (w + 2) * 128), BF16),
        pltpu.VMEM((8, 8, (w + 2) * 128), F32),
        pltpu.VMEM((8, 4, 2, w + 1, 8, 128), F32),
        pltpu.SemaphoreType.DMA((8,)),
    ]
    own, oth, cur = call(
        last_step_kernel, [part, part, (4, w + 1, 8, 128)], tab, gathered, scratch, True
    )
    parts = reduce_group(tab, own, oth, w + 2)
    (full,) = call(finish_kernel, [(8, 4, 4, 8, 128)], tab, parts + [cur])
    full = exchange(full)
    (out,) = call(join_kernel, [(256, 512)], tab, [full])
    return out


def solution(mesh):
    return jax.shard_map(
        shards,
        mesh=mesh,
        in_specs=(P("row", GROUP), P(), P(), P()),
        out_specs=P("row", GROUP),
        check_vma=False,
    )
```

time: 604 us -> 259 us (0.43)
  waiting for transfers between devices: 519 us -> 113 us
  starting transfers between devices: 0.76 us -> 85.2 us
  matrix products: 57.3 us -> 0 us
  blocking collectives: 0 us -> 30 us
  Pallas kernels: 0 us -> 23.9 us
  between operations: 16.9 us -> 0.32 us
    all_gather x10 -> x0, waiting for transfers between devices: 516 us -> none  [the longest x5 360 us: shards(): lax.all_gather(current, 'row', axis=0, tiled=True)]
    ppermute x0 -> x58, waiting for transfers between devices: none -> 113 us  [the longest x15 42.8 us: z_swap(): return lax.ppermute(value, 'col', [(i, i ^ k) for i in range(4)])]
    ppermute x0 -> x58, starting transfers between devices: none -> 85.2 us  [the longest x24 35.3 us: xy_shift(): lax.ppermute(value, 'row', [(i, (i // 4 + dx) % 4 * 4 + (i % 4 + dy) % 4)...]
    dot_general x5 -> x0, matrix products: 57.3 us -> none  [shards(): jnp.dot(panel, lax.all_gather(current, 'row', axis=0, tiled=True), prefer...]
    all_to_all x0 -> x2, blocking collectives: none -> 30 us  [exchange(): return lax.all_to_all(value, GROUP, 0, 0, tiled=True)]
    pallas_call x0 -> x18, Pallas kernels: none -> 23.9 us  [call(): pl.pallas_call(kernel, out_shape=[jax.ShapeDtypeStruct(o, F32) for o in o...]
  transfers between devices with their start and end apart: 10 -> 58, of which waited for: 10 -> 45; matrix products, arithmetic and copies ran while one was open for 1% -> 0% of each run, Pallas kernels for 0% -> 0%
where the time goes in v1:
time: 259 us; the launch traced here: 257 us
  waiting for transfers between devices  113 us (44%)
  starting transfers between devices  85.2 us (33%)
  blocking collectives  30 us (12%)
  Pallas kernels  23.9 us (9%)
  local copies, waits for them, and re-layouts  3.31 us (1%)
    ppermute x15, waiting for transfers between devices, z_swap(): return lax.ppermute(value, 'col', [(i, i ^ k) for i in range(4)])  42.8 us
    ppermute x24, starting transfers between devices, xy_shift(): lax.ppermute(value, 'row', [(i, (i // 4 + dx) % 4 * 4 + (i % 4 + dy) % 4)...  35.3 us
    ppermute x24, waiting for transfers between devices, xy_shift(): lax.ppermute(value, 'row', [(i, (i // 4 + dx) % 4 * 4 + (i % 4 + dy) % 4)...  35.3 us
    all_to_all x2, blocking collectives, exchange(): return lax.all_to_all(value, GROUP, 0, 0, tiled=True)  30 us
    ppermute x14, waiting for transfers between devices, ring_shift(): lax.ppermute(value, 'row', [(RING[p], RING[(p + k) % 16]) for p in range(...  26.5 us
    pallas_call x18, Pallas kernels, call(): pl.pallas_call(kernel, out_shape=[jax.ShapeDtypeStruct(o, F32) for o in o...  23.9 us
    ppermute x15, starting transfers between devices, z_swap(): return lax.ppermute(value, 'col', [(i, i ^ k) for i in range(4)])  19.7 us
    ppermute x5, starting transfers between devices, core_swap(): return lax.ppermute(value, 'layer', [(0, 1), (1, 0)])  17.5 us
  transfers between devices with their start and end apart: 58, of which 45 were waited for; matrix products, arithmetic and copies ran while one was open for 0% of the time, Pallas kernels for 0%

profile of v1, /device:TPU:1, one launch (start us, length us, event | category | flops | bytes accessed | tf_op | source)
XLA Modules:
  0.0 256.9 jit_solution(17788723807626287282)
XLA Ops:
  4.8 16.0 %all_to_all.10.x_ref = f32[8,4,4,8,128]{4,3,2,1,0:T(8,128)S(1)} all-to-all(f32[8,4,4,8,128]{4,3,2,1,0:T(8,128)S(1)} %shard_map.55), channel_id=1, replica_groups=mesh['row'=16,'col'=4,'layer'=2] {'col','layer'}, dimensions={0} | all-to-all | bytes 1048576 | tf_op jit(solution)/shard_map/all_to_all | solution.py:362
  21.8 2.8 %collective-permute-start.8 = (f32[2,7,8,128]{3,2,1,0:T(8,128)S(1)}, f32[2,7,8,128]{3,2,1,0:T(8,128)S(1)}, u32[]{:S(2)}, u32[]{:S(2)}) collective-permute-start(f32[2,7,8,128]{3,2,1,0:T(8,128)S(1)} %get-tuple-element.48), channel_id=1, source_target_pairs={{0,24},{8,0},{16,8},{24,16},{32,56},{40,32},{48,40},{56,48},{64,88... | collective-permute-start | bytes 172040 | tf_op jit(solution)/shard_map/ppermute | solution.py:29
  25.8 3.3 %collective-permute-done.7 = f32[2,7,8,128]{3,2,1,0:T(8,128)S(1)} collective-permute-done((f32[2,7,8,128]{3,2,1,0:T(8,128)S(1)}, f32[2,7,8,128]{3,2,1,0:T(8,128)S(1)}, u32[]{:S(2)}, u32[]{:S(2)}) %collective-permute-start.7) | collective-permute-done | bytes 57376 | tf_op jit(solution)/shard_map/ppermute | solution.py:29
  29.7 2.5 collective-permute-start.11
  33.8 3.6 %collective-permute-start.10 = (f32[4,2,7,8,128]{4,3,2,1,0:T(8,128)S(1)}, f32[4,2,7,8,128]{4,3,2,1,0:T(8,128)S(1)}, u32[]{:S(2)}, u32[]{:S(2)}) collective-permute-start(f32[4,2,7,8,128]{4,3,2,1,0:T(8,128)S(1)} %pad_maximum_fusion.3.refs_4_), channel_id=1, source_target_pairs={{0,64},{8,72},{16,80},{24,88},{32,96},{40,104},{48,112},{56,120},{... | collective-permute-start | bytes 688136 | tf_op jit(solution)/shard_map/ppermute | solution.py:29
  42.1 5.4 %collective-permute-done.9.refs_5_ = f32[4,2,7,8,128]{4,3,2,1,0:T(8,128)S(1)} collective-permute-done((f32[4,2,7,8,128]{4,3,2,1,0:T(8,128)S(1)}, f32[4,2,7,8,128]{4,3,2,1,0:T(8,128)S(1)}, u32[]{:S(2)}, u32[]{:S(2)}) %collective-permute-start.9) | collective-permute-done | bytes 229408 | tf_op jit(solution)/shard_map/ppermute | solution.py:29
  47.8 4.1 %shard_map.57 = (f32[4,4,8,8,128]{4,3,2,1,0:T(8,128)S(1)}, f32[4,4,8,8,128]{4,3,2,1,0:T(8,128)S(1)}, f32[4,7,8,128]{3,2,1,0:T(8,128)S(1)}) custom-call(s32[912]{0:T(1024)S(1)} %concatenate.3.tab.refs_0_, f32[4,2,7,8,128]{4,3,2,1,0:T(8,128)S(1)} %pad_maximum_fusion.2.refs_0_, f32[4,2,7,8,128]{4,3,2,1,0:T(8,128)S(1)} %collective-permute-done.3.refs_1_, ...), custom_call_target="tpu_custom_call" | custom-call | tf_op jit(solution)/shard_map/pallas_call | solution.py:96
  51.9 8.8 %collective-permute-start.12 = (f32[4,4,8,8,128]{4,3,2,1,0:T(8,128)S(1)}, f32[4,4,8,8,128]{4,3,2,1,0:T(8,128)S(1)}, u32[]{:S(2)}, u32[]{:S(2)}) collective-permute-start(f32[4,4,8,8,128]{4,3,2,1,0:T(8,128)S(1)} %get-tuple-element.50), channel_id=1, source_target_pairs={{0,1},{1,0},{2,3},{3,2},{4,5},{5,4},{6,7},{7,6},{8,9},{9,8},{10,11... | collective-permute-start | bytes 1572872 | tf_op jit(solution)/shard_map/ppermute | solution.py:39
  67.7 3.4 %collective-permute-done.14.refs_3_ = f32[4,8,8,128]{3,2,1,0:T(8,128)S(1)} collective-permute-done((f32[4,8,8,128]{3,2,1,0:T(8,128)S(1)}, f32[4,8,8,128]{3,2,1,0:T(8,128)S(1)}, u32[]{:S(2)}, u32[]{:S(2)}) %collective-permute-start.14) | collective-permute-done | bytes 131104 | tf_op jit(solution)/shard_map/ppermute | solution.py:35
  71.1 2.5 collective-permute-done.15.refs_4_
  75.9 2.7 %collective-permute-start.19 = (f32[3,8,8,128]{3,2,1,0:T(8,128)S(1)}, f32[3,8,8,128]{3,2,1,0:T(8,128)S(1)}, u32[]{:S(2)}, u32[]{:S(2)}) collective-permute-start(f32[3,8,8,128]{3,2,1,0:T(8,128)S(1)} %get-tuple-element.58), channel_id=1, source_target_pairs={{0,24},{8,16},{32,0},{40,8},{64,32},{72,40},{96,64},{104,72},{120,... | collective-permute-start | bytes 294920 | tf_op jit(solution)/shard_map/ppermute | solution.py:25
  90.2 3.0 %collective-permute-start.22 = (f32[4,9,8,128]{3,2,1,0:T(8,128)S(1)}, f32[4,9,8,128]{3,2,1,0:T(8,128)S(1)}, u32[]{:S(2)}, u32[]{:S(2)}) collective-permute-start(f32[4,9,8,128]{3,2,1,0:T(8,128)S(1)} %get-tuple-element.63), channel_id=1, source_target_pairs={{0,4},{2,6},{4,0},{6,2},{1,5},{3,7},{5,1},{7,3},{8,12},{10,14},{12... | collective-permute-start | bytes 442376 | tf_op jit(solution)/shard_map/ppermute | solution.py:35
  95.2 4.7 %collective-permute-done.22.refs_3_ = f32[4,9,8,128]{3,2,1,0:T(8,128)S(1)} collective-permute-done((f32[4,9,8,128]{3,2,1,0:T(8,128)S(1)}, f32[4,9,8,128]{3,2,1,0:T(8,128)S(1)}, u32[]{:S(2)}, u32[]{:S(2)}) %collective-permute-start.22) | collective-permute-done | bytes 147488 | tf_op jit(solution)/shard_map/ppermute | solution.py:35
  109.5 6.5 %collective-permute-done.24.refs_2_ = f32[4,9,8,128]{3,2,1,0:T(8,128)S(1)} collective-permute-done((f32[4,9,8,128]{3,2,1,0:T(8,128)S(1)}, f32[4,9,8,128]{3,2,1,0:T(8,128)S(1)}, u32[]{:S(2)}, u32[]{:S(2)}) %collective-permute-start.24) | collective-permute-done | bytes 147488 | tf_op jit(solution)/shard_map/ppermute | solution.py:25
  117.8 2.6 %collective-permute-start.28 = (f32[4,4,10,8,128]{4,3,2,1,0:T(8,128)S(1)}, f32[4,4,10,8,128]{4,3,2,1,0:T(8,128)S(1)}, u32[]{:S(2)}, u32[]{:S(2)}) collective-permute-start(f32[4,4,10,8,128]{4,3,2,1,0:T(8,128)S(1)} %get-tuple-element.66), channel_id=1, source_target_pairs={{0,1},{1,0},{2,3},{3,2},{4,5},{5,4},{6,7},{7,6},{8,9},{9,8},{10,11... | collective-permute-start | bytes 1966088 | tf_op jit(solution)/shard_map/ppermute | solution.py:39
  128.3 4.2 %collective-permute-done.30.refs_3_ = f32[4,10,8,128]{3,2,1,0:T(8,128)S(1)} collective-permute-done((f32[4,10,8,128]{3,2,1,0:T(8,128)S(1)}, f32[4,10,8,128]{3,2,1,0:T(8,128)S(1)}, u32[]{:S(2)}, u32[]{:S(2)}) %collective-permute-start.30) | collective-permute-done | bytes 163872 | tf_op jit(solution)/shard_map/ppermute | solution.py:35
  132.4 2.7 %collective-permute-done.31.refs_4_ = f32[4,10,8,128]{3,2,1,0:T(8,128)S(1)} collective-permute-done((f32[4,10,8,128]{3,2,1,0:T(8,128)S(1)}, f32[4,10,8,128]{3,2,1,0:T(8,128)S(1)}, u32[]{:S(2)}, u32[]{:S(2)}) %collective-permute-start.31) | collective-permute-done | bytes 163872 | tf_op jit(solution)/shard_map/ppermute | solution.py:35
  139.3 5.3 %collective-permute-done.36.refs_6_ = f32[1,10,8,128]{3,2,1,0:T(8,128)S(1)} collective-permute-done((f32[1,10,8,128]{3,2,1,0:T(8,128)S(1)}, f32[1,10,8,128]{3,2,1,0:T(8,128)S(1)}, u32[]{:S(2)}, u32[]{:S(2)}) %collective-permute-start.36) | collective-permute-done | bytes 40992 | tf_op jit(solution)/shard_map/ppermute | solution.py:25
  148.7 3.7 %collective-permute-done.32.refs_2_ = f32[4,10,8,128]{3,2,1,0:T(8,128)S(1)} collective-permute-done((f32[4,10,8,128]{3,2,1,0:T(8,128)S(1)}, f32[4,10,8,128]{3,2,1,0:T(8,128)S(1)}, u32[]{:S(2)}, u32[]{:S(2)}) %collective-permute-start.32) | collective-permute-done | bytes 163872 | tf_op jit(solution)/shard_map/ppermute | solution.py:25
  158.4 3.0 %collective-permute-start.40 = (f32[4,11,8,128]{3,2,1,0:T(8,128)S(1)}, f32[4,11,8,128]{3,2,1,0:T(8,128)S(1)}, u32[]{:S(2)}, u32[]{:S(2)}) collective-permute-start(f32[4,11,8,128]{3,2,1,0:T(8,128)S(1)} %get-tuple-element.78), channel_id=1, source_target_pairs={{0,4},{2,6},{4,0},{6,2},{1,5},{3,7},{5,1},{7,3},{8,12},{10,14},{12... | collective-permute-start | bytes 540680 | tf_op jit(solution)/shard_map/ppermute | solution.py:35
  164.1 5.4 %collective-permute-done.40.refs_3_ = f32[4,11,8,128]{3,2,1,0:T(8,128)S(1)} collective-permute-done((f32[4,11,8,128]{3,2,1,0:T(8,128)S(1)}, f32[4,11,8,128]{3,2,1,0:T(8,128)S(1)}, u32[]{:S(2)}, u32[]{:S(2)}) %collective-permute-start.40) | collective-permute-done | bytes 180256 | tf_op jit(solution)/shard_map/ppermute | solution.py:35
  169.5 2.5 collective-permute-done.41.refs_4_
  180.3 4.1 %collective-permute-start.53 = (f32[4,2,11,8,128]{4,3,2,1,0:T(8,128)S(1)}, f32[4,2,11,8,128]{4,3,2,1,0:T(8,128)S(1)}, u32[]{:S(2)}, u32[]{:S(2)}) collective-permute-start(f32[4,2,11,8,128]{4,3,2,1,0:T(8,128)S(1)} %pad_maximum_fusion.1.refs_4_), channel_id=1, source_target_pairs={{0,96},{8,104},{16,112},{24,120},{32,0},{40,8},{48,16},{56,24},{64... | collective-permute-start | bytes 1081352 | tf_op jit(solution)/shard_map/ppermute | solution.py:29
  185.8 3.6 %collective-permute-start.52 = (f32[4,2,11,8,128]{4,3,2,1,0:T(8,128)S(1)}, f32[4,2,11,8,128]{4,3,2,1,0:T(8,128)S(1)}, u32[]{:S(2)}, u32[]{:S(2)}) collective-permute-start(f32[4,2,11,8,128]{4,3,2,1,0:T(8,128)S(1)} %pad_maximum_fusion.1.refs_4_), channel_id=1, source_target_pairs={{0,64},{8,72},{16,80},{24,88},{32,96},{40,104},{48,112},{56,120},{... | collective-permute-start | bytes 1081352 | tf_op jit(solution)/shard_map/ppermute | solution.py:29
  189.4 3.8 %collective-permute-done.44 = f32[2,11,8,128]{3,2,1,0:T(8,128)S(1)} collective-permute-done((f32[2,11,8,128]{3,2,1,0:T(8,128)S(1)}, f32[2,11,8,128]{3,2,1,0:T(8,128)S(1)}, u32[]{:S(2)}, u32[]{:S(2)}) %collective-permute-start.44) | collective-permute-done | bytes 90144 | tf_op jit(solution)/shard_map/ppermute | solution.py:29
  194.2 9.1 %collective-permute-start.46 = (f32[4,2,11,8,128]{4,3,2,1,0:T(8,128)S(1)}, f32[4,2,11,8,128]{4,3,2,1,0:T(8,128)S(1)}, u32[]{:S(2)}, u32[]{:S(2)}) collective-permute-start(f32[4,2,11,8,128]{4,3,2,1,0:T(8,128)S(1)} %pad_maximum_fusion.refs_0_), channel_id=1, source_target_pairs={{0,16},{8,24},{16,0},{24,8},{32,48},{40,56},{48,32},{56,40},{64,80... | collective-permute-start | bytes 1081352 | tf_op jit(solution)/shard_map/ppermute | solution.py:29
  204.8 3.4 %collective-permute-done.46.refs_2_ = f32[4,2,11,8,128]{4,3,2,1,0:T(8,128)S(1)} collective-permute-done((f32[4,2,11,8,128]{4,3,2,1,0:T(8,128)S(1)}, f32[4,2,11,8,128]{4,3,2,1,0:T(8,128)S(1)}, u32[]{:S(2)}, u32[]{:S(2)}) %collective-permute-start.46) | collective-permute-done | bytes 360480 | tf_op jit(solution)/shard_map/ppermute | solution.py:29
  208.2 9.3 %collective-permute-done.45.refs_1_ = f32[4,2,11,8,128]{4,3,2,1,0:T(8,128)S(1)} collective-permute-done((f32[4,2,11,8,128]{4,3,2,1,0:T(8,128)S(1)}, f32[4,2,11,8,128]{4,3,2,1,0:T(8,128)S(1)}, u32[]{:S(2)}, u32[]{:S(2)}) %collective-permute-start.45) | collective-permute-done | bytes 360480 | tf_op jit(solution)/shard_map/ppermute | solution.py:29
  217.5 3.8 %shard_map.69 = (f32[4,4,12,8,128]{4,3,2,1,0:T(8,128)S(1)}, f32[4,4,12,8,128]{4,3,2,1,0:T(8,128)S(1)}, f32[4,11,8,128]{3,2,1,0:T(8,128)S(1)}) custom-call(s32[912]{0:T(1024)S(1)} %concatenate.3.tab.refs_0_, f32[4,2,11,8,128]{4,3,2,1,0:T(8,128)S(1)} %pad_maximum_fusion.refs_0_, f32[4,2,11,8,128]{4,3,2,1,0:T(8,128)S(1)} %collective-permute-done.45.refs_1_, ...), custom_call_target="tpu_custom_call" | custom-call | tf_op jit(solution)/shard_map/pallas_call | solution.py:96
  221.3 2.9 %collective-permute-start.54 = (f32[4,4,12,8,128]{4,3,2,1,0:T(8,128)S(1)}, f32[4,4,12,8,128]{4,3,2,1,0:T(8,128)S(1)}, u32[]{:S(2)}, u32[]{:S(2)}) collective-permute-start(f32[4,4,12,8,128]{4,3,2,1,0:T(8,128)S(1)} %get-tuple-element.83), channel_id=1, source_target_pairs={{0,1},{1,0},{2,3},{3,2},{4,5},{5,4},{6,7},{7,6},{8,9},{9,8},{10,11... | collective-permute-start | bytes 2359304 | tf_op jit(solution)/shard_map/ppermute | solution.py:39
  233.0 4.9 %collective-permute-done.56.p2 = f32[4,12,8,128]{3,2,1,0:T(8,128)S(1)} collective-permute-done((f32[4,12,8,128]{3,2,1,0:T(8,128)S(1)}, f32[4,12,8,128]{3,2,1,0:T(8,128)S(1)}, u32[]{:S(2)}, u32[]{:S(2)}) %collective-permute-start.56) | collective-permute-done | bytes 196640 | tf_op jit(solution)/shard_map/ppermute | solution.py:35
  241.5 14.0 %all_to_all.11.y_ref = f32[8,4,4,8,128]{4,3,2,1,0:T(8,128)S(1)} all-to-all(f32[8,4,4,8,128]{4,3,2,1,0:T(8,128)S(1)} %shard_map.71), channel_id=1, replica_groups=mesh['row'=16,'col'=4,'layer'=2] {'col','layer'}, dimensions={0} | all-to-all | bytes 1048576 | tf_op jit(solution)/shard_map/all_to_all | solution.py:362
  (124 shorter events, 99.1 us)
Async XLA Ops:
  29.7 9.3 %collective-permute-start.11 = (f32[4,2,7,8,128]{4,3,2,1,0:T(8,128)S(1)}, f32[4,2,7,8,128]{4,3,2,1,0:T(8,128)S(1)}, u32[]{:S(2)}, u32[]{:S(2)}) collective-permute-start(f32[4,2,7,8,128]{4,3,2,1,0:T(8,128)S(1)} %pad_maximum_fusion.3.refs_4_), channel_id=1, source_target_pairs={{0,96},{8,104},{16,112},{24,120},{32,0},{40,8},{48,16},{56,24},{64... | collective-permute-start | bytes 688136 | tf_op jit(solution)/shard_map/ppermute | solution.py:29
  33.8 8.3 %collective-permute-start.10 = (f32[4,2,7,8,128]{4,3,2,1,0:T(8,128)S(1)}, f32[4,2,7,8,128]{4,3,2,1,0:T(8,128)S(1)}, u32[]{:S(2)}, u32[]{:S(2)}) collective-permute-start(f32[4,2,7,8,128]{4,3,2,1,0:T(8,128)S(1)} %pad_maximum_fusion.3.refs_4_), channel_id=1, source_target_pairs={{0,64},{8,72},{16,80},{24,88},{32,96},{40,104},{48,112},{56,120},{... | collective-permute-start | bytes 688136 | tf_op jit(solution)/shard_map/ppermute | solution.py:29
  37.3 10.2 %collective-permute-start.9 = (f32[4,2,7,8,128]{4,3,2,1,0:T(8,128)S(1)}, f32[4,2,7,8,128]{4,3,2,1,0:T(8,128)S(1)}, u32[]{:S(2)}, u32[]{:S(2)}) collective-permute-start(f32[4,2,7,8,128]{4,3,2,1,0:T(8,128)S(1)} %pad_maximum_fusion.3.refs_4_), channel_id=1, source_target_pairs={{0,32},{8,40},{16,48},{24,56},{32,64},{40,72},{48,80},{56,88},{64,... | collective-permute-start | bytes 688136 | tf_op jit(solution)/shard_map/ppermute | solution.py:29
  38.0 9.5 %collective-permute-start.5 = (f32[4,2,7,8,128]{4,3,2,1,0:T(8,128)S(1)}, f32[4,2,7,8,128]{4,3,2,1,0:T(8,128)S(1)}, u32[]{:S(2)}, u32[]{:S(2)}) collective-permute-start(f32[4,2,7,8,128]{4,3,2,1,0:T(8,128)S(1)} %pad_maximum_fusion.2.refs_0_), channel_id=1, source_target_pairs={{0,24},{8,0},{16,8},{24,16},{32,56},{40,32},{48,40},{56,48},{64,88... | collective-permute-start | bytes 688136 | tf_op jit(solution)/shard_map/ppermute | solution.py:29
  38.6 8.9 %collective-permute-start.4 = (f32[4,2,7,8,128]{4,3,2,1,0:T(8,128)S(1)}, f32[4,2,7,8,128]{4,3,2,1,0:T(8,128)S(1)}, u32[]{:S(2)}, u32[]{:S(2)}) collective-permute-start(f32[4,2,7,8,128]{4,3,2,1,0:T(8,128)S(1)} %pad_maximum_fusion.2.refs_0_), channel_id=1, source_target_pairs={{0,16},{8,24},{16,0},{24,8},{32,48},{40,56},{48,32},{56,40},{64,80... | collective-permute-start | bytes 688136 | tf_op jit(solution)/shard_map/ppermute | solution.py:29
  39.0 8.8 %collective-permute-start.3 = (f32[4,2,7,8,128]{4,3,2,1,0:T(8,128)S(1)}, f32[4,2,7,8,128]{4,3,2,1,0:T(8,128)S(1)}, u32[]{:S(2)}, u32[]{:S(2)}) collective-permute-start(f32[4,2,7,8,128]{4,3,2,1,0:T(8,128)S(1)} %pad_maximum_fusion.2.refs_0_), channel_id=1, source_target_pairs={{0,8},{8,16},{16,24},{24,0},{32,40},{40,48},{48,56},{56,32},{64,72... | collective-permute-start | bytes 688136 | tf_op jit(solution)/shard_map/ppermute | solution.py:29
  51.9 10.3 %collective-permute-start.12 = (f32[4,4,8,8,128]{4,3,2,1,0:T(8,128)S(1)}, f32[4,4,8,8,128]{4,3,2,1,0:T(8,128)S(1)}, u32[]{:S(2)}, u32[]{:S(2)}) collective-permute-start(f32[4,4,8,8,128]{4,3,2,1,0:T(8,128)S(1)} %get-tuple-element.50), channel_id=1, source_target_pairs={{0,1},{1,0},{2,3},{3,2},{4,5},{5,4},{6,7},{7,6},{8,9},{9,8},{10,11... | collective-permute-start | bytes 1572872 | tf_op jit(solution)/shard_map/ppermute | solution.py:39
  65.0 8.6 %collective-permute-start.15 = (f32[4,8,8,128]{3,2,1,0:T(8,128)S(1)}, f32[4,8,8,128]{3,2,1,0:T(8,128)S(1)}, u32[]{:S(2)}, u32[]{:S(2)}) collective-permute-start(f32[4,8,8,128]{3,2,1,0:T(8,128)S(1)} %get-tuple-element.54), channel_id=1, source_target_pairs={{0,6},{2,4},{4,2},{6,0},{1,7},{3,5},{5,3},{7,1},{8,14},{10,12},{12... | collective-permute-start | bytes 393224 | tf_op jit(solution)/shard_map/ppermute | solution.py:35
  74.4 8.3 %collective-permute-start.17 = (f32[4,8,8,128]{3,2,1,0:T(8,128)S(1)}, f32[4,8,8,128]{3,2,1,0:T(8,128)S(1)}, u32[]{:S(2)}, u32[]{:S(2)}) collective-permute-start(f32[4,8,8,128]{3,2,1,0:T(8,128)S(1)} %get-tuple-element.56.refs_1_.refs_5_), channel_id=1, source_target_pairs={{0,16},{8,0},{32,8},{40,32},{64,40},{72,64},{96,72},{104,96},{120,... | collective-permute-start | bytes 393224 | tf_op jit(solution)/shard_map/ppermute | solution.py:25
  74.6 9.9 %collective-permute-start.16 = (f32[4,8,8,128]{3,2,1,0:T(8,128)S(1)}, f32[4,8,8,128]{3,2,1,0:T(8,128)S(1)}, u32[]{:S(2)}, u32[]{:S(2)}) collective-permute-start(f32[4,8,8,128]{3,2,1,0:T(8,128)S(1)} %get-tuple-element.56.refs_1_.refs_5_), channel_id=1, source_target_pairs={{0,8},{8,32},{32,40},{40,64},{64,72},{72,96},{96,104},{104,120},{1... | collective-permute-start | bytes 393224 | tf_op jit(solution)/shard_map/ppermute | solution.py:25
  90.2 9.8 %collective-permute-start.22 = (f32[4,9,8,128]{3,2,1,0:T(8,128)S(1)}, f32[4,9,8,128]{3,2,1,0:T(8,128)S(1)}, u32[]{:S(2)}, u32[]{:S(2)}) collective-permute-start(f32[4,9,8,128]{3,2,1,0:T(8,128)S(1)} %get-tuple-element.63), channel_id=1, source_target_pairs={{0,4},{2,6},{4,0},{6,2},{1,5},{3,7},{5,1},{7,3},{8,12},{10,14},{12... | collective-permute-start | bytes 442376 | tf_op jit(solution)/shard_map/ppermute | solution.py:35
  93.1 9.3 %collective-permute-start.23 = (f32[4,9,8,128]{3,2,1,0:T(8,128)S(1)}, f32[4,9,8,128]{3,2,1,0:T(8,128)S(1)}, u32[]{:S(2)}, u32[]{:S(2)}) collective-permute-start(f32[4,9,8,128]{3,2,1,0:T(8,128)S(1)} %get-tuple-element.64), channel_id=1, source_target_pairs={{0,6},{2,4},{4,2},{6,0},{1,7},{3,5},{5,3},{7,1},{8,14},{10,12},{12... | collective-permute-start | bytes 442376 | tf_op jit(solution)/shard_map/ppermute | solution.py:35
  105.7 10.2 %collective-permute-start.24 = (f32[4,9,8,128]{3,2,1,0:T(8,128)S(1)}, f32[4,9,8,128]{3,2,1,0:T(8,128)S(1)}, u32[]{:S(2)}, u32[]{:S(2)}) collective-permute-start(f32[4,9,8,128]{3,2,1,0:T(8,128)S(1)} %shard_map.62.refs_1_.refs_5_), channel_id=1, source_target_pairs={{0,8},{8,32},{32,40},{40,64},{64,72},{72,96},{96,104},{104,120},{1... | collective-permute-start | bytes 442376 | tf_op jit(solution)/shard_map/ppermute | solution.py:25
  122.9 9.6 %collective-permute-start.30 = (f32[4,10,8,128]{3,2,1,0:T(8,128)S(1)}, f32[4,10,8,128]{3,2,1,0:T(8,128)S(1)}, u32[]{:S(2)}, u32[]{:S(2)}) collective-permute-start(f32[4,10,8,128]{3,2,1,0:T(8,128)S(1)} %get-tuple-element.69), channel_id=1, source_target_pairs={{0,4},{2,6},{4,0},{6,2},{1,5},{3,7},{5,1},{7,3},{8,12},{10,14},{12... | collective-permute-start | bytes 491528 | tf_op jit(solution)/shard_map/ppermute | solution.py:35
  124.9 10.2 %collective-permute-start.31 = (f32[4,10,8,128]{3,2,1,0:T(8,128)S(1)}, f32[4,10,8,128]{3,2,1,0:T(8,128)S(1)}, u32[]{:S(2)}, u32[]{:S(2)}) collective-permute-start(f32[4,10,8,128]{3,2,1,0:T(8,128)S(1)} %get-tuple-element.70), channel_id=1, source_target_pairs={{0,6},{2,4},{4,2},{6,0},{1,7},{3,5},{5,3},{7,1},{8,14},{10,12},{12... | collective-permute-start | bytes 491528 | tf_op jit(solution)/shard_map/ppermute | solution.py:35
  135.9 12.8 %collective-permute-start.35 = (f32[4,10,8,128]{3,2,1,0:T(8,128)S(1)}, f32[4,10,8,128]{3,2,1,0:T(8,128)S(1)}, u32[]{:S(2)}, u32[]{:S(2)}) collective-permute-start(f32[4,10,8,128]{3,2,1,0:T(8,128)S(1)} %get-tuple-element.71.refs_1_.refs_5_), channel_id=1, source_target_pairs={{0,24},{8,16},{32,0},{40,8},{64,32},{72,40},{96,64},{104,72},{120,... | collective-permute-start | bytes 491528 | tf_op jit(solution)/shard_map/ppermute | solution.py:25
  136.0 12.7 %collective-permute-start.34 = (f32[4,10,8,128]{3,2,1,0:T(8,128)S(1)}, f32[4,10,8,128]{3,2,1,0:T(8,128)S(1)}, u32[]{:S(2)}, u32[]{:S(2)}) collective-permute-start(f32[4,10,8,128]{3,2,1,0:T(8,128)S(1)} %get-tuple-element.71.refs_1_.refs_5_), channel_id=1, source_target_pairs={{0,32},{8,40},{32,64},{40,72},{64,96},{72,104},{96,120},{104,112},... | collective-permute-start | bytes 491528 | tf_op jit(solution)/shard_map/ppermute | solution.py:25
  137.4 11.2 %collective-permute-start.33 = (f32[4,10,8,128]{3,2,1,0:T(8,128)S(1)}, f32[4,10,8,128]{3,2,1,0:T(8,128)S(1)}, u32[]{:S(2)}, u32[]{:S(2)}) collective-permute-start(f32[4,10,8,128]{3,2,1,0:T(8,128)S(1)} %get-tuple-element.71.refs_1_.refs_5_), channel_id=1, source_target_pairs={{0,16},{8,0},{32,8},{40,32},{64,40},{72,64},{96,72},{104,96},{120,... | collective-permute-start | bytes 491528 | tf_op jit(solution)/shard_map/ppermute | solution.py:25
  137.6 14.7 %collective-permute-start.32 = (f32[4,10,8,128]{3,2,1,0:T(8,128)S(1)}, f32[4,10,8,128]{3,2,1,0:T(8,128)S(1)}, u32[]{:S(2)}, u32[]{:S(2)}) collective-permute-start(f32[4,10,8,128]{3,2,1,0:T(8,128)S(1)} %get-tuple-element.71.refs_1_.refs_5_), channel_id=1, source_target_pairs={{0,8},{8,32},{32,40},{40,64},{64,72},{72,96},{96,104},{104,120},{1... | collective-permute-start | bytes 491528 | tf_op jit(solution)/shard_map/ppermute | solution.py:25
  158.4 11.2 %collective-permute-start.40 = (f32[4,11,8,128]{3,2,1,0:T(8,128)S(1)}, f32[4,11,8,128]{3,2,1,0:T(8,128)S(1)}, u32[]{:S(2)}, u32[]{:S(2)}) collective-permute-start(f32[4,11,8,128]{3,2,1,0:T(8,128)S(1)} %get-tuple-element.78), channel_id=1, source_target_pairs={{0,4},{2,6},{4,0},{6,2},{1,5},{3,7},{5,1},{7,3},{8,12},{10,14},{12... | collective-permute-start | bytes 540680 | tf_op jit(solution)/shard_map/ppermute | solution.py:35
  161.3 10.7 %collective-permute-start.41 = (f32[4,11,8,128]{3,2,1,0:T(8,128)S(1)}, f32[4,11,8,128]{3,2,1,0:T(8,128)S(1)}, u32[]{:S(2)}, u32[]{:S(2)}) collective-permute-start(f32[4,11,8,128]{3,2,1,0:T(8,128)S(1)} %get-tuple-element.79), channel_id=1, source_target_pairs={{0,6},{2,4},{4,2},{6,0},{1,7},{3,5},{5,3},{7,1},{8,14},{10,12},{12... | collective-permute-start | bytes 540680 | tf_op jit(solution)/shard_map/ppermute | solution.py:35
  180.3 23.0 %collective-permute-start.53 = (f32[4,2,11,8,128]{4,3,2,1,0:T(8,128)S(1)}, f32[4,2,11,8,128]{4,3,2,1,0:T(8,128)S(1)}, u32[]{:S(2)}, u32[]{:S(2)}) collective-permute-start(f32[4,2,11,8,128]{4,3,2,1,0:T(8,128)S(1)} %pad_maximum_fusion.1.refs_4_), channel_id=1, source_target_pairs={{0,96},{8,104},{16,112},{24,120},{32,0},{40,8},{48,16},{56,24},{64... | collective-permute-start | bytes 1081352 | tf_op jit(solution)/shard_map/ppermute | solution.py:29
  184.4 8.8 %collective-permute-start.44 = (f32[2,11,8,128]{3,2,1,0:T(8,128)S(1)}, f32[2,11,8,128]{3,2,1,0:T(8,128)S(1)}, u32[]{:S(2)}, u32[]{:S(2)}) collective-permute-start(f32[2,11,8,128]{3,2,1,0:T(8,128)S(1)} %get-tuple-element.80), channel_id=1, source_target_pairs={{0,96},{8,104},{16,112},{24,120},{32,0},{40,8},{48,16},{56,24},{64... | collective-permute-start | bytes 270344 | tf_op jit(solution)/shard_map/ppermute | solution.py:29
  184.4 8.8 %collective-permute-start.43 = (f32[2,11,8,128]{3,2,1,0:T(8,128)S(1)}, f32[2,11,8,128]{3,2,1,0:T(8,128)S(1)}, u32[]{:S(2)}, u32[]{:S(2)}) collective-permute-start(f32[2,11,8,128]{3,2,1,0:T(8,128)S(1)} %get-tuple-element.80), channel_id=1, source_target_pairs={{0,64},{8,72},{16,80},{24,88},{32,96},{40,104},{48,112},{56,120},{... | collective-permute-start | bytes 270344 | tf_op jit(solution)/shard_map/ppermute | solution.py:29
  184.4 8.8 %collective-permute-start.42 = (f32[2,11,8,128]{3,2,1,0:T(8,128)S(1)}, f32[2,11,8,128]{3,2,1,0:T(8,128)S(1)}, u32[]{:S(2)}, u32[]{:S(2)}) collective-permute-start(f32[2,11,8,128]{3,2,1,0:T(8,128)S(1)} %get-tuple-element.80), channel_id=1, source_target_pairs={{0,32},{8,40},{16,48},{24,56},{32,64},{40,72},{48,80},{56,88},{64,... | collective-permute-start | bytes 270344 | tf_op jit(solution)/shard_map/ppermute | solution.py:29
  185.8 18.3 %collective-permute-start.52 = (f32[4,2,11,8,128]{4,3,2,1,0:T(8,128)S(1)}, f32[4,2,11,8,128]{4,3,2,1,0:T(8,128)S(1)}, u32[]{:S(2)}, u32[]{:S(2)}) collective-permute-start(f32[4,2,11,8,128]{4,3,2,1,0:T(8,128)S(1)} %pad_maximum_fusion.1.refs_4_), channel_id=1, source_target_pairs={{0,64},{8,72},{16,80},{24,88},{32,96},{40,104},{48,112},{56,120},{... | collective-permute-start | bytes 1081352 | tf_op jit(solution)/shard_map/ppermute | solution.py:29
  193.2 11.6 %collective-permute-start.51 = (f32[4,2,11,8,128]{4,3,2,1,0:T(8,128)S(1)}, f32[4,2,11,8,128]{4,3,2,1,0:T(8,128)S(1)}, u32[]{:S(2)}, u32[]{:S(2)}) collective-permute-start(f32[4,2,11,8,128]{4,3,2,1,0:T(8,128)S(1)} %pad_maximum_fusion.1.refs_4_), channel_id=1, source_target_pairs={{0,32},{8,40},{16,48},{24,56},{32,64},{40,72},{48,80},{56,88},{64,... | collective-permute-start | bytes 1081352 | tf_op jit(solution)/shard_map/ppermute | solution.py:29
  193.2 11.6 %collective-permute-start.47 = (f32[4,2,11,8,128]{4,3,2,1,0:T(8,128)S(1)}, f32[4,2,11,8,128]{4,3,2,1,0:T(8,128)S(1)}, u32[]{:S(2)}, u32[]{:S(2)}) collective-permute-start(f32[4,2,11,8,128]{4,3,2,1,0:T(8,128)S(1)} %pad_maximum_fusion.refs_0_), channel_id=1, source_target_pairs={{0,24},{8,0},{16,8},{24,16},{32,56},{40,32},{48,40},{56,48},{64,88... | collective-permute-start | bytes 1081352 | tf_op jit(solution)/shard_map/ppermute | solution.py:29
  194.2 14.0 %collective-permute-start.46 = (f32[4,2,11,8,128]{4,3,2,1,0:T(8,128)S(1)}, f32[4,2,11,8,128]{4,3,2,1,0:T(8,128)S(1)}, u32[]{:S(2)}, u32[]{:S(2)}) collective-permute-start(f32[4,2,11,8,128]{4,3,2,1,0:T(8,128)S(1)} %pad_maximum_fusion.refs_0_), channel_id=1, source_target_pairs={{0,16},{8,24},{16,0},{24,8},{32,48},{40,56},{48,32},{56,40},{64,80... | collective-permute-start | bytes 1081352 | tf_op jit(solution)/shard_map/ppermute | solution.py:29
  203.3 14.2 %collective-permute-start.45 = (f32[4,2,11,8,128]{4,3,2,1,0:T(8,128)S(1)}, f32[4,2,11,8,128]{4,3,2,1,0:T(8,128)S(1)}, u32[]{:S(2)}, u32[]{:S(2)}) collective-permute-start(f32[4,2,11,8,128]{4,3,2,1,0:T(8,128)S(1)} %pad_maximum_fusion.refs_0_), channel_id=1, source_target_pairs={{0,8},{8,16},{16,24},{24,0},{32,40},{40,48},{48,56},{56,32},{64,72... | collective-permute-start | bytes 1081352 | tf_op jit(solution)/shard_map/ppermute | solution.py:29
  226.9 11.0 %collective-permute-start.56 = (f32[4,12,8,128]{3,2,1,0:T(8,128)S(1)}, f32[4,12,8,128]{3,2,1,0:T(8,128)S(1)}, u32[]{:S(2)}, u32[]{:S(2)}) collective-permute-start(f32[4,12,8,128]{3,2,1,0:T(8,128)S(1)} %get-tuple-element.86), channel_id=1, source_target_pairs={{0,4},{2,6},{4,0},{6,2},{1,5},{3,7},{5,1},{7,3},{8,12},{10,14},{12... | collective-permute-start | bytes 589832 | tf_op jit(solution)/shard_map/ppermute | solution.py:35
  229.0 11.2 %collective-permute-start.57 = (f32[4,12,8,128]{3,2,1,0:T(8,128)S(1)}, f32[4,12,8,128]{3,2,1,0:T(8,128)S(1)}, u32[]{:S(2)}, u32[]{:S(2)}) collective-permute-start(f32[4,12,8,128]{3,2,1,0:T(8,128)S(1)} %get-tuple-element.87), channel_id=1, source_target_pairs={{0,6},{2,4},{4,2},{6,0},{1,7},{3,5},{5,3},{7,1},{8,14},{10,12},{12... | collective-permute-start | bytes 589832 | tf_op jit(solution)/shard_map/ppermute | solution.py:35
  (30 other events, 134.8 us)

commit v2 on v1

--- a/solution.py
+++ b/solution.py
@@ -23,12 +23,6 @@
 
 def ring_shift(value, k):
     return lax.ppermute(value, "row", [(RING[p], RING[(p + k) % 16]) for p in range(16)])
-
-
-def xy_shift(value, dx, dy):
-    return lax.ppermute(
-        value, "row", [(i, ((i // 4 + dx) % 4) * 4 + (i % 4 + dy) % 4) for i in range(16)]
-    )
 
 
 def z_swap(value, k):
@@ -91,33 +85,46 @@
     return tdot(xh, zh) + tdot(xh, lo_ref[...]) + tdot(xl, zh)
 
 
-def call(kernel, outs, tab, args, scratch=(), anyspace=False):
-    space = pl.ANY if anyspace else pltpu.VMEM
+def call(kernel, outs, args, scratch=(), tab=None, here=(), there=()):
+    space = lambda n, rest: pl.BlockSpec(memory_space=pl.ANY if n in rest else pltpu.VMEM)
+    table = [] if tab is None else [pl.BlockSpec(memory_space=pltpu.SMEM)]
     return pl.pallas_call(
         kernel,
         out_shape=[jax.ShapeDtypeStruct(o, F32) for o in outs],
-        in_specs=[pl.BlockSpec(memory_space=pltpu.SMEM)]
-        + [pl.BlockSpec(memory_space=space)] * len(args),
-        out_specs=[pl.BlockSpec(memory_space=pltpu.VMEM)] * len(outs),
+        in_specs=table + [space(n, here) for n in range(len(args))],
+        out_specs=[space(n, there) for n in range(len(outs))],
         scratch_shapes=list(scratch),
         compiler_params=pltpu.CompilerParams(vmem_limit_bytes=48 * 1024 * 1024),
-    )(tab, *args)
-
-
-def split_kernel(tab, d_ref, out_ref):
-    for c in range(8):
+    )(*([] if tab is None else [tab]), *args)
+
+
+def split_kernel(d_ref, *outs):
+    me = lax.axis_index("col") * 2 + lax.axis_index("layer")
+    for k in range(8):
         for e in range(4):
-            rows = d_ref[e * 64 + c * 8 : e * 64 + c * 8 + 8, :]
+            start = pl.multiple_of(e * 64 + (me ^ k) * 8, 8)
+            rows = d_ref[pl.ds(start, 8), :]
             for t in range(4):
-                out_ref[c, e, t] = rows[:, t * 128 : (t + 1) * 128]
-
-
-def compact_kernel(tab, x_ref, a_ref, b_ref):
+                outs[k][e, t] = rows[:, t * 128 : (t + 1) * 128]
+
+
+def copies_out(src_ref, out_ref, sem):
+    copies = [pltpu.make_async_copy(src_ref, out_ref.at[n], sem.at[n]) for n in range(16)]
+    for copy in copies:
+        copy.start()
+    for copy in copies:
+        copy.wait()
+
+
+def compact_kernel(tab, *refs):
+    ins, (out_ref, x_ref, a_ref, sem) = refs[:8], refs[8:]
+    for k in range(8):
+        x_ref[k] = ins[k][...]
     low = low_half()
     row0 = tab[PLACE] * 4
+    me = tab[PLACE + 1]
     for e in range(4):
         i = tab[PERM + row0 + e]
-        out_ref = a_ref if e < 2 else b_ref
         halves = []
         for t in range(2 * BAND + 2):
             if t > 2 * BAND:
@@ -125,34 +132,16 @@
                 continue
             j = (i + t - BAND) & 63
             sj = tab[INV + j]
-            tile = x_ref[sj >> 3, e, (sj & 7) >> 1]
+            tile = x_ref[(sj >> 3) ^ me, e, (sj & 7) >> 1]
             tile = jnp.where((sj & 1) == (t & 1), tile, swap_halves(tile))
             halves.append(jnp.where(bit(tab, 0, i, j) == 1, tile, 0.0))
         for t in range(BAND + 1):
-            out_ref[e % 2, t] = jnp.where(low, halves[2 * t], halves[2 * t + 1])
-
-
-def gather_rows(half_a, half_b):
-    stack_a = jnp.stack([half_a] + [xy_shift(half_a, k, 0) for k in (1, 2, 3)])
-    stack_b = jnp.stack([half_b] + [xy_shift(half_b, 0, k) for k in (1, 2, 3)])
-    all_a = [stack_a] + [xy_shift(stack_a, 0, k) for k in (1, 2, 3)]
-    all_b = [stack_b] + [xy_shift(stack_b, k, 0) for k in (1, 2, 3)]
-    return all_a + all_b
-
-
-def fetch(refs, g_ref, sem):
-    copies = [pltpu.make_async_copy(refs[n], g_ref.at[n], sem.at[n]) for n in range(8)]
-    for copy in copies:
-        copy.start()
-    for copy in copies:
-        copy.wait()
-
-
-def seat(tab, r, e):
-    dx = (tab[PLACE + 2] - (r >> 2)) & 3
-    dy = (tab[PLACE + 3] - (r & 3)) & 3
-    first = e < 2
-    return jnp.where(first, dy, 4 + dx), jnp.where(first, dx, dy), e & 1
+            a_ref[e, t] = jnp.where(low, halves[2 * t], halves[2 * t + 1])
+    copies_out(a_ref, out_ref, sem)
+
+
+def gather_rows(copies):
+    return lax.all_to_all(copies, "row", 0, 0, tiled=True)
 
 
 def write_slabs(tab, p_ref, own_ref, oth_ref, e, base, d, tiles):
@@ -189,56 +178,60 @@
     for a in range(0, nk, 2):
         pair = []
         for b in (a, a + 1):
-            pair.append(shifted(strips(b), left - 2 * w + b, count))
+            tiles, first = strips(b)
+            pair.append(shifted(tiles, left - 2 * w + b + 2 * first, count))
         store_split(hi_ref, lo_ref, a * 8, pair[0], pair[1])
     p_ref[...] = product(hi_ref, lo_ref, left * 64, 256).reshape(32, 8, count * 128)
     for e in range(4):
         write_slabs(tab, p_ref, own_ref, oth_ref, e, e * 8, left - (w + 1) + e, w + 2)
 
 
-def first_step_kernel(tab, *refs):
-    ins, (own_ref, oth_ref, cur_ref, hi_ref, lo_ref, p_ref, g_ref, sem) = refs[:8], refs[8:]
-    fetch(ins, g_ref, sem)
+def first_step_kernel(tab, all_ref, own_ref, oth_ref, cur_ref, hi_ref, lo_ref, p_ref, g_ref, sem):
     w = BAND
     base = tab[PLACE + 5] * 4 + 64 - w
+    copies = []
+    for b in range(4 + 2 * w):
+        sk = tab[INV + ((base + b) & 63)]
+        copies.append(pltpu.make_async_copy(all_ref.at[sk >> 2, sk & 3], g_ref.at[b], sem.at[b]))
+    for copy in copies:
+        copy.start()
+    for copy in copies:
+        copy.wait()
+    cur_ref[...] = g_ref[w : w + 4]
 
     def strips(b):
-        sk = tab[INV + ((base + b) & 63)]
-        u, v, e = seat(tab, sk >> 2, sk & 3)
-        strip = g_ref[u, v, e]
-        if w <= b < w + 4:
-            cur_ref[b - w] = strip
-        return [strip[t] for t in range(w + 1)]
+        return [g_ref[b, t] for t in range(w + 1)], 0
 
     step_body(tab, strips, w, own_ref, oth_ref, hi_ref, lo_ref, p_ref)
 
 
-def step_kernel(w, reach, tab, *refs):
-    n = 1 + 2 * len(reach)
+def step_kernel(w, pieces, tab, *refs):
+    n = 1 + len(pieces)
     ins, (own_ref, oth_ref, hi_ref, lo_ref, p_ref) = refs[:n], refs[n:]
 
     def strips(b):
         off = b - w
         if 0 <= off < 4:
-            ref, row = ins[0], off
-        elif off < 0:
-            d = (-off + 3) // 4
-            ref, row = ins[2 * d - 1], off + 4 * (d - 1) + reach[d - 1]
-        else:
-            d = off // 4
-            ref, row = ins[2 * d], off - 4 * d
-        return [ref[row, t] for t in range(w + 1)]
+            return [ins[0][off, t] for t in range(w + 1)], 0
+        d = (-off + 3) // 4 if off < 0 else -(off // 4)
+        at = [piece[0] for piece in pieces].index(d)
+        _, (lo, hi, first, last) = pieces[at]
+        row = off + 4 * d - lo
+        return [ins[1 + at][row, t] for t in range(last - first)], first
 
     step_body(tab, strips, w, own_ref, oth_ref, hi_ref, lo_ref, p_ref)
 
 
-def reach_of(w):
-    return [min(4, w - 4 * d) for d in range((w + 3) // 4)]
-
-
-def last_step_kernel(tab, *refs):
-    ins, (own_ref, oth_ref, cur_ref, hi_ref, lo_ref, p_ref, g_ref, sem) = refs[:8], refs[8:]
-    fetch(ins, g_ref, sem)
+def halo_pieces(w):
+    out = []
+    for d in range(1, (w + 3) // 4 + 1):
+        n = min(4, w - 4 * (d - 1))
+        out.append((d, (4 - n, 4, 2 * (d - 1), w + 1)))
+        out.append((-d, (0, n, 0, w + 1 - 2 * (d - 1))))
+    return out
+
+
+def last_step_kernel(tab, g_ref, own_ref, oth_ref, cur_ref, hi_ref, lo_ref, p_ref):
     w = BAND + STEPS - 1
     row0 = tab[PLACE] * 4
     left, count = w + 2, w + 2
@@ -250,8 +243,7 @@
             pos = k >> 2
             a, odd = pos >> 1, pos & 1
             r = jnp.where(a < 4, a * 4 + odd, (7 - a) * 4 + 3 - odd)
-            u, v, ee = seat(tab, r, k & 3)
-            strip = g_ref[u, v, ee]
+            strip = g_ref[r, k & 3]
             if b == w:
                 cur_ref[e] = strip
             return [strip[t] for t in range(w + 1)]
@@ -276,12 +268,13 @@
     return jnp.where(tab[BRANCH + step] == 1, 2.0 * cur - square, square)
 
 
-def close_kernel(step, cuts, tab, p0, p1, p2, p3, *refs):
+def close_kernel(step, cuts, tab, p0, p1, p2, p3, cur_ref, *refs):
     w = BAND + step
-    if step == 0:
-        cur_ref, refs = refs[0], refs[1:]
+    if cuts is None:
+        copies_ref, refs, sem = refs[0], refs[1:2], refs[2]
+        cuts, spread = [(0, 4, 0, w + 2)], True
     else:
-        cur_ref, refs = refs[0], refs[1:]
+        spread = False
     low = low_half()
     i0 = tab[PLACE + 5] * 4
     for e in range(4):
@@ -299,9 +292,11 @@
                 two = bit(tab, step + 1, i, (i + 2 * m + 64 - w) & 63)
             keep = jnp.where(low, one, two) == 1
             value = jnp.where(keep, polynomial(tab, step, cur, square), 0.0)
-            for ref, (lo, hi) in zip(refs, cuts):
-                if lo <= e < hi:
-                    ref[e - lo, m] = value
+            for ref, (lo, hi, first, last) in zip(refs, cuts):
+                if lo <= e < hi and first <= m < last:
+                    ref[e - lo, m - first] = value
+    if spread:
+        copies_out(refs[0], copies_ref, sem)
 
 
 def finish_kernel(tab, p0, p1, p2, p3, cur_ref, y_ref):
@@ -330,7 +325,7 @@
                 y_ref[c, e, t] = jnp.where(side, piece, y_ref[c, e, t])
 
 
-def join_kernel(tab, y_ref, out_ref):
+def join_kernel(y_ref, out_ref):
     for c in range(8):
         for e in range(4):
             for t in range(4):
@@ -354,7 +349,7 @@
 
 def reduce_group(tab, own, oth, tiles):
     got = core_swap(oth)
-    parts = call(pair_kernel, [(4, tiles, 8, 128)] * 4, tab, [own, got])
+    parts = call(pair_kernel, [(4, tiles, 8, 128)] * 4, [own, got], tab=tab)
     return [parts[0]] + [z_swap(parts[k], k) for k in (1, 2, 3)]
 
 
@@ -362,12 +357,24 @@
     return lax.all_to_all(value, GROUP, 0, 0, tiled=True)
 
 
+def group_swap(value, k):
+    return lax.ppermute(value, GROUP, [(i, i ^ k) for i in range(8)])
+
+
 def shards(density, masks, branch, perm):
+    split = call(split_kernel, [(4, 4, 8, 128)] * 8, [density])
+    split = [split[0]] + [group_swap(split[k], k) for k in range(1, 8)]
     tab = tables(masks, branch, perm)
-    (split,) = call(split_kernel, [(8, 4, 4, 8, 128)], tab, [density])
-    split = exchange(split)
-    halves = call(compact_kernel, [(2, BAND + 1, 8, 128)] * 2, tab, [split])
-    gathered = gather_rows(*halves)
+    spread = [pltpu.SemaphoreType.DMA((16,))]
+    (copies,) = call(
+        compact_kernel,
+        [(16, 4, BAND + 1, 8, 128)],
+        split,
+        [pltpu.VMEM((8, 4, 4, 8, 128), F32), pltpu.VMEM((4, BAND + 1, 8, 128), F32)] + spread,
+        tab=tab,
+        there=(0,),
+    )
+    gathered = gather_rows(copies)
     for step in range(STEPS - 1):
         w = BAND + step
         left, count = geometry(w)
@@ -379,51 +386,52 @@
             pltpu.VMEM((32, 8, count * 128), F32),
         ]
         if step == 0:
-            scratch += [pltpu.VMEM((8, 4, 2, w + 1, 8, 128), F32), pltpu.SemaphoreType.DMA((8,))]
+            strips = 4 + 2 * w
+            scratch += [pltpu.VMEM((strips, w + 1, 8, 128), F32), pltpu.SemaphoreType.DMA((strips,))]
             own, oth, cur = call(
-                first_step_kernel, [part, part, (4, w + 1, 8, 128)], tab, gathered, scratch, True
+                first_step_kernel,
+                [part, part, (4, w + 1, 8, 128)],
+                [gathered],
+                scratch,
+                tab=tab,
+                here=(0,),
             )
         else:
-            reach = reach_of(w)
-            kernel = lambda *refs, w=w, reach=reach: step_kernel(w, reach, *refs)
-            own, oth = call(kernel, [part, part], tab, around, scratch)
+            kernel = lambda *refs, w=w, pieces=pieces: step_kernel(w, pieces, *refs)
+            own, oth = call(kernel, [part, part], [cur] + around, scratch, tab=tab)
         parts = reduce_group(tab, own, oth, w + 2)
         if step < STEPS - 2:
-            reach = reach_of(w + 1)
-            cuts = [(0, 4)]
-            for n in reach:
-                for cut in ((4 - n, 4), (0, n)):
-                    if cut not in cuts:
-                        cuts.append(cut)
+            pieces = halo_pieces(w + 1)
+            cuts = [(0, 4, 0, w + 2)]
+            for _, cut in pieces:
+                if cut not in cuts:
+                    cuts.append(cut)
+            kernel = lambda *refs, step=step, cuts=cuts: close_kernel(step, cuts, *refs)
+            shapes = [(hi - lo, last - first, 8, 128) for lo, hi, first, last in cuts]
+            sent = call(kernel, shapes, parts + [cur], tab=tab)
+            cur = sent[0]
+            around = [ring_shift(sent[cuts.index(cut)], d) for d, cut in pieces]
         else:
-            cuts = [(0, 2), (2, 4)]
-        kernel = lambda *refs, step=step, cuts=cuts: close_kernel(step, cuts, *refs)
-        shapes = [(hi - lo, w + 2, 8, 128) for lo, hi in cuts]
-        pieces = call(kernel, shapes, tab, parts + [cur])
-        if step < STEPS - 2:
-            cur = pieces[0]
-            around = [cur]
-            for d, n in enumerate(reach):
-                around.append(ring_shift(pieces[cuts.index((4 - n, 4))], d + 1))
-                around.append(ring_shift(pieces[cuts.index((0, n))], -(d + 1)))
-        else:
-            gathered = gather_rows(*pieces)
+            kernel = lambda *refs, step=step: close_kernel(step, None, *refs)
+            scratch = [pltpu.VMEM((4, w + 2, 8, 128), F32)] + spread
+            (copies,) = call(
+                kernel, [(16, 4, w + 2, 8, 128)], parts + [cur], scratch, tab=tab, there=(0,)
+            )
+            gathered = gather_rows(copies)
     w = BAND + STEPS - 1
     part = (4, 4, w + 2, 8, 128)
     scratch = [
         pltpu.VMEM(((2 * w + 2) * 8, (w + 2) * 128), BF16),
         pltpu.VMEM(((2 * w + 2) * 8, (w + 2) * 128), BF16),
         pltpu.VMEM((8, 8, (w + 2) * 128), F32),
-        pltpu.VMEM((8, 4, 2, w + 1, 8, 128), F32),
-        pltpu.SemaphoreType.DMA((8,)),
     ]
     own, oth, cur = call(
-        last_step_kernel, [part, part, (4, w + 1, 8, 128)], tab, gathered, scratch, True
+        last_step_kernel, [part, part, (4, w + 1, 8, 128)], [gathered], scratch, tab=tab
     )
     parts = reduce_group(tab, own, oth, w + 2)
-    (full,) = call(finish_kernel, [(8, 4, 4, 8, 128)], tab, parts + [cur])
+    (full,) = call(finish_kernel, [(8, 4, 4, 8, 128)], parts + [cur], tab=tab)
     full = exchange(full)
-    (out,) = call(join_kernel, [(256, 512)], tab, [full])
+    (out,) = call(join_kernel, [(256, 512)], [full])
     return out
 
 

time: 259 us -> 249 us (0.961)
  blocking collectives: 30 us -> 83.2 us
  waiting for transfers between devices: 113 us -> 75.6 us
  starting transfers between devices: 85.2 us -> 55.8 us
  Pallas kernels: 23.9 us -> 27.6 us
    all_to_all x0 -> x2, blocking collectives: none -> 69.5 us  [gather_rows(): return lax.all_to_all(copies, 'row', 0, 0, tiled=True)]
    ppermute x24 -> x7, waiting for transfers between devices: 35.3 us -> 2.47 us  [group_swap(): return lax.ppermute(value, GROUP, [(i, i ^ k) for i in range(8)])]
    ppermute x24 -> x7, starting transfers between devices: 35.3 us -> 10.5 us  [group_swap(): return lax.ppermute(value, GROUP, [(i, i ^ k) for i in range(8)])]
    all_to_all x2 -> x1, blocking collectives: 30 us -> 13.7 us  [exchange(): return lax.all_to_all(value, GROUP, 0, 0, tiled=True)]
    ppermute x14, waiting for transfers between devices: 26.5 us -> 21.4 us  [ring_shift(): lax.ppermute(value, 'row', [(RING[p], RING[(p + k) % 16]) for p in range(...]
    ppermute x5, starting transfers between devices: 17.5 us -> 12.9 us  [core_swap(): return lax.ppermute(value, 'layer', [(0, 1), (1, 0)])]
    pallas_call x18, Pallas kernels: 23.9 us -> 27.6 us  [call(): pl.pallas_call(kernel, out_shape=[jax.ShapeDtypeStruct(o, F32) for o in o...]
  transfers between devices with their start and end apart: 58 -> 41, of which waited for: 45 -> 29; matrix products, arithmetic and copies ran while one was open for 0% -> 2% of each run, Pallas kernels for 0% -> 0%
where the time goes in v2:
time: 249 us; the launch traced here: 248 us
  blocking collectives  83.2 us (33%)
  waiting for transfers between devices  75.6 us (30%)
  starting transfers between devices  55.8 us (22%)
  Pallas kernels  27.6 us (11%)
  local copies, waits for them, and re-layouts  3.72 us (1%)
    all_to_all x2, blocking collectives, gather_rows(): return lax.all_to_all(copies, 'row', 0, 0, tiled=True)  69.5 us
    ppermute x15, waiting for transfers between devices, z_swap(): return lax.ppermute(value, 'col', [(i, i ^ k) for i in range(4)])  43.1 us
    pallas_call x18, Pallas kernels, call(): pl.pallas_call(kernel, out_shape=[jax.ShapeDtypeStruct(o, F32) for o in o...  27.6 us
    ppermute x14, waiting for transfers between devices, ring_shift(): lax.ppermute(value, 'row', [(RING[p], RING[(p + k) % 16]) for p in range(...  21.4 us
    ppermute x15, starting transfers between devices, z_swap(): return lax.ppermute(value, 'col', [(i, i ^ k) for i in range(4)])  19.7 us
    all_to_all x1, blocking collectives, exchange(): return lax.all_to_all(value, GROUP, 0, 0, tiled=True)  13.7 us
    ppermute x5, starting transfers between devices, core_swap(): return lax.ppermute(value, 'layer', [(0, 1), (1, 0)])  12.9 us
    ppermute x14, starting transfers between devices, ring_shift(): lax.ppermute(value, 'row', [(RING[p], RING[(p + k) % 16]) for p in range(...  12.7 us
  transfers between devices with their start and end apart: 41, of which 29 were waited for; matrix products, arithmetic and copies ran while one was open for 2% of the time, Pallas kernels for 0%

profile of v2, /device:TPU:1, one launch (start us, length us, event | category | flops | bytes accessed | tf_op | source)
XLA Modules:
  0.0 248.4 jit_solution(14519751742793463003)
XLA Ops:
  4.4 3.6 %collective-permute-start.3 = (f32[4,4,8,128]{3,2,1,0:T(8,128)S(1)}, f32[4,4,8,128]{3,2,1,0:T(8,128)S(1)}, u32[]{:S(2)}, u32[]{:S(2)}) collective-permute-start(f32[4,4,8,128]{3,2,1,0:T(8,128)S(1)} %get-tuple-element.60), channel_id=1, source_target_pairs={{0,4},{1,5},{2,6},{3,7},{4,0},{5,1},{6,2},{7,3},{8,12},{9,13},{10,... | collective-permute-start | bytes 196616 | tf_op jit(solution)/shard_map/ppermute | solution.py:361
  10.2 3.5 %collective-permute-start.5 = (f32[4,4,8,128]{3,2,1,0:T(8,128)S(1)}, f32[4,4,8,128]{3,2,1,0:T(8,128)S(1)}, u32[]{:S(2)}, u32[]{:S(2)}) collective-permute-start(f32[4,4,8,128]{3,2,1,0:T(8,128)S(1)} %get-tuple-element.62), channel_id=1, source_target_pairs={{0,6},{1,7},{2,4},{3,5},{4,2},{5,3},{6,0},{7,1},{8,14},{9,15},{10,... | collective-permute-start | bytes 196616 | tf_op jit(solution)/shard_map/ppermute | solution.py:361
  16.5 2.5 collective-permute-done.6.refs_7_
  18.9 4.0 %shard_map.56 = f32[16,4,7,8,128]{4,3,2,1,0:T(8,128)S(1)} custom-call(s32[912]{0:T(1024)S(1)} %concatenate.3.tab.refs_0_, f32[4,4,8,128]{3,2,1,0:T(8,128)S(1)} %get-tuple-element.56.refs_0_, f32[4,4,8,128]{3,2,1,0:T(8,128)S(1)} %collective-permute-done.refs_1_, f32[4,4,8,128]{3,2,1,0:T(8,128)S(1)} %collective-permute-done.1.refs_2_, ...), custom_call_target="tpu_custom_call" | custom-call | tf_op jit(solution)/shard_map/pallas_call | solution.py:91
  23.0 31.1 %all_to_all.15.all_ref = f32[16,4,7,8,128]{4,3,2,1,0:T(8,128)S(1)} all-to-all(f32[16,4,7,8,128]{4,3,2,1,0:T(8,128)S(1)} %shard_map.56), channel_id=1, replica_groups=mesh['row'=16,'col'=4,'layer'=2] {'row'}, dimensions={0} | all-to-all | bytes 3670016 | tf_op jit(solution)/shard_map/all_to_all | solution.py:144
  54.1 2.5 %shard_map.57 = (f32[4,4,8,8,128]{4,3,2,1,0:T(8,128)S(1)}, f32[4,4,8,8,128]{4,3,2,1,0:T(8,128)S(1)}, f32[4,7,8,128]{3,2,1,0:T(8,128)S(1)}) custom-call(s32[912]{0:T(1024)S(1)} %concatenate.3.tab.refs_0_, f32[16,4,7,8,128]{4,3,2,1,0:T(8,128)S(1)} %all_to_all.15.all_ref), custom_call_target="tpu_custom_call" | custom-call | tf_op jit(solution)/shard_map/pallas_call | solution.py:91
  60.8 2.3 collective-permute-start.9
  65.5 3.7 %collective-permute-done.9.refs_3_ = f32[4,8,8,128]{3,2,1,0:T(8,128)S(1)} collective-permute-done((f32[4,8,8,128]{3,2,1,0:T(8,128)S(1)}, f32[4,8,8,128]{3,2,1,0:T(8,128)S(1)}, u32[]{:S(2)}, u32[]{:S(2)}) %collective-permute-start.9) | collective-permute-done | bytes 131104 | tf_op jit(solution)/shard_map/ppermute | solution.py:29
  69.2 2.5 %collective-permute-done.10.refs_4_ = f32[4,8,8,128]{3,2,1,0:T(8,128)S(1)} collective-permute-done((f32[4,8,8,128]{3,2,1,0:T(8,128)S(1)}, f32[4,8,8,128]{3,2,1,0:T(8,128)S(1)}, u32[]{:S(2)}, u32[]{:S(2)}) %collective-permute-start.10) | collective-permute-done | bytes 131104 | tf_op jit(solution)/shard_map/ppermute | solution.py:29
  74.0 2.7 %collective-permute-start.14 = (f32[3,6,8,128]{3,2,1,0:T(8,128)S(1)}, f32[3,6,8,128]{3,2,1,0:T(8,128)S(1)}, u32[]{:S(2)}, u32[]{:S(2)}) collective-permute-start(f32[3,6,8,128]{3,2,1,0:T(8,128)S(1)} %get-tuple-element.73), channel_id=1, source_target_pairs={{0,24},{8,16},{32,0},{40,8},{64,32},{72,40},{96,64},{104,72},{120,... | collective-permute-start | bytes 221192 | tf_op jit(solution)/shard_map/ppermute | solution.py:25
  79.5 3.3 %collective-permute-done.11.refs_2_ = f32[4,8,8,128]{3,2,1,0:T(8,128)S(1)} collective-permute-done((f32[4,8,8,128]{3,2,1,0:T(8,128)S(1)}, f32[4,8,8,128]{3,2,1,0:T(8,128)S(1)}, u32[]{:S(2)}, u32[]{:S(2)}) %collective-permute-start.11) | collective-permute-done | bytes 131104 | tf_op jit(solution)/shard_map/ppermute | solution.py:25
  88.6 2.7 %collective-permute-start.17 = (f32[4,9,8,128]{3,2,1,0:T(8,128)S(1)}, f32[4,9,8,128]{3,2,1,0:T(8,128)S(1)}, u32[]{:S(2)}, u32[]{:S(2)}) collective-permute-start(f32[4,9,8,128]{3,2,1,0:T(8,128)S(1)} %get-tuple-element.78), channel_id=1, source_target_pairs={{0,4},{2,6},{4,0},{6,2},{1,5},{3,7},{5,1},{7,3},{8,12},{10,14},{12... | collective-permute-start | bytes 442376 | tf_op jit(solution)/shard_map/ppermute | solution.py:29
  93.7 4.4 %collective-permute-done.17.refs_3_ = f32[4,9,8,128]{3,2,1,0:T(8,128)S(1)} collective-permute-done((f32[4,9,8,128]{3,2,1,0:T(8,128)S(1)}, f32[4,9,8,128]{3,2,1,0:T(8,128)S(1)}, u32[]{:S(2)}, u32[]{:S(2)}) %collective-permute-start.17) | collective-permute-done | bytes 147488 | tf_op jit(solution)/shard_map/ppermute | solution.py:29
  98.1 2.5 %collective-permute-done.18.refs_4_ = f32[4,9,8,128]{3,2,1,0:T(8,128)S(1)} collective-permute-done((f32[4,9,8,128]{3,2,1,0:T(8,128)S(1)}, f32[4,9,8,128]{3,2,1,0:T(8,128)S(1)}, u32[]{:S(2)}, u32[]{:S(2)}) %collective-permute-start.18) | collective-permute-done | bytes 147488 | tf_op jit(solution)/shard_map/ppermute | solution.py:29
  103.2 2.4 collective-permute-start.22
  105.6 2.4 collective-permute-done.21.refs_4_
  108.1 3.5 %collective-permute-done.19.refs_2_ = f32[4,9,8,128]{3,2,1,0:T(8,128)S(1)} collective-permute-done((f32[4,9,8,128]{3,2,1,0:T(8,128)S(1)}, f32[4,9,8,128]{3,2,1,0:T(8,128)S(1)}, u32[]{:S(2)}, u32[]{:S(2)}) %collective-permute-start.19) | collective-permute-done | bytes 147488 | tf_op jit(solution)/shard_map/ppermute | solution.py:25
  123.2 4.4 %collective-permute-done.25.refs_3_ = f32[4,10,8,128]{3,2,1,0:T(8,128)S(1)} collective-permute-done((f32[4,10,8,128]{3,2,1,0:T(8,128)S(1)}, f32[4,10,8,128]{3,2,1,0:T(8,128)S(1)}, u32[]{:S(2)}, u32[]{:S(2)}) %collective-permute-start.25) | collective-permute-done | bytes 163872 | tf_op jit(solution)/shard_map/ppermute | solution.py:29
  127.7 2.7 %collective-permute-done.26.refs_4_ = f32[4,10,8,128]{3,2,1,0:T(8,128)S(1)} collective-permute-done((f32[4,10,8,128]{3,2,1,0:T(8,128)S(1)}, f32[4,10,8,128]{3,2,1,0:T(8,128)S(1)}, u32[]{:S(2)}, u32[]{:S(2)}) %collective-permute-start.26) | collective-permute-done | bytes 163872 | tf_op jit(solution)/shard_map/ppermute | solution.py:29
  135.4 5.3 %collective-permute-done.31.refs_6_ = f32[1,6,8,128]{3,2,1,0:T(8,128)S(1)} collective-permute-done((f32[1,6,8,128]{3,2,1,0:T(8,128)S(1)}, f32[1,6,8,128]{3,2,1,0:T(8,128)S(1)}, u32[]{:S(2)}, u32[]{:S(2)}) %collective-permute-start.31) | collective-permute-done | bytes 24608 | tf_op jit(solution)/shard_map/ppermute | solution.py:25
  140.8 3.9 %collective-permute-done.32.refs_7_ = f32[1,6,8,128]{3,2,1,0:T(8,128)S(1)} collective-permute-done((f32[1,6,8,128]{3,2,1,0:T(8,128)S(1)}, f32[1,6,8,128]{3,2,1,0:T(8,128)S(1)}, u32[]{:S(2)}, u32[]{:S(2)}) %collective-permute-start.32) | collective-permute-done | bytes 24608 | tf_op jit(solution)/shard_map/ppermute | solution.py:25
  146.5 4.0 %collective-permute-start.33 = (f32[4,4,11,8,128]{4,3,2,1,0:T(8,128)S(1)}, f32[4,4,11,8,128]{4,3,2,1,0:T(8,128)S(1)}, u32[]{:S(2)}, u32[]{:S(2)}) collective-permute-start(f32[4,4,11,8,128]{4,3,2,1,0:T(8,128)S(1)} %get-tuple-element.95), channel_id=1, source_target_pairs={{0,1},{1,0},{2,3},{3,2},{4,5},{5,4},{6,7},{7,6},{8,9},{9,8},{10,11... | collective-permute-start | bytes 2162696 | tf_op jit(solution)/shard_map/ppermute | solution.py:33
  153.2 2.7 %collective-permute-start.35 = (f32[4,11,8,128]{3,2,1,0:T(8,128)S(1)}, f32[4,11,8,128]{3,2,1,0:T(8,128)S(1)}, u32[]{:S(2)}, u32[]{:S(2)}) collective-permute-start(f32[4,11,8,128]{3,2,1,0:T(8,128)S(1)} %get-tuple-element.98), channel_id=1, source_target_pairs={{0,4},{2,6},{4,0},{6,2},{1,5},{3,7},{5,1},{7,3},{8,12},{10,14},{12... | collective-permute-start | bytes 540680 | tf_op jit(solution)/shard_map/ppermute | solution.py:29
  158.9 5.1 %collective-permute-done.35.refs_3_ = f32[4,11,8,128]{3,2,1,0:T(8,128)S(1)} collective-permute-done((f32[4,11,8,128]{3,2,1,0:T(8,128)S(1)}, f32[4,11,8,128]{3,2,1,0:T(8,128)S(1)}, u32[]{:S(2)}, u32[]{:S(2)}) %collective-permute-start.35) | collective-permute-done | bytes 180256 | tf_op jit(solution)/shard_map/ppermute | solution.py:29
  164.0 2.5 %collective-permute-done.36.refs_4_ = f32[4,11,8,128]{3,2,1,0:T(8,128)S(1)} collective-permute-done((f32[4,11,8,128]{3,2,1,0:T(8,128)S(1)}, f32[4,11,8,128]{3,2,1,0:T(8,128)S(1)}, u32[]{:S(2)}, u32[]{:S(2)}) %collective-permute-start.36) | collective-permute-done | bytes 180256 | tf_op jit(solution)/shard_map/ppermute | solution.py:29
  166.5 5.4 %shard_map.68 = f32[16,4,11,8,128]{4,3,2,1,0:T(8,128)S(1)} custom-call(s32[912]{0:T(1024)S(1)} %concatenate.3.tab.refs_0_, f32[4,11,8,128]{3,2,1,0:T(8,128)S(1)} %get-tuple-element.96.refs_1_, f32[4,11,8,128]{3,2,1,0:T(8,128)S(1)} %collective-permute-done.34.refs_2_, f32[4,11,8,128]{3,2,1,0:T(8,128)S(1)} %collective-permute-done.35.refs_3_, ...), custom_call_target="tpu_custom_call" | custom-call | tf_op jit(solution)/shard_map/pallas_call | solution.py:91
  172.0 38.4 %all_to_all.16.g_ref = f32[16,4,11,8,128]{4,3,2,1,0:T(8,128)S(1)} all-to-all(f32[16,4,11,8,128]{4,3,2,1,0:T(8,128)S(1)} %shard_map.68), channel_id=1, replica_groups=mesh['row'=16,'col'=4,'layer'=2] {'row'}, dimensions={0} | all-to-all | bytes 5767168 | tf_op jit(solution)/shard_map/all_to_all | solution.py:144
  210.4 2.4 shard_map.69
  212.8 3.4 %collective-permute-start.37 = (f32[4,4,12,8,128]{4,3,2,1,0:T(8,128)S(1)}, f32[4,4,12,8,128]{4,3,2,1,0:T(8,128)S(1)}, u32[]{:S(2)}, u32[]{:S(2)}) collective-permute-start(f32[4,4,12,8,128]{4,3,2,1,0:T(8,128)S(1)} %get-tuple-element.101), channel_id=1, source_target_pairs={{0,1},{1,0},{2,3},{3,2},{4,5},{5,4},{6,7},{7,6},{8,9},{9,8},{10,11... | collective-permute-start | bytes 2359304 | tf_op jit(solution)/shard_map/ppermute | solution.py:33
  219.0 2.3 collective-permute-start.39
  225.1 5.1 %collective-permute-done.39.p2 = f32[4,12,8,128]{3,2,1,0:T(8,128)S(1)} collective-permute-done((f32[4,12,8,128]{3,2,1,0:T(8,128)S(1)}, f32[4,12,8,128]{3,2,1,0:T(8,128)S(1)}, u32[]{:S(2)}, u32[]{:S(2)}) %collective-permute-start.39) | collective-permute-done | bytes 196640 | tf_op jit(solution)/shard_map/ppermute | solution.py:29
  233.8 13.7 %all_to_all.17.y_ref = f32[8,4,4,8,128]{4,3,2,1,0:T(8,128)S(1)} all-to-all(f32[8,4,4,8,128]{4,3,2,1,0:T(8,128)S(1)} %shard_map.71), channel_id=1, replica_groups=mesh['row'=16,'col'=4,'layer'=2] {'col','layer'}, dimensions={0} | all-to-all | bytes 1048576 | tf_op jit(solution)/shard_map/all_to_all | solution.py:357
  (81 shorter events, 66.9 us)
Async XLA Ops:
  1.1 9.1 %collective-permute-start = (f32[4,4,8,128]{3,2,1,0:T(8,128)S(1)}, f32[4,4,8,128]{3,2,1,0:T(8,128)S(1)}, u32[]{:S(2)}, u32[]{:S(2)}) collective-permute-start(f32[4,4,8,128]{3,2,1,0:T(8,128)S(1)} %get-tuple-element.57), channel_id=1, source_target_pairs={{0,1},{1,0},{2,3},{3,2},{4,5},{5,4},{6,7},{7,6},{8,9},{9,8},{10,11... | collective-permute-start | bytes 196616 | tf_op jit(solution)/shard_map/ppermute | solution.py:361
  2.6 11.1 %collective-permute-start.1 = (f32[4,4,8,128]{3,2,1,0:T(8,128)S(1)}, f32[4,4,8,128]{3,2,1,0:T(8,128)S(1)}, u32[]{:S(2)}, u32[]{:S(2)}) collective-permute-start(f32[4,4,8,128]{3,2,1,0:T(8,128)S(1)} %get-tuple-element.58), channel_id=1, source_target_pairs={{0,2},{1,3},{2,0},{3,1},{4,6},{5,7},{6,4},{7,5},{8,10},{9,11},{10,... | collective-permute-start | bytes 196616 | tf_op jit(solution)/shard_map/ppermute | solution.py:361
  4.3 12.1 %collective-permute-start.2 = (f32[4,4,8,128]{3,2,1,0:T(8,128)S(1)}, f32[4,4,8,128]{3,2,1,0:T(8,128)S(1)}, u32[]{:S(2)}, u32[]{:S(2)}) collective-permute-start(f32[4,4,8,128]{3,2,1,0:T(8,128)S(1)} %get-tuple-element.59), channel_id=1, source_target_pairs={{0,3},{1,2},{2,1},{3,0},{4,7},{5,6},{6,5},{7,4},{8,11},{9,10},{10,... | collective-permute-start | bytes 196616 | tf_op jit(solution)/shard_map/ppermute | solution.py:361
  4.4 12.1 %collective-permute-start.3 = (f32[4,4,8,128]{3,2,1,0:T(8,128)S(1)}, f32[4,4,8,128]{3,2,1,0:T(8,128)S(1)}, u32[]{:S(2)}, u32[]{:S(2)}) collective-permute-start(f32[4,4,8,128]{3,2,1,0:T(8,128)S(1)} %get-tuple-element.60), channel_id=1, source_target_pairs={{0,4},{1,5},{2,6},{3,7},{4,0},{5,1},{6,2},{7,3},{8,12},{9,13},{10,... | collective-permute-start | bytes 196616 | tf_op jit(solution)/shard_map/ppermute | solution.py:361
  8.0 8.5 %collective-permute-start.4 = (f32[4,4,8,128]{3,2,1,0:T(8,128)S(1)}, f32[4,4,8,128]{3,2,1,0:T(8,128)S(1)}, u32[]{:S(2)}, u32[]{:S(2)}) collective-permute-start(f32[4,4,8,128]{3,2,1,0:T(8,128)S(1)} %get-tuple-element.61), channel_id=1, source_target_pairs={{0,5},{1,4},{2,7},{3,6},{4,1},{5,0},{6,3},{7,2},{8,13},{9,12},{10,... | collective-permute-start | bytes 196616 | tf_op jit(solution)/shard_map/ppermute | solution.py:361
  10.2 6.3 %collective-permute-start.5 = (f32[4,4,8,128]{3,2,1,0:T(8,128)S(1)}, f32[4,4,8,128]{3,2,1,0:T(8,128)S(1)}, u32[]{:S(2)}, u32[]{:S(2)}) collective-permute-start(f32[4,4,8,128]{3,2,1,0:T(8,128)S(1)} %get-tuple-element.62), channel_id=1, source_target_pairs={{0,6},{1,7},{2,4},{3,5},{4,2},{5,3},{6,0},{7,1},{8,14},{9,15},{10,... | collective-permute-start | bytes 196616 | tf_op jit(solution)/shard_map/ppermute | solution.py:361
  13.7 5.3 %collective-permute-start.6 = (f32[4,4,8,128]{3,2,1,0:T(8,128)S(1)}, f32[4,4,8,128]{3,2,1,0:T(8,128)S(1)}, u32[]{:S(2)}, u32[]{:S(2)}) collective-permute-start(f32[4,4,8,128]{3,2,1,0:T(8,128)S(1)} %get-tuple-element.63), channel_id=1, source_target_pairs={{0,7},{1,6},{2,5},{3,4},{4,3},{5,2},{6,1},{7,0},{8,15},{9,14},{10,... | collective-permute-start | bytes 196616 | tf_op jit(solution)/shard_map/ppermute | solution.py:361
  60.8 8.4 %collective-permute-start.9 = (f32[4,8,8,128]{3,2,1,0:T(8,128)S(1)}, f32[4,8,8,128]{3,2,1,0:T(8,128)S(1)}, u32[]{:S(2)}, u32[]{:S(2)}) collective-permute-start(f32[4,8,8,128]{3,2,1,0:T(8,128)S(1)} %get-tuple-element.68), channel_id=1, source_target_pairs={{0,4},{2,6},{4,0},{6,2},{1,5},{3,7},{5,1},{7,3},{8,12},{10,14},{12... | collective-permute-start | bytes 393224 | tf_op jit(solution)/shard_map/ppermute | solution.py:29
  63.1 8.6 %collective-permute-start.10 = (f32[4,8,8,128]{3,2,1,0:T(8,128)S(1)}, f32[4,8,8,128]{3,2,1,0:T(8,128)S(1)}, u32[]{:S(2)}, u32[]{:S(2)}) collective-permute-start(f32[4,8,8,128]{3,2,1,0:T(8,128)S(1)} %get-tuple-element.69), channel_id=1, source_target_pairs={{0,6},{2,4},{4,2},{6,0},{1,7},{3,5},{5,3},{7,1},{8,14},{10,12},{12... | collective-permute-start | bytes 393224 | tf_op jit(solution)/shard_map/ppermute | solution.py:29
  72.4 7.1 %collective-permute-start.12 = (f32[4,8,8,128]{3,2,1,0:T(8,128)S(1)}, f32[4,8,8,128]{3,2,1,0:T(8,128)S(1)}, u32[]{:S(2)}, u32[]{:S(2)}) collective-permute-start(f32[4,8,8,128]{3,2,1,0:T(8,128)S(1)} %get-tuple-element.71.refs_1_.refs_5_), channel_id=1, source_target_pairs={{0,16},{8,0},{32,8},{40,32},{64,40},{72,64},{96,72},{104,96},{120,... | collective-permute-start | bytes 393224 | tf_op jit(solution)/shard_map/ppermute | solution.py:25
  73.7 9.2 %collective-permute-start.11 = (f32[4,8,8,128]{3,2,1,0:T(8,128)S(1)}, f32[4,8,8,128]{3,2,1,0:T(8,128)S(1)}, u32[]{:S(2)}, u32[]{:S(2)}) collective-permute-start(f32[4,8,8,128]{3,2,1,0:T(8,128)S(1)} %get-tuple-element.71.refs_1_.refs_5_), channel_id=1, source_target_pairs={{0,8},{8,32},{32,40},{40,64},{64,72},{72,96},{96,104},{104,120},{1... | collective-permute-start | bytes 393224 | tf_op jit(solution)/shard_map/ppermute | solution.py:25
  88.5 5.1 %collective-permute-start.16 = (f32[4,9,8,128]{3,2,1,0:T(8,128)S(1)}, f32[4,9,8,128]{3,2,1,0:T(8,128)S(1)}, u32[]{:S(2)}, u32[]{:S(2)}) collective-permute-start(f32[4,9,8,128]{3,2,1,0:T(8,128)S(1)} %get-tuple-element.77), channel_id=1, source_target_pairs={{0,2},{2,0},{4,6},{6,4},{1,3},{3,1},{5,7},{7,5},{8,10},{10,8},{12,... | collective-permute-start | bytes 442376 | tf_op jit(solution)/shard_map/ppermute | solution.py:29
  88.6 9.5 %collective-permute-start.17 = (f32[4,9,8,128]{3,2,1,0:T(8,128)S(1)}, f32[4,9,8,128]{3,2,1,0:T(8,128)S(1)}, u32[]{:S(2)}, u32[]{:S(2)}) collective-permute-start(f32[4,9,8,128]{3,2,1,0:T(8,128)S(1)} %get-tuple-element.78), channel_id=1, source_target_pairs={{0,4},{2,6},{4,0},{6,2},{1,5},{3,7},{5,1},{7,3},{8,12},{10,14},{12... | collective-permute-start | bytes 442376 | tf_op jit(solution)/shard_map/ppermute | solution.py:29
  91.3 9.3 %collective-permute-start.18 = (f32[4,9,8,128]{3,2,1,0:T(8,128)S(1)}, f32[4,9,8,128]{3,2,1,0:T(8,128)S(1)}, u32[]{:S(2)}, u32[]{:S(2)}) collective-permute-start(f32[4,9,8,128]{3,2,1,0:T(8,128)S(1)} %get-tuple-element.79), channel_id=1, source_target_pairs={{0,6},{2,4},{4,2},{6,0},{1,7},{3,5},{5,3},{7,1},{8,14},{10,12},{12... | collective-permute-start | bytes 442376 | tf_op jit(solution)/shard_map/ppermute | solution.py:29
  101.4 6.8 %collective-permute-start.20 = (f32[4,9,8,128]{3,2,1,0:T(8,128)S(1)}, f32[4,9,8,128]{3,2,1,0:T(8,128)S(1)}, u32[]{:S(2)}, u32[]{:S(2)}) collective-permute-start(f32[4,9,8,128]{3,2,1,0:T(8,128)S(1)} %get-tuple-element.80.refs_1_.refs_5_), channel_id=1, source_target_pairs={{0,16},{8,0},{32,8},{40,32},{64,40},{72,64},{96,72},{104,96},{120,... | collective-permute-start | bytes 442376 | tf_op jit(solution)/shard_map/ppermute | solution.py:25
  101.5 10.1 %collective-permute-start.19 = (f32[4,9,8,128]{3,2,1,0:T(8,128)S(1)}, f32[4,9,8,128]{3,2,1,0:T(8,128)S(1)}, u32[]{:S(2)}, u32[]{:S(2)}) collective-permute-start(f32[4,9,8,128]{3,2,1,0:T(8,128)S(1)} %get-tuple-element.80.refs_1_.refs_5_), channel_id=1, source_target_pairs={{0,8},{8,32},{32,40},{40,64},{64,72},{72,96},{96,104},{104,120},{1... | collective-permute-start | bytes 442376 | tf_op jit(solution)/shard_map/ppermute | solution.py:25
  117.8 5.5 %collective-permute-start.24 = (f32[4,10,8,128]{3,2,1,0:T(8,128)S(1)}, f32[4,10,8,128]{3,2,1,0:T(8,128)S(1)}, u32[]{:S(2)}, u32[]{:S(2)}) collective-permute-start(f32[4,10,8,128]{3,2,1,0:T(8,128)S(1)} %get-tuple-element.86), channel_id=1, source_target_pairs={{0,2},{2,0},{4,6},{6,4},{1,3},{3,1},{5,7},{7,5},{8,10},{10,8},{12,... | collective-permute-start | bytes 491528 | tf_op jit(solution)/shard_map/ppermute | solution.py:29
  117.8 9.8 %collective-permute-start.25 = (f32[4,10,8,128]{3,2,1,0:T(8,128)S(1)}, f32[4,10,8,128]{3,2,1,0:T(8,128)S(1)}, u32[]{:S(2)}, u32[]{:S(2)}) collective-permute-start(f32[4,10,8,128]{3,2,1,0:T(8,128)S(1)} %get-tuple-element.87), channel_id=1, source_target_pairs={{0,4},{2,6},{4,0},{6,2},{1,5},{3,7},{5,1},{7,3},{8,12},{10,14},{12... | collective-permute-start | bytes 491528 | tf_op jit(solution)/shard_map/ppermute | solution.py:29
  120.2 10.2 %collective-permute-start.26 = (f32[4,10,8,128]{3,2,1,0:T(8,128)S(1)}, f32[4,10,8,128]{3,2,1,0:T(8,128)S(1)}, u32[]{:S(2)}, u32[]{:S(2)}) collective-permute-start(f32[4,10,8,128]{3,2,1,0:T(8,128)S(1)} %get-tuple-element.88), channel_id=1, source_target_pairs={{0,6},{2,4},{4,2},{6,0},{1,7},{3,5},{5,3},{7,1},{8,14},{10,12},{12... | collective-permute-start | bytes 491528 | tf_op jit(solution)/shard_map/ppermute | solution.py:29
  131.1 13.5 %collective-permute-start.28 = (f32[4,10,8,128]{3,2,1,0:T(8,128)S(1)}, f32[4,10,8,128]{3,2,1,0:T(8,128)S(1)}, u32[]{:S(2)}, u32[]{:S(2)}) collective-permute-start(f32[4,10,8,128]{3,2,1,0:T(8,128)S(1)} %get-tuple-element.89.refs_1_.refs_5_), channel_id=1, source_target_pairs={{0,16},{8,0},{32,8},{40,32},{64,40},{72,64},{96,72},{104,96},{120,... | collective-permute-start | bytes 491528 | tf_op jit(solution)/shard_map/ppermute | solution.py:25
  131.8 12.8 %collective-permute-start.27 = (f32[4,10,8,128]{3,2,1,0:T(8,128)S(1)}, f32[4,10,8,128]{3,2,1,0:T(8,128)S(1)}, u32[]{:S(2)}, u32[]{:S(2)}) collective-permute-start(f32[4,10,8,128]{3,2,1,0:T(8,128)S(1)} %get-tuple-element.89.refs_1_.refs_5_), channel_id=1, source_target_pairs={{0,8},{8,32},{32,40},{40,64},{64,72},{72,96},{96,104},{104,120},{1... | collective-permute-start | bytes 491528 | tf_op jit(solution)/shard_map/ppermute | solution.py:25
  132.7 12.0 %collective-permute-start.29 = (f32[4,8,8,128]{3,2,1,0:T(8,128)S(1)}, f32[4,8,8,128]{3,2,1,0:T(8,128)S(1)}, u32[]{:S(2)}, u32[]{:S(2)}) collective-permute-start(f32[4,8,8,128]{3,2,1,0:T(8,128)S(1)} %get-tuple-element.90), channel_id=1, source_target_pairs={{0,32},{8,40},{32,64},{40,72},{64,96},{72,104},{96,120},{104,112},... | collective-permute-start | bytes 393224 | tf_op jit(solution)/shard_map/ppermute | solution.py:25
  133.0 11.6 %collective-permute-start.30 = (f32[4,8,8,128]{3,2,1,0:T(8,128)S(1)}, f32[4,8,8,128]{3,2,1,0:T(8,128)S(1)}, u32[]{:S(2)}, u32[]{:S(2)}) collective-permute-start(f32[4,8,8,128]{3,2,1,0:T(8,128)S(1)} %get-tuple-element.91), channel_id=1, source_target_pairs={{0,24},{8,16},{32,0},{40,8},{64,32},{72,40},{96,64},{104,72},{120,... | collective-permute-start | bytes 393224 | tf_op jit(solution)/shard_map/ppermute | solution.py:25
  135.4 5.4 %collective-permute-start.31 = (f32[1,6,8,128]{3,2,1,0:T(8,128)S(1)}, f32[1,6,8,128]{3,2,1,0:T(8,128)S(1)}, u32[]{:S(2)}, u32[]{:S(2)}) collective-permute-start(f32[1,6,8,128]{3,2,1,0:T(8,128)S(1)} %get-tuple-element.92), channel_id=1, source_target_pairs={{0,40},{8,64},{32,72},{40,96},{64,104},{72,120},{96,112},{104,88},... | collective-permute-start | bytes 73736 | tf_op jit(solution)/shard_map/ppermute | solution.py:25
  146.5 5.9 %collective-permute-start.33 = (f32[4,4,11,8,128]{4,3,2,1,0:T(8,128)S(1)}, f32[4,4,11,8,128]{4,3,2,1,0:T(8,128)S(1)}, u32[]{:S(2)}, u32[]{:S(2)}) collective-permute-start(f32[4,4,11,8,128]{4,3,2,1,0:T(8,128)S(1)} %get-tuple-element.95), channel_id=1, source_target_pairs={{0,1},{1,0},{2,3},{3,2},{4,5},{5,4},{6,7},{7,6},{8,9},{9,8},{10,11... | collective-permute-start | bytes 2162696 | tf_op jit(solution)/shard_map/ppermute | solution.py:33
  153.1 5.8 %collective-permute-start.34 = (f32[4,11,8,128]{3,2,1,0:T(8,128)S(1)}, f32[4,11,8,128]{3,2,1,0:T(8,128)S(1)}, u32[]{:S(2)}, u32[]{:S(2)}) collective-permute-start(f32[4,11,8,128]{3,2,1,0:T(8,128)S(1)} %get-tuple-element.97), channel_id=1, source_target_pairs={{0,2},{2,0},{4,6},{6,4},{1,3},{3,1},{5,7},{7,5},{8,10},{10,8},{12,... | collective-permute-start | bytes 540680 | tf_op jit(solution)/shard_map/ppermute | solution.py:29
  153.2 10.9 %collective-permute-start.35 = (f32[4,11,8,128]{3,2,1,0:T(8,128)S(1)}, f32[4,11,8,128]{3,2,1,0:T(8,128)S(1)}, u32[]{:S(2)}, u32[]{:S(2)}) collective-permute-start(f32[4,11,8,128]{3,2,1,0:T(8,128)S(1)} %get-tuple-element.98), channel_id=1, source_target_pairs={{0,4},{2,6},{4,0},{6,2},{1,5},{3,7},{5,1},{7,3},{8,12},{10,14},{12... | collective-permute-start | bytes 540680 | tf_op jit(solution)/shard_map/ppermute | solution.py:29
  155.8 10.7 %collective-permute-start.36 = (f32[4,11,8,128]{3,2,1,0:T(8,128)S(1)}, f32[4,11,8,128]{3,2,1,0:T(8,128)S(1)}, u32[]{:S(2)}, u32[]{:S(2)}) collective-permute-start(f32[4,11,8,128]{3,2,1,0:T(8,128)S(1)} %get-tuple-element.99), channel_id=1, source_target_pairs={{0,6},{2,4},{4,2},{6,0},{1,7},{3,5},{5,3},{7,1},{8,14},{10,12},{12... | collective-permute-start | bytes 540680 | tf_op jit(solution)/shard_map/ppermute | solution.py:29
  212.8 5.3 %collective-permute-start.37 = (f32[4,4,12,8,128]{4,3,2,1,0:T(8,128)S(1)}, f32[4,4,12,8,128]{4,3,2,1,0:T(8,128)S(1)}, u32[]{:S(2)}, u32[]{:S(2)}) collective-permute-start(f32[4,4,12,8,128]{4,3,2,1,0:T(8,128)S(1)} %get-tuple-element.101), channel_id=1, source_target_pairs={{0,1},{1,0},{2,3},{3,2},{4,5},{5,4},{6,7},{7,6},{8,9},{9,8},{10,11... | collective-permute-start | bytes 2359304 | tf_op jit(solution)/shard_map/ppermute | solution.py:33
  218.9 6.2 %collective-permute-start.38 = (f32[4,12,8,128]{3,2,1,0:T(8,128)S(1)}, f32[4,12,8,128]{3,2,1,0:T(8,128)S(1)}, u32[]{:S(2)}, u32[]{:S(2)}) collective-permute-start(f32[4,12,8,128]{3,2,1,0:T(8,128)S(1)} %get-tuple-element.103), channel_id=1, source_target_pairs={{0,2},{2,0},{4,6},{6,4},{1,3},{3,1},{5,7},{7,5},{8,10},{10,8},{12,... | collective-permute-start | bytes 589832 | tf_op jit(solution)/shard_map/ppermute | solution.py:29
  219.0 11.2 %collective-permute-start.39 = (f32[4,12,8,128]{3,2,1,0:T(8,128)S(1)}, f32[4,12,8,128]{3,2,1,0:T(8,128)S(1)}, u32[]{:S(2)}, u32[]{:S(2)}) collective-permute-start(f32[4,12,8,128]{3,2,1,0:T(8,128)S(1)} %get-tuple-element.104), channel_id=1, source_target_pairs={{0,4},{2,6},{4,0},{6,2},{1,5},{3,7},{5,1},{7,3},{8,12},{10,14},{12... | collective-permute-start | bytes 589832 | tf_op jit(solution)/shard_map/ppermute | solution.py:29
  221.3 11.2 %collective-permute-start.40 = (f32[4,12,8,128]{3,2,1,0:T(8,128)S(1)}, f32[4,12,8,128]{3,2,1,0:T(8,128)S(1)}, u32[]{:S(2)}, u32[]{:S(2)}) collective-permute-start(f32[4,12,8,128]{3,2,1,0:T(8,128)S(1)} %get-tuple-element.105), channel_id=1, source_target_pairs={{0,6},{2,4},{4,2},{6,0},{1,7},{3,5},{5,3},{7,1},{8,14},{10,12},{12... | collective-permute-start | bytes 589832 | tf_op jit(solution)/shard_map/ppermute | solution.py:29
  (10 other events, 38.9 us)

commit v3 on v2

--- a/solution.py
+++ b/solution.py
@@ -23,10 +23,6 @@
 
 def ring_shift(value, k):
     return lax.ppermute(value, "row", [(RING[p], RING[(p + k) % 16]) for p in range(16)])
-
-
-def z_swap(value, k):
-    return lax.ppermute(value, "col", [(i, i ^ k) for i in range(4)])
 
 
 def core_swap(value):
@@ -108,16 +104,8 @@
                 outs[k][e, t] = rows[:, t * 128 : (t + 1) * 128]
 
 
-def copies_out(src_ref, out_ref, sem):
-    copies = [pltpu.make_async_copy(src_ref, out_ref.at[n], sem.at[n]) for n in range(16)]
-    for copy in copies:
-        copy.start()
-    for copy in copies:
-        copy.wait()
-
-
 def compact_kernel(tab, *refs):
-    ins, (out_ref, x_ref, a_ref, sem) = refs[:8], refs[8:]
+    ins, (a_ref, x_ref) = refs[:8], refs[8:]
     for k in range(8):
         x_ref[k] = ins[k][...]
     low = low_half()
@@ -137,10 +125,10 @@
             halves.append(jnp.where(bit(tab, 0, i, j) == 1, tile, 0.0))
         for t in range(BAND + 1):
             a_ref[e, t] = jnp.where(low, halves[2 * t], halves[2 * t + 1])
-    copies_out(a_ref, out_ref, sem)
-
-
-def gather_rows(copies):
+
+
+def gather_rows(rows):
+    copies = jnp.broadcast_to(rows[None], (16,) + rows.shape)
     return lax.all_to_all(copies, "row", 0, 0, tiled=True)
 
 
@@ -258,23 +246,20 @@
         write_slabs(tab, p_ref, own_ref, oth_ref, e, 0, 0, count)
 
 
-def pair_kernel(tab, own_ref, got_ref, *outs):
-    z = tab[PLACE + 6]
-    for k in range(4):
-        outs[k][...] = own_ref[z ^ k] + got_ref[z ^ k]
+def pair_kernel(own_ref, got_ref, out_ref):
+    out_ref[...] = own_ref[...] + got_ref[...]
+
+
+def total(ref, e, m):
+    return (ref[0, e, m] + ref[1, e, m]) + (ref[2, e, m] + ref[3, e, m])
 
 
 def polynomial(tab, step, cur, square):
     return jnp.where(tab[BRANCH + step] == 1, 2.0 * cur - square, square)
 
 
-def close_kernel(step, cuts, tab, p0, p1, p2, p3, cur_ref, *refs):
+def close_kernel(step, cuts, tab, part_ref, cur_ref, *refs):
     w = BAND + step
-    if cuts is None:
-        copies_ref, refs, sem = refs[0], refs[1:2], refs[2]
-        cuts, spread = [(0, 4, 0, w + 2)], True
-    else:
-        spread = False
     low = low_half()
     i0 = tab[PLACE + 5] * 4
     for e in range(4):
@@ -285,7 +270,7 @@
             before = turned[m - 1] if m >= 1 else zero
             after = turned[m] if m <= w else zero
             cur = jnp.where(low, before, after)
-            square = (p0[e, m] + p1[e, m]) + (p2[e, m] + p3[e, m])
+            square = total(part_ref, e, m)
             one = bit(tab, step + 1, i, (i + 2 * m + 63 - w) & 63)
             two = 0
             if 2 * m + 1 <= 2 * w + 2:
@@ -295,11 +280,9 @@
             for ref, (lo, hi, first, last) in zip(refs, cuts):
                 if lo <= e < hi and first <= m < last:
                     ref[e - lo, m - first] = value
-    if spread:
-        copies_out(refs[0], copies_ref, sem)
-
-
-def finish_kernel(tab, p0, p1, p2, p3, cur_ref, y_ref):
+
+
+def finish_kernel(tab, part_ref, cur_ref, y_ref):
     w = BAND + STEPS - 1
     low = low_half()
     row0 = tab[PLACE] * 4
@@ -308,7 +291,7 @@
         i = tab[PERM + row0 + e]
         for m in range(w + 2):
             cur = cur_ref[e, m - 1] if 1 <= m <= w + 1 else jnp.zeros((8, 128), F32)
-            square = (p0[e, m] + p1[e, m]) + (p2[e, m] + p3[e, m])
+            square = total(part_ref, e, m)
             value = polynomial(tab, STEPS - 1, cur, square)
             turned = swap_halves(value)
             for half in (0, 1):
@@ -347,10 +330,9 @@
     )
 
 
-def reduce_group(tab, own, oth, tiles):
-    got = core_swap(oth)
-    parts = call(pair_kernel, [(4, tiles, 8, 128)] * 4, [own, got], tab=tab)
-    return [parts[0]] + [z_swap(parts[k], k) for k in (1, 2, 3)]
+def reduce_group(own, oth):
+    (pair,) = call(pair_kernel, [own.shape], [own, core_swap(oth)])
+    return lax.all_to_all(pair, "col", 0, 0, tiled=True)
 
 
 def exchange(value):
@@ -365,16 +347,14 @@
     split = call(split_kernel, [(4, 4, 8, 128)] * 8, [density])
     split = [split[0]] + [group_swap(split[k], k) for k in range(1, 8)]
     tab = tables(masks, branch, perm)
-    spread = [pltpu.SemaphoreType.DMA((16,))]
-    (copies,) = call(
+    (rows,) = call(
         compact_kernel,
-        [(16, 4, BAND + 1, 8, 128)],
+        [(4, BAND + 1, 8, 128)],
         split,
-        [pltpu.VMEM((8, 4, 4, 8, 128), F32), pltpu.VMEM((4, BAND + 1, 8, 128), F32)] + spread,
+        [pltpu.VMEM((8, 4, 4, 8, 128), F32)],
         tab=tab,
-        there=(0,),
     )
-    gathered = gather_rows(copies)
+    gathered = gather_rows(rows)
     for step in range(STEPS - 1):
         w = BAND + step
         left, count = geometry(w)
@@ -399,25 +379,18 @@
         else:
             kernel = lambda *refs, w=w, pieces=pieces: step_kernel(w, pieces, *refs)
             own, oth = call(kernel, [part, part], [cur] + around, scratch, tab=tab)
-        parts = reduce_group(tab, own, oth, w + 2)
-        if step < STEPS - 2:
-            pieces = halo_pieces(w + 1)
-            cuts = [(0, 4, 0, w + 2)]
-            for _, cut in pieces:
-                if cut not in cuts:
-                    cuts.append(cut)
-            kernel = lambda *refs, step=step, cuts=cuts: close_kernel(step, cuts, *refs)
-            shapes = [(hi - lo, last - first, 8, 128) for lo, hi, first, last in cuts]
-            sent = call(kernel, shapes, parts + [cur], tab=tab)
-            cur = sent[0]
-            around = [ring_shift(sent[cuts.index(cut)], d) for d, cut in pieces]
-        else:
-            kernel = lambda *refs, step=step: close_kernel(step, None, *refs)
-            scratch = [pltpu.VMEM((4, w + 2, 8, 128), F32)] + spread
-            (copies,) = call(
-                kernel, [(16, 4, w + 2, 8, 128)], parts + [cur], scratch, tab=tab, there=(0,)
-            )
-            gathered = gather_rows(copies)
+        parts = reduce_group(own, oth)
+        pieces = halo_pieces(w + 1) if step < STEPS - 2 else []
+        cuts = [(0, 4, 0, w + 2)]
+        for _, cut in pieces:
+            if cut not in cuts:
+                cuts.append(cut)
+        kernel = lambda *refs, step=step, cuts=cuts: close_kernel(step, cuts, *refs)
+        shapes = [(hi - lo, last - first, 8, 128) for lo, hi, first, last in cuts]
+        sent = call(kernel, shapes, [parts, cur], tab=tab)
+        cur = sent[0]
+        around = [ring_shift(sent[cuts.index(cut)], d) for d, cut in pieces]
+    gathered = gather_rows(cur)
     w = BAND + STEPS - 1
     part = (4, 4, w + 2, 8, 128)
     scratch = [
@@ -428,8 +401,8 @@
     own, oth, cur = call(
         last_step_kernel, [part, part, (4, w + 1, 8, 128)], [gathered], scratch, tab=tab
     )
-    parts = reduce_group(tab, own, oth, w + 2)
-    (full,) = call(finish_kernel, [(8, 4, 4, 8, 128)], parts + [cur], tab=tab)
+    parts = reduce_group(own, oth)
+    (full,) = call(finish_kernel, [(8, 4, 4, 8, 128)], [parts, cur], tab=tab)
     full = exchange(full)
     (out,) = call(join_kernel, [(256, 512)], [full])
     return out

time: 249 us -> 239 us (0.960)
  blocking collectives: 83.2 us -> 147 us
  waiting for transfers between devices: 75.6 us -> 32.9 us
  starting transfers between devices: 55.8 us -> 36.1 us
  Pallas kernels: 27.6 us -> 16.8 us
    all_to_all x0 -> x5, blocking collectives: none -> 64.4 us  [reduce_group(): return lax.all_to_all(pair, 'col', 0, 0, tiled=True)]
    ppermute x15 -> x0, waiting for transfers between devices: 43.1 us -> none  [z_swap(): return lax.ppermute(value, 'col', [(i, i ^ k) for i in range(4)])]
    ppermute x15 -> x0, starting transfers between devices: 19.7 us -> none  [z_swap(): return lax.ppermute(value, 'col', [(i, i ^ k) for i in range(4)])]
    pallas_call x18, Pallas kernels: 27.6 us -> 16.8 us  [call(): pl.pallas_call(kernel, out_shape=[jax.ShapeDtypeStruct(o, F32) for o in o...]
  transfers between devices with their start and end apart: 41 -> 26, of which waited for: 29 -> 13; matrix products, arithmetic and copies ran while one was open for 2% -> 2% of each run, Pallas kernels for 0% -> 0%
where the time goes in v3:
time: 239 us
  blocking collectives  147 us (62%)
  starting transfers between devices  36.1 us (15%)
  waiting for transfers between devices  32.9 us (14%)
  Pallas kernels  16.8 us (7%)
  local copies, waits for them, and re-layouts  4.14 us (2%)
    all_to_all x2, blocking collectives, gather_rows(): return lax.all_to_all(copies, 'row', 0, 0, tiled=True)  69.3 us
    all_to_all x5, blocking collectives, reduce_group(): return lax.all_to_all(pair, 'col', 0, 0, tiled=True)  64.4 us
    ppermute x14, waiting for transfers between devices, ring_shift(): lax.ppermute(value, 'row', [(RING[p], RING[(p + k) % 16]) for p in range(...  21.7 us
    pallas_call x18, Pallas kernels, call(): pl.pallas_call(kernel, out_shape=[jax.ShapeDtypeStruct(o, F32) for o in o...  16.8 us
    ppermute x5, starting transfers between devices, core_swap(): return lax.ppermute(value, 'layer', [(0, 1), (1, 0)])  13 us
    all_to_all x1, blocking collectives, exchange(): return lax.all_to_all(value, GROUP, 0, 0, tiled=True)  13 us
    ppermute x14, starting transfers between devices, ring_shift(): lax.ppermute(value, 'row', [(RING[p], RING[(p + k) % 16]) for p in range(...  12.6 us
    ppermute x7, starting transfers between devices, group_swap(): return lax.ppermute(value, GROUP, [(i, i ^ k) for i in range(8)])  10.5 us
  transfers between devices with their start and end apart: 26, of which 13 were waited for; matrix products, arithmetic and copies ran while one was open for 2% of the time, Pallas kernels for 0%

profile of v3, /device:TPU:1, one launch (start us, length us, event | category | flops | bytes accessed | tf_op | source)
XLA Modules:
  0.0 238.9 jit_solution(11273231107689796267)
XLA Ops:
  2.6 1.7 collective-permute-start.1
  4.4 3.6 %collective-permute-start.3 = (f32[4,4,8,128]{3,2,1,0:T(8,128)S(1)}, f32[4,4,8,128]{3,2,1,0:T(8,128)S(1)}, u32[]{:S(2)}, u32[]{:S(2)}) collective-permute-start(f32[4,4,8,128]{3,2,1,0:T(8,128)S(1)} %get-tuple-element.40), channel_id=1, source_target_pairs={{0,4},{1,5},{2,6},{3,7},{4,0},{5,1},{6,2},{7,3},{8,12},{9,13},{10,... | collective-permute-start | bytes 196616 | tf_op jit(solution)/shard_map/ppermute | solution.py:343
  10.2 3.5 %collective-permute-start.5 = (f32[4,4,8,128]{3,2,1,0:T(8,128)S(1)}, f32[4,4,8,128]{3,2,1,0:T(8,128)S(1)}, u32[]{:S(2)}, u32[]{:S(2)}) collective-permute-start(f32[4,4,8,128]{3,2,1,0:T(8,128)S(1)} %get-tuple-element.42), channel_id=1, source_target_pairs={{0,6},{1,7},{2,4},{3,5},{4,2},{5,3},{6,0},{7,1},{8,14},{9,15},{10,... | collective-permute-start | bytes 196616 | tf_op jit(solution)/shard_map/ppermute | solution.py:343
  16.4 2.6 %collective-permute-done.6.refs_7_ = f32[4,4,8,128]{3,2,1,0:T(8,128)S(1)} collective-permute-done((f32[4,4,8,128]{3,2,1,0:T(8,128)S(1)}, f32[4,4,8,128]{3,2,1,0:T(8,128)S(1)}, u32[]{:S(2)}, u32[]{:S(2)}) %collective-permute-start.6) | collective-permute-done | bytes 65568 | tf_op jit(solution)/shard_map/ppermute | solution.py:343
  20.2 31.1 %all_to_all.40.all_ref = f32[16,4,7,8,128]{4,3,2,1,0:T(8,128)S(1)} all-to-all(f32[16,4,7,8,128]{4,3,2,1,0:T(8,128)S(1)} %broadcast_in_dim.35), channel_id=1, replica_groups=mesh['row'=16,'col'=4,'layer'=2] {'row'}, dimensions={0} | all-to-all | bytes 3670016 | tf_op jit(solution)/shard_map/all_to_all | solution.py:132
  51.3 2.5 %shard_map.57 = (f32[4,4,8,8,128]{4,3,2,1,0:T(8,128)S(1)}, f32[4,4,8,8,128]{4,3,2,1,0:T(8,128)S(1)}, f32[4,7,8,128]{3,2,1,0:T(8,128)S(1)}) custom-call(s32[912]{0:T(1024)S(1)} %concatenate.3.tab.refs_0_, f32[16,4,7,8,128]{4,3,2,1,0:T(8,128)S(1)} %all_to_all.40.all_ref), custom_call_target="tpu_custom_call" | custom-call | tf_op jit(solution)/shard_map/pallas_call | solution.py:87
  53.8 1.8 collective-permute-start.7
  57.2 11.5 %all_to_all.41.refs_1_ = f32[4,4,8,8,128]{4,3,2,1,0:T(8,128)S(1)} all-to-all(f32[4,4,8,8,128]{4,3,2,1,0:T(8,128)S(1)} %shard_map.58), channel_id=1, replica_groups=mesh['row'=16,'col'=4,'layer'=2] {'col'}, dimensions={0} | all-to-all | bytes 1048576 | tf_op jit(solution)/shard_map/all_to_all | solution.py:335
  71.0 2.7 %collective-permute-start.11 = (f32[3,6,8,128]{3,2,1,0:T(8,128)S(1)}, f32[3,6,8,128]{3,2,1,0:T(8,128)S(1)}, u32[]{:S(2)}, u32[]{:S(2)}) collective-permute-start(f32[3,6,8,128]{3,2,1,0:T(8,128)S(1)} %get-tuple-element.49), channel_id=1, source_target_pairs={{0,24},{8,16},{32,0},{40,8},{64,32},{72,40},{96,64},{104,72},{120,... | collective-permute-start | bytes 221192 | tf_op jit(solution)/shard_map/ppermute | solution.py:25
  73.7 1.8 collective-permute-done.10.refs_4_
  76.1 3.7 %collective-permute-done.8.refs_2_ = f32[4,8,8,128]{3,2,1,0:T(8,128)S(1)} collective-permute-done((f32[4,8,8,128]{3,2,1,0:T(8,128)S(1)}, f32[4,8,8,128]{3,2,1,0:T(8,128)S(1)}, u32[]{:S(2)}, u32[]{:S(2)}) %collective-permute-start.8) | collective-permute-done | bytes 131104 | tf_op jit(solution)/shard_map/ppermute | solution.py:25
  81.5 1.8 collective-permute-start.12
  85.0 12.0 %all_to_all.42.refs_1_ = f32[4,4,9,8,128]{4,3,2,1,0:T(8,128)S(1)} all-to-all(f32[4,4,9,8,128]{4,3,2,1,0:T(8,128)S(1)} %shard_map.61), channel_id=1, replica_groups=mesh['row'=16,'col'=4,'layer'=2] {'col'}, dimensions={0} | all-to-all | bytes 1179648 | tf_op jit(solution)/shard_map/all_to_all | solution.py:335
  99.6 2.4 %collective-permute-start.16 = (f32[4,7,8,128]{3,2,1,0:T(8,128)S(1)}, f32[4,7,8,128]{3,2,1,0:T(8,128)S(1)}, u32[]{:S(2)}, u32[]{:S(2)}) collective-permute-start(f32[4,7,8,128]{3,2,1,0:T(8,128)S(1)} %get-tuple-element.54), channel_id=1, source_target_pairs={{0,24},{8,16},{32,0},{40,8},{64,32},{72,40},{96,64},{104,72},{120,... | collective-permute-start | bytes 344072 | tf_op jit(solution)/shard_map/ppermute | solution.py:25
  102.0 2.5 %collective-permute-done.15.refs_4_ = f32[4,7,8,128]{3,2,1,0:T(8,128)S(1)} collective-permute-done((f32[4,7,8,128]{3,2,1,0:T(8,128)S(1)}, f32[4,7,8,128]{3,2,1,0:T(8,128)S(1)}, u32[]{:S(2)}, u32[]{:S(2)}) %collective-permute-start.15) | collective-permute-done | bytes 114720 | tf_op jit(solution)/shard_map/ppermute | solution.py:25
  104.5 3.8 %collective-permute-done.13.refs_2_ = f32[4,9,8,128]{3,2,1,0:T(8,128)S(1)} collective-permute-done((f32[4,9,8,128]{3,2,1,0:T(8,128)S(1)}, f32[4,9,8,128]{3,2,1,0:T(8,128)S(1)}, u32[]{:S(2)}, u32[]{:S(2)}) %collective-permute-start.13) | collective-permute-done | bytes 147488 | tf_op jit(solution)/shard_map/ppermute | solution.py:25
  108.3 1.8 shard_map.63
  110.1 1.8 collective-permute-start.17
  113.7 13.0 %all_to_all.43.refs_1_ = f32[4,4,10,8,128]{4,3,2,1,0:T(8,128)S(1)} all-to-all(f32[4,4,10,8,128]{4,3,2,1,0:T(8,128)S(1)} %shard_map.64), channel_id=1, replica_groups=mesh['row'=16,'col'=4,'layer'=2] {'col'}, dimensions={0} | all-to-all | bytes 1310720 | tf_op jit(solution)/shard_map/all_to_all | solution.py:335
  129.2 2.5 %collective-permute-start.21 = (f32[4,8,8,128]{3,2,1,0:T(8,128)S(1)}, f32[4,8,8,128]{3,2,1,0:T(8,128)S(1)}, u32[]{:S(2)}, u32[]{:S(2)}) collective-permute-start(f32[4,8,8,128]{3,2,1,0:T(8,128)S(1)} %get-tuple-element.59), channel_id=1, source_target_pairs={{0,24},{8,16},{32,0},{40,8},{64,32},{72,40},{96,64},{104,72},{120,... | collective-permute-start | bytes 393224 | tf_op jit(solution)/shard_map/ppermute | solution.py:25
  131.8 5.4 %collective-permute-done.22.refs_6_ = f32[1,6,8,128]{3,2,1,0:T(8,128)S(1)} collective-permute-done((f32[1,6,8,128]{3,2,1,0:T(8,128)S(1)}, f32[1,6,8,128]{3,2,1,0:T(8,128)S(1)}, u32[]{:S(2)}, u32[]{:S(2)}) %collective-permute-start.22) | collective-permute-done | bytes 24608 | tf_op jit(solution)/shard_map/ppermute | solution.py:25
  137.2 3.9 %collective-permute-done.23.refs_7_ = f32[1,6,8,128]{3,2,1,0:T(8,128)S(1)} collective-permute-done((f32[1,6,8,128]{3,2,1,0:T(8,128)S(1)}, f32[1,6,8,128]{3,2,1,0:T(8,128)S(1)}, u32[]{:S(2)}, u32[]{:S(2)}) %collective-permute-start.23) | collective-permute-done | bytes 24608 | tf_op jit(solution)/shard_map/ppermute | solution.py:25
  141.1 1.9 shard_map.66
  142.9 4.1 %collective-permute-start.24 = (f32[4,4,11,8,128]{4,3,2,1,0:T(8,128)S(1)}, f32[4,4,11,8,128]{4,3,2,1,0:T(8,128)S(1)}, u32[]{:S(2)}, u32[]{:S(2)}) collective-permute-start(f32[4,4,11,8,128]{4,3,2,1,0:T(8,128)S(1)} %get-tuple-element.63), channel_id=1, source_target_pairs={{0,1},{1,0},{2,3},{3,2},{4,5},{5,4},{6,7},{7,6},{8,9},{9,8},{10,11... | collective-permute-start | bytes 2162696 | tf_op jit(solution)/shard_map/ppermute | solution.py:29
  147.0 1.8 collective-permute-done.24.got_ref
  148.9 13.4 %all_to_all.44.refs_1_ = f32[4,4,11,8,128]{4,3,2,1,0:T(8,128)S(1)} all-to-all(f32[4,4,11,8,128]{4,3,2,1,0:T(8,128)S(1)} %shard_map.67), channel_id=1, replica_groups=mesh['row'=16,'col'=4,'layer'=2] {'col'}, dimensions={0} | all-to-all | bytes 1441792 | tf_op jit(solution)/shard_map/all_to_all | solution.py:335
  163.4 38.2 %all_to_all.45.g_ref = f32[16,4,11,8,128]{4,3,2,1,0:T(8,128)S(1)} all-to-all(f32[16,4,11,8,128]{4,3,2,1,0:T(8,128)S(1)} %broadcast_in_dim.36), channel_id=1, replica_groups=mesh['row'=16,'col'=4,'layer'=2] {'row'}, dimensions={0} | all-to-all | bytes 5767168 | tf_op jit(solution)/shard_map/all_to_all | solution.py:132
  201.6 2.4 %shard_map.69 = (f32[4,4,12,8,128]{4,3,2,1,0:T(8,128)S(1)}, f32[4,4,12,8,128]{4,3,2,1,0:T(8,128)S(1)}, f32[4,11,8,128]{3,2,1,0:T(8,128)S(1)}) custom-call(s32[912]{0:T(1024)S(1)} %concatenate.3.tab.refs_0_, f32[16,4,11,8,128]{4,3,2,1,0:T(8,128)S(1)} %all_to_all.45.g_ref), custom_call_target="tpu_custom_call" | custom-call | tf_op jit(solution)/shard_map/pallas_call | solution.py:87
  204.0 3.4 %collective-permute-start.25 = (f32[4,4,12,8,128]{4,3,2,1,0:T(8,128)S(1)}, f32[4,4,12,8,128]{4,3,2,1,0:T(8,128)S(1)}, u32[]{:S(2)}, u32[]{:S(2)}) collective-permute-start(f32[4,4,12,8,128]{4,3,2,1,0:T(8,128)S(1)} %get-tuple-element.65), channel_id=1, source_target_pairs={{0,1},{1,0},{2,3},{3,2},{4,5},{5,4},{6,7},{7,6},{8,9},{9,8},{10,11... | collective-permute-start | bytes 2359304 | tf_op jit(solution)/shard_map/ppermute | solution.py:29
  207.5 1.9 collective-permute-done.25.got_ref
  209.5 14.4 %all_to_all.46.part_ref = f32[4,4,12,8,128]{4,3,2,1,0:T(8,128)S(1)} all-to-all(f32[4,4,12,8,128]{4,3,2,1,0:T(8,128)S(1)} %shard_map.70), channel_id=1, replica_groups=mesh['row'=16,'col'=4,'layer'=2] {'col'}, dimensions={0} | all-to-all | bytes 1572864 | tf_op jit(solution)/shard_map/all_to_all | solution.py:335
  225.1 13.0 %all_to_all.47.y_ref = f32[8,4,4,8,128]{4,3,2,1,0:T(8,128)S(1)} all-to-all(f32[8,4,4,8,128]{4,3,2,1,0:T(8,128)S(1)} %shard_map.71), channel_id=1, replica_groups=mesh['row'=16,'col'=4,'layer'=2] {'col','layer'}, dimensions={0} | all-to-all | bytes 1048576 | tf_op jit(solution)/shard_map/all_to_all | solution.py:339
  (58 shorter events, 26.5 us)
Async XLA Ops:
  0.0 1.0 copy-start
  1.1 9.1 %collective-permute-start = (f32[4,4,8,128]{3,2,1,0:T(8,128)S(1)}, f32[4,4,8,128]{3,2,1,0:T(8,128)S(1)}, u32[]{:S(2)}, u32[]{:S(2)}) collective-permute-start(f32[4,4,8,128]{3,2,1,0:T(8,128)S(1)} %get-tuple-element.37), channel_id=1, source_target_pairs={{0,1},{1,0},{2,3},{3,2},{4,5},{5,4},{6,7},{7,6},{8,9},{9,8},{10,11... | collective-permute-start | bytes 196616 | tf_op jit(solution)/shard_map/ppermute | solution.py:343
  2.6 11.1 %collective-permute-start.1 = (f32[4,4,8,128]{3,2,1,0:T(8,128)S(1)}, f32[4,4,8,128]{3,2,1,0:T(8,128)S(1)}, u32[]{:S(2)}, u32[]{:S(2)}) collective-permute-start(f32[4,4,8,128]{3,2,1,0:T(8,128)S(1)} %get-tuple-element.38), channel_id=1, source_target_pairs={{0,2},{1,3},{2,0},{3,1},{4,6},{5,7},{6,4},{7,5},{8,10},{9,11},{10,... | collective-permute-start | bytes 196616 | tf_op jit(solution)/shard_map/ppermute | solution.py:343
  4.3 12.0 %collective-permute-start.2 = (f32[4,4,8,128]{3,2,1,0:T(8,128)S(1)}, f32[4,4,8,128]{3,2,1,0:T(8,128)S(1)}, u32[]{:S(2)}, u32[]{:S(2)}) collective-permute-start(f32[4,4,8,128]{3,2,1,0:T(8,128)S(1)} %get-tuple-element.39), channel_id=1, source_target_pairs={{0,3},{1,2},{2,1},{3,0},{4,7},{5,6},{6,5},{7,4},{8,11},{9,10},{10,... | collective-permute-start | bytes 196616 | tf_op jit(solution)/shard_map/ppermute | solution.py:343
  4.4 12.0 %collective-permute-start.3 = (f32[4,4,8,128]{3,2,1,0:T(8,128)S(1)}, f32[4,4,8,128]{3,2,1,0:T(8,128)S(1)}, u32[]{:S(2)}, u32[]{:S(2)}) collective-permute-start(f32[4,4,8,128]{3,2,1,0:T(8,128)S(1)} %get-tuple-element.40), channel_id=1, source_target_pairs={{0,4},{1,5},{2,6},{3,7},{4,0},{5,1},{6,2},{7,3},{8,12},{9,13},{10,... | collective-permute-start | bytes 196616 | tf_op jit(solution)/shard_map/ppermute | solution.py:343
  8.0 8.4 %collective-permute-start.4 = (f32[4,4,8,128]{3,2,1,0:T(8,128)S(1)}, f32[4,4,8,128]{3,2,1,0:T(8,128)S(1)}, u32[]{:S(2)}, u32[]{:S(2)}) collective-permute-start(f32[4,4,8,128]{3,2,1,0:T(8,128)S(1)} %get-tuple-element.41), channel_id=1, source_target_pairs={{0,5},{1,4},{2,7},{3,6},{4,1},{5,0},{6,3},{7,2},{8,13},{9,12},{10,... | collective-permute-start | bytes 196616 | tf_op jit(solution)/shard_map/ppermute | solution.py:343
  10.2 6.2 %collective-permute-start.5 = (f32[4,4,8,128]{3,2,1,0:T(8,128)S(1)}, f32[4,4,8,128]{3,2,1,0:T(8,128)S(1)}, u32[]{:S(2)}, u32[]{:S(2)}) collective-permute-start(f32[4,4,8,128]{3,2,1,0:T(8,128)S(1)} %get-tuple-element.42), channel_id=1, source_target_pairs={{0,6},{1,7},{2,4},{3,5},{4,2},{5,3},{6,0},{7,1},{8,14},{9,15},{10,... | collective-permute-start | bytes 196616 | tf_op jit(solution)/shard_map/ppermute | solution.py:343
  13.7 5.3 %collective-permute-start.6 = (f32[4,4,8,128]{3,2,1,0:T(8,128)S(1)}, f32[4,4,8,128]{3,2,1,0:T(8,128)S(1)}, u32[]{:S(2)}, u32[]{:S(2)}) collective-permute-start(f32[4,4,8,128]{3,2,1,0:T(8,128)S(1)} %get-tuple-element.43), channel_id=1, source_target_pairs={{0,7},{1,6},{2,5},{3,4},{4,3},{5,2},{6,1},{7,0},{8,15},{9,14},{10,... | collective-permute-start | bytes 196616 | tf_op jit(solution)/shard_map/ppermute | solution.py:343
  53.8 3.4 %collective-permute-start.7 = (f32[4,4,8,8,128]{4,3,2,1,0:T(8,128)S(1)}, f32[4,4,8,8,128]{4,3,2,1,0:T(8,128)S(1)}, u32[]{:S(2)}, u32[]{:S(2)}) collective-permute-start(f32[4,4,8,8,128]{4,3,2,1,0:T(8,128)S(1)} %get-tuple-element.45), channel_id=1, source_target_pairs={{0,1},{1,0},{2,3},{3,2},{4,5},{5,4},{6,7},{7,6},{8,9},{9,8},{10,11... | collective-permute-start | bytes 1572872 | tf_op jit(solution)/shard_map/ppermute | solution.py:29
  69.4 6.7 %collective-permute-start.9 = (f32[4,8,8,128]{3,2,1,0:T(8,128)S(1)}, f32[4,8,8,128]{3,2,1,0:T(8,128)S(1)}, u32[]{:S(2)}, u32[]{:S(2)}) collective-permute-start(f32[4,8,8,128]{3,2,1,0:T(8,128)S(1)} %get-tuple-element.47.refs_1_.refs_2_), channel_id=1, source_target_pairs={{0,16},{8,0},{32,8},{40,32},{64,40},{72,64},{96,72},{104,96},{120,... | collective-permute-start | bytes 393224 | tf_op jit(solution)/shard_map/ppermute | solution.py:25
  70.7 9.1 %collective-permute-start.8 = (f32[4,8,8,128]{3,2,1,0:T(8,128)S(1)}, f32[4,8,8,128]{3,2,1,0:T(8,128)S(1)}, u32[]{:S(2)}, u32[]{:S(2)}) collective-permute-start(f32[4,8,8,128]{3,2,1,0:T(8,128)S(1)} %get-tuple-element.47.refs_1_.refs_2_), channel_id=1, source_target_pairs={{0,8},{8,32},{32,40},{40,64},{64,72},{72,96},{96,104},{104,120},{1... | collective-permute-start | bytes 393224 | tf_op jit(solution)/shard_map/ppermute | solution.py:25
  71.0 4.5 %collective-permute-start.10 = (f32[3,6,8,128]{3,2,1,0:T(8,128)S(1)}, f32[3,6,8,128]{3,2,1,0:T(8,128)S(1)}, u32[]{:S(2)}, u32[]{:S(2)}) collective-permute-start(f32[3,6,8,128]{3,2,1,0:T(8,128)S(1)} %get-tuple-element.48), channel_id=1, source_target_pairs={{0,32},{8,40},{32,64},{40,72},{64,96},{72,104},{96,120},{104,112},... | collective-permute-start | bytes 221192 | tf_op jit(solution)/shard_map/ppermute | solution.py:25
  71.0 4.5 %collective-permute-start.11 = (f32[3,6,8,128]{3,2,1,0:T(8,128)S(1)}, f32[3,6,8,128]{3,2,1,0:T(8,128)S(1)}, u32[]{:S(2)}, u32[]{:S(2)}) collective-permute-start(f32[3,6,8,128]{3,2,1,0:T(8,128)S(1)} %get-tuple-element.49), channel_id=1, source_target_pairs={{0,24},{8,16},{32,0},{40,8},{64,32},{72,40},{96,64},{104,72},{120,... | collective-permute-start | bytes 221192 | tf_op jit(solution)/shard_map/ppermute | solution.py:25
  81.5 3.5 %collective-permute-start.12 = (f32[4,4,9,8,128]{4,3,2,1,0:T(8,128)S(1)}, f32[4,4,9,8,128]{4,3,2,1,0:T(8,128)S(1)}, u32[]{:S(2)}, u32[]{:S(2)}) collective-permute-start(f32[4,4,9,8,128]{4,3,2,1,0:T(8,128)S(1)} %get-tuple-element.51), channel_id=1, source_target_pairs={{0,1},{1,0},{2,3},{3,2},{4,5},{5,4},{6,7},{7,6},{8,9},{9,8},{10,11... | collective-permute-start | bytes 1769480 | tf_op jit(solution)/shard_map/ppermute | solution.py:29
  97.8 6.7 %collective-permute-start.14 = (f32[4,9,8,128]{3,2,1,0:T(8,128)S(1)}, f32[4,9,8,128]{3,2,1,0:T(8,128)S(1)}, u32[]{:S(2)}, u32[]{:S(2)}) collective-permute-start(f32[4,9,8,128]{3,2,1,0:T(8,128)S(1)} %get-tuple-element.52.refs_1_.refs_2_), channel_id=1, source_target_pairs={{0,16},{8,0},{32,8},{40,32},{64,40},{72,64},{96,72},{104,96},{120,... | collective-permute-start | bytes 442376 | tf_op jit(solution)/shard_map/ppermute | solution.py:25
  97.9 10.4 %collective-permute-start.13 = (f32[4,9,8,128]{3,2,1,0:T(8,128)S(1)}, f32[4,9,8,128]{3,2,1,0:T(8,128)S(1)}, u32[]{:S(2)}, u32[]{:S(2)}) collective-permute-start(f32[4,9,8,128]{3,2,1,0:T(8,128)S(1)} %get-tuple-element.52.refs_1_.refs_2_), channel_id=1, source_target_pairs={{0,8},{8,32},{32,40},{40,64},{64,72},{72,96},{96,104},{104,120},{1... | collective-permute-start | bytes 442376 | tf_op jit(solution)/shard_map/ppermute | solution.py:25
  99.3 5.1 %collective-permute-start.15 = (f32[4,7,8,128]{3,2,1,0:T(8,128)S(1)}, f32[4,7,8,128]{3,2,1,0:T(8,128)S(1)}, u32[]{:S(2)}, u32[]{:S(2)}) collective-permute-start(f32[4,7,8,128]{3,2,1,0:T(8,128)S(1)} %get-tuple-element.53), channel_id=1, source_target_pairs={{0,32},{8,40},{32,64},{40,72},{64,96},{72,104},{96,120},{104,112},... | collective-permute-start | bytes 344072 | tf_op jit(solution)/shard_map/ppermute | solution.py:25
  99.6 4.9 %collective-permute-start.16 = (f32[4,7,8,128]{3,2,1,0:T(8,128)S(1)}, f32[4,7,8,128]{3,2,1,0:T(8,128)S(1)}, u32[]{:S(2)}, u32[]{:S(2)}) collective-permute-start(f32[4,7,8,128]{3,2,1,0:T(8,128)S(1)} %get-tuple-element.54), channel_id=1, source_target_pairs={{0,24},{8,16},{32,0},{40,8},{64,32},{72,40},{96,64},{104,72},{120,... | collective-permute-start | bytes 344072 | tf_op jit(solution)/shard_map/ppermute | solution.py:25
  110.1 3.5 %collective-permute-start.17 = (f32[4,4,10,8,128]{4,3,2,1,0:T(8,128)S(1)}, f32[4,4,10,8,128]{4,3,2,1,0:T(8,128)S(1)}, u32[]{:S(2)}, u32[]{:S(2)}) collective-permute-start(f32[4,4,10,8,128]{4,3,2,1,0:T(8,128)S(1)} %get-tuple-element.56), channel_id=1, source_target_pairs={{0,1},{1,0},{2,3},{3,2},{4,5},{5,4},{6,7},{7,6},{8,9},{9,8},{10,11... | collective-permute-start | bytes 1966088 | tf_op jit(solution)/shard_map/ppermute | solution.py:29
  127.6 13.5 %collective-permute-start.19 = (f32[4,10,8,128]{3,2,1,0:T(8,128)S(1)}, f32[4,10,8,128]{3,2,1,0:T(8,128)S(1)}, u32[]{:S(2)}, u32[]{:S(2)}) collective-permute-start(f32[4,10,8,128]{3,2,1,0:T(8,128)S(1)} %get-tuple-element.57.refs_1_.refs_2_), channel_id=1, source_target_pairs={{0,16},{8,0},{32,8},{40,32},{64,40},{72,64},{96,72},{104,96},{120,... | collective-permute-start | bytes 491528 | tf_op jit(solution)/shard_map/ppermute | solution.py:25
  128.2 12.8 %collective-permute-start.18 = (f32[4,10,8,128]{3,2,1,0:T(8,128)S(1)}, f32[4,10,8,128]{3,2,1,0:T(8,128)S(1)}, u32[]{:S(2)}, u32[]{:S(2)}) collective-permute-start(f32[4,10,8,128]{3,2,1,0:T(8,128)S(1)} %get-tuple-element.57.refs_1_.refs_2_), channel_id=1, source_target_pairs={{0,8},{8,32},{32,40},{40,64},{64,72},{72,96},{96,104},{104,120},{1... | collective-permute-start | bytes 491528 | tf_op jit(solution)/shard_map/ppermute | solution.py:25
  129.1 12.0 %collective-permute-start.20 = (f32[4,8,8,128]{3,2,1,0:T(8,128)S(1)}, f32[4,8,8,128]{3,2,1,0:T(8,128)S(1)}, u32[]{:S(2)}, u32[]{:S(2)}) collective-permute-start(f32[4,8,8,128]{3,2,1,0:T(8,128)S(1)} %get-tuple-element.58), channel_id=1, source_target_pairs={{0,32},{8,40},{32,64},{40,72},{64,96},{72,104},{96,120},{104,112},... | collective-permute-start | bytes 393224 | tf_op jit(solution)/shard_map/ppermute | solution.py:25
  129.2 11.8 %collective-permute-start.21 = (f32[4,8,8,128]{3,2,1,0:T(8,128)S(1)}, f32[4,8,8,128]{3,2,1,0:T(8,128)S(1)}, u32[]{:S(2)}, u32[]{:S(2)}) collective-permute-start(f32[4,8,8,128]{3,2,1,0:T(8,128)S(1)} %get-tuple-element.59), channel_id=1, source_target_pairs={{0,24},{8,16},{32,0},{40,8},{64,32},{72,40},{96,64},{104,72},{120,... | collective-permute-start | bytes 393224 | tf_op jit(solution)/shard_map/ppermute | solution.py:25
  131.8 5.4 %collective-permute-start.22 = (f32[1,6,8,128]{3,2,1,0:T(8,128)S(1)}, f32[1,6,8,128]{3,2,1,0:T(8,128)S(1)}, u32[]{:S(2)}, u32[]{:S(2)}) collective-permute-start(f32[1,6,8,128]{3,2,1,0:T(8,128)S(1)} %get-tuple-element.60), channel_id=1, source_target_pairs={{0,40},{8,64},{32,72},{40,96},{64,104},{72,120},{96,112},{104,88},... | collective-permute-start | bytes 73736 | tf_op jit(solution)/shard_map/ppermute | solution.py:25
  137.2 3.9 %collective-permute-start.23 = (f32[1,6,8,128]{3,2,1,0:T(8,128)S(1)}, f32[1,6,8,128]{3,2,1,0:T(8,128)S(1)}, u32[]{:S(2)}, u32[]{:S(2)}) collective-permute-start(f32[1,6,8,128]{3,2,1,0:T(8,128)S(1)} %get-tuple-element.61), channel_id=1, source_target_pairs={{0,48},{8,24},{32,16},{40,0},{64,8},{72,32},{96,40},{104,64},{120,... | collective-permute-start | bytes 73736 | tf_op jit(solution)/shard_map/ppermute | solution.py:25
  142.9 5.9 %collective-permute-start.24 = (f32[4,4,11,8,128]{4,3,2,1,0:T(8,128)S(1)}, f32[4,4,11,8,128]{4,3,2,1,0:T(8,128)S(1)}, u32[]{:S(2)}, u32[]{:S(2)}) collective-permute-start(f32[4,4,11,8,128]{4,3,2,1,0:T(8,128)S(1)} %get-tuple-element.63), channel_id=1, source_target_pairs={{0,1},{1,0},{2,3},{3,2},{4,5},{5,4},{6,7},{7,6},{8,9},{9,8},{10,11... | collective-permute-start | bytes 2162696 | tf_op jit(solution)/shard_map/ppermute | solution.py:29
  204.0 5.3 %collective-permute-start.25 = (f32[4,4,12,8,128]{4,3,2,1,0:T(8,128)S(1)}, f32[4,4,12,8,128]{4,3,2,1,0:T(8,128)S(1)}, u32[]{:S(2)}, u32[]{:S(2)}) collective-permute-start(f32[4,4,12,8,128]{4,3,2,1,0:T(8,128)S(1)} %get-tuple-element.65), channel_id=1, source_target_pairs={{0,1},{1,0},{2,3},{3,2},{4,5},{5,4},{6,7},{7,6},{8,9},{9,8},{10,11... | collective-permute-start | bytes 2359304 | tf_op jit(solution)/shard_map/ppermute | solution.py:29

commit v4 on v3

--- a/solution.py
+++ b/solution.py
@@ -21,12 +21,22 @@
 RING = [ring_xy(p)[0] * 4 + ring_xy(p)[1] for p in range(16)]
 
 
+def permute(value, axes, pairs):
+    flat = value.reshape(-1, 128)
+    return lax.ppermute(flat, axes, pairs).reshape(value.shape)
+
+
+def exchange(value, axes):
+    flat = value.reshape(value.shape[0], -1, 128)
+    return lax.all_to_all(flat, axes, 0, 0, tiled=True).reshape(value.shape)
+
+
 def ring_shift(value, k):
-    return lax.ppermute(value, "row", [(RING[p], RING[(p + k) % 16]) for p in range(16)])
+    return permute(value, "row", [(RING[p], RING[(p + k) % 16]) for p in range(16)])
 
 
 def core_swap(value):
-    return lax.ppermute(value, "layer", [(0, 1), (1, 0)])
+    return permute(value, "layer", [(0, 1), (1, 0)])
 
 
 def low_half():
@@ -129,7 +139,7 @@
 
 def gather_rows(rows):
     copies = jnp.broadcast_to(rows[None], (16,) + rows.shape)
-    return lax.all_to_all(copies, "row", 0, 0, tiled=True)
+    return exchange(copies, "row")
 
 
 def write_slabs(tab, p_ref, own_ref, oth_ref, e, base, d, tiles):
@@ -332,15 +342,11 @@
 
 def reduce_group(own, oth):
     (pair,) = call(pair_kernel, [own.shape], [own, core_swap(oth)])
-    return lax.all_to_all(pair, "col", 0, 0, tiled=True)
-
-
-def exchange(value):
-    return lax.all_to_all(value, GROUP, 0, 0, tiled=True)
+    return exchange(pair, "col")
 
 
 def group_swap(value, k):
-    return lax.ppermute(value, GROUP, [(i, i ^ k) for i in range(8)])
+    return permute(value, GROUP, [(i, i ^ k) for i in range(8)])
 
 
 def shards(density, masks, branch, perm):
@@ -403,7 +409,7 @@
     )
     parts = reduce_group(own, oth)
     (full,) = call(finish_kernel, [(8, 4, 4, 8, 128)], [parts, cur], tab=tab)
-    full = exchange(full)
+    full = exchange(full, GROUP)
     (out,) = call(join_kernel, [(256, 512)], [full])
     return out
 

time: 239 us -> 239 us (level)
  transfers between devices with their start and end apart: 26 -> 26, of which waited for: 13 -> 14; matrix products, arithmetic and copies ran while one was open for 2% -> 2% of each run, Pallas kernels for 0% -> 0%
where the time goes in v4:
time: 239 us
  blocking collectives  148 us (62%)
  starting transfers between devices  35.1 us (15%)
  waiting for transfers between devices  32.6 us (14%)
  Pallas kernels  16.8 us (7%)
  local copies, waits for them, and re-layouts  4.11 us (2%)
    all_to_all x8, blocking collectives, exchange(): return lax.all_to_all(flat, axes, 0, 0, tiled=True).reshape(value.shape)  148 us
    ppermute x26, starting transfers between devices, permute(): return lax.ppermute(flat, axes, pairs).reshape(value.shape)  35.1 us
    ppermute x26, waiting for transfers between devices, permute(): return lax.ppermute(flat, axes, pairs).reshape(value.shape)  32.6 us
    pallas_call x18, Pallas kernels, call(): pl.pallas_call(kernel, out_shape=[jax.ShapeDtypeStruct(o, F32) for o in o...  16.8 us
  transfers between devices with their start and end apart: 26, of which 14 were waited for; matrix products, arithmetic and copies ran while one was open for 2% of the time, Pallas kernels for 0%

profile of v4, /device:TPU:1, one launch (start us, length us, event | category | flops | bytes accessed | tf_op | source)
XLA Modules:
  0.0 239.0 jit_solution(15202898835602422588)
XLA Ops:
  2.6 1.7 collective-permute-start.1
  4.4 3.6 %collective-permute-start.3 = (f32[128,128]{1,0:T(8,128)S(1)}, f32[128,128]{1,0:T(8,128)S(1)}, u32[]{:S(2)}, u32[]{:S(2)}) collective-permute-start(f32[128,128]{1,0:T(8,128)S(1)} %bitcast.136), channel_id=1, source_target_pairs={{0,4},{1,5},{2,6},{3,7},{4,0},{5,1},{6,2},{7,3},{8,12},{9,13},{10,... | collective-permute-start | bytes 196616 | tf_op jit(solution)/shard_map/ppermute | solution.py:26
  10.2 3.5 %collective-permute-start.5 = (f32[128,128]{1,0:T(8,128)S(1)}, f32[128,128]{1,0:T(8,128)S(1)}, u32[]{:S(2)}, u32[]{:S(2)}) collective-permute-start(f32[128,128]{1,0:T(8,128)S(1)} %bitcast.134), channel_id=1, source_target_pairs={{0,6},{1,7},{2,4},{3,5},{4,2},{5,3},{6,0},{7,1},{8,14},{9,15},{10,... | collective-permute-start | bytes 196616 | tf_op jit(solution)/shard_map/ppermute | solution.py:26
  16.4 2.6 %collective-permute-done.6 = f32[128,128]{1,0:T(8,128)S(1)} collective-permute-done((f32[128,128]{1,0:T(8,128)S(1)}, f32[128,128]{1,0:T(8,128)S(1)}, u32[]{:S(2)}, u32[]{:S(2)}) %collective-permute-start.6) | collective-permute-done | bytes 65568 | tf_op jit(solution)/shard_map/ppermute | solution.py:26
  20.1 31.1 %all_to_all.40 = f32[16,224,128]{2,1,0:T(8,128)S(1)} all-to-all(f32[16,224,128]{2,1,0:T(8,128)S(1)} %broadcast_in_dim.40), channel_id=1, replica_groups=mesh['row'=16,'col'=4,'layer'=2] {'row'}, dimensions={0} | all-to-all | bytes 3670016 | tf_op jit(solution)/shard_map/all_to_all | solution.py:31
  51.2 2.5 %shard_map.57 = (f32[4,4,8,8,128]{4,3,2,1,0:T(8,128)S(1)}, f32[4,4,8,8,128]{4,3,2,1,0:T(8,128)S(1)}, f32[4,7,8,128]{3,2,1,0:T(8,128)S(1)}) custom-call(s32[912]{0:T(1024)S(1)} %concatenate.3.tab.refs_0_, f32[16,4,7,8,128]{4,3,2,1,0:T(8,128)S(1)} %bitcast.75), custom_call_target="tpu_custom_call" | custom-call | tf_op jit(solution)/shard_map/pallas_call | solution.py:97
  53.8 1.8 collective-permute-start.7
  57.2 11.5 %all_to_all.41 = f32[4,256,128]{2,1,0:T(8,128)S(1)} all-to-all(f32[4,256,128]{2,1,0:T(8,128)S(1)} %bitcast.85), channel_id=1, replica_groups=mesh['row'=16,'col'=4,'layer'=2] {'col'}, dimensions={0} | all-to-all | bytes 1048576 | tf_op jit(solution)/shard_map/all_to_all | solution.py:31
  72.4 2.7 %collective-permute-done.11 = f32[144,128]{1,0:T(8,128)S(1)} collective-permute-done((f32[144,128]{1,0:T(8,128)S(1)}, f32[144,128]{1,0:T(8,128)S(1)}, u32[]{:S(2)}, u32[]{:S(2)}) %collective-permute-start.11) | collective-permute-done | bytes 73760 | tf_op jit(solution)/shard_map/ppermute | solution.py:26
  76.5 3.3 %collective-permute-done.8 = f32[256,128]{1,0:T(8,128)S(1)} collective-permute-done((f32[256,128]{1,0:T(8,128)S(1)}, f32[256,128]{1,0:T(8,128)S(1)}, u32[]{:S(2)}, u32[]{:S(2)}) %collective-permute-start.8) | collective-permute-done | bytes 131104 | tf_op jit(solution)/shard_map/ppermute | solution.py:26
  79.8 1.7 shard_map.60
  81.5 1.8 collective-permute-start.12
  83.3 1.6 collective-permute-done.12
  85.0 12.0 %all_to_all.42 = f32[4,288,128]{2,1,0:T(8,128)S(1)} all-to-all(f32[4,288,128]{2,1,0:T(8,128)S(1)} %bitcast.82), channel_id=1, replica_groups=mesh['row'=16,'col'=4,'layer'=2] {'col'}, dimensions={0} | all-to-all | bytes 1179648 | tf_op jit(solution)/shard_map/all_to_all | solution.py:31
  100.8 3.4 %collective-permute-done.16 = f32[224,128]{1,0:T(8,128)S(1)} collective-permute-done((f32[224,128]{1,0:T(8,128)S(1)}, f32[224,128]{1,0:T(8,128)S(1)}, u32[]{:S(2)}, u32[]{:S(2)}) %collective-permute-start.16) | collective-permute-done | bytes 114720 | tf_op jit(solution)/shard_map/ppermute | solution.py:26
  104.3 3.1 %collective-permute-done.13 = f32[288,128]{1,0:T(8,128)S(1)} collective-permute-done((f32[288,128]{1,0:T(8,128)S(1)}, f32[288,128]{1,0:T(8,128)S(1)}, u32[]{:S(2)}, u32[]{:S(2)}) %collective-permute-start.13) | collective-permute-done | bytes 147488 | tf_op jit(solution)/shard_map/ppermute | solution.py:26
  107.4 1.8 shard_map.63
  109.3 2.4 %collective-permute-start.17 = (f32[1280,128]{1,0:T(8,128)S(1)}, f32[1280,128]{1,0:T(8,128)S(1)}, u32[]{:S(2)}, u32[]{:S(2)}) collective-permute-start(f32[1280,128]{1,0:T(8,128)S(1)} %bitcast.124), channel_id=1, source_target_pairs={{0,1},{1,0},{2,3},{3,2},{4,5},{5,4},{6,7},{7,6},{8,9},{9,8},{10,11... | collective-permute-start | bytes 1966088 | tf_op jit(solution)/shard_map/ppermute | solution.py:26
  111.7 1.7 collective-permute-done.17
  113.5 13.0 %all_to_all.43 = f32[4,320,128]{2,1,0:T(8,128)S(1)} all-to-all(f32[4,320,128]{2,1,0:T(8,128)S(1)} %bitcast.81), channel_id=1, replica_groups=mesh['row'=16,'col'=4,'layer'=2] {'col'}, dimensions={0} | all-to-all | bytes 1310720 | tf_op jit(solution)/shard_map/all_to_all | solution.py:31
  131.6 4.0 %collective-permute-done.22 = f32[48,128]{1,0:T(8,128)S(1)} collective-permute-done((f32[48,128]{1,0:T(8,128)S(1)}, f32[48,128]{1,0:T(8,128)S(1)}, u32[]{:S(2)}, u32[]{:S(2)}) %collective-permute-start.22) | collective-permute-done | bytes 24608 | tf_op jit(solution)/shard_map/ppermute | solution.py:26
  136.2 3.3 %collective-permute-done.23 = f32[48,128]{1,0:T(8,128)S(1)} collective-permute-done((f32[48,128]{1,0:T(8,128)S(1)}, f32[48,128]{1,0:T(8,128)S(1)}, u32[]{:S(2)}, u32[]{:S(2)}) %collective-permute-start.23) | collective-permute-done | bytes 24608 | tf_op jit(solution)/shard_map/ppermute | solution.py:26
  139.5 1.9 shard_map.66
  141.4 4.3 %collective-permute-start.24 = (f32[1408,128]{1,0:T(8,128)S(1)}, f32[1408,128]{1,0:T(8,128)S(1)}, u32[]{:S(2)}, u32[]{:S(2)}) collective-permute-start(f32[1408,128]{1,0:T(8,128)S(1)} %bitcast.123), channel_id=1, source_target_pairs={{0,1},{1,0},{2,3},{3,2},{4,5},{5,4},{6,7},{7,6},{8,9},{9,8},{10,11... | collective-permute-start | bytes 2162696 | tf_op jit(solution)/shard_map/ppermute | solution.py:26
  145.7 1.8 collective-permute-done.24
  147.6 13.4 %all_to_all.44 = f32[4,352,128]{2,1,0:T(8,128)S(1)} all-to-all(f32[4,352,128]{2,1,0:T(8,128)S(1)} %bitcast.78), channel_id=1, replica_groups=mesh['row'=16,'col'=4,'layer'=2] {'col'}, dimensions={0} | all-to-all | bytes 1441792 | tf_op jit(solution)/shard_map/all_to_all | solution.py:31
  162.1 39.6 %all_to_all.45 = f32[16,352,128]{2,1,0:T(8,128)S(1)} all-to-all(f32[16,352,128]{2,1,0:T(8,128)S(1)} %broadcast_in_dim.42), channel_id=1, replica_groups=mesh['row'=16,'col'=4,'layer'=2] {'row'}, dimensions={0} | all-to-all | bytes 5767168 | tf_op jit(solution)/shard_map/all_to_all | solution.py:31
  201.7 2.4 %shard_map.69 = (f32[4,4,12,8,128]{4,3,2,1,0:T(8,128)S(1)}, f32[4,4,12,8,128]{4,3,2,1,0:T(8,128)S(1)}, f32[4,11,8,128]{3,2,1,0:T(8,128)S(1)}) custom-call(s32[912]{0:T(1024)S(1)} %concatenate.3.tab.refs_0_, f32[16,4,11,8,128]{4,3,2,1,0:T(8,128)S(1)} %bitcast.74), custom_call_target="tpu_custom_call" | custom-call | tf_op jit(solution)/shard_map/pallas_call | solution.py:97
  204.1 3.4 %collective-permute-start.25 = (f32[1536,128]{1,0:T(8,128)S(1)}, f32[1536,128]{1,0:T(8,128)S(1)}, u32[]{:S(2)}, u32[]{:S(2)}) collective-permute-start(f32[1536,128]{1,0:T(8,128)S(1)} %bitcast.122), channel_id=1, source_target_pairs={{0,1},{1,0},{2,3},{3,2},{4,5},{5,4},{6,7},{7,6},{8,9},{9,8},{10,11... | collective-permute-start | bytes 2359304 | tf_op jit(solution)/shard_map/ppermute | solution.py:26
  207.5 1.9 collective-permute-done.25
  209.5 14.4 %all_to_all.46 = f32[4,384,128]{2,1,0:T(8,128)S(1)} all-to-all(f32[4,384,128]{2,1,0:T(8,128)S(1)} %bitcast.77), channel_id=1, replica_groups=mesh['row'=16,'col'=4,'layer'=2] {'col'}, dimensions={0} | all-to-all | bytes 1572864 | tf_op jit(solution)/shard_map/all_to_all | solution.py:31
  225.2 13.0 %all_to_all.47 = f32[8,128,128]{2,1,0:T(8,128)S(1)} all-to-all(f32[8,128,128]{2,1,0:T(8,128)S(1)} %bitcast.84), channel_id=1, replica_groups=mesh['row'=16,'col'=4,'layer'=2] {'col','layer'}, dimensions={0} | all-to-all | bytes 1048576 | tf_op jit(solution)/shard_map/all_to_all | solution.py:31
  (58 shorter events, 28.2 us)
Async XLA Ops:
  0.0 1.0 copy-start
  1.1 9.1 %collective-permute-start = (f32[128,128]{1,0:T(8,128)S(1)}, f32[128,128]{1,0:T(8,128)S(1)}, u32[]{:S(2)}, u32[]{:S(2)}) collective-permute-start(f32[128,128]{1,0:T(8,128)S(1)} %bitcast.139), channel_id=1, source_target_pairs={{0,1},{1,0},{2,3},{3,2},{4,5},{5,4},{6,7},{7,6},{8,9},{9,8},{10,11... | collective-permute-start | bytes 196616 | tf_op jit(solution)/shard_map/ppermute | solution.py:26
  2.6 11.1 %collective-permute-start.1 = (f32[128,128]{1,0:T(8,128)S(1)}, f32[128,128]{1,0:T(8,128)S(1)}, u32[]{:S(2)}, u32[]{:S(2)}) collective-permute-start(f32[128,128]{1,0:T(8,128)S(1)} %bitcast.138), channel_id=1, source_target_pairs={{0,2},{1,3},{2,0},{3,1},{4,6},{5,7},{6,4},{7,5},{8,10},{9,11},{10,... | collective-permute-start | bytes 196616 | tf_op jit(solution)/shard_map/ppermute | solution.py:26
  4.3 12.0 %collective-permute-start.2 = (f32[128,128]{1,0:T(8,128)S(1)}, f32[128,128]{1,0:T(8,128)S(1)}, u32[]{:S(2)}, u32[]{:S(2)}) collective-permute-start(f32[128,128]{1,0:T(8,128)S(1)} %bitcast.137), channel_id=1, source_target_pairs={{0,3},{1,2},{2,1},{3,0},{4,7},{5,6},{6,5},{7,4},{8,11},{9,10},{10,... | collective-permute-start | bytes 196616 | tf_op jit(solution)/shard_map/ppermute | solution.py:26
  4.4 12.0 %collective-permute-start.3 = (f32[128,128]{1,0:T(8,128)S(1)}, f32[128,128]{1,0:T(8,128)S(1)}, u32[]{:S(2)}, u32[]{:S(2)}) collective-permute-start(f32[128,128]{1,0:T(8,128)S(1)} %bitcast.136), channel_id=1, source_target_pairs={{0,4},{1,5},{2,6},{3,7},{4,0},{5,1},{6,2},{7,3},{8,12},{9,13},{10,... | collective-permute-start | bytes 196616 | tf_op jit(solution)/shard_map/ppermute | solution.py:26
  8.0 8.4 %collective-permute-start.4 = (f32[128,128]{1,0:T(8,128)S(1)}, f32[128,128]{1,0:T(8,128)S(1)}, u32[]{:S(2)}, u32[]{:S(2)}) collective-permute-start(f32[128,128]{1,0:T(8,128)S(1)} %bitcast.135), channel_id=1, source_target_pairs={{0,5},{1,4},{2,7},{3,6},{4,1},{5,0},{6,3},{7,2},{8,13},{9,12},{10,... | collective-permute-start | bytes 196616 | tf_op jit(solution)/shard_map/ppermute | solution.py:26
  10.2 6.2 %collective-permute-start.5 = (f32[128,128]{1,0:T(8,128)S(1)}, f32[128,128]{1,0:T(8,128)S(1)}, u32[]{:S(2)}, u32[]{:S(2)}) collective-permute-start(f32[128,128]{1,0:T(8,128)S(1)} %bitcast.134), channel_id=1, source_target_pairs={{0,6},{1,7},{2,4},{3,5},{4,2},{5,3},{6,0},{7,1},{8,14},{9,15},{10,... | collective-permute-start | bytes 196616 | tf_op jit(solution)/shard_map/ppermute | solution.py:26
  13.7 5.3 %collective-permute-start.6 = (f32[128,128]{1,0:T(8,128)S(1)}, f32[128,128]{1,0:T(8,128)S(1)}, u32[]{:S(2)}, u32[]{:S(2)}) collective-permute-start(f32[128,128]{1,0:T(8,128)S(1)} %bitcast.133), channel_id=1, source_target_pairs={{0,7},{1,6},{2,5},{3,4},{4,3},{5,2},{6,1},{7,0},{8,15},{9,14},{10,... | collective-permute-start | bytes 196616 | tf_op jit(solution)/shard_map/ppermute | solution.py:26
  53.8 3.4 %collective-permute-start.7 = (f32[1024,128]{1,0:T(8,128)S(1)}, f32[1024,128]{1,0:T(8,128)S(1)}, u32[]{:S(2)}, u32[]{:S(2)}) collective-permute-start(f32[1024,128]{1,0:T(8,128)S(1)} %bitcast.126), channel_id=1, source_target_pairs={{0,1},{1,0},{2,3},{3,2},{4,5},{5,4},{6,7},{7,6},{8,9},{9,8},{10,11... | collective-permute-start | bytes 1572872 | tf_op jit(solution)/shard_map/ppermute | solution.py:26
  69.4 7.0 %collective-permute-start.9 = (f32[256,128]{1,0:T(8,128)S(1)}, f32[256,128]{1,0:T(8,128)S(1)}, u32[]{:S(2)}, u32[]{:S(2)}) collective-permute-start(f32[256,128]{1,0:T(8,128)S(1)} %bitcast.98), channel_id=1, source_target_pairs={{0,16},{8,0},{32,8},{40,32},{64,40},{72,64},{96,72},{104,96},{120,... | collective-permute-start | bytes 393224 | tf_op jit(solution)/shard_map/ppermute | solution.py:26
  70.7 9.1 %collective-permute-start.8 = (f32[256,128]{1,0:T(8,128)S(1)}, f32[256,128]{1,0:T(8,128)S(1)}, u32[]{:S(2)}, u32[]{:S(2)}) collective-permute-start(f32[256,128]{1,0:T(8,128)S(1)} %bitcast.99), channel_id=1, source_target_pairs={{0,8},{8,32},{32,40},{40,64},{64,72},{72,96},{96,104},{104,120},{1... | collective-permute-start | bytes 393224 | tf_op jit(solution)/shard_map/ppermute | solution.py:26
  71.0 4.1 %collective-permute-start.11 = (f32[144,128]{1,0:T(8,128)S(1)}, f32[144,128]{1,0:T(8,128)S(1)}, u32[]{:S(2)}, u32[]{:S(2)}) collective-permute-start(f32[144,128]{1,0:T(8,128)S(1)} %bitcast.132), channel_id=1, source_target_pairs={{0,24},{8,16},{32,0},{40,8},{64,32},{72,40},{96,64},{104,72},{120,... | collective-permute-start | bytes 221192 | tf_op jit(solution)/shard_map/ppermute | solution.py:26
  71.6 4.8 %collective-permute-start.10 = (f32[144,128]{1,0:T(8,128)S(1)}, f32[144,128]{1,0:T(8,128)S(1)}, u32[]{:S(2)}, u32[]{:S(2)}) collective-permute-start(f32[144,128]{1,0:T(8,128)S(1)} %bitcast.131), channel_id=1, source_target_pairs={{0,32},{8,40},{32,64},{40,72},{64,96},{72,104},{96,120},{104,112},... | collective-permute-start | bytes 221192 | tf_op jit(solution)/shard_map/ppermute | solution.py:26
  81.5 3.5 %collective-permute-start.12 = (f32[1152,128]{1,0:T(8,128)S(1)}, f32[1152,128]{1,0:T(8,128)S(1)}, u32[]{:S(2)}, u32[]{:S(2)}) collective-permute-start(f32[1152,128]{1,0:T(8,128)S(1)} %bitcast.125), channel_id=1, source_target_pairs={{0,1},{1,0},{2,3},{3,2},{4,5},{5,4},{6,7},{7,6},{8,9},{9,8},{10,11... | collective-permute-start | bytes 1769480 | tf_op jit(solution)/shard_map/ppermute | solution.py:26
  97.8 6.6 %collective-permute-start.14 = (f32[288,128]{1,0:T(8,128)S(1)}, f32[288,128]{1,0:T(8,128)S(1)}, u32[]{:S(2)}, u32[]{:S(2)}) collective-permute-start(f32[288,128]{1,0:T(8,128)S(1)} %bitcast.95), channel_id=1, source_target_pairs={{0,16},{8,0},{32,8},{40,32},{64,40},{72,64},{96,72},{104,96},{120,... | collective-permute-start | bytes 442376 | tf_op jit(solution)/shard_map/ppermute | solution.py:26
  97.9 9.6 %collective-permute-start.13 = (f32[288,128]{1,0:T(8,128)S(1)}, f32[288,128]{1,0:T(8,128)S(1)}, u32[]{:S(2)}, u32[]{:S(2)}) collective-permute-start(f32[288,128]{1,0:T(8,128)S(1)} %bitcast.96), channel_id=1, source_target_pairs={{0,8},{8,32},{32,40},{40,64},{64,72},{72,96},{96,104},{104,120},{1... | collective-permute-start | bytes 442376 | tf_op jit(solution)/shard_map/ppermute | solution.py:26
  99.3 4.9 %collective-permute-start.16 = (f32[224,128]{1,0:T(8,128)S(1)}, f32[224,128]{1,0:T(8,128)S(1)}, u32[]{:S(2)}, u32[]{:S(2)}) collective-permute-start(f32[224,128]{1,0:T(8,128)S(1)} %bitcast.130), channel_id=1, source_target_pairs={{0,24},{8,16},{32,0},{40,8},{64,32},{72,40},{96,64},{104,72},{120,... | collective-permute-start | bytes 344072 | tf_op jit(solution)/shard_map/ppermute | solution.py:26
  99.3 5.0 %collective-permute-start.15 = (f32[224,128]{1,0:T(8,128)S(1)}, f32[224,128]{1,0:T(8,128)S(1)}, u32[]{:S(2)}, u32[]{:S(2)}) collective-permute-start(f32[224,128]{1,0:T(8,128)S(1)} %bitcast.129), channel_id=1, source_target_pairs={{0,32},{8,40},{32,64},{40,72},{64,96},{72,104},{96,120},{104,112},... | collective-permute-start | bytes 344072 | tf_op jit(solution)/shard_map/ppermute | solution.py:26
  109.3 4.2 %collective-permute-start.17 = (f32[1280,128]{1,0:T(8,128)S(1)}, f32[1280,128]{1,0:T(8,128)S(1)}, u32[]{:S(2)}, u32[]{:S(2)}) collective-permute-start(f32[1280,128]{1,0:T(8,128)S(1)} %bitcast.124), channel_id=1, source_target_pairs={{0,1},{1,0},{2,3},{3,2},{4,5},{5,4},{6,7},{7,6},{8,9},{9,8},{10,11... | collective-permute-start | bytes 1966088 | tf_op jit(solution)/shard_map/ppermute | solution.py:26
  127.3 12.2 %collective-permute-start.19 = (f32[320,128]{1,0:T(8,128)S(1)}, f32[320,128]{1,0:T(8,128)S(1)}, u32[]{:S(2)}, u32[]{:S(2)}) collective-permute-start(f32[320,128]{1,0:T(8,128)S(1)} %bitcast.92), channel_id=1, source_target_pairs={{0,16},{8,0},{32,8},{40,32},{64,40},{72,64},{96,72},{104,96},{120,... | collective-permute-start | bytes 491528 | tf_op jit(solution)/shard_map/ppermute | solution.py:26
  127.9 11.6 %collective-permute-start.18 = (f32[320,128]{1,0:T(8,128)S(1)}, f32[320,128]{1,0:T(8,128)S(1)}, u32[]{:S(2)}, u32[]{:S(2)}) collective-permute-start(f32[320,128]{1,0:T(8,128)S(1)} %bitcast.93), channel_id=1, source_target_pairs={{0,8},{8,32},{32,40},{40,64},{64,72},{72,96},{96,104},{104,120},{1... | collective-permute-start | bytes 491528 | tf_op jit(solution)/shard_map/ppermute | solution.py:26
  128.9 10.6 %collective-permute-start.21 = (f32[256,128]{1,0:T(8,128)S(1)}, f32[256,128]{1,0:T(8,128)S(1)}, u32[]{:S(2)}, u32[]{:S(2)}) collective-permute-start(f32[256,128]{1,0:T(8,128)S(1)} %bitcast.128), channel_id=1, source_target_pairs={{0,24},{8,16},{32,0},{40,8},{64,32},{72,40},{96,64},{104,72},{120,... | collective-permute-start | bytes 393224 | tf_op jit(solution)/shard_map/ppermute | solution.py:26
  128.9 10.6 %collective-permute-start.20 = (f32[256,128]{1,0:T(8,128)S(1)}, f32[256,128]{1,0:T(8,128)S(1)}, u32[]{:S(2)}, u32[]{:S(2)}) collective-permute-start(f32[256,128]{1,0:T(8,128)S(1)} %bitcast.127), channel_id=1, source_target_pairs={{0,32},{8,40},{32,64},{40,72},{64,96},{72,104},{96,120},{104,112},... | collective-permute-start | bytes 393224 | tf_op jit(solution)/shard_map/ppermute | solution.py:26
  130.3 5.3 %collective-permute-start.22 = (f32[48,128]{1,0:T(8,128)S(1)}, f32[48,128]{1,0:T(8,128)S(1)}, u32[]{:S(2)}, u32[]{:S(2)}) collective-permute-start(f32[48,128]{1,0:T(8,128)S(1)} %bitcast.141), channel_id=1, source_target_pairs={{0,40},{8,64},{32,72},{40,96},{64,104},{72,120},{96,112},{104,88},... | collective-permute-start | bytes 73736 | tf_op jit(solution)/shard_map/ppermute | solution.py:26
  135.6 3.9 %collective-permute-start.23 = (f32[48,128]{1,0:T(8,128)S(1)}, f32[48,128]{1,0:T(8,128)S(1)}, u32[]{:S(2)}, u32[]{:S(2)}) collective-permute-start(f32[48,128]{1,0:T(8,128)S(1)} %bitcast.140), channel_id=1, source_target_pairs={{0,48},{8,24},{32,16},{40,0},{64,8},{72,32},{96,40},{104,64},{120,... | collective-permute-start | bytes 73736 | tf_op jit(solution)/shard_map/ppermute | solution.py:26
  141.4 6.1 %collective-permute-start.24 = (f32[1408,128]{1,0:T(8,128)S(1)}, f32[1408,128]{1,0:T(8,128)S(1)}, u32[]{:S(2)}, u32[]{:S(2)}) collective-permute-start(f32[1408,128]{1,0:T(8,128)S(1)} %bitcast.123), channel_id=1, source_target_pairs={{0,1},{1,0},{2,3},{3,2},{4,5},{5,4},{6,7},{7,6},{8,9},{9,8},{10,11... | collective-permute-start | bytes 2162696 | tf_op jit(solution)/shard_map/ppermute | solution.py:26
  204.1 5.3 %collective-permute-start.25 = (f32[1536,128]{1,0:T(8,128)S(1)}, f32[1536,128]{1,0:T(8,128)S(1)}, u32[]{:S(2)}, u32[]{:S(2)}) collective-permute-start(f32[1536,128]{1,0:T(8,128)S(1)} %bitcast.122), channel_id=1, source_target_pairs={{0,1},{1,0},{2,3},{3,2},{4,5},{5,4},{6,7},{7,6},{8,9},{9,8},{10,11... | collective-permute-start | bytes 2359304 | tf_op jit(solution)/shard_map/ppermute | solution.py:26

commit v5 on v4

--- a/solution.py
+++ b/solution.py
@@ -26,13 +26,18 @@
     return lax.ppermute(flat, axes, pairs).reshape(value.shape)
 
 
-def exchange(value, axes):
-    flat = value.reshape(value.shape[0], -1, 128)
-    return lax.all_to_all(flat, axes, 0, 0, tiled=True).reshape(value.shape)
-
-
 def ring_shift(value, k):
     return permute(value, "row", [(RING[p], RING[(p + k) % 16]) for p in range(16)])
+
+
+def xy_shift(value, dx, dy):
+    return permute(
+        value, "row", [(i, ((i // 4 + dx) % 4) * 4 + (i % 4 + dy) % 4) for i in range(16)]
+    )
+
+
+def z_swap(value, k):
+    return permute(value, "col", [(i, i ^ k) for i in range(4)])
 
 
 def core_swap(value):
@@ -91,38 +96,46 @@
     return tdot(xh, zh) + tdot(xh, lo_ref[...]) + tdot(xl, zh)
 
 
-def call(kernel, outs, args, scratch=(), tab=None, here=(), there=()):
-    space = lambda n, rest: pl.BlockSpec(memory_space=pl.ANY if n in rest else pltpu.VMEM)
+def call(kernel, outs, args, scratch=(), tab=None):
+    vmem = pl.BlockSpec(memory_space=pltpu.VMEM)
     table = [] if tab is None else [pl.BlockSpec(memory_space=pltpu.SMEM)]
     return pl.pallas_call(
         kernel,
         out_shape=[jax.ShapeDtypeStruct(o, F32) for o in outs],
-        in_specs=table + [space(n, here) for n in range(len(args))],
-        out_specs=[space(n, there) for n in range(len(outs))],
+        in_specs=table + [vmem] * len(args),
+        out_specs=[vmem] * len(outs),
         scratch_shapes=list(scratch),
         compiler_params=pltpu.CompilerParams(vmem_limit_bytes=48 * 1024 * 1024),
     )(*([] if tab is None else [tab]), *args)
 
 
-def split_kernel(d_ref, *outs):
-    me = lax.axis_index("col") * 2 + lax.axis_index("layer")
-    for k in range(8):
-        for e in range(4):
-            start = pl.multiple_of(e * 64 + (me ^ k) * 8, 8)
-            rows = d_ref[pl.ds(start, 8), :]
-            for t in range(4):
-                outs[k][e, t] = rows[:, t * 128 : (t + 1) * 128]
+def split_kernel(d_ref, own_ref, oth_ref):
+    z, h = lax.axis_index("col"), lax.axis_index("layer")
+    for k in range(4):
+        for ref, core in ((own_ref, h), (oth_ref, 1 - h)):
+            for e in range(4):
+                start = pl.multiple_of(e * 64 + (2 * (z ^ k) + core) * 8, 8)
+                rows = d_ref[pl.ds(start, 8), :]
+                for t in range(4):
+                    ref[k, e, t] = rows[:, t * 128 : (t + 1) * 128]
+
+
+def pack_kernel(own_ref, got_ref, *outs):
+    for k in range(4):
+        outs[k][0] = own_ref[k]
+        outs[k][1] = got_ref[k]
 
 
 def compact_kernel(tab, *refs):
-    ins, (a_ref, x_ref) = refs[:8], refs[8:]
-    for k in range(8):
+    ins, (a_ref, b_ref, x_ref) = refs[:4], refs[4:]
+    for k in range(4):
         x_ref[k] = ins[k][...]
     low = low_half()
     row0 = tab[PLACE] * 4
-    me = tab[PLACE + 1]
+    z, h = tab[PLACE + 6], tab[PLACE + 4]
     for e in range(4):
         i = tab[PERM + row0 + e]
+        out_ref = a_ref if e < 2 else b_ref
         halves = []
         for t in range(2 * BAND + 2):
             if t > 2 * BAND:
@@ -130,24 +143,43 @@
                 continue
             j = (i + t - BAND) & 63
             sj = tab[INV + j]
-            tile = x_ref[(sj >> 3) ^ me, e, (sj & 7) >> 1]
+            tile = x_ref[(sj >> 4) ^ z, ((sj >> 3) & 1) ^ h, e, (sj & 7) >> 1]
             tile = jnp.where((sj & 1) == (t & 1), tile, swap_halves(tile))
             halves.append(jnp.where(bit(tab, 0, i, j) == 1, tile, 0.0))
         for t in range(BAND + 1):
-            a_ref[e, t] = jnp.where(low, halves[2 * t], halves[2 * t + 1])
-
-
-def gather_rows(rows):
-    copies = jnp.broadcast_to(rows[None], (16,) + rows.shape)
-    return exchange(copies, "row")
+            out_ref[e % 2, t] = jnp.where(low, halves[2 * t], halves[2 * t + 1])
+
+
+def gather_rows(half_a, half_b):
+    near_a = [xy_shift(half_a, k, 0) for k in (1, 3, 2)]
+    near_b = [xy_shift(half_b, 0, k) for k in (1, 3, 2)]
+    half_a, half_b, *near = lax.optimization_barrier((half_a, half_b, *near_a, *near_b))
+    a = jnp.stack([half_a, near[0], near[2], near[1]])
+    b = jnp.stack([half_b, near[3], near[5], near[4]])
+    a, b = lax.optimization_barrier((a, b))
+    far_a = [xy_shift(a, 0, k) for k in (1, 3, 2)]
+    far_b = [xy_shift(b, k, 0) for k in (1, 3, 2)]
+    return [a, far_a[0], far_a[2], far_a[1], b, far_b[0], far_b[2], far_b[1]]
+
+
+def collect(ins, g_ref):
+    for n in range(8):
+        g_ref[n] = ins[n][...]
+
+
+def seat(tab, r, e):
+    dx = (tab[PLACE + 2] - (r >> 2)) & 3
+    dy = (tab[PLACE + 3] - (r & 3)) & 3
+    first = e < 2
+    return jnp.where(first, dy, 4 + dx), jnp.where(first, dx, dy), e & 1
 
 
 def write_slabs(tab, p_ref, own_ref, oth_ref, e, base, d, tiles):
-    h = tab[PLACE + 4]
+    z, h = tab[PLACE + 6], tab[PLACE + 4]
     low = low_half()
     for zz in range(4):
         for ref, core in ((own_ref, h), (oth_ref, 1 - h)):
-            rows = p_ref[base + 2 * zz + core]
+            rows = p_ref[base + 2 * (z ^ zz) + core]
             if d % 2 == 0:
                 for m in range(tiles):
                     at = (d // 2 + m) * 128
@@ -184,21 +216,19 @@
         write_slabs(tab, p_ref, own_ref, oth_ref, e, e * 8, left - (w + 1) + e, w + 2)
 
 
-def first_step_kernel(tab, all_ref, own_ref, oth_ref, cur_ref, hi_ref, lo_ref, p_ref, g_ref, sem):
+def first_step_kernel(tab, *refs):
+    ins, (own_ref, oth_ref, cur_ref, hi_ref, lo_ref, p_ref, g_ref) = refs[:8], refs[8:]
+    collect(ins, g_ref)
     w = BAND
     base = tab[PLACE + 5] * 4 + 64 - w
-    copies = []
-    for b in range(4 + 2 * w):
+
+    def strips(b):
         sk = tab[INV + ((base + b) & 63)]
-        copies.append(pltpu.make_async_copy(all_ref.at[sk >> 2, sk & 3], g_ref.at[b], sem.at[b]))
-    for copy in copies:
-        copy.start()
-    for copy in copies:
-        copy.wait()
-    cur_ref[...] = g_ref[w : w + 4]
-
-    def strips(b):
-        return [g_ref[b, t] for t in range(w + 1)], 0
+        u, v, e = seat(tab, sk >> 2, sk & 3)
+        strip = g_ref[u, v, e]
+        if w <= b < w + 4:
+            cur_ref[b - w] = strip
+        return [strip[t] for t in range(w + 1)], 0
 
     step_body(tab, strips, w, own_ref, oth_ref, hi_ref, lo_ref, p_ref)
 
@@ -229,7 +259,9 @@
     return out
 
 
-def last_step_kernel(tab, g_ref, own_ref, oth_ref, cur_ref, hi_ref, lo_ref, p_ref):
+def last_step_kernel(tab, *refs):
+    ins, (own_ref, oth_ref, cur_ref, hi_ref, lo_ref, p_ref, g_ref) = refs[:8], refs[8:]
+    collect(ins, g_ref)
     w = BAND + STEPS - 1
     row0 = tab[PLACE] * 4
     left, count = w + 2, w + 2
@@ -241,7 +273,8 @@
             pos = k >> 2
             a, odd = pos >> 1, pos & 1
             r = jnp.where(a < 4, a * 4 + odd, (7 - a) * 4 + 3 - odd)
-            strip = g_ref[r, k & 3]
+            u, v, ee = seat(tab, r, k & 3)
+            strip = g_ref[u, v, ee]
             if b == w:
                 cur_ref[e] = strip
             return [strip[t] for t in range(w + 1)]
@@ -256,19 +289,20 @@
         write_slabs(tab, p_ref, own_ref, oth_ref, e, 0, 0, count)
 
 
-def pair_kernel(own_ref, got_ref, out_ref):
-    out_ref[...] = own_ref[...] + got_ref[...]
-
-
-def total(ref, e, m):
-    return (ref[0, e, m] + ref[1, e, m]) + (ref[2, e, m] + ref[3, e, m])
+def pair_kernel(own_ref, got_ref, *outs):
+    for k in range(4):
+        outs[k][...] = own_ref[k] + got_ref[k]
+
+
+def total(parts, e, m):
+    return (parts[0][e, m] + parts[1][e, m]) + (parts[2][e, m] + parts[3][e, m])
 
 
 def polynomial(tab, step, cur, square):
     return jnp.where(tab[BRANCH + step] == 1, 2.0 * cur - square, square)
 
 
-def close_kernel(step, cuts, tab, part_ref, cur_ref, *refs):
+def close_kernel(step, cuts, tab, p0, p1, p2, p3, cur_ref, *refs):
     w = BAND + step
     low = low_half()
     i0 = tab[PLACE + 5] * 4
@@ -280,7 +314,7 @@
             before = turned[m - 1] if m >= 1 else zero
             after = turned[m] if m <= w else zero
             cur = jnp.where(low, before, after)
-            square = total(part_ref, e, m)
+            square = total((p0, p1, p2, p3), e, m)
             one = bit(tab, step + 1, i, (i + 2 * m + 63 - w) & 63)
             two = 0
             if 2 * m + 1 <= 2 * w + 2:
@@ -292,16 +326,17 @@
                     ref[e - lo, m - first] = value
 
 
-def finish_kernel(tab, part_ref, cur_ref, y_ref):
+def finish_kernel(tab, p0, p1, p2, p3, cur_ref, own_ref, oth_ref, y_ref):
     w = BAND + STEPS - 1
     low = low_half()
     row0 = tab[PLACE] * 4
+    z, h = tab[PLACE + 6], tab[PLACE + 4]
     y_ref[...] = jnp.zeros_like(y_ref)
     for e in range(4):
         i = tab[PERM + row0 + e]
         for m in range(w + 2):
             cur = cur_ref[e, m - 1] if 1 <= m <= w + 1 else jnp.zeros((8, 128), F32)
-            square = total(part_ref, e, m)
+            square = total((p0, p1, p2, p3), e, m)
             value = polynomial(tab, STEPS - 1, cur, square)
             turned = swap_halves(value)
             for half in (0, 1):
@@ -314,15 +349,20 @@
                 piece = jnp.where(odd == half, value, turned)
                 piece = jnp.where(bit(tab, STEPS, i, j) == 1, piece, 0.0)
                 side = jnp.where(low, 0, 1) == odd
-                c, t = sj >> 3, (sj & 7) >> 1
-                y_ref[c, e, t] = jnp.where(side, piece, y_ref[c, e, t])
-
-
-def join_kernel(y_ref, out_ref):
-    for c in range(8):
-        for e in range(4):
-            for t in range(4):
-                out_ref[e * 64 + c * 8 : e * 64 + c * 8 + 8, t * 128 : (t + 1) * 128] = y_ref[c, e, t]
+                at = ((sj >> 3) & 1) ^ h, (sj >> 4) ^ z, e, (sj & 7) >> 1
+                y_ref[at] = jnp.where(side, piece, y_ref[at])
+    own_ref[...] = y_ref[0]
+    oth_ref[...] = y_ref[1]
+
+
+def join_kernel(y0, y1, y2, y3, out_ref):
+    z, h = lax.axis_index("col"), lax.axis_index("layer")
+    for k, y_ref in enumerate((y0, y1, y2, y3)):
+        for core in (0, 1):
+            for e in range(4):
+                start = pl.multiple_of(e * 64 + (2 * (z ^ k) + (core ^ h)) * 8, 8)
+                for t in range(4):
+                    out_ref[pl.ds(start, 8), t * 128 : (t + 1) * 128] = y_ref[core, e, t]
 
 
 def tables(masks, branch, perm):
@@ -340,27 +380,31 @@
     )
 
 
+def z_exchange(parts):
+    return [parts[0]] + [z_swap(parts[k], k) for k in (1, 2, 3)]
+
+
 def reduce_group(own, oth):
-    (pair,) = call(pair_kernel, [own.shape], [own, core_swap(oth)])
-    return exchange(pair, "col")
-
-
-def group_swap(value, k):
-    return permute(value, GROUP, [(i, i ^ k) for i in range(8)])
+    return z_exchange(call(pair_kernel, [own.shape[1:]] * 4, [own, core_swap(oth)]))
+
+
+def spread_group(own, oth):
+    shape = (2,) + own.shape[1:]
+    return z_exchange(call(pack_kernel, [shape] * 4, [own, core_swap(oth)]))
 
 
 def shards(density, masks, branch, perm):
-    split = call(split_kernel, [(4, 4, 8, 128)] * 8, [density])
-    split = [split[0]] + [group_swap(split[k], k) for k in range(1, 8)]
+    slabs = (4, 4, 4, 8, 128)
+    split = spread_group(*call(split_kernel, [slabs] * 2, [density]))
     tab = tables(masks, branch, perm)
-    (rows,) = call(
+    halves = call(
         compact_kernel,
-        [(4, BAND + 1, 8, 128)],
+        [(2, BAND + 1, 8, 128)] * 2,
         split,
-        [pltpu.VMEM((8, 4, 4, 8, 128), F32)],
+        [pltpu.VMEM((4, 2, 4, 4, 8, 128), F32)],
         tab=tab,
     )
-    gathered = gather_rows(rows)
+    gathered = gather_rows(*halves)
     for step in range(STEPS - 1):
         w = BAND + step
         left, count = geometry(w)
@@ -372,45 +416,42 @@
             pltpu.VMEM((32, 8, count * 128), F32),
         ]
         if step == 0:
-            strips = 4 + 2 * w
-            scratch += [pltpu.VMEM((strips, w + 1, 8, 128), F32), pltpu.SemaphoreType.DMA((strips,))]
+            scratch.append(pltpu.VMEM((8, 4, 2, w + 1, 8, 128), F32))
             own, oth, cur = call(
-                first_step_kernel,
-                [part, part, (4, w + 1, 8, 128)],
-                [gathered],
-                scratch,
-                tab=tab,
-                here=(0,),
+                first_step_kernel, [part, part, (4, w + 1, 8, 128)], gathered, scratch, tab=tab
             )
         else:
             kernel = lambda *refs, w=w, pieces=pieces: step_kernel(w, pieces, *refs)
             own, oth = call(kernel, [part, part], [cur] + around, scratch, tab=tab)
         parts = reduce_group(own, oth)
         pieces = halo_pieces(w + 1) if step < STEPS - 2 else []
-        cuts = [(0, 4, 0, w + 2)]
+        cuts = [(0, 4, 0, w + 2)] if pieces else [(0, 2, 0, w + 2), (2, 4, 0, w + 2)]
         for _, cut in pieces:
             if cut not in cuts:
                 cuts.append(cut)
         kernel = lambda *refs, step=step, cuts=cuts: close_kernel(step, cuts, *refs)
         shapes = [(hi - lo, last - first, 8, 128) for lo, hi, first, last in cuts]
-        sent = call(kernel, shapes, [parts, cur], tab=tab)
+        sent = call(kernel, shapes, parts + [cur], tab=tab)
         cur = sent[0]
         around = [ring_shift(sent[cuts.index(cut)], d) for d, cut in pieces]
-    gathered = gather_rows(cur)
+        cur, *around = lax.optimization_barrier((cur, *around))
+    gathered = gather_rows(*sent)
     w = BAND + STEPS - 1
     part = (4, 4, w + 2, 8, 128)
     scratch = [
         pltpu.VMEM(((2 * w + 2) * 8, (w + 2) * 128), BF16),
         pltpu.VMEM(((2 * w + 2) * 8, (w + 2) * 128), BF16),
         pltpu.VMEM((8, 8, (w + 2) * 128), F32),
+        pltpu.VMEM((8, 4, 2, w + 1, 8, 128), F32),
     ]
     own, oth, cur = call(
-        last_step_kernel, [part, part, (4, w + 1, 8, 128)], [gathered], scratch, tab=tab
+        last_step_kernel, [part, part, (4, w + 1, 8, 128)], gathered, scratch, tab=tab
     )
     parts = reduce_group(own, oth)
-    (full,) = call(finish_kernel, [(8, 4, 4, 8, 128)], [parts, cur], tab=tab)
-    full = exchange(full, GROUP)
-    (out,) = call(join_kernel, [(256, 512)], [full])
+    own, oth = call(
+        finish_kernel, [slabs] * 2, parts + [cur], [pltpu.VMEM((2,) + slabs, F32)], tab=tab
+    )
+    (out,) = call(join_kernel, [(256, 512)], spread_group(own, oth))
     return out
 
 

time: 239 us -> 228 us (0.954)
  blocking collectives: 148 us -> 0 us
  waiting for transfers between devices: 32.6 us -> 119 us
  starting transfers between devices: 35.1 us -> 86.8 us
    all_to_all x8 -> x0, blocking collectives: 148 us -> none  [exchange(): return lax.all_to_all(flat, axes, 0, 0, tiled=True).reshape(value.shape)]
    ppermute x26 -> x66, waiting for transfers between devices: 32.6 us -> 119 us  [permute(): return lax.ppermute(flat, axes, pairs).reshape(value.shape)]
    ppermute x26 -> x66, starting transfers between devices: 35.1 us -> 86.8 us  [permute(): return lax.ppermute(flat, axes, pairs).reshape(value.shape)]
    pallas_call x18 -> x20, Pallas kernels: 16.8 us -> 16.5 us  [call(): pl.pallas_call(kernel, out_shape=[jax.ShapeDtypeStruct(o, F32) for o in o...]
  transfers between devices with their start and end apart: 26 -> 66, of which waited for: 14 -> 50; matrix products, arithmetic and copies ran while one was open for 2% -> 1% of each run, Pallas kernels for 0% -> 0%
where the time goes in v5:
time: 228 us
  waiting for transfers between devices  119 us (52%)
  starting transfers between devices  86.8 us (38%)
  Pallas kernels  16.5 us (7%)
  local copies, waits for them, and re-layouts  4.08 us (2%)
    ppermute x66, waiting for transfers between devices, permute(): return lax.ppermute(flat, axes, pairs).reshape(value.shape)  119 us
    ppermute x66, starting transfers between devices, permute(): return lax.ppermute(flat, axes, pairs).reshape(value.shape)  86.8 us
    pallas_call x20, Pallas kernels, call(): pl.pallas_call(kernel, out_shape=[jax.ShapeDtypeStruct(o, F32) for o in o...  16.5 us
  transfers between devices with their start and end apart: 66, of which 50 were waited for; matrix products, arithmetic and copies ran while one was open for 1% of the time, Pallas kernels for 0%

profile of v5, /device:TPU:1, one launch (start us, length us, event | category | flops | bytes accessed | tf_op | source)
XLA Modules:
  0.0 227.7 jit_solution(5370197657220715443)
XLA Ops:
  5.6 3.3 %collective-permute-start.2 = (f32[256,128]{1,0:T(8,128)S(1)}, f32[256,128]{1,0:T(8,128)S(1)}, u32[]{:S(2)}, u32[]{:S(2)}) collective-permute-start(f32[256,128]{1,0:T(8,128)S(1)} %bitcast.246), channel_id=1, source_target_pairs={{0,4},{2,6},{4,0},{6,2},{1,5},{3,7},{5,1},{7,3},{8,12},{10,14},{12... | collective-permute-start | bytes 393224 | tf_op jit(solution)/shard_map/ppermute | solution.py:26
  12.6 2.4 %collective-permute-done.2 = f32[256,128]{1,0:T(8,128)S(1)} collective-permute-done((f32[256,128]{1,0:T(8,128)S(1)}, f32[256,128]{1,0:T(8,128)S(1)}, u32[]{:S(2)}, u32[]{:S(2)}) %collective-permute-start.2) | collective-permute-done | bytes 131104 | tf_op jit(solution)/shard_map/ppermute | solution.py:26
  15.0 2.5 %collective-permute-done.3 = f32[256,128]{1,0:T(8,128)S(1)} collective-permute-done((f32[256,128]{1,0:T(8,128)S(1)}, f32[256,128]{1,0:T(8,128)S(1)}, u32[]{:S(2)}, u32[]{:S(2)}) %collective-permute-start.3) | collective-permute-done | bytes 131104 | tf_op jit(solution)/shard_map/ppermute | solution.py:26
  18.6 3.0 %collective-permute-start.9 = (f32[112,128]{1,0:T(8,128)S(1)}, f32[112,128]{1,0:T(8,128)S(1)}, u32[]{:S(2)}, u32[]{:S(2)}) collective-permute-start(f32[112,128]{1,0:T(8,128)S(1)} %bitcast.220), channel_id=1, source_target_pairs={{0,16},{8,24},{16,0},{24,8},{32,48},{40,56},{48,32},{56,40},{64,80... | collective-permute-start | bytes 172040 | tf_op jit(solution)/shard_map/ppermute | solution.py:26
  23.0 2.7 %collective-permute-start.6 = (f32[112,128]{1,0:T(8,128)S(1)}, f32[112,128]{1,0:T(8,128)S(1)}, u32[]{:S(2)}, u32[]{:S(2)}) collective-permute-start(f32[112,128]{1,0:T(8,128)S(1)} %bitcast.216), channel_id=1, source_target_pairs={{0,64},{8,72},{16,80},{24,88},{32,96},{40,104},{48,112},{56,120},{... | collective-permute-start | bytes 172040 | tf_op jit(solution)/shard_map/ppermute | solution.py:26
  37.7 5.4 %collective-permute-done.13 = f32[448,128]{1,0:T(8,128)S(1)} collective-permute-done((f32[448,128]{1,0:T(8,128)S(1)}, f32[448,128]{1,0:T(8,128)S(1)}, u32[]{:S(2)}, u32[]{:S(2)}) %collective-permute-start.13) | collective-permute-done | bytes 229408 | tf_op jit(solution)/shard_map/ppermute | solution.py:26
  45.3 5.4 %collective-permute-start.16 = (f32[1024,128]{1,0:T(8,128)S(1)}, f32[1024,128]{1,0:T(8,128)S(1)}, u32[]{:S(2)}, u32[]{:S(2)}) collective-permute-start(f32[1024,128]{1,0:T(8,128)S(1)} %bitcast.230), channel_id=1, source_target_pairs={{0,1},{1,0},{2,3},{3,2},{4,5},{5,4},{6,7},{7,6},{8,9},{9,8},{10,11... | collective-permute-start | bytes 1572872 | tf_op jit(solution)/shard_map/ppermute | solution.py:26
  57.1 3.0 %collective-permute-done.18 = f32[256,128]{1,0:T(8,128)S(1)} collective-permute-done((f32[256,128]{1,0:T(8,128)S(1)}, f32[256,128]{1,0:T(8,128)S(1)}, u32[]{:S(2)}, u32[]{:S(2)}) %collective-permute-start.18) | collective-permute-done | bytes 131104 | tf_op jit(solution)/shard_map/ppermute | solution.py:26
  60.1 2.5 %collective-permute-done.19 = f32[256,128]{1,0:T(8,128)S(1)} collective-permute-done((f32[256,128]{1,0:T(8,128)S(1)}, f32[256,128]{1,0:T(8,128)S(1)}, u32[]{:S(2)}, u32[]{:S(2)}) %collective-permute-start.19) | collective-permute-done | bytes 131104 | tf_op jit(solution)/shard_map/ppermute | solution.py:26
  66.3 2.7 %collective-permute-done.23 = f32[144,128]{1,0:T(8,128)S(1)} collective-permute-done((f32[144,128]{1,0:T(8,128)S(1)}, f32[144,128]{1,0:T(8,128)S(1)}, u32[]{:S(2)}, u32[]{:S(2)}) %collective-permute-start.23) | collective-permute-done | bytes 73760 | tf_op jit(solution)/shard_map/ppermute | solution.py:26
  69.7 3.7 %collective-permute-done.20 = f32[256,128]{1,0:T(8,128)S(1)} collective-permute-done((f32[256,128]{1,0:T(8,128)S(1)}, f32[256,128]{1,0:T(8,128)S(1)}, u32[]{:S(2)}, u32[]{:S(2)}) %collective-permute-start.20) | collective-permute-done | bytes 131104 | tf_op jit(solution)/shard_map/ppermute | solution.py:26
  78.6 3.6 %collective-permute-start.26 = (f32[288,128]{1,0:T(8,128)S(1)}, f32[288,128]{1,0:T(8,128)S(1)}, u32[]{:S(2)}, u32[]{:S(2)}) collective-permute-start(f32[288,128]{1,0:T(8,128)S(1)} %bitcast.243), channel_id=1, source_target_pairs={{0,4},{2,6},{4,0},{6,2},{1,5},{3,7},{5,1},{7,3},{8,12},{10,14},{12... | collective-permute-start | bytes 442376 | tf_op jit(solution)/shard_map/ppermute | solution.py:26
  83.6 5.4 %collective-permute-done.26 = f32[288,128]{1,0:T(8,128)S(1)} collective-permute-done((f32[288,128]{1,0:T(8,128)S(1)}, f32[288,128]{1,0:T(8,128)S(1)}, u32[]{:S(2)}, u32[]{:S(2)}) %collective-permute-start.26) | collective-permute-done | bytes 147488 | tf_op jit(solution)/shard_map/ppermute | solution.py:26
  89.0 2.5 %collective-permute-done.27 = f32[288,128]{1,0:T(8,128)S(1)} collective-permute-done((f32[288,128]{1,0:T(8,128)S(1)}, f32[288,128]{1,0:T(8,128)S(1)}, u32[]{:S(2)}, u32[]{:S(2)}) %collective-permute-start.27) | collective-permute-done | bytes 147488 | tf_op jit(solution)/shard_map/ppermute | solution.py:26
  95.3 3.4 %collective-permute-done.31 = f32[224,128]{1,0:T(8,128)S(1)} collective-permute-done((f32[224,128]{1,0:T(8,128)S(1)}, f32[224,128]{1,0:T(8,128)S(1)}, u32[]{:S(2)}, u32[]{:S(2)}) %collective-permute-start.31) | collective-permute-done | bytes 114720 | tf_op jit(solution)/shard_map/ppermute | solution.py:26
  99.1 3.5 %collective-permute-done.28 = f32[288,128]{1,0:T(8,128)S(1)} collective-permute-done((f32[288,128]{1,0:T(8,128)S(1)}, f32[288,128]{1,0:T(8,128)S(1)}, u32[]{:S(2)}, u32[]{:S(2)}) %collective-permute-start.28) | collective-permute-done | bytes 147488 | tf_op jit(solution)/shard_map/ppermute | solution.py:26
  109.3 2.5 %collective-permute-start.35 = (f32[320,128]{1,0:T(8,128)S(1)}, f32[320,128]{1,0:T(8,128)S(1)}, u32[]{:S(2)}, u32[]{:S(2)}) collective-permute-start(f32[320,128]{1,0:T(8,128)S(1)} %bitcast.239), channel_id=1, source_target_pairs={{0,6},{2,4},{4,2},{6,0},{1,7},{3,5},{5,3},{7,1},{8,14},{10,12},{12... | collective-permute-start | bytes 491528 | tf_op jit(solution)/shard_map/ppermute | solution.py:26
  113.3 3.5 %collective-permute-done.34 = f32[320,128]{1,0:T(8,128)S(1)} collective-permute-done((f32[320,128]{1,0:T(8,128)S(1)}, f32[320,128]{1,0:T(8,128)S(1)}, u32[]{:S(2)}, u32[]{:S(2)}) %collective-permute-start.34) | collective-permute-done | bytes 163872 | tf_op jit(solution)/shard_map/ppermute | solution.py:26
  116.8 2.7 %collective-permute-done.35 = f32[320,128]{1,0:T(8,128)S(1)} collective-permute-done((f32[320,128]{1,0:T(8,128)S(1)}, f32[320,128]{1,0:T(8,128)S(1)}, u32[]{:S(2)}, u32[]{:S(2)}) %collective-permute-start.35) | collective-permute-done | bytes 163872 | tf_op jit(solution)/shard_map/ppermute | solution.py:26
  124.7 4.5 %collective-permute-done.40 = f32[48,128]{1,0:T(8,128)S(1)} collective-permute-done((f32[48,128]{1,0:T(8,128)S(1)}, f32[48,128]{1,0:T(8,128)S(1)}, u32[]{:S(2)}, u32[]{:S(2)}) %collective-permute-start.40) | collective-permute-done | bytes 24608 | tf_op jit(solution)/shard_map/ppermute | solution.py:26
  134.9 3.6 %collective-permute-start.42 = (f32[1408,128]{1,0:T(8,128)S(1)}, f32[1408,128]{1,0:T(8,128)S(1)}, u32[]{:S(2)}, u32[]{:S(2)}) collective-permute-start(f32[1408,128]{1,0:T(8,128)S(1)} %bitcast.227), channel_id=1, source_target_pairs={{0,1},{1,0},{2,3},{3,2},{4,5},{5,4},{6,7},{7,6},{8,9},{9,8},{10,11... | collective-permute-start | bytes 2162696 | tf_op jit(solution)/shard_map/ppermute | solution.py:26
  140.5 3.8 %collective-permute-start.44 = (f32[352,128]{1,0:T(8,128)S(1)}, f32[352,128]{1,0:T(8,128)S(1)}, u32[]{:S(2)}, u32[]{:S(2)}) collective-permute-start(f32[352,128]{1,0:T(8,128)S(1)} %bitcast.237), channel_id=1, source_target_pairs={{0,4},{2,6},{4,0},{6,2},{1,5},{3,7},{5,1},{7,3},{8,12},{10,14},{12... | collective-permute-start | bytes 540680 | tf_op jit(solution)/shard_map/ppermute | solution.py:26
  146.3 6.3 %collective-permute-done.44 = f32[352,128]{1,0:T(8,128)S(1)} collective-permute-done((f32[352,128]{1,0:T(8,128)S(1)}, f32[352,128]{1,0:T(8,128)S(1)}, u32[]{:S(2)}, u32[]{:S(2)}) %collective-permute-start.44) | collective-permute-done | bytes 180256 | tf_op jit(solution)/shard_map/ppermute | solution.py:26
  152.6 2.5 %collective-permute-done.45 = f32[352,128]{1,0:T(8,128)S(1)} collective-permute-done((f32[352,128]{1,0:T(8,128)S(1)}, f32[352,128]{1,0:T(8,128)S(1)}, u32[]{:S(2)}, u32[]{:S(2)}) %collective-permute-start.45) | collective-permute-done | bytes 180256 | tf_op jit(solution)/shard_map/ppermute | solution.py:26
  155.9 2.7 %collective-permute-start.51 = (f32[176,128]{1,0:T(8,128)S(1)}, f32[176,128]{1,0:T(8,128)S(1)}, u32[]{:S(2)}, u32[]{:S(2)}) collective-permute-start(f32[176,128]{1,0:T(8,128)S(1)} %bitcast.206), channel_id=1, source_target_pairs={{0,16},{8,24},{16,0},{24,8},{32,48},{40,56},{48,32},{56,40},{64,80... | collective-permute-start | bytes 270344 | tf_op jit(solution)/shard_map/ppermute | solution.py:26
  177.2 11.1 %collective-permute-done.55 = f32[704,128]{1,0:T(8,128)S(1)} collective-permute-done((f32[704,128]{1,0:T(8,128)S(1)}, f32[704,128]{1,0:T(8,128)S(1)}, u32[]{:S(2)}, u32[]{:S(2)}) %collective-permute-start.55) | collective-permute-done | bytes 360480 | tf_op jit(solution)/shard_map/ppermute | solution.py:26
  189.2 2.6 %shard_map.70 = (f32[4,4,12,8,128]{4,3,2,1,0:T(8,128)S(1)}, f32[4,4,12,8,128]{4,3,2,1,0:T(8,128)S(1)}, f32[4,11,8,128]{3,2,1,0:T(8,128)S(1)}) custom-call(s32[912]{0:T(1024)S(1)} %concatenate.3.tab.refs_0_, f32[4,2,11,8,128]{4,3,2,1,0:T(8,128)S(1)} %pad_maximum_fusion.refs_0_, f32[4,2,11,8,128]{4,3,2,1,0:T(8,128)S(1)} %bitcast.166, ...), custom_call_target="tpu_custom_call" | custom-call | tf_op jit(solution)/shard_map/pallas_call | solution.py:102
  191.8 3.9 %collective-permute-start.58 = (f32[1536,128]{1,0:T(8,128)S(1)}, f32[1536,128]{1,0:T(8,128)S(1)}, u32[]{:S(2)}, u32[]{:S(2)}) collective-permute-start(f32[1536,128]{1,0:T(8,128)S(1)} %bitcast.226), channel_id=1, source_target_pairs={{0,1},{1,0},{2,3},{3,2},{4,5},{5,4},{6,7},{7,6},{8,9},{9,8},{10,11... | collective-permute-start | bytes 2359304 | tf_op jit(solution)/shard_map/ppermute | solution.py:26
  203.9 4.3 %collective-permute-done.60 = f32[384,128]{1,0:T(8,128)S(1)} collective-permute-done((f32[384,128]{1,0:T(8,128)S(1)}, f32[384,128]{1,0:T(8,128)S(1)}, u32[]{:S(2)}, u32[]{:S(2)}) %collective-permute-start.60) | collective-permute-done | bytes 196640 | tf_op jit(solution)/shard_map/ppermute | solution.py:26
  214.8 3.5 %collective-permute-start.64 = (f32[256,128]{1,0:T(8,128)S(1)}, f32[256,128]{1,0:T(8,128)S(1)}, u32[]{:S(2)}, u32[]{:S(2)}) collective-permute-start(f32[256,128]{1,0:T(8,128)S(1)} %bitcast.253), channel_id=1, source_target_pairs={{0,4},{2,6},{4,0},{6,2},{1,5},{3,7},{5,1},{7,3},{8,12},{10,14},{12... | collective-permute-start | bytes 393224 | tf_op jit(solution)/shard_map/ppermute | solution.py:26
  219.5 4.9 %collective-permute-done.64 = f32[256,128]{1,0:T(8,128)S(1)} collective-permute-done((f32[256,128]{1,0:T(8,128)S(1)}, f32[256,128]{1,0:T(8,128)S(1)}, u32[]{:S(2)}, u32[]{:S(2)}) %collective-permute-start.64) | collective-permute-done | bytes 131104 | tf_op jit(solution)/shard_map/ppermute | solution.py:26
  224.4 2.5 %collective-permute-done.65 = f32[256,128]{1,0:T(8,128)S(1)} collective-permute-done((f32[256,128]{1,0:T(8,128)S(1)}, f32[256,128]{1,0:T(8,128)S(1)}, u32[]{:S(2)}, u32[]{:S(2)}) %collective-permute-start.65) | collective-permute-done | bytes 131104 | tf_op jit(solution)/shard_map/ppermute | solution.py:26
  (141 shorter events, 107.5 us)
Async XLA Ops:
  3.8 8.8 %collective-permute-start.1 = (f32[256,128]{1,0:T(8,128)S(1)}, f32[256,128]{1,0:T(8,128)S(1)}, u32[]{:S(2)}, u32[]{:S(2)}) collective-permute-start(f32[256,128]{1,0:T(8,128)S(1)} %bitcast.247), channel_id=1, source_target_pairs={{0,2},{2,0},{4,6},{6,4},{1,3},{3,1},{5,7},{7,5},{8,10},{10,8},{12,... | collective-permute-start | bytes 393224 | tf_op jit(solution)/shard_map/ppermute | solution.py:26
  5.6 9.4 %collective-permute-start.2 = (f32[256,128]{1,0:T(8,128)S(1)}, f32[256,128]{1,0:T(8,128)S(1)}, u32[]{:S(2)}, u32[]{:S(2)}) collective-permute-start(f32[256,128]{1,0:T(8,128)S(1)} %bitcast.246), channel_id=1, source_target_pairs={{0,4},{2,6},{4,0},{6,2},{1,5},{3,7},{5,1},{7,3},{8,12},{10,14},{12... | collective-permute-start | bytes 393224 | tf_op jit(solution)/shard_map/ppermute | solution.py:26
  8.9 8.6 %collective-permute-start.3 = (f32[256,128]{1,0:T(8,128)S(1)}, f32[256,128]{1,0:T(8,128)S(1)}, u32[]{:S(2)}, u32[]{:S(2)}) collective-permute-start(f32[256,128]{1,0:T(8,128)S(1)} %bitcast.245), channel_id=1, source_target_pairs={{0,6},{2,4},{4,2},{6,0},{1,7},{3,5},{5,3},{7,1},{8,14},{10,12},{12... | collective-permute-start | bytes 393224 | tf_op jit(solution)/shard_map/ppermute | solution.py:26
  18.6 8.1 %collective-permute-start.9 = (f32[112,128]{1,0:T(8,128)S(1)}, f32[112,128]{1,0:T(8,128)S(1)}, u32[]{:S(2)}, u32[]{:S(2)}) collective-permute-start(f32[112,128]{1,0:T(8,128)S(1)} %bitcast.220), channel_id=1, source_target_pairs={{0,16},{8,24},{16,0},{24,8},{32,48},{40,56},{48,32},{56,40},{64,80... | collective-permute-start | bytes 172040 | tf_op jit(solution)/shard_map/ppermute | solution.py:26
  32.2 11.0 %collective-permute-start.13 = (f32[448,128]{1,0:T(8,128)S(1)}, f32[448,128]{1,0:T(8,128)S(1)}, u32[]{:S(2)}, u32[]{:S(2)}) collective-permute-start(f32[448,128]{1,0:T(8,128)S(1)} %bitcast.149), channel_id=1, source_target_pairs={{0,32},{8,40},{16,48},{24,56},{32,64},{40,72},{48,80},{56,88},{64,... | collective-permute-start | bytes 688136 | tf_op jit(solution)/shard_map/ppermute | solution.py:26
  32.4 10.7 %collective-permute-start.12 = (f32[448,128]{1,0:T(8,128)S(1)}, f32[448,128]{1,0:T(8,128)S(1)}, u32[]{:S(2)}, u32[]{:S(2)}) collective-permute-start(f32[448,128]{1,0:T(8,128)S(1)} %bitcast.144), channel_id=1, source_target_pairs={{0,24},{8,0},{16,8},{24,16},{32,56},{40,32},{48,40},{56,48},{64,88... | collective-permute-start | bytes 688136 | tf_op jit(solution)/shard_map/ppermute | solution.py:26
  34.4 8.7 %collective-permute-start.11 = (f32[448,128]{1,0:T(8,128)S(1)}, f32[448,128]{1,0:T(8,128)S(1)}, u32[]{:S(2)}, u32[]{:S(2)}) collective-permute-start(f32[448,128]{1,0:T(8,128)S(1)} %bitcast.145), channel_id=1, source_target_pairs={{0,16},{8,24},{16,0},{24,8},{32,48},{40,56},{48,32},{56,40},{64,80... | collective-permute-start | bytes 688136 | tf_op jit(solution)/shard_map/ppermute | solution.py:26
  35.8 7.7 %collective-permute-start.10 = (f32[448,128]{1,0:T(8,128)S(1)}, f32[448,128]{1,0:T(8,128)S(1)}, u32[]{:S(2)}, u32[]{:S(2)}) collective-permute-start(f32[448,128]{1,0:T(8,128)S(1)} %bitcast.146), channel_id=1, source_target_pairs={{0,8},{8,16},{16,24},{24,0},{32,40},{40,48},{48,56},{56,32},{64,72... | collective-permute-start | bytes 688136 | tf_op jit(solution)/shard_map/ppermute | solution.py:26
  52.4 7.7 %collective-permute-start.18 = (f32[256,128]{1,0:T(8,128)S(1)}, f32[256,128]{1,0:T(8,128)S(1)}, u32[]{:S(2)}, u32[]{:S(2)}) collective-permute-start(f32[256,128]{1,0:T(8,128)S(1)} %bitcast.252), channel_id=1, source_target_pairs={{0,4},{2,6},{4,0},{6,2},{1,5},{3,7},{5,1},{7,3},{8,12},{10,14},{12... | collective-permute-start | bytes 393224 | tf_op jit(solution)/shard_map/ppermute | solution.py:26
  54.0 8.6 %collective-permute-start.19 = (f32[256,128]{1,0:T(8,128)S(1)}, f32[256,128]{1,0:T(8,128)S(1)}, u32[]{:S(2)}, u32[]{:S(2)}) collective-permute-start(f32[256,128]{1,0:T(8,128)S(1)} %bitcast.250), channel_id=1, source_target_pairs={{0,6},{2,4},{4,2},{6,0},{1,7},{3,5},{5,3},{7,1},{8,14},{10,12},{12... | collective-permute-start | bytes 393224 | tf_op jit(solution)/shard_map/ppermute | solution.py:26
  63.6 9.8 %collective-permute-start.20 = (f32[256,128]{1,0:T(8,128)S(1)}, f32[256,128]{1,0:T(8,128)S(1)}, u32[]{:S(2)}, u32[]{:S(2)}) collective-permute-start(f32[256,128]{1,0:T(8,128)S(1)} %bitcast.160), channel_id=1, source_target_pairs={{0,8},{8,32},{32,40},{40,64},{64,72},{72,96},{96,104},{104,120},{1... | collective-permute-start | bytes 393224 | tf_op jit(solution)/shard_map/ppermute | solution.py:26
  78.6 10.4 %collective-permute-start.26 = (f32[288,128]{1,0:T(8,128)S(1)}, f32[288,128]{1,0:T(8,128)S(1)}, u32[]{:S(2)}, u32[]{:S(2)}) collective-permute-start(f32[288,128]{1,0:T(8,128)S(1)} %bitcast.243), channel_id=1, source_target_pairs={{0,4},{2,6},{4,0},{6,2},{1,5},{3,7},{5,1},{7,3},{8,12},{10,14},{12... | collective-permute-start | bytes 442376 | tf_op jit(solution)/shard_map/ppermute | solution.py:26
  82.2 9.3 %collective-permute-start.27 = (f32[288,128]{1,0:T(8,128)S(1)}, f32[288,128]{1,0:T(8,128)S(1)}, u32[]{:S(2)}, u32[]{:S(2)}) collective-permute-start(f32[288,128]{1,0:T(8,128)S(1)} %bitcast.242), channel_id=1, source_target_pairs={{0,6},{2,4},{4,2},{6,0},{1,7},{3,5},{5,3},{7,1},{8,14},{10,12},{12... | collective-permute-start | bytes 442376 | tf_op jit(solution)/shard_map/ppermute | solution.py:26
  92.3 10.2 %collective-permute-start.28 = (f32[288,128]{1,0:T(8,128)S(1)}, f32[288,128]{1,0:T(8,128)S(1)}, u32[]{:S(2)}, u32[]{:S(2)}) collective-permute-start(f32[288,128]{1,0:T(8,128)S(1)} %bitcast.157), channel_id=1, source_target_pairs={{0,8},{8,32},{32,40},{40,64},{64,72},{72,96},{96,104},{104,120},{1... | collective-permute-start | bytes 442376 | tf_op jit(solution)/shard_map/ppermute | solution.py:26
  107.9 8.9 %collective-permute-start.34 = (f32[320,128]{1,0:T(8,128)S(1)}, f32[320,128]{1,0:T(8,128)S(1)}, u32[]{:S(2)}, u32[]{:S(2)}) collective-permute-start(f32[320,128]{1,0:T(8,128)S(1)} %bitcast.240), channel_id=1, source_target_pairs={{0,4},{2,6},{4,0},{6,2},{1,5},{3,7},{5,1},{7,3},{8,12},{10,14},{12... | collective-permute-start | bytes 491528 | tf_op jit(solution)/shard_map/ppermute | solution.py:26
  109.3 10.2 %collective-permute-start.35 = (f32[320,128]{1,0:T(8,128)S(1)}, f32[320,128]{1,0:T(8,128)S(1)}, u32[]{:S(2)}, u32[]{:S(2)}) collective-permute-start(f32[320,128]{1,0:T(8,128)S(1)} %bitcast.239), channel_id=1, source_target_pairs={{0,6},{2,4},{4,2},{6,0},{1,7},{3,5},{5,3},{7,1},{8,14},{10,12},{12... | collective-permute-start | bytes 491528 | tf_op jit(solution)/shard_map/ppermute | solution.py:26
  120.2 12.8 %collective-permute-start.37 = (f32[320,128]{1,0:T(8,128)S(1)}, f32[320,128]{1,0:T(8,128)S(1)}, u32[]{:S(2)}, u32[]{:S(2)}) collective-permute-start(f32[320,128]{1,0:T(8,128)S(1)} %bitcast.153), channel_id=1, source_target_pairs={{0,16},{8,0},{32,8},{40,32},{64,40},{72,64},{96,72},{104,96},{120,... | collective-permute-start | bytes 491528 | tf_op jit(solution)/shard_map/ppermute | solution.py:26
  120.6 12.5 %collective-permute-start.36 = (f32[320,128]{1,0:T(8,128)S(1)}, f32[320,128]{1,0:T(8,128)S(1)}, u32[]{:S(2)}, u32[]{:S(2)}) collective-permute-start(f32[320,128]{1,0:T(8,128)S(1)} %bitcast.154), channel_id=1, source_target_pairs={{0,8},{8,32},{32,40},{40,64},{64,72},{72,96},{96,104},{104,120},{1... | collective-permute-start | bytes 491528 | tf_op jit(solution)/shard_map/ppermute | solution.py:26
  121.8 11.3 %collective-permute-start.39 = (f32[256,128]{1,0:T(8,128)S(1)}, f32[256,128]{1,0:T(8,128)S(1)}, u32[]{:S(2)}, u32[]{:S(2)}) collective-permute-start(f32[256,128]{1,0:T(8,128)S(1)} %bitcast.249), channel_id=1, source_target_pairs={{0,24},{8,16},{32,0},{40,8},{64,32},{72,40},{96,64},{104,72},{120,... | collective-permute-start | bytes 393224 | tf_op jit(solution)/shard_map/ppermute | solution.py:26
  121.8 11.3 %collective-permute-start.38 = (f32[256,128]{1,0:T(8,128)S(1)}, f32[256,128]{1,0:T(8,128)S(1)}, u32[]{:S(2)}, u32[]{:S(2)}) collective-permute-start(f32[256,128]{1,0:T(8,128)S(1)} %bitcast.248), channel_id=1, source_target_pairs={{0,32},{8,40},{32,64},{40,72},{64,96},{72,104},{96,120},{104,112},... | collective-permute-start | bytes 393224 | tf_op jit(solution)/shard_map/ppermute | solution.py:26
  140.5 12.0 %collective-permute-start.44 = (f32[352,128]{1,0:T(8,128)S(1)}, f32[352,128]{1,0:T(8,128)S(1)}, u32[]{:S(2)}, u32[]{:S(2)}) collective-permute-start(f32[352,128]{1,0:T(8,128)S(1)} %bitcast.237), channel_id=1, source_target_pairs={{0,4},{2,6},{4,0},{6,2},{1,5},{3,7},{5,1},{7,3},{8,12},{10,14},{12... | collective-permute-start | bytes 540680 | tf_op jit(solution)/shard_map/ppermute | solution.py:26
  144.4 10.7 %collective-permute-start.45 = (f32[352,128]{1,0:T(8,128)S(1)}, f32[352,128]{1,0:T(8,128)S(1)}, u32[]{:S(2)}, u32[]{:S(2)}) collective-permute-start(f32[352,128]{1,0:T(8,128)S(1)} %bitcast.236), channel_id=1, source_target_pairs={{0,6},{2,4},{4,2},{6,0},{1,7},{3,5},{5,3},{7,1},{8,14},{10,12},{12... | collective-permute-start | bytes 540680 | tf_op jit(solution)/shard_map/ppermute | solution.py:26
  155.9 7.7 %collective-permute-start.51 = (f32[176,128]{1,0:T(8,128)S(1)}, f32[176,128]{1,0:T(8,128)S(1)}, u32[]{:S(2)}, u32[]{:S(2)}) collective-permute-start(f32[176,128]{1,0:T(8,128)S(1)} %bitcast.206), channel_id=1, source_target_pairs={{0,16},{8,24},{16,0},{24,8},{32,48},{40,56},{48,32},{56,40},{64,80... | collective-permute-start | bytes 270344 | tf_op jit(solution)/shard_map/ppermute | solution.py:26
  169.4 7.9 %collective-permute-start.56 = (f32[704,128]{1,0:T(8,128)S(1)}, f32[704,128]{1,0:T(8,128)S(1)}, u32[]{:S(2)}, u32[]{:S(2)}) collective-permute-start(f32[704,128]{1,0:T(8,128)S(1)} %bitcast.142), channel_id=1, source_target_pairs={{0,64},{8,72},{16,80},{24,88},{32,96},{40,104},{48,112},{56,120},{... | collective-permute-start | bytes 1081352 | tf_op jit(solution)/shard_map/ppermute | solution.py:26
  170.7 17.6 %collective-permute-start.55 = (f32[704,128]{1,0:T(8,128)S(1)}, f32[704,128]{1,0:T(8,128)S(1)}, u32[]{:S(2)}, u32[]{:S(2)}) collective-permute-start(f32[704,128]{1,0:T(8,128)S(1)} %bitcast.143), channel_id=1, source_target_pairs={{0,32},{8,40},{16,48},{24,56},{32,64},{40,72},{48,80},{56,88},{64,... | collective-permute-start | bytes 1081352 | tf_op jit(solution)/shard_map/ppermute | solution.py:26
  171.5 16.9 %collective-permute-start.54 = (f32[704,128]{1,0:T(8,128)S(1)}, f32[704,128]{1,0:T(8,128)S(1)}, u32[]{:S(2)}, u32[]{:S(2)}) collective-permute-start(f32[704,128]{1,0:T(8,128)S(1)} %bitcast.138), channel_id=1, source_target_pairs={{0,24},{8,0},{16,8},{24,16},{32,56},{40,32},{48,40},{56,48},{64,88... | collective-permute-start | bytes 1081352 | tf_op jit(solution)/shard_map/ppermute | solution.py:26
  172.9 15.4 %collective-permute-start.53 = (f32[704,128]{1,0:T(8,128)S(1)}, f32[704,128]{1,0:T(8,128)S(1)}, u32[]{:S(2)}, u32[]{:S(2)}) collective-permute-start(f32[704,128]{1,0:T(8,128)S(1)} %bitcast.139), channel_id=1, source_target_pairs={{0,16},{8,24},{16,0},{24,8},{32,48},{40,56},{48,32},{56,40},{64,80... | collective-permute-start | bytes 1081352 | tf_op jit(solution)/shard_map/ppermute | solution.py:26
  175.6 13.5 %collective-permute-start.52 = (f32[704,128]{1,0:T(8,128)S(1)}, f32[704,128]{1,0:T(8,128)S(1)}, u32[]{:S(2)}, u32[]{:S(2)}) collective-permute-start(f32[704,128]{1,0:T(8,128)S(1)} %bitcast.140), channel_id=1, source_target_pairs={{0,8},{8,16},{16,24},{24,0},{32,40},{40,48},{48,56},{56,32},{64,72... | collective-permute-start | bytes 1081352 | tf_op jit(solution)/shard_map/ppermute | solution.py:26
  197.8 10.5 %collective-permute-start.60 = (f32[384,128]{1,0:T(8,128)S(1)}, f32[384,128]{1,0:T(8,128)S(1)}, u32[]{:S(2)}, u32[]{:S(2)}) collective-permute-start(f32[384,128]{1,0:T(8,128)S(1)} %bitcast.234), channel_id=1, source_target_pairs={{0,4},{2,6},{4,0},{6,2},{1,5},{3,7},{5,1},{7,3},{8,12},{10,14},{12... | collective-permute-start | bytes 589832 | tf_op jit(solution)/shard_map/ppermute | solution.py:26
  199.4 11.2 %collective-permute-start.61 = (f32[384,128]{1,0:T(8,128)S(1)}, f32[384,128]{1,0:T(8,128)S(1)}, u32[]{:S(2)}, u32[]{:S(2)}) collective-permute-start(f32[384,128]{1,0:T(8,128)S(1)} %bitcast.233), channel_id=1, source_target_pairs={{0,6},{2,4},{4,2},{6,0},{1,7},{3,5},{5,3},{7,1},{8,14},{10,12},{12... | collective-permute-start | bytes 589832 | tf_op jit(solution)/shard_map/ppermute | solution.py:26
  214.8 9.6 %collective-permute-start.64 = (f32[256,128]{1,0:T(8,128)S(1)}, f32[256,128]{1,0:T(8,128)S(1)}, u32[]{:S(2)}, u32[]{:S(2)}) collective-permute-start(f32[256,128]{1,0:T(8,128)S(1)} %bitcast.253), channel_id=1, source_target_pairs={{0,4},{2,6},{4,0},{6,2},{1,5},{3,7},{5,1},{7,3},{8,12},{10,14},{12... | collective-permute-start | bytes 393224 | tf_op jit(solution)/shard_map/ppermute | solution.py:26
  218.3 8.6 %collective-permute-start.65 = (f32[256,128]{1,0:T(8,128)S(1)}, f32[256,128]{1,0:T(8,128)S(1)}, u32[]{:S(2)}, u32[]{:S(2)}) collective-permute-start(f32[256,128]{1,0:T(8,128)S(1)} %bitcast.251), channel_id=1, source_target_pairs={{0,6},{2,4},{4,2},{6,0},{1,7},{3,5},{5,3},{7,1},{8,14},{10,12},{12... | collective-permute-start | bytes 393224 | tf_op jit(solution)/shard_map/ppermute | solution.py:26
  (39 other events, 174.6 us)

commit v6 on v5

--- a/solution.py
+++ b/solution.py
@@ -150,28 +150,45 @@
             out_ref[e % 2, t] = jnp.where(low, halves[2 * t], halves[2 * t + 1])
 
 
-def gather_rows(half_a, half_b):
-    near_a = [xy_shift(half_a, k, 0) for k in (1, 3, 2)]
+LINES = [[x * 4 + y for x in range(4)] for y in range(4)]
+
+
+def gather_x(value):
+    flat = value.reshape(-1, 128)
+    out = lax.all_gather(flat, "row", axis=0, tiled=True, axis_index_groups=LINES)
+    return out.reshape((4,) + value.shape)
+
+
+def gather_rows(half_a, half_b, small):
     near_b = [xy_shift(half_b, 0, k) for k in (1, 3, 2)]
-    half_a, half_b, *near = lax.optimization_barrier((half_a, half_b, *near_a, *near_b))
-    a = jnp.stack([half_a, near[0], near[2], near[1]])
-    b = jnp.stack([half_b, near[3], near[5], near[4]])
+    a = gather_x(half_a)
+    a, half_b, *near = lax.optimization_barrier((a, half_b, *near_b))
+    b = jnp.stack([half_b, near[0], near[2], near[1]])
     a, b = lax.optimization_barrier((a, b))
     far_a = [xy_shift(a, 0, k) for k in (1, 3, 2)]
+    far_a = [a, far_a[0], far_a[2], far_a[1]]
+    if small:
+        return far_a + [gather_x(b)]
     far_b = [xy_shift(b, k, 0) for k in (1, 3, 2)]
-    return [a, far_a[0], far_a[2], far_a[1], b, far_b[0], far_b[2], far_b[1]]
+    return far_a + [b, far_b[0], far_b[2], far_b[1]]
 
 
 def collect(ins, g_ref):
-    for n in range(8):
+    for n in range(4):
         g_ref[n] = ins[n][...]
-
-
-def seat(tab, r, e):
-    dx = (tab[PLACE + 2] - (r >> 2)) & 3
+    if len(ins) == 5:
+        g_ref[4:8] = ins[4][...]
+    else:
+        for n in range(4, 8):
+            g_ref[n] = ins[n][...]
+
+
+def seat(tab, r, e, small):
+    x = r >> 2
+    dx = x if small else (tab[PLACE + 2] - x) & 3
     dy = (tab[PLACE + 3] - (r & 3)) & 3
     first = e < 2
-    return jnp.where(first, dy, 4 + dx), jnp.where(first, dx, dy), e & 1
+    return jnp.where(first, dy, 4 + dx), jnp.where(first, x, dy), e & 1
 
 
 def write_slabs(tab, p_ref, own_ref, oth_ref, e, base, d, tiles):
@@ -217,14 +234,14 @@
 
 
 def first_step_kernel(tab, *refs):
-    ins, (own_ref, oth_ref, cur_ref, hi_ref, lo_ref, p_ref, g_ref) = refs[:8], refs[8:]
+    ins, (own_ref, oth_ref, cur_ref, hi_ref, lo_ref, p_ref, g_ref) = refs[:5], refs[5:]
     collect(ins, g_ref)
     w = BAND
     base = tab[PLACE + 5] * 4 + 64 - w
 
     def strips(b):
         sk = tab[INV + ((base + b) & 63)]
-        u, v, e = seat(tab, sk >> 2, sk & 3)
+        u, v, e = seat(tab, sk >> 2, sk & 3, True)
         strip = g_ref[u, v, e]
         if w <= b < w + 4:
             cur_ref[b - w] = strip
@@ -273,7 +290,7 @@
             pos = k >> 2
             a, odd = pos >> 1, pos & 1
             r = jnp.where(a < 4, a * 4 + odd, (7 - a) * 4 + 3 - odd)
-            u, v, ee = seat(tab, r, k & 3)
+            u, v, ee = seat(tab, r, k & 3, False)
             strip = g_ref[u, v, ee]
             if b == w:
                 cur_ref[e] = strip
@@ -404,7 +421,7 @@
         [pltpu.VMEM((4, 2, 4, 4, 8, 128), F32)],
         tab=tab,
     )
-    gathered = gather_rows(*halves)
+    gathered = gather_rows(*halves, True)
     for step in range(STEPS - 1):
         w = BAND + step
         left, count = geometry(w)
@@ -435,7 +452,7 @@
         cur = sent[0]
         around = [ring_shift(sent[cuts.index(cut)], d) for d, cut in pieces]
         cur, *around = lax.optimization_barrier((cur, *around))
-    gathered = gather_rows(*sent)
+    gathered = gather_rows(*sent, False)
     w = BAND + STEPS - 1
     part = (4, 4, w + 2, 8, 128)
     scratch = [

time: 228 us -> 242 us (1.061)
  blocking collectives: 0 us -> 30.9 us
  waiting for transfers between devices: 119 us -> 104 us
  starting transfers between devices: 86.8 us -> 84.2 us
    all_gather x0 -> x3, blocking collectives: none -> 30.9 us  [gather_x(): lax.all_gather(flat, 'row', axis=0, tiled=True, axis_index_groups=LINES)]
    ppermute x66 -> x57, waiting for transfers between devices: 119 us -> 104 us  [permute(): return lax.ppermute(flat, axes, pairs).reshape(value.shape)]
    ppermute x66 -> x57, starting transfers between devices: 86.8 us -> 84.2 us  [permute(): return lax.ppermute(flat, axes, pairs).reshape(value.shape)]
  transfers between devices with their start and end apart: 66 -> 57, of which waited for: 50 -> 38; matrix products, arithmetic and copies ran while one was open for 1% -> 1% of each run, Pallas kernels for 0% -> 0%
where the time goes in v6:
time: 242 us; the launch traced here: 241 us
  waiting for transfers between devices  104 us (43%)
  starting transfers between devices  84.2 us (35%)
  blocking collectives  30.9 us (13%)
  Pallas kernels  16.5 us (7%)
  local copies, waits for them, and re-layouts  4.02 us (2%)
    ppermute x57, waiting for transfers between devices, permute(): return lax.ppermute(flat, axes, pairs).reshape(value.shape)  104 us
    ppermute x57, starting transfers between devices, permute(): return lax.ppermute(flat, axes, pairs).reshape(value.shape)  84.2 us
    all_gather x3, blocking collectives, gather_x(): lax.all_gather(flat, 'row', axis=0, tiled=True, axis_index_groups=LINES)  30.9 us
    pallas_call x20, Pallas kernels, call(): pl.pallas_call(kernel, out_shape=[jax.ShapeDtypeStruct(o, F32) for o in o...  16.5 us
  transfers between devices with their start and end apart: 57, of which 38 were waited for; matrix products, arithmetic and copies ran while one was open for 1% of the time, Pallas kernels for 0%

profile of v6, /device:TPU:1, one launch (start us, length us, event | category | flops | bytes accessed | tf_op | source)
XLA Modules:
  0.0 241.1 jit_solution(11490636865011805734)
XLA Ops:
  5.6 3.3 %collective-permute-start.2 = (f32[256,128]{1,0:T(8,128)S(1)}, f32[256,128]{1,0:T(8,128)S(1)}, u32[]{:S(2)}, u32[]{:S(2)}) collective-permute-start(f32[256,128]{1,0:T(8,128)S(1)} %bitcast.217), channel_id=1, source_target_pairs={{0,4},{2,6},{4,0},{6,2},{1,5},{3,7},{5,1},{7,3},{8,12},{10,14},{12... | collective-permute-start | bytes 393224 | tf_op jit(solution)/shard_map/ppermute | solution.py:26
  18.6 3.0 %collective-permute-start.6 = (f32[112,128]{1,0:T(8,128)S(1)}, f32[112,128]{1,0:T(8,128)S(1)}, u32[]{:S(2)}, u32[]{:S(2)}) collective-permute-start(f32[112,128]{1,0:T(8,128)S(1)} %bitcast.190), channel_id=1, source_target_pairs={{0,16},{8,24},{16,0},{24,8},{32,48},{40,56},{48,32},{56,40},{64,80... | collective-permute-start | bytes 172040 | tf_op jit(solution)/shard_map/ppermute | solution.py:26
  23.0 9.6 %all_gather.9 = f32[448,128]{1,0:T(8,128)S(1)} all-gather(f32[112,128]{1,0:T(8,128)S(1)} %bitcast.194), channel_id=1, replica_groups={{0,32,64,96},{8,40,72,104},{16,48,80,112},{24,56,88,120},{1,33,65,97},{..., dimensions={0}, use_global_device_ids=true | all-gather | bytes 286720 | tf_op jit(solution)/shard_map/all_gather | solution.py:158
  35.4 11.5 %all_gather.10 = f32[1792,128]{1,0:T(8,128)S(1)} all-gather(f32[448,128]{1,0:T(8,128)S(1)} %bitcast.233), channel_id=1, replica_groups={{0,32,64,96},{8,40,72,104},{16,48,80,112},{24,56,88,120},{1,33,65,97},{..., dimensions={0}, use_global_device_ids=true | all-gather | bytes 1146880 | tf_op jit(solution)/shard_map/all_gather | solution.py:158
  48.7 8.2 %collective-permute-start.10 = (f32[1024,128]{1,0:T(8,128)S(1)}, f32[1024,128]{1,0:T(8,128)S(1)}, u32[]{:S(2)}, u32[]{:S(2)}) collective-permute-start(f32[1024,128]{1,0:T(8,128)S(1)} %bitcast.201), channel_id=1, source_target_pairs={{0,1},{1,0},{2,3},{3,2},{4,5},{5,4},{6,7},{7,6},{8,9},{9,8},{10,11... | collective-permute-start | bytes 1572872 | tf_op jit(solution)/shard_map/ppermute | solution.py:26
  59.5 2.9 %collective-permute-start.13 = (f32[256,128]{1,0:T(8,128)S(1)}, f32[256,128]{1,0:T(8,128)S(1)}, u32[]{:S(2)}, u32[]{:S(2)}) collective-permute-start(f32[256,128]{1,0:T(8,128)S(1)} %bitcast.221), channel_id=1, source_target_pairs={{0,6},{2,4},{4,2},{6,0},{1,7},{3,5},{5,3},{7,1},{8,14},{10,12},{12... | collective-permute-start | bytes 393224 | tf_op jit(solution)/shard_map/ppermute | solution.py:26
  65.7 2.7 %collective-permute-done.13 = f32[256,128]{1,0:T(8,128)S(1)} collective-permute-done((f32[256,128]{1,0:T(8,128)S(1)}, f32[256,128]{1,0:T(8,128)S(1)}, u32[]{:S(2)}, u32[]{:S(2)}) %collective-permute-start.13) | collective-permute-done | bytes 131104 | tf_op jit(solution)/shard_map/ppermute | solution.py:26
  69.2 2.7 %collective-permute-start.15 = (f32[256,128]{1,0:T(8,128)S(1)}, f32[256,128]{1,0:T(8,128)S(1)}, u32[]{:S(2)}, u32[]{:S(2)}) collective-permute-start(f32[256,128]{1,0:T(8,128)S(1)} %bitcast.139), channel_id=1, source_target_pairs={{0,16},{8,0},{32,8},{40,32},{64,40},{72,64},{96,72},{104,96},{120,... | collective-permute-start | bytes 393224 | tf_op jit(solution)/shard_map/ppermute | solution.py:26
  73.4 3.0 %collective-permute-done.17 = f32[144,128]{1,0:T(8,128)S(1)} collective-permute-done((f32[144,128]{1,0:T(8,128)S(1)}, f32[144,128]{1,0:T(8,128)S(1)}, u32[]{:S(2)}, u32[]{:S(2)}) %collective-permute-start.17) | collective-permute-done | bytes 73760 | tf_op jit(solution)/shard_map/ppermute | solution.py:26
  77.7 4.0 %collective-permute-done.14 = f32[256,128]{1,0:T(8,128)S(1)} collective-permute-done((f32[256,128]{1,0:T(8,128)S(1)}, f32[256,128]{1,0:T(8,128)S(1)}, u32[]{:S(2)}, u32[]{:S(2)}) %collective-permute-start.14) | collective-permute-done | bytes 131104 | tf_op jit(solution)/shard_map/ppermute | solution.py:26
  86.6 3.7 %collective-permute-start.20 = (f32[288,128]{1,0:T(8,128)S(1)}, f32[288,128]{1,0:T(8,128)S(1)}, u32[]{:S(2)}, u32[]{:S(2)}) collective-permute-start(f32[288,128]{1,0:T(8,128)S(1)} %bitcast.214), channel_id=1, source_target_pairs={{0,4},{2,6},{4,0},{6,2},{1,5},{3,7},{5,1},{7,3},{8,12},{10,14},{12... | collective-permute-start | bytes 442376 | tf_op jit(solution)/shard_map/ppermute | solution.py:26
  91.7 5.5 %collective-permute-done.20 = f32[288,128]{1,0:T(8,128)S(1)} collective-permute-done((f32[288,128]{1,0:T(8,128)S(1)}, f32[288,128]{1,0:T(8,128)S(1)}, u32[]{:S(2)}, u32[]{:S(2)}) %collective-permute-start.20) | collective-permute-done | bytes 147488 | tf_op jit(solution)/shard_map/ppermute | solution.py:26
  103.4 3.4 %collective-permute-done.25 = f32[224,128]{1,0:T(8,128)S(1)} collective-permute-done((f32[224,128]{1,0:T(8,128)S(1)}, f32[224,128]{1,0:T(8,128)S(1)}, u32[]{:S(2)}, u32[]{:S(2)}) %collective-permute-start.25) | collective-permute-done | bytes 114720 | tf_op jit(solution)/shard_map/ppermute | solution.py:26
  107.2 2.9 %collective-permute-done.22 = f32[288,128]{1,0:T(8,128)S(1)} collective-permute-done((f32[288,128]{1,0:T(8,128)S(1)}, f32[288,128]{1,0:T(8,128)S(1)}, u32[]{:S(2)}, u32[]{:S(2)}) %collective-permute-start.22) | collective-permute-done | bytes 147488 | tf_op jit(solution)/shard_map/ppermute | solution.py:26
  117.3 2.5 %collective-permute-start.29 = (f32[320,128]{1,0:T(8,128)S(1)}, f32[320,128]{1,0:T(8,128)S(1)}, u32[]{:S(2)}, u32[]{:S(2)}) collective-permute-start(f32[320,128]{1,0:T(8,128)S(1)} %bitcast.210), channel_id=1, source_target_pairs={{0,6},{2,4},{4,2},{6,0},{1,7},{3,5},{5,3},{7,1},{8,14},{10,12},{12... | collective-permute-start | bytes 491528 | tf_op jit(solution)/shard_map/ppermute | solution.py:26
  121.4 3.4 %collective-permute-done.28 = f32[320,128]{1,0:T(8,128)S(1)} collective-permute-done((f32[320,128]{1,0:T(8,128)S(1)}, f32[320,128]{1,0:T(8,128)S(1)}, u32[]{:S(2)}, u32[]{:S(2)}) %collective-permute-start.28) | collective-permute-done | bytes 163872 | tf_op jit(solution)/shard_map/ppermute | solution.py:26
  124.8 2.7 %collective-permute-done.29 = f32[320,128]{1,0:T(8,128)S(1)} collective-permute-done((f32[320,128]{1,0:T(8,128)S(1)}, f32[320,128]{1,0:T(8,128)S(1)}, u32[]{:S(2)}, u32[]{:S(2)}) %collective-permute-start.29) | collective-permute-done | bytes 163872 | tf_op jit(solution)/shard_map/ppermute | solution.py:26
  132.7 4.6 %collective-permute-done.34 = f32[48,128]{1,0:T(8,128)S(1)} collective-permute-done((f32[48,128]{1,0:T(8,128)S(1)}, f32[48,128]{1,0:T(8,128)S(1)}, u32[]{:S(2)}, u32[]{:S(2)}) %collective-permute-start.34) | collective-permute-done | bytes 24608 | tf_op jit(solution)/shard_map/ppermute | solution.py:26
  138.6 2.6 %collective-permute-done.35 = f32[48,128]{1,0:T(8,128)S(1)} collective-permute-done((f32[48,128]{1,0:T(8,128)S(1)}, f32[48,128]{1,0:T(8,128)S(1)}, u32[]{:S(2)}, u32[]{:S(2)}) %collective-permute-start.35) | collective-permute-done | bytes 24608 | tf_op jit(solution)/shard_map/ppermute | solution.py:26
  143.0 3.5 %collective-permute-start.36 = (f32[1408,128]{1,0:T(8,128)S(1)}, f32[1408,128]{1,0:T(8,128)S(1)}, u32[]{:S(2)}, u32[]{:S(2)}) collective-permute-start(f32[1408,128]{1,0:T(8,128)S(1)} %bitcast.198), channel_id=1, source_target_pairs={{0,1},{1,0},{2,3},{3,2},{4,5},{5,4},{6,7},{7,6},{8,9},{9,8},{10,11... | collective-permute-start | bytes 2162696 | tf_op jit(solution)/shard_map/ppermute | solution.py:26
  148.5 3.7 %collective-permute-start.38 = (f32[352,128]{1,0:T(8,128)S(1)}, f32[352,128]{1,0:T(8,128)S(1)}, u32[]{:S(2)}, u32[]{:S(2)}) collective-permute-start(f32[352,128]{1,0:T(8,128)S(1)} %bitcast.208), channel_id=1, source_target_pairs={{0,4},{2,6},{4,0},{6,2},{1,5},{3,7},{5,1},{7,3},{8,12},{10,14},{12... | collective-permute-start | bytes 540680 | tf_op jit(solution)/shard_map/ppermute | solution.py:26
  154.3 6.1 %collective-permute-done.38 = f32[352,128]{1,0:T(8,128)S(1)} collective-permute-done((f32[352,128]{1,0:T(8,128)S(1)}, f32[352,128]{1,0:T(8,128)S(1)}, u32[]{:S(2)}, u32[]{:S(2)}) %collective-permute-start.38) | collective-permute-done | bytes 180256 | tf_op jit(solution)/shard_map/ppermute | solution.py:26
  165.8 2.7 %collective-permute-start.41 = (f32[176,128]{1,0:T(8,128)S(1)}, f32[176,128]{1,0:T(8,128)S(1)}, u32[]{:S(2)}, u32[]{:S(2)}) collective-permute-start(f32[176,128]{1,0:T(8,128)S(1)} %bitcast.185), channel_id=1, source_target_pairs={{0,24},{8,0},{16,8},{24,16},{32,56},{40,32},{48,40},{56,48},{64,88... | collective-permute-start | bytes 270344 | tf_op jit(solution)/shard_map/ppermute | solution.py:26
  168.5 9.8 %all_gather.11 = f32[704,128]{1,0:T(8,128)S(1)} all-gather(f32[176,128]{1,0:T(8,128)S(1)} %bitcast.183), channel_id=1, replica_groups={{0,32,64,96},{8,40,72,104},{16,48,80,112},{24,56,88,120},{1,33,65,97},{..., dimensions={0}, use_global_device_ids=true | all-gather | bytes 450560 | tf_op jit(solution)/shard_map/all_gather | solution.py:158
  178.3 2.6 %collective-permute-start.48 = (f32[704,128]{1,0:T(8,128)S(1)}, f32[704,128]{1,0:T(8,128)S(1)}, u32[]{:S(2)}, u32[]{:S(2)}) collective-permute-start(f32[704,128]{1,0:T(8,128)S(1)} %bitcast.126), channel_id=1, source_target_pairs={{0,96},{8,104},{16,112},{24,120},{32,0},{40,8},{48,16},{56,24},{64... | collective-permute-start | bytes 1081352 | tf_op jit(solution)/shard_map/ppermute | solution.py:26
  184.0 4.7 %collective-permute-done.48 = f32[704,128]{1,0:T(8,128)S(1)} collective-permute-done((f32[704,128]{1,0:T(8,128)S(1)}, f32[704,128]{1,0:T(8,128)S(1)}, u32[]{:S(2)}, u32[]{:S(2)}) %collective-permute-start.48) | collective-permute-done | bytes 360480 | tf_op jit(solution)/shard_map/ppermute | solution.py:26
  189.1 9.4 %collective-permute-done.46 = f32[704,128]{1,0:T(8,128)S(1)} collective-permute-done((f32[704,128]{1,0:T(8,128)S(1)}, f32[704,128]{1,0:T(8,128)S(1)}, u32[]{:S(2)}, u32[]{:S(2)}) %collective-permute-start.46) | collective-permute-done | bytes 360480 | tf_op jit(solution)/shard_map/ppermute | solution.py:26
  200.4 2.7 %shard_map.70 = (f32[4,4,12,8,128]{4,3,2,1,0:T(8,128)S(1)}, f32[4,4,12,8,128]{4,3,2,1,0:T(8,128)S(1)}, f32[4,11,8,128]{3,2,1,0:T(8,128)S(1)}) custom-call(s32[912]{0:T(1024)S(1)} %concatenate.3.tab.refs_0_, f32[4,2,11,8,128]{4,3,2,1,0:T(8,128)S(1)} %bitcast.125, f32[4,2,11,8,128]{4,3,2,1,0:T(8,128)S(1)} %bitcast.146, f32[4,2,11,8,128]{4,3,2,1,0:T(8,128)S(1)} %bitcast.145, ...), custom_call_target="tpu_custom_call" | custom-call | tf_op jit(solution)/shard_map/pallas_call | solution.py:102
  203.0 6.1 %collective-permute-start.49 = (f32[1536,128]{1,0:T(8,128)S(1)}, f32[1536,128]{1,0:T(8,128)S(1)}, u32[]{:S(2)}, u32[]{:S(2)}) collective-permute-start(f32[1536,128]{1,0:T(8,128)S(1)} %bitcast.197), channel_id=1, source_target_pairs={{0,1},{1,0},{2,3},{3,2},{4,5},{5,4},{6,7},{7,6},{8,9},{9,8},{10,11... | collective-permute-start | bytes 2359304 | tf_op jit(solution)/shard_map/ppermute | solution.py:26
  217.3 4.5 %collective-permute-done.51 = f32[384,128]{1,0:T(8,128)S(1)} collective-permute-done((f32[384,128]{1,0:T(8,128)S(1)}, f32[384,128]{1,0:T(8,128)S(1)}, u32[]{:S(2)}, u32[]{:S(2)}) %collective-permute-start.51) | collective-permute-done | bytes 196640 | tf_op jit(solution)/shard_map/ppermute | solution.py:26
  228.4 3.3 %collective-permute-start.55 = (f32[256,128]{1,0:T(8,128)S(1)}, f32[256,128]{1,0:T(8,128)S(1)}, u32[]{:S(2)}, u32[]{:S(2)}) collective-permute-start(f32[256,128]{1,0:T(8,128)S(1)} %bitcast.224), channel_id=1, source_target_pairs={{0,4},{2,6},{4,0},{6,2},{1,5},{3,7},{5,1},{7,3},{8,12},{10,14},{12... | collective-permute-start | bytes 393224 | tf_op jit(solution)/shard_map/ppermute | solution.py:26
  233.1 4.7 %collective-permute-done.55 = f32[256,128]{1,0:T(8,128)S(1)} collective-permute-done((f32[256,128]{1,0:T(8,128)S(1)}, f32[256,128]{1,0:T(8,128)S(1)}, u32[]{:S(2)}, u32[]{:S(2)}) %collective-permute-start.55) | collective-permute-done | bytes 131104 | tf_op jit(solution)/shard_map/ppermute | solution.py:26
  (125 shorter events, 95.0 us)
Async XLA Ops:
  5.6 9.4 %collective-permute-start.2 = (f32[256,128]{1,0:T(8,128)S(1)}, f32[256,128]{1,0:T(8,128)S(1)}, u32[]{:S(2)}, u32[]{:S(2)}) collective-permute-start(f32[256,128]{1,0:T(8,128)S(1)} %bitcast.217), channel_id=1, source_target_pairs={{0,4},{2,6},{4,0},{6,2},{1,5},{3,7},{5,1},{7,3},{8,12},{10,14},{12... | collective-permute-start | bytes 393224 | tf_op jit(solution)/shard_map/ppermute | solution.py:26
  18.6 14.1 %collective-permute-start.6 = (f32[112,128]{1,0:T(8,128)S(1)}, f32[112,128]{1,0:T(8,128)S(1)}, u32[]{:S(2)}, u32[]{:S(2)}) collective-permute-start(f32[112,128]{1,0:T(8,128)S(1)} %bitcast.190), channel_id=1, source_target_pairs={{0,16},{8,24},{16,0},{24,8},{32,48},{40,56},{48,32},{56,40},{64,80... | collective-permute-start | bytes 172040 | tf_op jit(solution)/shard_map/ppermute | solution.py:26
  21.6 11.1 %collective-permute-start.5 = (f32[112,128]{1,0:T(8,128)S(1)}, f32[112,128]{1,0:T(8,128)S(1)}, u32[]{:S(2)}, u32[]{:S(2)}) collective-permute-start(f32[112,128]{1,0:T(8,128)S(1)} %bitcast.191), channel_id=1, source_target_pairs={{0,24},{8,0},{16,8},{24,16},{32,56},{40,32},{48,40},{56,48},{64,88... | collective-permute-start | bytes 172040 | tf_op jit(solution)/shard_map/ppermute | solution.py:26
  22.3 10.3 %collective-permute-start.4 = (f32[112,128]{1,0:T(8,128)S(1)}, f32[112,128]{1,0:T(8,128)S(1)}, u32[]{:S(2)}, u32[]{:S(2)}) collective-permute-start(f32[112,128]{1,0:T(8,128)S(1)} %bitcast.192), channel_id=1, source_target_pairs={{0,8},{8,16},{16,24},{24,0},{32,40},{40,48},{48,56},{56,32},{64,72... | collective-permute-start | bytes 172040 | tf_op jit(solution)/shard_map/ppermute | solution.py:26
  32.7 14.2 %collective-permute-start.9 = (f32[448,128]{1,0:T(8,128)S(1)}, f32[448,128]{1,0:T(8,128)S(1)}, u32[]{:S(2)}, u32[]{:S(2)}) collective-permute-start(f32[448,128]{1,0:T(8,128)S(1)} %all_gather.9), channel_id=1, source_target_pairs={{0,24},{8,0},{16,8},{24,16},{32,56},{40,32},{48,40},{56,48},{64,88... | collective-permute-start | bytes 688136 | tf_op jit(solution)/shard_map/ppermute | solution.py:26
  34.8 12.1 %collective-permute-start.8 = (f32[448,128]{1,0:T(8,128)S(1)}, f32[448,128]{1,0:T(8,128)S(1)}, u32[]{:S(2)}, u32[]{:S(2)}) collective-permute-start(f32[448,128]{1,0:T(8,128)S(1)} %all_gather.9), channel_id=1, source_target_pairs={{0,16},{8,24},{16,0},{24,8},{32,48},{40,56},{48,32},{56,40},{64,80... | collective-permute-start | bytes 688136 | tf_op jit(solution)/shard_map/ppermute | solution.py:26
  35.0 11.9 %collective-permute-start.7 = (f32[448,128]{1,0:T(8,128)S(1)}, f32[448,128]{1,0:T(8,128)S(1)}, u32[]{:S(2)}, u32[]{:S(2)}) collective-permute-start(f32[448,128]{1,0:T(8,128)S(1)} %all_gather.9), channel_id=1, source_target_pairs={{0,8},{8,16},{16,24},{24,0},{32,40},{40,48},{48,56},{56,32},{64,72... | collective-permute-start | bytes 688136 | tf_op jit(solution)/shard_map/ppermute | solution.py:26
  48.7 9.7 %collective-permute-start.10 = (f32[1024,128]{1,0:T(8,128)S(1)}, f32[1024,128]{1,0:T(8,128)S(1)}, u32[]{:S(2)}, u32[]{:S(2)}) collective-permute-start(f32[1024,128]{1,0:T(8,128)S(1)} %bitcast.201), channel_id=1, source_target_pairs={{0,1},{1,0},{2,3},{3,2},{4,5},{5,4},{6,7},{7,6},{8,9},{9,8},{10,11... | collective-permute-start | bytes 1572872 | tf_op jit(solution)/shard_map/ppermute | solution.py:26
  59.5 9.0 %collective-permute-start.13 = (f32[256,128]{1,0:T(8,128)S(1)}, f32[256,128]{1,0:T(8,128)S(1)}, u32[]{:S(2)}, u32[]{:S(2)}) collective-permute-start(f32[256,128]{1,0:T(8,128)S(1)} %bitcast.221), channel_id=1, source_target_pairs={{0,6},{2,4},{4,2},{6,0},{1,7},{3,5},{5,3},{7,1},{8,14},{10,12},{12... | collective-permute-start | bytes 393224 | tf_op jit(solution)/shard_map/ppermute | solution.py:26
  71.9 9.8 %collective-permute-start.14 = (f32[256,128]{1,0:T(8,128)S(1)}, f32[256,128]{1,0:T(8,128)S(1)}, u32[]{:S(2)}, u32[]{:S(2)}) collective-permute-start(f32[256,128]{1,0:T(8,128)S(1)} %bitcast.140), channel_id=1, source_target_pairs={{0,8},{8,32},{32,40},{40,64},{64,72},{72,96},{96,104},{104,120},{1... | collective-permute-start | bytes 393224 | tf_op jit(solution)/shard_map/ppermute | solution.py:26
  86.6 10.5 %collective-permute-start.20 = (f32[288,128]{1,0:T(8,128)S(1)}, f32[288,128]{1,0:T(8,128)S(1)}, u32[]{:S(2)}, u32[]{:S(2)}) collective-permute-start(f32[288,128]{1,0:T(8,128)S(1)} %bitcast.214), channel_id=1, source_target_pairs={{0,4},{2,6},{4,0},{6,2},{1,5},{3,7},{5,1},{7,3},{8,12},{10,14},{12... | collective-permute-start | bytes 442376 | tf_op jit(solution)/shard_map/ppermute | solution.py:26
  90.3 9.3 %collective-permute-start.21 = (f32[288,128]{1,0:T(8,128)S(1)}, f32[288,128]{1,0:T(8,128)S(1)}, u32[]{:S(2)}, u32[]{:S(2)}) collective-permute-start(f32[288,128]{1,0:T(8,128)S(1)} %bitcast.213), channel_id=1, source_target_pairs={{0,6},{2,4},{4,2},{6,0},{1,7},{3,5},{5,3},{7,1},{8,14},{10,12},{12... | collective-permute-start | bytes 442376 | tf_op jit(solution)/shard_map/ppermute | solution.py:26
  100.4 9.6 %collective-permute-start.22 = (f32[288,128]{1,0:T(8,128)S(1)}, f32[288,128]{1,0:T(8,128)S(1)}, u32[]{:S(2)}, u32[]{:S(2)}) collective-permute-start(f32[288,128]{1,0:T(8,128)S(1)} %bitcast.137), channel_id=1, source_target_pairs={{0,8},{8,32},{32,40},{40,64},{64,72},{72,96},{96,104},{104,120},{1... | collective-permute-start | bytes 442376 | tf_op jit(solution)/shard_map/ppermute | solution.py:26
  116.0 8.8 %collective-permute-start.28 = (f32[320,128]{1,0:T(8,128)S(1)}, f32[320,128]{1,0:T(8,128)S(1)}, u32[]{:S(2)}, u32[]{:S(2)}) collective-permute-start(f32[320,128]{1,0:T(8,128)S(1)} %bitcast.211), channel_id=1, source_target_pairs={{0,4},{2,6},{4,0},{6,2},{1,5},{3,7},{5,1},{7,3},{8,12},{10,14},{12... | collective-permute-start | bytes 491528 | tf_op jit(solution)/shard_map/ppermute | solution.py:26
  117.3 10.2 %collective-permute-start.29 = (f32[320,128]{1,0:T(8,128)S(1)}, f32[320,128]{1,0:T(8,128)S(1)}, u32[]{:S(2)}, u32[]{:S(2)}) collective-permute-start(f32[320,128]{1,0:T(8,128)S(1)} %bitcast.210), channel_id=1, source_target_pairs={{0,6},{2,4},{4,2},{6,0},{1,7},{3,5},{5,3},{7,1},{8,14},{10,12},{12... | collective-permute-start | bytes 491528 | tf_op jit(solution)/shard_map/ppermute | solution.py:26
  128.3 12.9 %collective-permute-start.31 = (f32[320,128]{1,0:T(8,128)S(1)}, f32[320,128]{1,0:T(8,128)S(1)}, u32[]{:S(2)}, u32[]{:S(2)}) collective-permute-start(f32[320,128]{1,0:T(8,128)S(1)} %bitcast.133), channel_id=1, source_target_pairs={{0,16},{8,0},{32,8},{40,32},{64,40},{72,64},{96,72},{104,96},{120,... | collective-permute-start | bytes 491528 | tf_op jit(solution)/shard_map/ppermute | solution.py:26
  128.9 12.3 %collective-permute-start.30 = (f32[320,128]{1,0:T(8,128)S(1)}, f32[320,128]{1,0:T(8,128)S(1)}, u32[]{:S(2)}, u32[]{:S(2)}) collective-permute-start(f32[320,128]{1,0:T(8,128)S(1)} %bitcast.134), channel_id=1, source_target_pairs={{0,8},{8,32},{32,40},{40,64},{64,72},{72,96},{96,104},{104,120},{1... | collective-permute-start | bytes 491528 | tf_op jit(solution)/shard_map/ppermute | solution.py:26
  129.8 11.4 %collective-permute-start.33 = (f32[256,128]{1,0:T(8,128)S(1)}, f32[256,128]{1,0:T(8,128)S(1)}, u32[]{:S(2)}, u32[]{:S(2)}) collective-permute-start(f32[256,128]{1,0:T(8,128)S(1)} %bitcast.220), channel_id=1, source_target_pairs={{0,24},{8,16},{32,0},{40,8},{64,32},{72,40},{96,64},{104,72},{120,... | collective-permute-start | bytes 393224 | tf_op jit(solution)/shard_map/ppermute | solution.py:26
  129.8 11.4 %collective-permute-start.32 = (f32[256,128]{1,0:T(8,128)S(1)}, f32[256,128]{1,0:T(8,128)S(1)}, u32[]{:S(2)}, u32[]{:S(2)}) collective-permute-start(f32[256,128]{1,0:T(8,128)S(1)} %bitcast.219), channel_id=1, source_target_pairs={{0,32},{8,40},{32,64},{40,72},{64,96},{72,104},{96,120},{104,112},... | collective-permute-start | bytes 393224 | tf_op jit(solution)/shard_map/ppermute | solution.py:26
  148.5 11.9 %collective-permute-start.38 = (f32[352,128]{1,0:T(8,128)S(1)}, f32[352,128]{1,0:T(8,128)S(1)}, u32[]{:S(2)}, u32[]{:S(2)}) collective-permute-start(f32[352,128]{1,0:T(8,128)S(1)} %bitcast.208), channel_id=1, source_target_pairs={{0,4},{2,6},{4,0},{6,2},{1,5},{3,7},{5,1},{7,3},{8,12},{10,14},{12... | collective-permute-start | bytes 540680 | tf_op jit(solution)/shard_map/ppermute | solution.py:26
  152.2 10.7 %collective-permute-start.39 = (f32[352,128]{1,0:T(8,128)S(1)}, f32[352,128]{1,0:T(8,128)S(1)}, u32[]{:S(2)}, u32[]{:S(2)}) collective-permute-start(f32[352,128]{1,0:T(8,128)S(1)} %bitcast.207), channel_id=1, source_target_pairs={{0,6},{2,4},{4,2},{6,0},{1,7},{3,5},{5,3},{7,1},{8,14},{10,12},{12... | collective-permute-start | bytes 540680 | tf_op jit(solution)/shard_map/ppermute | solution.py:26
  163.7 14.6 %collective-permute-start.42 = (f32[176,128]{1,0:T(8,128)S(1)}, f32[176,128]{1,0:T(8,128)S(1)}, u32[]{:S(2)}, u32[]{:S(2)}) collective-permute-start(f32[176,128]{1,0:T(8,128)S(1)} %bitcast.184), channel_id=1, source_target_pairs={{0,16},{8,24},{16,0},{24,8},{32,48},{40,56},{48,32},{56,40},{64,80... | collective-permute-start | bytes 270344 | tf_op jit(solution)/shard_map/ppermute | solution.py:26
  165.8 12.4 %collective-permute-start.41 = (f32[176,128]{1,0:T(8,128)S(1)}, f32[176,128]{1,0:T(8,128)S(1)}, u32[]{:S(2)}, u32[]{:S(2)}) collective-permute-start(f32[176,128]{1,0:T(8,128)S(1)} %bitcast.185), channel_id=1, source_target_pairs={{0,24},{8,0},{16,8},{24,16},{32,56},{40,32},{48,40},{56,48},{64,88... | collective-permute-start | bytes 270344 | tf_op jit(solution)/shard_map/ppermute | solution.py:26
  168.5 9.8 %collective-permute-start.40 = (f32[176,128]{1,0:T(8,128)S(1)}, f32[176,128]{1,0:T(8,128)S(1)}, u32[]{:S(2)}, u32[]{:S(2)}) collective-permute-start(f32[176,128]{1,0:T(8,128)S(1)} %bitcast.186), channel_id=1, source_target_pairs={{0,8},{8,16},{16,24},{24,0},{32,40},{40,48},{48,56},{56,32},{64,72... | collective-permute-start | bytes 270344 | tf_op jit(solution)/shard_map/ppermute | solution.py:26
  178.3 10.4 %collective-permute-start.48 = (f32[704,128]{1,0:T(8,128)S(1)}, f32[704,128]{1,0:T(8,128)S(1)}, u32[]{:S(2)}, u32[]{:S(2)}) collective-permute-start(f32[704,128]{1,0:T(8,128)S(1)} %bitcast.126), channel_id=1, source_target_pairs={{0,96},{8,104},{16,112},{24,120},{32,0},{40,8},{48,16},{56,24},{64... | collective-permute-start | bytes 1081352 | tf_op jit(solution)/shard_map/ppermute | solution.py:26
  181.5 17.0 %collective-permute-start.46 = (f32[704,128]{1,0:T(8,128)S(1)}, f32[704,128]{1,0:T(8,128)S(1)}, u32[]{:S(2)}, u32[]{:S(2)}) collective-permute-start(f32[704,128]{1,0:T(8,128)S(1)} %bitcast.128), channel_id=1, source_target_pairs={{0,32},{8,40},{16,48},{24,56},{32,64},{40,72},{48,80},{56,88},{64,... | collective-permute-start | bytes 1081352 | tf_op jit(solution)/shard_map/ppermute | solution.py:26
  181.6 16.9 %collective-permute-start.45 = (f32[704,128]{1,0:T(8,128)S(1)}, f32[704,128]{1,0:T(8,128)S(1)}, u32[]{:S(2)}, u32[]{:S(2)}) collective-permute-start(f32[704,128]{1,0:T(8,128)S(1)} %all_gather.11), channel_id=1, source_target_pairs={{0,24},{8,0},{16,8},{24,16},{32,56},{40,32},{48,40},{56,48},{64,88... | collective-permute-start | bytes 1081352 | tf_op jit(solution)/shard_map/ppermute | solution.py:26
  184.0 14.5 %collective-permute-start.44 = (f32[704,128]{1,0:T(8,128)S(1)}, f32[704,128]{1,0:T(8,128)S(1)}, u32[]{:S(2)}, u32[]{:S(2)}) collective-permute-start(f32[704,128]{1,0:T(8,128)S(1)} %all_gather.11), channel_id=1, source_target_pairs={{0,16},{8,24},{16,0},{24,8},{32,48},{40,56},{48,32},{56,40},{64,80... | collective-permute-start | bytes 1081352 | tf_op jit(solution)/shard_map/ppermute | solution.py:26
  188.7 11.6 %collective-permute-start.43 = (f32[704,128]{1,0:T(8,128)S(1)}, f32[704,128]{1,0:T(8,128)S(1)}, u32[]{:S(2)}, u32[]{:S(2)}) collective-permute-start(f32[704,128]{1,0:T(8,128)S(1)} %all_gather.11), channel_id=1, source_target_pairs={{0,8},{8,16},{16,24},{24,0},{32,40},{40,48},{48,56},{56,32},{64,72... | collective-permute-start | bytes 1081352 | tf_op jit(solution)/shard_map/ppermute | solution.py:26
  211.2 10.6 %collective-permute-start.51 = (f32[384,128]{1,0:T(8,128)S(1)}, f32[384,128]{1,0:T(8,128)S(1)}, u32[]{:S(2)}, u32[]{:S(2)}) collective-permute-start(f32[384,128]{1,0:T(8,128)S(1)} %bitcast.205), channel_id=1, source_target_pairs={{0,4},{2,6},{4,0},{6,2},{1,5},{3,7},{5,1},{7,3},{8,12},{10,14},{12... | collective-permute-start | bytes 589832 | tf_op jit(solution)/shard_map/ppermute | solution.py:26
  212.9 11.2 %collective-permute-start.52 = (f32[384,128]{1,0:T(8,128)S(1)}, f32[384,128]{1,0:T(8,128)S(1)}, u32[]{:S(2)}, u32[]{:S(2)}) collective-permute-start(f32[384,128]{1,0:T(8,128)S(1)} %bitcast.204), channel_id=1, source_target_pairs={{0,6},{2,4},{4,2},{6,0},{1,7},{3,5},{5,3},{7,1},{8,14},{10,12},{12... | collective-permute-start | bytes 589832 | tf_op jit(solution)/shard_map/ppermute | solution.py:26
  228.4 9.4 %collective-permute-start.55 = (f32[256,128]{1,0:T(8,128)S(1)}, f32[256,128]{1,0:T(8,128)S(1)}, u32[]{:S(2)}, u32[]{:S(2)}) collective-permute-start(f32[256,128]{1,0:T(8,128)S(1)} %bitcast.224), channel_id=1, source_target_pairs={{0,4},{2,6},{4,0},{6,2},{1,5},{3,7},{5,1},{7,3},{8,12},{10,14},{12... | collective-permute-start | bytes 393224 | tf_op jit(solution)/shard_map/ppermute | solution.py:26
  (30 other events, 148.0 us)

commit v7 on v5

--- a/solution.py
+++ b/solution.py
@@ -30,10 +30,14 @@
     return permute(value, "row", [(RING[p], RING[(p + k) % 16]) for p in range(16)])
 
 
-def xy_shift(value, dx, dy):
-    return permute(
-        value, "row", [(i, ((i // 4 + dx) % 4) * 4 + (i % 4 + dy) % 4) for i in range(16)]
-    )
+def line_shift(value, k, swapped):
+    pairs = []
+    for i in range(16):
+        for core in (0, 1):
+            x, y = i // 4, i % 4
+            x, y = (x, (y + k) % 4) if core ^ swapped else ((x + k) % 4, y)
+            pairs.append((i * 2 + core, (x * 4 + y) * 2 + core))
+    return permute(value, ("row", "layer"), pairs)
 
 
 def z_swap(value, k):
@@ -127,7 +131,7 @@
 
 
 def compact_kernel(tab, *refs):
-    ins, (a_ref, b_ref, x_ref) = refs[:4], refs[4:]
+    ins, (out_ref, x_ref) = refs[:4], refs[4:]
     for k in range(4):
         x_ref[k] = ins[k][...]
     low = low_half()
@@ -135,7 +139,6 @@
     z, h = tab[PLACE + 6], tab[PLACE + 4]
     for e in range(4):
         i = tab[PERM + row0 + e]
-        out_ref = a_ref if e < 2 else b_ref
         halves = []
         for t in range(2 * BAND + 2):
             if t > 2 * BAND:
@@ -147,31 +150,28 @@
             tile = jnp.where((sj & 1) == (t & 1), tile, swap_halves(tile))
             halves.append(jnp.where(bit(tab, 0, i, j) == 1, tile, 0.0))
         for t in range(BAND + 1):
-            out_ref[e % 2, t] = jnp.where(low, halves[2 * t], halves[2 * t + 1])
-
-
-def gather_rows(half_a, half_b):
-    near_a = [xy_shift(half_a, k, 0) for k in (1, 3, 2)]
-    near_b = [xy_shift(half_b, 0, k) for k in (1, 3, 2)]
-    half_a, half_b, *near = lax.optimization_barrier((half_a, half_b, *near_a, *near_b))
-    a = jnp.stack([half_a, near[0], near[2], near[1]])
-    b = jnp.stack([half_b, near[3], near[5], near[4]])
-    a, b = lax.optimization_barrier((a, b))
-    far_a = [xy_shift(a, 0, k) for k in (1, 3, 2)]
-    far_b = [xy_shift(b, k, 0) for k in (1, 3, 2)]
-    return [a, far_a[0], far_a[2], far_a[1], b, far_b[0], far_b[2], far_b[1]]
+            out_ref[e, t] = jnp.where(low, halves[2 * t], halves[2 * t + 1])
+
+
+def gather_rows(rows):
+    near = [line_shift(rows, k, 0) for k in (1, 3, 2)]
+    rows, *near = lax.optimization_barrier((rows, *near))
+    line = jnp.stack([rows, near[0], near[2], near[1]])
+    line = lax.optimization_barrier(line)
+    far = [line_shift(line, k, 1) for k in (1, 3, 2)]
+    return [line, far[0], far[2], far[1]]
 
 
 def collect(ins, g_ref):
-    for n in range(8):
+    for n in range(4):
         g_ref[n] = ins[n][...]
 
 
 def seat(tab, r, e):
     dx = (tab[PLACE + 2] - (r >> 2)) & 3
     dy = (tab[PLACE + 3] - (r & 3)) & 3
-    first = e < 2
-    return jnp.where(first, dy, 4 + dx), jnp.where(first, dx, dy), e & 1
+    first = tab[PLACE + 4] == 0
+    return jnp.where(first, dy, dx), jnp.where(first, dx, dy), e
 
 
 def write_slabs(tab, p_ref, own_ref, oth_ref, e, base, d, tiles):
@@ -217,7 +217,7 @@
 
 
 def first_step_kernel(tab, *refs):
-    ins, (own_ref, oth_ref, cur_ref, hi_ref, lo_ref, p_ref, g_ref) = refs[:8], refs[8:]
+    ins, (own_ref, oth_ref, cur_ref, hi_ref, lo_ref, p_ref, g_ref) = refs[:4], refs[4:]
     collect(ins, g_ref)
     w = BAND
     base = tab[PLACE + 5] * 4 + 64 - w
@@ -260,7 +260,7 @@
 
 
 def last_step_kernel(tab, *refs):
-    ins, (own_ref, oth_ref, cur_ref, hi_ref, lo_ref, p_ref, g_ref) = refs[:8], refs[8:]
+    ins, (own_ref, oth_ref, cur_ref, hi_ref, lo_ref, p_ref, g_ref) = refs[:4], refs[4:]
     collect(ins, g_ref)
     w = BAND + STEPS - 1
     row0 = tab[PLACE] * 4
@@ -397,26 +397,26 @@
     slabs = (4, 4, 4, 8, 128)
     split = spread_group(*call(split_kernel, [slabs] * 2, [density]))
     tab = tables(masks, branch, perm)
-    halves = call(
+    (rows,) = call(
         compact_kernel,
-        [(2, BAND + 1, 8, 128)] * 2,
+        [(4, BAND + 1, 8, 128)],
         split,
         [pltpu.VMEM((4, 2, 4, 4, 8, 128), F32)],
         tab=tab,
     )
-    gathered = gather_rows(*halves)
+    gathered = gather_rows(rows)
     for step in range(STEPS - 1):
         w = BAND + step
         left, count = geometry(w)
-        rows = (4 + 2 * w) * 8
+        depth = (4 + 2 * w) * 8
         part = (4, 4, w + 2, 8, 128)
         scratch = [
-            pltpu.VMEM((rows, count * 128), BF16),
-            pltpu.VMEM((rows, count * 128), BF16),
+            pltpu.VMEM((depth, count * 128), BF16),
+            pltpu.VMEM((depth, count * 128), BF16),
             pltpu.VMEM((32, 8, count * 128), F32),
         ]
         if step == 0:
-            scratch.append(pltpu.VMEM((8, 4, 2, w + 1, 8, 128), F32))
+            scratch.append(pltpu.VMEM((4, 4, 4, w + 1, 8, 128), F32))
             own, oth, cur = call(
                 first_step_kernel, [part, part, (4, w + 1, 8, 128)], gathered, scratch, tab=tab
             )
@@ -425,7 +425,7 @@
             own, oth = call(kernel, [part, part], [cur] + around, scratch, tab=tab)
         parts = reduce_group(own, oth)
         pieces = halo_pieces(w + 1) if step < STEPS - 2 else []
-        cuts = [(0, 4, 0, w + 2)] if pieces else [(0, 2, 0, w + 2), (2, 4, 0, w + 2)]
+        cuts = [(0, 4, 0, w + 2)]
         for _, cut in pieces:
             if cut not in cuts:
                 cuts.append(cut)
@@ -435,14 +435,14 @@
         cur = sent[0]
         around = [ring_shift(sent[cuts.index(cut)], d) for d, cut in pieces]
         cur, *around = lax.optimization_barrier((cur, *around))
-    gathered = gather_rows(*sent)
+    gathered = gather_rows(cur)
     w = BAND + STEPS - 1
     part = (4, 4, w + 2, 8, 128)
     scratch = [
         pltpu.VMEM(((2 * w + 2) * 8, (w + 2) * 128), BF16),
         pltpu.VMEM(((2 * w + 2) * 8, (w + 2) * 128), BF16),
         pltpu.VMEM((8, 8, (w + 2) * 128), F32),
-        pltpu.VMEM((8, 4, 2, w + 1, 8, 128), F32),
+        pltpu.VMEM((4, 4, 4, w + 1, 8, 128), F32),
     ]
     own, oth, cur = call(
         last_step_kernel, [part, part, (4, w + 1, 8, 128)], gathered, scratch, tab=tab

time: 228 us -> 224 us (0.982)
  starting transfers between devices: 86.8 us -> 73.2 us
  waiting for transfers between devices: 119 us -> 129 us
    ppermute x66 -> x54, starting transfers between devices: 86.8 us -> 73.2 us  [permute(): return lax.ppermute(flat, axes, pairs).reshape(value.shape)]
    ppermute x66 -> x54, waiting for transfers between devices: 119 us -> 129 us  [permute(): return lax.ppermute(flat, axes, pairs).reshape(value.shape)]
  transfers between devices with their start and end apart: 66 -> 54, of which waited for: 50 -> 46; matrix products, arithmetic and copies ran while one was open for 1% -> 1% of each run, Pallas kernels for 0% -> 0%
where the time goes in v7:
time: 224 us
  waiting for transfers between devices  129 us (58%)
  starting transfers between devices  73.2 us (33%)
  Pallas kernels  16.5 us (7%)
  local copies, waits for them, and re-layouts  4.07 us (2%)
    ppermute x54, waiting for transfers between devices, permute(): return lax.ppermute(flat, axes, pairs).reshape(value.shape)  129 us
    ppermute x54, starting transfers between devices, permute(): return lax.ppermute(flat, axes, pairs).reshape(value.shape)  73.2 us
    pallas_call x20, Pallas kernels, call(): pl.pallas_call(kernel, out_shape=[jax.ShapeDtypeStruct(o, F32) for o in o...  16.5 us
  transfers between devices with their start and end apart: 54, of which 46 were waited for; matrix products, arithmetic and copies ran while one was open for 1% of the time, Pallas kernels for 0%

profile of v7, /device:TPU:1, one launch (start us, length us, event | category | flops | bytes accessed | tf_op | source)
XLA Modules:
  0.0 223.5 jit_solution(5852530182256100359)
XLA Ops:
  5.6 3.3 %collective-permute-start.2 = (f32[256,128]{1,0:T(8,128)S(1)}, f32[256,128]{1,0:T(8,128)S(1)}, u32[]{:S(2)}, u32[]{:S(2)}) collective-permute-start(f32[256,128]{1,0:T(8,128)S(1)} %bitcast.202), channel_id=1, source_target_pairs={{0,4},{2,6},{4,0},{6,2},{1,5},{3,7},{5,1},{7,3},{8,12},{10,14},{12... | collective-permute-start | bytes 393224 | tf_op jit(solution)/shard_map/ppermute | solution.py:26
  15.0 2.5 %collective-permute-done.3 = f32[256,128]{1,0:T(8,128)S(1)} collective-permute-done((f32[256,128]{1,0:T(8,128)S(1)}, f32[256,128]{1,0:T(8,128)S(1)}, u32[]{:S(2)}, u32[]{:S(2)}) %collective-permute-start.3) | collective-permute-done | bytes 131104 | tf_op jit(solution)/shard_map/ppermute | solution.py:26
  18.6 3.0 %collective-permute-start.6 = (f32[224,128]{1,0:T(8,128)S(1)}, f32[224,128]{1,0:T(8,128)S(1)}, u32[]{:S(2)}, u32[]{:S(2)}) collective-permute-start(f32[224,128]{1,0:T(8,128)S(1)} %bitcast.141), channel_id=1, source_target_pairs={{0,64},{1,17},{8,72},{9,25},{16,80},{17,1},{24,88},{25,9},{32,96},... | collective-permute-start | bytes 344072 | tf_op jit(solution)/shard_map/ppermute | solution.py:26
  27.2 2.5 %collective-permute-start.9 = (f32[896,128]{1,0:T(8,128)S(1)}, f32[896,128]{1,0:T(8,128)S(1)}, u32[]{:S(2)}, u32[]{:S(2)}) collective-permute-start(f32[896,128]{1,0:T(8,128)S(1)} %bitcast.117), channel_id=1, source_target_pairs={{0,24},{1,97},{8,0},{9,105},{16,8},{17,113},{24,16},{25,121},{32,5... | collective-permute-start | bytes 1376264 | tf_op jit(solution)/shard_map/ppermute | solution.py:26
  30.9 9.2 %collective-permute-done.9 = f32[896,128]{1,0:T(8,128)S(1)} collective-permute-done((f32[896,128]{1,0:T(8,128)S(1)}, f32[896,128]{1,0:T(8,128)S(1)}, u32[]{:S(2)}, u32[]{:S(2)}) %collective-permute-start.9) | collective-permute-done | bytes 458784 | tf_op jit(solution)/shard_map/ppermute | solution.py:26
  40.1 3.7 %collective-permute-done.7 = f32[896,128]{1,0:T(8,128)S(1)} collective-permute-done((f32[896,128]{1,0:T(8,128)S(1)}, f32[896,128]{1,0:T(8,128)S(1)}, u32[]{:S(2)}, u32[]{:S(2)}) %collective-permute-start.7) | collective-permute-done | bytes 458784 | tf_op jit(solution)/shard_map/ppermute | solution.py:26
  45.6 4.1 %collective-permute-start.10 = (f32[1024,128]{1,0:T(8,128)S(1)}, f32[1024,128]{1,0:T(8,128)S(1)}, u32[]{:S(2)}, u32[]{:S(2)}) collective-permute-start(f32[1024,128]{1,0:T(8,128)S(1)} %bitcast.186), channel_id=1, source_target_pairs={{0,1},{1,0},{2,3},{3,2},{4,5},{5,4},{6,7},{7,6},{8,9},{9,8},{10,11... | collective-permute-start | bytes 1572872 | tf_op jit(solution)/shard_map/ppermute | solution.py:26
  52.1 3.1 %collective-permute-start.13 = (f32[256,128]{1,0:T(8,128)S(1)}, f32[256,128]{1,0:T(8,128)S(1)}, u32[]{:S(2)}, u32[]{:S(2)}) collective-permute-start(f32[256,128]{1,0:T(8,128)S(1)} %bitcast.206), channel_id=1, source_target_pairs={{0,6},{2,4},{4,2},{6,0},{1,7},{3,5},{5,3},{7,1},{8,14},{10,12},{12... | collective-permute-start | bytes 393224 | tf_op jit(solution)/shard_map/ppermute | solution.py:26
  56.1 2.5 %collective-permute-done.12 = f32[256,128]{1,0:T(8,128)S(1)} collective-permute-done((f32[256,128]{1,0:T(8,128)S(1)}, f32[256,128]{1,0:T(8,128)S(1)}, u32[]{:S(2)}, u32[]{:S(2)}) %collective-permute-start.12) | collective-permute-done | bytes 131104 | tf_op jit(solution)/shard_map/ppermute | solution.py:26
  58.6 3.0 %collective-permute-done.13 = f32[256,128]{1,0:T(8,128)S(1)} collective-permute-done((f32[256,128]{1,0:T(8,128)S(1)}, f32[256,128]{1,0:T(8,128)S(1)}, u32[]{:S(2)}, u32[]{:S(2)}) %collective-permute-start.13) | collective-permute-done | bytes 131104 | tf_op jit(solution)/shard_map/ppermute | solution.py:26
  68.6 4.0 %collective-permute-done.14 = f32[256,128]{1,0:T(8,128)S(1)} collective-permute-done((f32[256,128]{1,0:T(8,128)S(1)}, f32[256,128]{1,0:T(8,128)S(1)}, u32[]{:S(2)}, u32[]{:S(2)}) %collective-permute-start.14) | collective-permute-done | bytes 131104 | tf_op jit(solution)/shard_map/ppermute | solution.py:26
  77.5 3.5 %collective-permute-start.20 = (f32[288,128]{1,0:T(8,128)S(1)}, f32[288,128]{1,0:T(8,128)S(1)}, u32[]{:S(2)}, u32[]{:S(2)}) collective-permute-start(f32[288,128]{1,0:T(8,128)S(1)} %bitcast.199), channel_id=1, source_target_pairs={{0,4},{2,6},{4,0},{6,2},{1,5},{3,7},{5,1},{7,3},{8,12},{10,14},{12... | collective-permute-start | bytes 442376 | tf_op jit(solution)/shard_map/ppermute | solution.py:26
  82.5 5.2 %collective-permute-done.20 = f32[288,128]{1,0:T(8,128)S(1)} collective-permute-done((f32[288,128]{1,0:T(8,128)S(1)}, f32[288,128]{1,0:T(8,128)S(1)}, u32[]{:S(2)}, u32[]{:S(2)}) %collective-permute-start.20) | collective-permute-done | bytes 147488 | tf_op jit(solution)/shard_map/ppermute | solution.py:26
  94.0 3.3 %collective-permute-done.25 = f32[224,128]{1,0:T(8,128)S(1)} collective-permute-done((f32[224,128]{1,0:T(8,128)S(1)}, f32[224,128]{1,0:T(8,128)S(1)}, u32[]{:S(2)}, u32[]{:S(2)}) %collective-permute-start.25) | collective-permute-done | bytes 114720 | tf_op jit(solution)/shard_map/ppermute | solution.py:26
  97.8 2.6 %collective-permute-done.22 = f32[288,128]{1,0:T(8,128)S(1)} collective-permute-done((f32[288,128]{1,0:T(8,128)S(1)}, f32[288,128]{1,0:T(8,128)S(1)}, u32[]{:S(2)}, u32[]{:S(2)}) %collective-permute-start.22) | collective-permute-done | bytes 147488 | tf_op jit(solution)/shard_map/ppermute | solution.py:26
  112.0 3.6 %collective-permute-done.28 = f32[320,128]{1,0:T(8,128)S(1)} collective-permute-done((f32[320,128]{1,0:T(8,128)S(1)}, f32[320,128]{1,0:T(8,128)S(1)}, u32[]{:S(2)}, u32[]{:S(2)}) %collective-permute-start.28) | collective-permute-done | bytes 163872 | tf_op jit(solution)/shard_map/ppermute | solution.py:26
  115.6 2.7 %collective-permute-done.29 = f32[320,128]{1,0:T(8,128)S(1)} collective-permute-done((f32[320,128]{1,0:T(8,128)S(1)}, f32[320,128]{1,0:T(8,128)S(1)}, u32[]{:S(2)}, u32[]{:S(2)}) %collective-permute-start.29) | collective-permute-done | bytes 163872 | tf_op jit(solution)/shard_map/ppermute | solution.py:26
  123.6 3.8 %collective-permute-done.34 = f32[48,128]{1,0:T(8,128)S(1)} collective-permute-done((f32[48,128]{1,0:T(8,128)S(1)}, f32[48,128]{1,0:T(8,128)S(1)}, u32[]{:S(2)}, u32[]{:S(2)}) %collective-permute-start.34) | collective-permute-done | bytes 24608 | tf_op jit(solution)/shard_map/ppermute | solution.py:26
  127.5 3.8 %collective-permute-done.35 = f32[48,128]{1,0:T(8,128)S(1)} collective-permute-done((f32[48,128]{1,0:T(8,128)S(1)}, f32[48,128]{1,0:T(8,128)S(1)}, u32[]{:S(2)}, u32[]{:S(2)}) %collective-permute-start.35) | collective-permute-done | bytes 24608 | tf_op jit(solution)/shard_map/ppermute | solution.py:26
  133.1 4.2 %collective-permute-start.36 = (f32[1408,128]{1,0:T(8,128)S(1)}, f32[1408,128]{1,0:T(8,128)S(1)}, u32[]{:S(2)}, u32[]{:S(2)}) collective-permute-start(f32[1408,128]{1,0:T(8,128)S(1)} %bitcast.183), channel_id=1, source_target_pairs={{0,1},{1,0},{2,3},{3,2},{4,5},{5,4},{6,7},{7,6},{8,9},{9,8},{10,11... | collective-permute-start | bytes 2162696 | tf_op jit(solution)/shard_map/ppermute | solution.py:26
  139.3 3.5 %collective-permute-start.38 = (f32[352,128]{1,0:T(8,128)S(1)}, f32[352,128]{1,0:T(8,128)S(1)}, u32[]{:S(2)}, u32[]{:S(2)}) collective-permute-start(f32[352,128]{1,0:T(8,128)S(1)} %bitcast.193), channel_id=1, source_target_pairs={{0,4},{2,6},{4,0},{6,2},{1,5},{3,7},{5,1},{7,3},{8,12},{10,14},{12... | collective-permute-start | bytes 540680 | tf_op jit(solution)/shard_map/ppermute | solution.py:26
  145.1 6.0 %collective-permute-done.38 = f32[352,128]{1,0:T(8,128)S(1)} collective-permute-done((f32[352,128]{1,0:T(8,128)S(1)}, f32[352,128]{1,0:T(8,128)S(1)}, u32[]{:S(2)}, u32[]{:S(2)}) %collective-permute-start.38) | collective-permute-done | bytes 180256 | tf_op jit(solution)/shard_map/ppermute | solution.py:26
  151.0 2.5 %collective-permute-done.39 = f32[352,128]{1,0:T(8,128)S(1)} collective-permute-done((f32[352,128]{1,0:T(8,128)S(1)}, f32[352,128]{1,0:T(8,128)S(1)}, u32[]{:S(2)}, u32[]{:S(2)}) %collective-permute-start.39) | collective-permute-done | bytes 180256 | tf_op jit(solution)/shard_map/ppermute | solution.py:26
  156.2 3.0 %collective-permute-start.41 = (f32[352,128]{1,0:T(8,128)S(1)}, f32[352,128]{1,0:T(8,128)S(1)}, u32[]{:S(2)}, u32[]{:S(2)}) collective-permute-start(f32[352,128]{1,0:T(8,128)S(1)} %bitcast.126), channel_id=1, source_target_pairs={{0,96},{1,25},{8,104},{9,1},{16,112},{17,9},{24,120},{25,17},{32,0... | collective-permute-start | bytes 540680 | tf_op jit(solution)/shard_map/ppermute | solution.py:26
  161.8 3.1 %collective-permute-done.40 = f32[352,128]{1,0:T(8,128)S(1)} collective-permute-done((f32[352,128]{1,0:T(8,128)S(1)}, f32[352,128]{1,0:T(8,128)S(1)}, u32[]{:S(2)}, u32[]{:S(2)}) %collective-permute-start.40) | collective-permute-done | bytes 180256 | tf_op jit(solution)/shard_map/ppermute | solution.py:26
  166.6 9.0 %collective-permute-done.45 = f32[1408,128]{1,0:T(8,128)S(1)} collective-permute-done((f32[1408,128]{1,0:T(8,128)S(1)}, f32[1408,128]{1,0:T(8,128)S(1)}, u32[]{:S(2)}, u32[]{:S(2)}) %collective-permute-start.45) | collective-permute-done | bytes 720928 | tf_op jit(solution)/shard_map/ppermute | solution.py:26
  177.2 7.7 %collective-permute-done.43 = f32[1408,128]{1,0:T(8,128)S(1)} collective-permute-done((f32[1408,128]{1,0:T(8,128)S(1)}, f32[1408,128]{1,0:T(8,128)S(1)}, u32[]{:S(2)}, u32[]{:S(2)}) %collective-permute-start.43) | collective-permute-done | bytes 720928 | tf_op jit(solution)/shard_map/ppermute | solution.py:26
  184.8 2.6 %shard_map.70 = (f32[4,4,12,8,128]{4,3,2,1,0:T(8,128)S(1)}, f32[4,4,12,8,128]{4,3,2,1,0:T(8,128)S(1)}, f32[4,11,8,128]{3,2,1,0:T(8,128)S(1)}) custom-call(s32[912]{0:T(1024)S(1)} %concatenate.3.tab.refs_0_, f32[4,4,11,8,128]{4,3,2,1,0:T(8,128)S(1)} %pad_maximum_fusion.refs_0_, f32[4,4,11,8,128]{4,3,2,1,0:T(8,128)S(1)} %bitcast.124, ...), custom_call_target="tpu_custom_call" | custom-call | tf_op jit(solution)/shard_map/pallas_call | solution.py:106
  187.4 4.1 %collective-permute-start.46 = (f32[1536,128]{1,0:T(8,128)S(1)}, f32[1536,128]{1,0:T(8,128)S(1)}, u32[]{:S(2)}, u32[]{:S(2)}) collective-permute-start(f32[1536,128]{1,0:T(8,128)S(1)} %bitcast.182), channel_id=1, source_target_pairs={{0,1},{1,0},{2,3},{3,2},{4,5},{5,4},{6,7},{7,6},{8,9},{9,8},{10,11... | collective-permute-start | bytes 2359304 | tf_op jit(solution)/shard_map/ppermute | solution.py:26
  199.7 4.4 %collective-permute-done.48 = f32[384,128]{1,0:T(8,128)S(1)} collective-permute-done((f32[384,128]{1,0:T(8,128)S(1)}, f32[384,128]{1,0:T(8,128)S(1)}, u32[]{:S(2)}, u32[]{:S(2)}) %collective-permute-start.48) | collective-permute-done | bytes 196640 | tf_op jit(solution)/shard_map/ppermute | solution.py:26
  210.7 3.4 %collective-permute-start.52 = (f32[256,128]{1,0:T(8,128)S(1)}, f32[256,128]{1,0:T(8,128)S(1)}, u32[]{:S(2)}, u32[]{:S(2)}) collective-permute-start(f32[256,128]{1,0:T(8,128)S(1)} %bitcast.209), channel_id=1, source_target_pairs={{0,4},{2,6},{4,0},{6,2},{1,5},{3,7},{5,1},{7,3},{8,12},{10,14},{12... | collective-permute-start | bytes 393224 | tf_op jit(solution)/shard_map/ppermute | solution.py:26
  215.4 4.8 %collective-permute-done.52 = f32[256,128]{1,0:T(8,128)S(1)} collective-permute-done((f32[256,128]{1,0:T(8,128)S(1)}, f32[256,128]{1,0:T(8,128)S(1)}, u32[]{:S(2)}, u32[]{:S(2)}) %collective-permute-start.52) | collective-permute-done | bytes 131104 | tf_op jit(solution)/shard_map/ppermute | solution.py:26
  (116 shorter events, 95.7 us)
Async XLA Ops:
  3.8 8.8 %collective-permute-start.1 = (f32[256,128]{1,0:T(8,128)S(1)}, f32[256,128]{1,0:T(8,128)S(1)}, u32[]{:S(2)}, u32[]{:S(2)}) collective-permute-start(f32[256,128]{1,0:T(8,128)S(1)} %bitcast.203), channel_id=1, source_target_pairs={{0,2},{2,0},{4,6},{6,4},{1,3},{3,1},{5,7},{7,5},{8,10},{10,8},{12,... | collective-permute-start | bytes 393224 | tf_op jit(solution)/shard_map/ppermute | solution.py:26
  5.6 9.4 %collective-permute-start.2 = (f32[256,128]{1,0:T(8,128)S(1)}, f32[256,128]{1,0:T(8,128)S(1)}, u32[]{:S(2)}, u32[]{:S(2)}) collective-permute-start(f32[256,128]{1,0:T(8,128)S(1)} %bitcast.202), channel_id=1, source_target_pairs={{0,4},{2,6},{4,0},{6,2},{1,5},{3,7},{5,1},{7,3},{8,12},{10,14},{12... | collective-permute-start | bytes 393224 | tf_op jit(solution)/shard_map/ppermute | solution.py:26
  8.9 8.6 %collective-permute-start.3 = (f32[256,128]{1,0:T(8,128)S(1)}, f32[256,128]{1,0:T(8,128)S(1)}, u32[]{:S(2)}, u32[]{:S(2)}) collective-permute-start(f32[256,128]{1,0:T(8,128)S(1)} %bitcast.201), channel_id=1, source_target_pairs={{0,6},{2,4},{4,2},{6,0},{1,7},{3,5},{5,3},{7,1},{8,14},{10,12},{12... | collective-permute-start | bytes 393224 | tf_op jit(solution)/shard_map/ppermute | solution.py:26
  27.2 12.9 %collective-permute-start.9 = (f32[896,128]{1,0:T(8,128)S(1)}, f32[896,128]{1,0:T(8,128)S(1)}, u32[]{:S(2)}, u32[]{:S(2)}) collective-permute-start(f32[896,128]{1,0:T(8,128)S(1)} %bitcast.117), channel_id=1, source_target_pairs={{0,24},{1,97},{8,0},{9,105},{16,8},{17,113},{24,16},{25,121},{32,5... | collective-permute-start | bytes 1376264 | tf_op jit(solution)/shard_map/ppermute | solution.py:26
  29.8 10.3 %collective-permute-start.8 = (f32[896,128]{1,0:T(8,128)S(1)}, f32[896,128]{1,0:T(8,128)S(1)}, u32[]{:S(2)}, u32[]{:S(2)}) collective-permute-start(f32[896,128]{1,0:T(8,128)S(1)} %bitcast.118), channel_id=1, source_target_pairs={{0,16},{1,65},{8,24},{9,73},{16,0},{17,81},{24,8},{25,89},{32,48},... | collective-permute-start | bytes 1376264 | tf_op jit(solution)/shard_map/ppermute | solution.py:26
  30.3 13.5 %collective-permute-start.7 = (f32[896,128]{1,0:T(8,128)S(1)}, f32[896,128]{1,0:T(8,128)S(1)}, u32[]{:S(2)}, u32[]{:S(2)}) collective-permute-start(f32[896,128]{1,0:T(8,128)S(1)} %bitcast.119), channel_id=1, source_target_pairs={{0,8},{1,33},{8,16},{9,41},{16,24},{17,49},{24,0},{25,57},{32,40},... | collective-permute-start | bytes 1376264 | tf_op jit(solution)/shard_map/ppermute | solution.py:26
  51.4 7.2 %collective-permute-start.12 = (f32[256,128]{1,0:T(8,128)S(1)}, f32[256,128]{1,0:T(8,128)S(1)}, u32[]{:S(2)}, u32[]{:S(2)}) collective-permute-start(f32[256,128]{1,0:T(8,128)S(1)} %bitcast.208), channel_id=1, source_target_pairs={{0,4},{2,6},{4,0},{6,2},{1,5},{3,7},{5,1},{7,3},{8,12},{10,14},{12... | collective-permute-start | bytes 393224 | tf_op jit(solution)/shard_map/ppermute | solution.py:26
  52.1 9.4 %collective-permute-start.13 = (f32[256,128]{1,0:T(8,128)S(1)}, f32[256,128]{1,0:T(8,128)S(1)}, u32[]{:S(2)}, u32[]{:S(2)}) collective-permute-start(f32[256,128]{1,0:T(8,128)S(1)} %bitcast.206), channel_id=1, source_target_pairs={{0,6},{2,4},{4,2},{6,0},{1,7},{3,5},{5,3},{7,1},{8,14},{10,12},{12... | collective-permute-start | bytes 393224 | tf_op jit(solution)/shard_map/ppermute | solution.py:26
  62.3 6.3 %collective-permute-start.15 = (f32[256,128]{1,0:T(8,128)S(1)}, f32[256,128]{1,0:T(8,128)S(1)}, u32[]{:S(2)}, u32[]{:S(2)}) collective-permute-start(f32[256,128]{1,0:T(8,128)S(1)} %bitcast.136), channel_id=1, source_target_pairs={{0,16},{8,0},{32,8},{40,32},{64,40},{72,64},{96,72},{104,96},{120,... | collective-permute-start | bytes 393224 | tf_op jit(solution)/shard_map/ppermute | solution.py:26
  62.7 9.8 %collective-permute-start.14 = (f32[256,128]{1,0:T(8,128)S(1)}, f32[256,128]{1,0:T(8,128)S(1)}, u32[]{:S(2)}, u32[]{:S(2)}) collective-permute-start(f32[256,128]{1,0:T(8,128)S(1)} %bitcast.137), channel_id=1, source_target_pairs={{0,8},{8,32},{32,40},{40,64},{64,72},{72,96},{96,104},{104,120},{1... | collective-permute-start | bytes 393224 | tf_op jit(solution)/shard_map/ppermute | solution.py:26
  77.5 10.3 %collective-permute-start.20 = (f32[288,128]{1,0:T(8,128)S(1)}, f32[288,128]{1,0:T(8,128)S(1)}, u32[]{:S(2)}, u32[]{:S(2)}) collective-permute-start(f32[288,128]{1,0:T(8,128)S(1)} %bitcast.199), channel_id=1, source_target_pairs={{0,4},{2,6},{4,0},{6,2},{1,5},{3,7},{5,1},{7,3},{8,12},{10,14},{12... | collective-permute-start | bytes 442376 | tf_op jit(solution)/shard_map/ppermute | solution.py:26
  81.0 9.3 %collective-permute-start.21 = (f32[288,128]{1,0:T(8,128)S(1)}, f32[288,128]{1,0:T(8,128)S(1)}, u32[]{:S(2)}, u32[]{:S(2)}) collective-permute-start(f32[288,128]{1,0:T(8,128)S(1)} %bitcast.198), channel_id=1, source_target_pairs={{0,6},{2,4},{4,2},{6,0},{1,7},{3,5},{5,3},{7,1},{8,14},{10,12},{12... | collective-permute-start | bytes 442376 | tf_op jit(solution)/shard_map/ppermute | solution.py:26
  91.0 6.8 %collective-permute-start.23 = (f32[288,128]{1,0:T(8,128)S(1)}, f32[288,128]{1,0:T(8,128)S(1)}, u32[]{:S(2)}, u32[]{:S(2)}) collective-permute-start(f32[288,128]{1,0:T(8,128)S(1)} %bitcast.133), channel_id=1, source_target_pairs={{0,16},{8,0},{32,8},{40,32},{64,40},{72,64},{96,72},{104,96},{120,... | collective-permute-start | bytes 442376 | tf_op jit(solution)/shard_map/ppermute | solution.py:26
  91.1 9.3 %collective-permute-start.22 = (f32[288,128]{1,0:T(8,128)S(1)}, f32[288,128]{1,0:T(8,128)S(1)}, u32[]{:S(2)}, u32[]{:S(2)}) collective-permute-start(f32[288,128]{1,0:T(8,128)S(1)} %bitcast.134), channel_id=1, source_target_pairs={{0,8},{8,32},{32,40},{40,64},{64,72},{72,96},{96,104},{104,120},{1... | collective-permute-start | bytes 442376 | tf_op jit(solution)/shard_map/ppermute | solution.py:26
  106.6 9.0 %collective-permute-start.28 = (f32[320,128]{1,0:T(8,128)S(1)}, f32[320,128]{1,0:T(8,128)S(1)}, u32[]{:S(2)}, u32[]{:S(2)}) collective-permute-start(f32[320,128]{1,0:T(8,128)S(1)} %bitcast.196), channel_id=1, source_target_pairs={{0,4},{2,6},{4,0},{6,2},{1,5},{3,7},{5,1},{7,3},{8,12},{10,14},{12... | collective-permute-start | bytes 491528 | tf_op jit(solution)/shard_map/ppermute | solution.py:26
  108.1 10.2 %collective-permute-start.29 = (f32[320,128]{1,0:T(8,128)S(1)}, f32[320,128]{1,0:T(8,128)S(1)}, u32[]{:S(2)}, u32[]{:S(2)}) collective-permute-start(f32[320,128]{1,0:T(8,128)S(1)} %bitcast.195), channel_id=1, source_target_pairs={{0,6},{2,4},{4,2},{6,0},{1,7},{3,5},{5,3},{7,1},{8,14},{10,12},{12... | collective-permute-start | bytes 491528 | tf_op jit(solution)/shard_map/ppermute | solution.py:26
  119.0 12.2 %collective-permute-start.31 = (f32[320,128]{1,0:T(8,128)S(1)}, f32[320,128]{1,0:T(8,128)S(1)}, u32[]{:S(2)}, u32[]{:S(2)}) collective-permute-start(f32[320,128]{1,0:T(8,128)S(1)} %bitcast.130), channel_id=1, source_target_pairs={{0,16},{8,0},{32,8},{40,32},{64,40},{72,64},{96,72},{104,96},{120,... | collective-permute-start | bytes 491528 | tf_op jit(solution)/shard_map/ppermute | solution.py:26
  119.2 12.0 %collective-permute-start.30 = (f32[320,128]{1,0:T(8,128)S(1)}, f32[320,128]{1,0:T(8,128)S(1)}, u32[]{:S(2)}, u32[]{:S(2)}) collective-permute-start(f32[320,128]{1,0:T(8,128)S(1)} %bitcast.131), channel_id=1, source_target_pairs={{0,8},{8,32},{32,40},{40,64},{64,72},{72,96},{96,104},{104,120},{1... | collective-permute-start | bytes 491528 | tf_op jit(solution)/shard_map/ppermute | solution.py:26
  120.6 10.7 %collective-permute-start.33 = (f32[256,128]{1,0:T(8,128)S(1)}, f32[256,128]{1,0:T(8,128)S(1)}, u32[]{:S(2)}, u32[]{:S(2)}) collective-permute-start(f32[256,128]{1,0:T(8,128)S(1)} %bitcast.205), channel_id=1, source_target_pairs={{0,24},{8,16},{32,0},{40,8},{64,32},{72,40},{96,64},{104,72},{120,... | collective-permute-start | bytes 393224 | tf_op jit(solution)/shard_map/ppermute | solution.py:26
  120.6 10.7 %collective-permute-start.32 = (f32[256,128]{1,0:T(8,128)S(1)}, f32[256,128]{1,0:T(8,128)S(1)}, u32[]{:S(2)}, u32[]{:S(2)}) collective-permute-start(f32[256,128]{1,0:T(8,128)S(1)} %bitcast.204), channel_id=1, source_target_pairs={{0,32},{8,40},{32,64},{40,72},{64,96},{72,104},{96,120},{104,112},... | collective-permute-start | bytes 393224 | tf_op jit(solution)/shard_map/ppermute | solution.py:26
  133.1 6.0 %collective-permute-start.36 = (f32[1408,128]{1,0:T(8,128)S(1)}, f32[1408,128]{1,0:T(8,128)S(1)}, u32[]{:S(2)}, u32[]{:S(2)}) collective-permute-start(f32[1408,128]{1,0:T(8,128)S(1)} %bitcast.183), channel_id=1, source_target_pairs={{0,1},{1,0},{2,3},{3,2},{4,5},{5,4},{6,7},{7,6},{8,9},{9,8},{10,11... | collective-permute-start | bytes 2162696 | tf_op jit(solution)/shard_map/ppermute | solution.py:26
  139.3 11.7 %collective-permute-start.38 = (f32[352,128]{1,0:T(8,128)S(1)}, f32[352,128]{1,0:T(8,128)S(1)}, u32[]{:S(2)}, u32[]{:S(2)}) collective-permute-start(f32[352,128]{1,0:T(8,128)S(1)} %bitcast.193), channel_id=1, source_target_pairs={{0,4},{2,6},{4,0},{6,2},{1,5},{3,7},{5,1},{7,3},{8,12},{10,14},{12... | collective-permute-start | bytes 540680 | tf_op jit(solution)/shard_map/ppermute | solution.py:26
  142.8 10.7 %collective-permute-start.39 = (f32[352,128]{1,0:T(8,128)S(1)}, f32[352,128]{1,0:T(8,128)S(1)}, u32[]{:S(2)}, u32[]{:S(2)}) collective-permute-start(f32[352,128]{1,0:T(8,128)S(1)} %bitcast.192), channel_id=1, source_target_pairs={{0,6},{2,4},{4,2},{6,0},{1,7},{3,5},{5,3},{7,1},{8,14},{10,12},{12... | collective-permute-start | bytes 540680 | tf_op jit(solution)/shard_map/ppermute | solution.py:26
  154.3 6.2 %collective-permute-start.42 = (f32[352,128]{1,0:T(8,128)S(1)}, f32[352,128]{1,0:T(8,128)S(1)}, u32[]{:S(2)}, u32[]{:S(2)}) collective-permute-start(f32[352,128]{1,0:T(8,128)S(1)} %bitcast.125), channel_id=1, source_target_pairs={{0,64},{1,17},{8,72},{9,25},{16,80},{17,1},{24,88},{25,9},{32,96},... | collective-permute-start | bytes 540680 | tf_op jit(solution)/shard_map/ppermute | solution.py:26
  165.0 10.5 %collective-permute-start.45 = (f32[1408,128]{1,0:T(8,128)S(1)}, f32[1408,128]{1,0:T(8,128)S(1)}, u32[]{:S(2)}, u32[]{:S(2)}) collective-permute-start(f32[1408,128]{1,0:T(8,128)S(1)} %bitcast.114), channel_id=1, source_target_pairs={{0,24},{1,97},{8,0},{9,105},{16,8},{17,113},{24,16},{25,121},{32,5... | collective-permute-start | bytes 2162696 | tf_op jit(solution)/shard_map/ppermute | solution.py:26
  165.1 12.1 %collective-permute-start.44 = (f32[1408,128]{1,0:T(8,128)S(1)}, f32[1408,128]{1,0:T(8,128)S(1)}, u32[]{:S(2)}, u32[]{:S(2)}) collective-permute-start(f32[1408,128]{1,0:T(8,128)S(1)} %bitcast.115), channel_id=1, source_target_pairs={{0,16},{1,65},{8,24},{9,73},{16,0},{17,81},{24,8},{25,89},{32,48},... | collective-permute-start | bytes 2162696 | tf_op jit(solution)/shard_map/ppermute | solution.py:26
  165.7 19.1 %collective-permute-start.43 = (f32[1408,128]{1,0:T(8,128)S(1)}, f32[1408,128]{1,0:T(8,128)S(1)}, u32[]{:S(2)}, u32[]{:S(2)}) collective-permute-start(f32[1408,128]{1,0:T(8,128)S(1)} %bitcast.116), channel_id=1, source_target_pairs={{0,8},{1,33},{8,16},{9,41},{16,24},{17,49},{24,0},{25,57},{32,40},... | collective-permute-start | bytes 2162696 | tf_op jit(solution)/shard_map/ppermute | solution.py:26
  193.5 6.2 %collective-permute-start.47 = (f32[384,128]{1,0:T(8,128)S(1)}, f32[384,128]{1,0:T(8,128)S(1)}, u32[]{:S(2)}, u32[]{:S(2)}) collective-permute-start(f32[384,128]{1,0:T(8,128)S(1)} %bitcast.191), channel_id=1, source_target_pairs={{0,2},{2,0},{4,6},{6,4},{1,3},{3,1},{5,7},{7,5},{8,10},{10,8},{12,... | collective-permute-start | bytes 589832 | tf_op jit(solution)/shard_map/ppermute | solution.py:26
  193.6 10.5 %collective-permute-start.48 = (f32[384,128]{1,0:T(8,128)S(1)}, f32[384,128]{1,0:T(8,128)S(1)}, u32[]{:S(2)}, u32[]{:S(2)}) collective-permute-start(f32[384,128]{1,0:T(8,128)S(1)} %bitcast.190), channel_id=1, source_target_pairs={{0,4},{2,6},{4,0},{6,2},{1,5},{3,7},{5,1},{7,3},{8,12},{10,14},{12... | collective-permute-start | bytes 589832 | tf_op jit(solution)/shard_map/ppermute | solution.py:26
  195.2 11.2 %collective-permute-start.49 = (f32[384,128]{1,0:T(8,128)S(1)}, f32[384,128]{1,0:T(8,128)S(1)}, u32[]{:S(2)}, u32[]{:S(2)}) collective-permute-start(f32[384,128]{1,0:T(8,128)S(1)} %bitcast.189), channel_id=1, source_target_pairs={{0,6},{2,4},{4,2},{6,0},{1,7},{3,5},{5,3},{7,1},{8,14},{10,12},{12... | collective-permute-start | bytes 589832 | tf_op jit(solution)/shard_map/ppermute | solution.py:26
  210.7 9.5 %collective-permute-start.52 = (f32[256,128]{1,0:T(8,128)S(1)}, f32[256,128]{1,0:T(8,128)S(1)}, u32[]{:S(2)}, u32[]{:S(2)}) collective-permute-start(f32[256,128]{1,0:T(8,128)S(1)} %bitcast.209), channel_id=1, source_target_pairs={{0,4},{2,6},{4,0},{6,2},{1,5},{3,7},{5,1},{7,3},{8,12},{10,14},{12... | collective-permute-start | bytes 393224 | tf_op jit(solution)/shard_map/ppermute | solution.py:26
  214.1 8.6 %collective-permute-start.53 = (f32[256,128]{1,0:T(8,128)S(1)}, f32[256,128]{1,0:T(8,128)S(1)}, u32[]{:S(2)}, u32[]{:S(2)}) collective-permute-start(f32[256,128]{1,0:T(8,128)S(1)} %bitcast.207), channel_id=1, source_target_pairs={{0,6},{2,4},{4,2},{6,0},{1,7},{3,5},{5,3},{7,1},{8,14},{10,12},{12... | collective-permute-start | bytes 393224 | tf_op jit(solution)/shard_map/ppermute | solution.py:26
  (27 other events, 107.8 us)

commit v8 on v7

--- a/solution.py
+++ b/solution.py
@@ -19,6 +19,9 @@
 
 
 RING = [ring_xy(p)[0] * 4 + ring_xy(p)[1] for p in range(16)]
+
+
+SLOTS = ((0, 2, 1, 3), (0, 2, 3, 1))
 
 
 def permute(value, axes, pairs):
@@ -40,8 +43,20 @@
     return permute(value, ("row", "layer"), pairs)
 
 
-def z_swap(value, k):
-    return permute(value, "col", [(i, i ^ k) for i in range(4)])
+def z_swap(value, slot):
+    pairs = [(z * 2 + h, (z ^ SLOTS[h][slot]) * 2 + h) for z in range(4) for h in (0, 1)]
+    return permute(value, GROUP, pairs)
+
+
+def slot_of(z, h, slot):
+    first, second = SLOTS[0][slot], SLOTS[1][slot]
+    return z ^ (first if first == second else jnp.where(h == 0, first, second))
+
+
+def slot_with(apart, h):
+    swapped = jnp.where(apart == 3, 1, jnp.where(apart == 1, 3, apart))
+    apart = jnp.where(h == 0, apart, swapped)
+    return jnp.where(apart == 2, 1, jnp.where(apart == 1, 2, apart))
 
 
 def core_swap(value):
@@ -118,7 +133,7 @@
     for k in range(4):
         for ref, core in ((own_ref, h), (oth_ref, 1 - h)):
             for e in range(4):
-                start = pl.multiple_of(e * 64 + (2 * (z ^ k) + core) * 8, 8)
+                start = pl.multiple_of(e * 64 + (2 * slot_of(z, core, k) + core) * 8, 8)
                 rows = d_ref[pl.ds(start, 8), :]
                 for t in range(4):
                     ref[k, e, t] = rows[:, t * 128 : (t + 1) * 128]
@@ -131,7 +146,7 @@
 
 
 def compact_kernel(tab, *refs):
-    ins, (out_ref, x_ref) = refs[:4], refs[4:]
+    ins, (keep_ref, out_ref, x_ref) = refs[:4], refs[4:]
     for k in range(4):
         x_ref[k] = ins[k][...]
     low = low_half()
@@ -146,11 +161,10 @@
                 continue
             j = (i + t - BAND) & 63
             sj = tab[INV + j]
-            tile = x_ref[(sj >> 4) ^ z, ((sj >> 3) & 1) ^ h, e, (sj & 7) >> 1]
-            tile = jnp.where((sj & 1) == (t & 1), tile, swap_halves(tile))
-            halves.append(jnp.where(bit(tab, 0, i, j) == 1, tile, 0.0))
+            tile = x_ref[slot_with((sj >> 4) ^ z, h), ((sj >> 3) & 1) ^ h, e, (sj & 7) >> 1]
+            halves.append(jnp.where((sj & 1) == (t & 1), tile, swap_halves(tile)))
         for t in range(BAND + 1):
-            out_ref[e, t] = jnp.where(low, halves[2 * t], halves[2 * t + 1])
+            out_ref[e, t] = jnp.where(low, halves[2 * t], halves[2 * t + 1]) * keep_ref[e, t]
 
 
 def gather_rows(rows):
@@ -179,7 +193,7 @@
     low = low_half()
     for zz in range(4):
         for ref, core in ((own_ref, h), (oth_ref, 1 - h)):
-            rows = p_ref[base + 2 * (z ^ zz) + core]
+            rows = p_ref[base + 2 * slot_of(z, core, zz) + core]
             if d % 2 == 0:
                 for m in range(tiles):
                     at = (d // 2 + m) * 128
@@ -302,12 +316,24 @@
     return jnp.where(tab[BRANCH + step] == 1, 2.0 * cur - square, square)
 
 
-def close_kernel(step, cuts, tab, p0, p1, p2, p3, cur_ref, *refs):
+def keep_kernel(tab, *refs):
+    low = low_half()
+    for s, ref in enumerate(refs):
+        w = BAND + s
+        margin = w + 1 if s == STEPS else w
+        for e in range(4):
+            i = tab[PLACE + 5] * 4 + e if 0 < s < STEPS else tab[PERM + tab[PLACE] * 4 + e]
+            for m in range(ref.shape[1]):
+                sides = []
+                for v in (2 * m - margin, 2 * m + 1 - margin):
+                    sides.append(bit(tab, s, i, (i + v + 64) & 63) if -w <= v <= w else 0)
+                ref[e, m] = jnp.where(low, sides[0], sides[1]).astype(F32)
+
+
+def close_kernel(step, cuts, tab, p0, p1, p2, p3, cur_ref, keep_ref, *refs):
     w = BAND + step
     low = low_half()
-    i0 = tab[PLACE + 5] * 4
     for e in range(4):
-        i = i0 + e
         turned = [swap_halves(cur_ref[e, t]) for t in range(w + 1)]
         zero = jnp.zeros((8, 128), F32)
         for m in range(w + 2):
@@ -315,18 +341,13 @@
             after = turned[m] if m <= w else zero
             cur = jnp.where(low, before, after)
             square = total((p0, p1, p2, p3), e, m)
-            one = bit(tab, step + 1, i, (i + 2 * m + 63 - w) & 63)
-            two = 0
-            if 2 * m + 1 <= 2 * w + 2:
-                two = bit(tab, step + 1, i, (i + 2 * m + 64 - w) & 63)
-            keep = jnp.where(low, one, two) == 1
-            value = jnp.where(keep, polynomial(tab, step, cur, square), 0.0)
+            value = polynomial(tab, step, cur, square) * keep_ref[e, m]
             for ref, (lo, hi, first, last) in zip(refs, cuts):
                 if lo <= e < hi and first <= m < last:
                     ref[e - lo, m - first] = value
 
 
-def finish_kernel(tab, p0, p1, p2, p3, cur_ref, own_ref, oth_ref, y_ref):
+def finish_kernel(tab, p0, p1, p2, p3, cur_ref, keep_ref, own_ref, oth_ref, y_ref):
     w = BAND + STEPS - 1
     low = low_half()
     row0 = tab[PLACE] * 4
@@ -337,7 +358,7 @@
         for m in range(w + 2):
             cur = cur_ref[e, m - 1] if 1 <= m <= w + 1 else jnp.zeros((8, 128), F32)
             square = total((p0, p1, p2, p3), e, m)
-            value = polynomial(tab, STEPS - 1, cur, square)
+            value = polynomial(tab, STEPS - 1, cur, square) * keep_ref[e, m]
             turned = swap_halves(value)
             for half in (0, 1):
                 v = 2 * m + half
@@ -347,9 +368,9 @@
                 sj = tab[INV + j]
                 odd = sj & 1
                 piece = jnp.where(odd == half, value, turned)
-                piece = jnp.where(bit(tab, STEPS, i, j) == 1, piece, 0.0)
                 side = jnp.where(low, 0, 1) == odd
-                at = ((sj >> 3) & 1) ^ h, (sj >> 4) ^ z, e, (sj & 7) >> 1
+                core = (sj >> 3) & 1
+                at = core ^ h, slot_with((sj >> 4) ^ z, core), e, (sj & 7) >> 1
                 y_ref[at] = jnp.where(side, piece, y_ref[at])
     own_ref[...] = y_ref[0]
     oth_ref[...] = y_ref[1]
@@ -360,7 +381,7 @@
     for k, y_ref in enumerate((y0, y1, y2, y3)):
         for core in (0, 1):
             for e in range(4):
-                start = pl.multiple_of(e * 64 + (2 * (z ^ k) + (core ^ h)) * 8, 8)
+                start = pl.multiple_of(e * 64 + (2 * slot_of(z, h, k) + (core ^ h)) * 8, 8)
                 for t in range(4):
                     out_ref[pl.ds(start, 8), t * 128 : (t + 1) * 128] = y_ref[core, e, t]
 
@@ -397,10 +418,12 @@
     slabs = (4, 4, 4, 8, 128)
     split = spread_group(*call(split_kernel, [slabs] * 2, [density]))
     tab = tables(masks, branch, perm)
+    tiles = [BAND + s + 1 for s in range(STEPS)] + [BAND + STEPS + 1]
+    keep = call(keep_kernel, [(4, n, 8, 128) for n in tiles], [], tab=tab)
     (rows,) = call(
         compact_kernel,
         [(4, BAND + 1, 8, 128)],
-        split,
+        split + [keep[0]],
         [pltpu.VMEM((4, 2, 4, 4, 8, 128), F32)],
         tab=tab,
     )
@@ -431,7 +454,7 @@
                 cuts.append(cut)
         kernel = lambda *refs, step=step, cuts=cuts: close_kernel(step, cuts, *refs)
         shapes = [(hi - lo, last - first, 8, 128) for lo, hi, first, last in cuts]
-        sent = call(kernel, shapes, parts + [cur], tab=tab)
+        sent = call(kernel, shapes, parts + [cur, keep[step + 1]], tab=tab)
         cur = sent[0]
         around = [ring_shift(sent[cuts.index(cut)], d) for d, cut in pieces]
         cur, *around = lax.optimization_barrier((cur, *around))
@@ -449,7 +472,7 @@
     )
     parts = reduce_group(own, oth)
     own, oth = call(
-        finish_kernel, [slabs] * 2, parts + [cur], [pltpu.VMEM((2,) + slabs, F32)], tab=tab
+        finish_kernel, [slabs] * 2, parts + [cur, keep[STEPS]], [pltpu.VMEM((2,) + slabs, F32)], tab=tab
     )
     (out,) = call(join_kernel, [(256, 512)], spread_group(own, oth))
     return out

time: 224 us -> 210 us (0.938)
  waiting for transfers between devices: 129 us -> 117 us
  starting transfers between devices: 73.2 us -> 69.9 us
    ppermute x54, waiting for transfers between devices: 129 us -> 117 us  [permute(): return lax.ppermute(flat, axes, pairs).reshape(value.shape)]
    ppermute x54, starting transfers between devices: 73.2 us -> 69.9 us  [permute(): return lax.ppermute(flat, axes, pairs).reshape(value.shape)]
    pallas_call x20 -> x21, Pallas kernels: 16.5 us -> 17.9 us  [call(): pl.pallas_call(kernel, out_shape=[jax.ShapeDtypeStruct(o, F32) for o in o...]
  transfers between devices with their start and end apart: 54 -> 54, of which waited for: 46 -> 44; matrix products, arithmetic and copies ran while one was open for 1% -> 1% of each run, Pallas kernels for 0% -> 1%
where the time goes in v8:
time: 210 us
  waiting for transfers between devices  117 us (56%)
  starting transfers between devices  69.9 us (33%)
  Pallas kernels  17.9 us (9%)
  local copies, waits for them, and re-layouts  3.75 us (2%)
    ppermute x54, waiting for transfers between devices, permute(): return lax.ppermute(flat, axes, pairs).reshape(value.shape)  117 us
    ppermute x54, starting transfers between devices, permute(): return lax.ppermute(flat, axes, pairs).reshape(value.shape)  69.9 us
    pallas_call x21, Pallas kernels, call(): pl.pallas_call(kernel, out_shape=[jax.ShapeDtypeStruct(o, F32) for o in o...  17.9 us
  transfers between devices with their start and end apart: 54, of which 44 were waited for; matrix products, arithmetic and copies ran while one was open for 1% of the time, Pallas kernels for 1%

profile of v8, /device:TPU:1, one launch (start us, length us, event | category | flops | bytes accessed | tf_op | source)
XLA Modules:
  0.0 209.6 jit_solution(15385842868687929463)
XLA Ops:
  3.8 3.8 %collective-permute-start.1 = (f32[256,128]{1,0:T(8,128)S(1)}, f32[256,128]{1,0:T(8,128)S(1)}, u32[]{:S(2)}, u32[]{:S(2)}) collective-permute-start(f32[256,128]{1,0:T(8,128)S(1)} %bitcast.203), channel_id=1, source_target_pairs={{0,4},{1,5},{2,6},{3,7},{4,0},{5,1},{6,2},{7,3},{8,12},{9,13},{10,... | collective-permute-start | bytes 393224 | tf_op jit(solution)/shard_map/ppermute | solution.py:29
  15.5 3.0 %collective-permute-start.6 = (f32[224,128]{1,0:T(8,128)S(1)}, f32[224,128]{1,0:T(8,128)S(1)}, u32[]{:S(2)}, u32[]{:S(2)}) collective-permute-start(f32[224,128]{1,0:T(8,128)S(1)} %bitcast.141), channel_id=1, source_target_pairs={{0,64},{1,17},{8,72},{9,25},{16,80},{17,1},{24,88},{25,9},{32,96},... | collective-permute-start | bytes 344072 | tf_op jit(solution)/shard_map/ppermute | solution.py:29
  24.1 2.5 %collective-permute-start.9 = (f32[896,128]{1,0:T(8,128)S(1)}, f32[896,128]{1,0:T(8,128)S(1)}, u32[]{:S(2)}, u32[]{:S(2)}) collective-permute-start(f32[896,128]{1,0:T(8,128)S(1)} %bitcast.117), channel_id=1, source_target_pairs={{0,24},{1,97},{8,0},{9,105},{16,8},{17,113},{24,16},{25,121},{32,5... | collective-permute-start | bytes 1376264 | tf_op jit(solution)/shard_map/ppermute | solution.py:29
  27.8 9.2 %collective-permute-done.9 = f32[896,128]{1,0:T(8,128)S(1)} collective-permute-done((f32[896,128]{1,0:T(8,128)S(1)}, f32[896,128]{1,0:T(8,128)S(1)}, u32[]{:S(2)}, u32[]{:S(2)}) %collective-permute-start.9) | collective-permute-done | bytes 458784 | tf_op jit(solution)/shard_map/ppermute | solution.py:29
  37.0 3.7 %collective-permute-done.7 = f32[896,128]{1,0:T(8,128)S(1)} collective-permute-done((f32[896,128]{1,0:T(8,128)S(1)}, f32[896,128]{1,0:T(8,128)S(1)}, u32[]{:S(2)}, u32[]{:S(2)}) %collective-permute-start.7) | collective-permute-done | bytes 458784 | tf_op jit(solution)/shard_map/ppermute | solution.py:29
  42.5 4.3 %collective-permute-start.10 = (f32[1024,128]{1,0:T(8,128)S(1)}, f32[1024,128]{1,0:T(8,128)S(1)}, u32[]{:S(2)}, u32[]{:S(2)}) collective-permute-start(f32[1024,128]{1,0:T(8,128)S(1)} %bitcast.186), channel_id=1, source_target_pairs={{0,1},{1,0},{2,3},{3,2},{4,5},{5,4},{6,7},{7,6},{8,9},{9,8},{10,11... | collective-permute-start | bytes 1572872 | tf_op jit(solution)/shard_map/ppermute | solution.py:29
  51.6 3.1 %collective-permute-done.11 = f32[256,128]{1,0:T(8,128)S(1)} collective-permute-done((f32[256,128]{1,0:T(8,128)S(1)}, f32[256,128]{1,0:T(8,128)S(1)}, u32[]{:S(2)}, u32[]{:S(2)}) %collective-permute-start.11) | collective-permute-done | bytes 131104 | tf_op jit(solution)/shard_map/ppermute | solution.py:29
  54.7 2.4 %collective-permute-done.12 = f32[256,128]{1,0:T(8,128)S(1)} collective-permute-done((f32[256,128]{1,0:T(8,128)S(1)}, f32[256,128]{1,0:T(8,128)S(1)}, u32[]{:S(2)}, u32[]{:S(2)}) %collective-permute-start.12) | collective-permute-done | bytes 131104 | tf_op jit(solution)/shard_map/ppermute | solution.py:29
  61.1 2.3 %collective-permute-done.17 = f32[144,128]{1,0:T(8,128)S(1)} collective-permute-done((f32[144,128]{1,0:T(8,128)S(1)}, f32[144,128]{1,0:T(8,128)S(1)}, u32[]{:S(2)}, u32[]{:S(2)}) %collective-permute-start.17) | collective-permute-done | bytes 73760 | tf_op jit(solution)/shard_map/ppermute | solution.py:29
  64.4 3.8 %collective-permute-done.14 = f32[256,128]{1,0:T(8,128)S(1)} collective-permute-done((f32[256,128]{1,0:T(8,128)S(1)}, f32[256,128]{1,0:T(8,128)S(1)}, u32[]{:S(2)}, u32[]{:S(2)}) %collective-permute-start.14) | collective-permute-done | bytes 131104 | tf_op jit(solution)/shard_map/ppermute | solution.py:29
  77.1 2.9 %collective-permute-done.19 = f32[288,128]{1,0:T(8,128)S(1)} collective-permute-done((f32[288,128]{1,0:T(8,128)S(1)}, f32[288,128]{1,0:T(8,128)S(1)}, u32[]{:S(2)}, u32[]{:S(2)}) %collective-permute-start.19) | collective-permute-done | bytes 147488 | tf_op jit(solution)/shard_map/ppermute | solution.py:29
  80.1 3.4 %collective-permute-done.20 = f32[288,128]{1,0:T(8,128)S(1)} collective-permute-done((f32[288,128]{1,0:T(8,128)S(1)}, f32[288,128]{1,0:T(8,128)S(1)}, u32[]{:S(2)}, u32[]{:S(2)}) %collective-permute-start.20) | collective-permute-done | bytes 147488 | tf_op jit(solution)/shard_map/ppermute | solution.py:29
  87.5 3.4 %collective-permute-done.25 = f32[224,128]{1,0:T(8,128)S(1)} collective-permute-done((f32[224,128]{1,0:T(8,128)S(1)}, f32[224,128]{1,0:T(8,128)S(1)}, u32[]{:S(2)}, u32[]{:S(2)}) %collective-permute-start.25) | collective-permute-done | bytes 114720 | tf_op jit(solution)/shard_map/ppermute | solution.py:29
  91.5 2.2 %collective-permute-done.22 = f32[288,128]{1,0:T(8,128)S(1)} collective-permute-done((f32[288,128]{1,0:T(8,128)S(1)}, f32[288,128]{1,0:T(8,128)S(1)}, u32[]{:S(2)}, u32[]{:S(2)}) %collective-permute-start.22) | collective-permute-done | bytes 147488 | tf_op jit(solution)/shard_map/ppermute | solution.py:29
  95.6 2.5 %collective-permute-start.26 = (f32[1280,128]{1,0:T(8,128)S(1)}, f32[1280,128]{1,0:T(8,128)S(1)}, u32[]{:S(2)}, u32[]{:S(2)}) collective-permute-start(f32[1280,128]{1,0:T(8,128)S(1)} %bitcast.184), channel_id=1, source_target_pairs={{0,1},{1,0},{2,3},{3,2},{4,5},{5,4},{6,7},{7,6},{8,9},{9,8},{10,11... | collective-permute-start | bytes 1966088 | tf_op jit(solution)/shard_map/ppermute | solution.py:29
  103.6 3.3 %collective-permute-done.27 = f32[320,128]{1,0:T(8,128)S(1)} collective-permute-done((f32[320,128]{1,0:T(8,128)S(1)}, f32[320,128]{1,0:T(8,128)S(1)}, u32[]{:S(2)}, u32[]{:S(2)}) %collective-permute-start.27) | collective-permute-done | bytes 163872 | tf_op jit(solution)/shard_map/ppermute | solution.py:29
  106.9 3.7 %collective-permute-done.28 = f32[320,128]{1,0:T(8,128)S(1)} collective-permute-done((f32[320,128]{1,0:T(8,128)S(1)}, f32[320,128]{1,0:T(8,128)S(1)}, u32[]{:S(2)}, u32[]{:S(2)}) %collective-permute-start.28) | collective-permute-done | bytes 163872 | tf_op jit(solution)/shard_map/ppermute | solution.py:29
  116.4 3.5 %collective-permute-done.34 = f32[48,128]{1,0:T(8,128)S(1)} collective-permute-done((f32[48,128]{1,0:T(8,128)S(1)}, f32[48,128]{1,0:T(8,128)S(1)}, u32[]{:S(2)}, u32[]{:S(2)}) %collective-permute-start.34) | collective-permute-done | bytes 24608 | tf_op jit(solution)/shard_map/ppermute | solution.py:29
  120.3 3.5 %collective-permute-done.35 = f32[48,128]{1,0:T(8,128)S(1)} collective-permute-done((f32[48,128]{1,0:T(8,128)S(1)}, f32[48,128]{1,0:T(8,128)S(1)}, u32[]{:S(2)}, u32[]{:S(2)}) %collective-permute-start.35) | collective-permute-done | bytes 24608 | tf_op jit(solution)/shard_map/ppermute | solution.py:29
  125.7 4.3 %collective-permute-start.36 = (f32[1408,128]{1,0:T(8,128)S(1)}, f32[1408,128]{1,0:T(8,128)S(1)}, u32[]{:S(2)}, u32[]{:S(2)}) collective-permute-start(f32[1408,128]{1,0:T(8,128)S(1)} %bitcast.183), channel_id=1, source_target_pairs={{0,1},{1,0},{2,3},{3,2},{4,5},{5,4},{6,7},{7,6},{8,9},{9,8},{10,11... | collective-permute-start | bytes 2162696 | tf_op jit(solution)/shard_map/ppermute | solution.py:29
  135.0 4.3 %collective-permute-done.37 = f32[352,128]{1,0:T(8,128)S(1)} collective-permute-done((f32[352,128]{1,0:T(8,128)S(1)}, f32[352,128]{1,0:T(8,128)S(1)}, u32[]{:S(2)}, u32[]{:S(2)}) %collective-permute-start.37) | collective-permute-done | bytes 180256 | tf_op jit(solution)/shard_map/ppermute | solution.py:29
  139.3 4.1 %collective-permute-done.38 = f32[352,128]{1,0:T(8,128)S(1)} collective-permute-done((f32[352,128]{1,0:T(8,128)S(1)}, f32[352,128]{1,0:T(8,128)S(1)}, u32[]{:S(2)}, u32[]{:S(2)}) %collective-permute-start.38) | collective-permute-done | bytes 180256 | tf_op jit(solution)/shard_map/ppermute | solution.py:29
  146.2 2.9 %collective-permute-start.41 = (f32[352,128]{1,0:T(8,128)S(1)}, f32[352,128]{1,0:T(8,128)S(1)}, u32[]{:S(2)}, u32[]{:S(2)}) collective-permute-start(f32[352,128]{1,0:T(8,128)S(1)} %bitcast.122), channel_id=1, source_target_pairs={{0,96},{1,25},{8,104},{9,1},{16,112},{17,9},{24,120},{25,17},{32,0... | collective-permute-start | bytes 540680 | tf_op jit(solution)/shard_map/ppermute | solution.py:29
  151.8 3.1 %collective-permute-done.40 = f32[352,128]{1,0:T(8,128)S(1)} collective-permute-done((f32[352,128]{1,0:T(8,128)S(1)}, f32[352,128]{1,0:T(8,128)S(1)}, u32[]{:S(2)}, u32[]{:S(2)}) %collective-permute-start.40) | collective-permute-done | bytes 180256 | tf_op jit(solution)/shard_map/ppermute | solution.py:29
  156.5 9.0 %collective-permute-done.45 = f32[1408,128]{1,0:T(8,128)S(1)} collective-permute-done((f32[1408,128]{1,0:T(8,128)S(1)}, f32[1408,128]{1,0:T(8,128)S(1)}, u32[]{:S(2)}, u32[]{:S(2)}) %collective-permute-start.45) | collective-permute-done | bytes 720928 | tf_op jit(solution)/shard_map/ppermute | solution.py:29
  167.2 7.7 %collective-permute-done.43 = f32[1408,128]{1,0:T(8,128)S(1)} collective-permute-done((f32[1408,128]{1,0:T(8,128)S(1)}, f32[1408,128]{1,0:T(8,128)S(1)}, u32[]{:S(2)}, u32[]{:S(2)}) %collective-permute-start.43) | collective-permute-done | bytes 720928 | tf_op jit(solution)/shard_map/ppermute | solution.py:29
  174.8 2.6 %shard_map.71 = (f32[4,4,12,8,128]{4,3,2,1,0:T(8,128)S(1)}, f32[4,4,12,8,128]{4,3,2,1,0:T(8,128)S(1)}, f32[4,11,8,128]{3,2,1,0:T(8,128)S(1)}) custom-call(s32[912]{0:T(1024)S(1)} %concatenate.3.tab.refs_0_, f32[4,4,11,8,128]{4,3,2,1,0:T(8,128)S(1)} %pad_maximum_fusion.refs_0_, f32[4,4,11,8,128]{4,3,2,1,0:T(8,128)S(1)} %bitcast.128, ...), custom_call_target="tpu_custom_call" | custom-call | tf_op jit(solution)/shard_map/pallas_call | solution.py:121
  177.5 4.4 %collective-permute-start.46 = (f32[1536,128]{1,0:T(8,128)S(1)}, f32[1536,128]{1,0:T(8,128)S(1)}, u32[]{:S(2)}, u32[]{:S(2)}) collective-permute-start(f32[1536,128]{1,0:T(8,128)S(1)} %bitcast.182), channel_id=1, source_target_pairs={{0,1},{1,0},{2,3},{3,2},{4,5},{5,4},{6,7},{7,6},{8,9},{9,8},{10,11... | collective-permute-start | bytes 2359304 | tf_op jit(solution)/shard_map/ppermute | solution.py:29
  187.0 4.6 %collective-permute-done.47 = f32[384,128]{1,0:T(8,128)S(1)} collective-permute-done((f32[384,128]{1,0:T(8,128)S(1)}, f32[384,128]{1,0:T(8,128)S(1)}, u32[]{:S(2)}, u32[]{:S(2)}) %collective-permute-start.47) | collective-permute-done | bytes 196640 | tf_op jit(solution)/shard_map/ppermute | solution.py:29
  191.6 4.6 %collective-permute-done.48 = f32[384,128]{1,0:T(8,128)S(1)} collective-permute-done((f32[384,128]{1,0:T(8,128)S(1)}, f32[384,128]{1,0:T(8,128)S(1)}, u32[]{:S(2)}, u32[]{:S(2)}) %collective-permute-start.48) | collective-permute-done | bytes 196640 | tf_op jit(solution)/shard_map/ppermute | solution.py:29
  202.9 3.2 %collective-permute-done.51 = f32[256,128]{1,0:T(8,128)S(1)} collective-permute-done((f32[256,128]{1,0:T(8,128)S(1)}, f32[256,128]{1,0:T(8,128)S(1)}, u32[]{:S(2)}, u32[]{:S(2)}) %collective-permute-start.51) | collective-permute-done | bytes 131104 | tf_op jit(solution)/shard_map/ppermute | solution.py:29
  206.0 2.5 %collective-permute-done.52 = f32[256,128]{1,0:T(8,128)S(1)} collective-permute-done((f32[256,128]{1,0:T(8,128)S(1)}, f32[256,128]{1,0:T(8,128)S(1)}, u32[]{:S(2)}, u32[]{:S(2)}) %collective-permute-start.52) | collective-permute-done | bytes 131104 | tf_op jit(solution)/shard_map/ppermute | solution.py:29
  (117 shorter events, 85.4 us)
Async XLA Ops:
  3.8 9.4 %collective-permute-start.1 = (f32[256,128]{1,0:T(8,128)S(1)}, f32[256,128]{1,0:T(8,128)S(1)}, u32[]{:S(2)}, u32[]{:S(2)}) collective-permute-start(f32[256,128]{1,0:T(8,128)S(1)} %bitcast.203), channel_id=1, source_target_pairs={{0,4},{1,5},{2,6},{3,7},{4,0},{5,1},{6,2},{7,3},{8,12},{9,13},{10,... | collective-permute-start | bytes 393224 | tf_op jit(solution)/shard_map/ppermute | solution.py:29
  7.6 6.4 %collective-permute-start.2 = (f32[256,128]{1,0:T(8,128)S(1)}, f32[256,128]{1,0:T(8,128)S(1)}, u32[]{:S(2)}, u32[]{:S(2)}) collective-permute-start(f32[256,128]{1,0:T(8,128)S(1)} %bitcast.202), channel_id=1, source_target_pairs={{0,2},{1,7},{2,0},{3,5},{4,6},{5,3},{6,4},{7,1},{8,10},{9,15},{10,... | collective-permute-start | bytes 393224 | tf_op jit(solution)/shard_map/ppermute | solution.py:29
  8.0 6.4 %collective-permute-start.3 = (f32[256,128]{1,0:T(8,128)S(1)}, f32[256,128]{1,0:T(8,128)S(1)}, u32[]{:S(2)}, u32[]{:S(2)}) collective-permute-start(f32[256,128]{1,0:T(8,128)S(1)} %bitcast.201), channel_id=1, source_target_pairs={{0,6},{1,3},{2,4},{3,1},{4,2},{5,7},{6,0},{7,5},{8,14},{9,11},{10,... | collective-permute-start | bytes 393224 | tf_op jit(solution)/shard_map/ppermute | solution.py:29
  24.1 12.9 %collective-permute-start.9 = (f32[896,128]{1,0:T(8,128)S(1)}, f32[896,128]{1,0:T(8,128)S(1)}, u32[]{:S(2)}, u32[]{:S(2)}) collective-permute-start(f32[896,128]{1,0:T(8,128)S(1)} %bitcast.117), channel_id=1, source_target_pairs={{0,24},{1,97},{8,0},{9,105},{16,8},{17,113},{24,16},{25,121},{32,5... | collective-permute-start | bytes 1376264 | tf_op jit(solution)/shard_map/ppermute | solution.py:29
  26.7 10.3 %collective-permute-start.8 = (f32[896,128]{1,0:T(8,128)S(1)}, f32[896,128]{1,0:T(8,128)S(1)}, u32[]{:S(2)}, u32[]{:S(2)}) collective-permute-start(f32[896,128]{1,0:T(8,128)S(1)} %bitcast.118), channel_id=1, source_target_pairs={{0,16},{1,65},{8,24},{9,73},{16,0},{17,81},{24,8},{25,89},{32,48},... | collective-permute-start | bytes 1376264 | tf_op jit(solution)/shard_map/ppermute | solution.py:29
  27.2 13.5 %collective-permute-start.7 = (f32[896,128]{1,0:T(8,128)S(1)}, f32[896,128]{1,0:T(8,128)S(1)}, u32[]{:S(2)}, u32[]{:S(2)}) collective-permute-start(f32[896,128]{1,0:T(8,128)S(1)} %bitcast.119), channel_id=1, source_target_pairs={{0,8},{1,33},{8,16},{9,41},{16,24},{17,49},{24,0},{25,57},{32,40},... | collective-permute-start | bytes 1376264 | tf_op jit(solution)/shard_map/ppermute | solution.py:29
  48.4 6.3 %collective-permute-start.11 = (f32[256,128]{1,0:T(8,128)S(1)}, f32[256,128]{1,0:T(8,128)S(1)}, u32[]{:S(2)}, u32[]{:S(2)}) collective-permute-start(f32[256,128]{1,0:T(8,128)S(1)} %bitcast.210), channel_id=1, source_target_pairs={{0,4},{1,5},{2,6},{3,7},{4,0},{5,1},{6,2},{7,3},{8,12},{9,13},{10,... | collective-permute-start | bytes 393224 | tf_op jit(solution)/shard_map/ppermute | solution.py:29
  50.2 6.9 %collective-permute-start.12 = (f32[256,128]{1,0:T(8,128)S(1)}, f32[256,128]{1,0:T(8,128)S(1)}, u32[]{:S(2)}, u32[]{:S(2)}) collective-permute-start(f32[256,128]{1,0:T(8,128)S(1)} %bitcast.208), channel_id=1, source_target_pairs={{0,2},{1,7},{2,0},{3,5},{4,6},{5,3},{6,4},{7,1},{8,10},{9,15},{10,... | collective-permute-start | bytes 393224 | tf_op jit(solution)/shard_map/ppermute | solution.py:29
  58.5 9.7 %collective-permute-start.14 = (f32[256,128]{1,0:T(8,128)S(1)}, f32[256,128]{1,0:T(8,128)S(1)}, u32[]{:S(2)}, u32[]{:S(2)}) collective-permute-start(f32[256,128]{1,0:T(8,128)S(1)} %bitcast.137), channel_id=1, source_target_pairs={{0,8},{8,32},{32,40},{40,64},{64,72},{72,96},{96,104},{104,120},{1... | collective-permute-start | bytes 393224 | tf_op jit(solution)/shard_map/ppermute | solution.py:29
  73.4 6.6 %collective-permute-start.19 = (f32[288,128]{1,0:T(8,128)S(1)}, f32[288,128]{1,0:T(8,128)S(1)}, u32[]{:S(2)}, u32[]{:S(2)}) collective-permute-start(f32[288,128]{1,0:T(8,128)S(1)} %bitcast.200), channel_id=1, source_target_pairs={{0,4},{1,5},{2,6},{3,7},{4,0},{5,1},{6,2},{7,3},{8,12},{9,13},{10,... | collective-permute-start | bytes 442376 | tf_op jit(solution)/shard_map/ppermute | solution.py:29
  75.6 7.8 %collective-permute-start.20 = (f32[288,128]{1,0:T(8,128)S(1)}, f32[288,128]{1,0:T(8,128)S(1)}, u32[]{:S(2)}, u32[]{:S(2)}) collective-permute-start(f32[288,128]{1,0:T(8,128)S(1)} %bitcast.199), channel_id=1, source_target_pairs={{0,2},{1,7},{2,0},{3,5},{4,6},{5,3},{6,4},{7,1},{8,10},{9,15},{10,... | collective-permute-start | bytes 442376 | tf_op jit(solution)/shard_map/ppermute | solution.py:29
  77.1 6.7 %collective-permute-start.21 = (f32[288,128]{1,0:T(8,128)S(1)}, f32[288,128]{1,0:T(8,128)S(1)}, u32[]{:S(2)}, u32[]{:S(2)}) collective-permute-start(f32[288,128]{1,0:T(8,128)S(1)} %bitcast.198), channel_id=1, source_target_pairs={{0,6},{1,3},{2,4},{3,1},{4,2},{5,7},{6,0},{7,5},{8,14},{9,11},{10,... | collective-permute-start | bytes 442376 | tf_op jit(solution)/shard_map/ppermute | solution.py:29
  84.5 7.0 %collective-permute-start.23 = (f32[288,128]{1,0:T(8,128)S(1)}, f32[288,128]{1,0:T(8,128)S(1)}, u32[]{:S(2)}, u32[]{:S(2)}) collective-permute-start(f32[288,128]{1,0:T(8,128)S(1)} %bitcast.133), channel_id=1, source_target_pairs={{0,16},{8,0},{32,8},{40,32},{64,40},{72,64},{96,72},{104,96},{120,... | collective-permute-start | bytes 442376 | tf_op jit(solution)/shard_map/ppermute | solution.py:29
  84.6 9.2 %collective-permute-start.22 = (f32[288,128]{1,0:T(8,128)S(1)}, f32[288,128]{1,0:T(8,128)S(1)}, u32[]{:S(2)}, u32[]{:S(2)}) collective-permute-start(f32[288,128]{1,0:T(8,128)S(1)} %bitcast.134), channel_id=1, source_target_pairs={{0,8},{8,32},{32,40},{40,64},{64,72},{72,96},{96,104},{104,120},{1... | collective-permute-start | bytes 442376 | tf_op jit(solution)/shard_map/ppermute | solution.py:29
  99.9 7.0 %collective-permute-start.27 = (f32[320,128]{1,0:T(8,128)S(1)}, f32[320,128]{1,0:T(8,128)S(1)}, u32[]{:S(2)}, u32[]{:S(2)}) collective-permute-start(f32[320,128]{1,0:T(8,128)S(1)} %bitcast.197), channel_id=1, source_target_pairs={{0,4},{1,5},{2,6},{3,7},{4,0},{5,1},{6,2},{7,3},{8,12},{9,13},{10,... | collective-permute-start | bytes 491528 | tf_op jit(solution)/shard_map/ppermute | solution.py:29
  102.1 8.5 %collective-permute-start.28 = (f32[320,128]{1,0:T(8,128)S(1)}, f32[320,128]{1,0:T(8,128)S(1)}, u32[]{:S(2)}, u32[]{:S(2)}) collective-permute-start(f32[320,128]{1,0:T(8,128)S(1)} %bitcast.196), channel_id=1, source_target_pairs={{0,2},{1,7},{2,0},{3,5},{4,6},{5,3},{6,4},{7,1},{8,10},{9,15},{10,... | collective-permute-start | bytes 491528 | tf_op jit(solution)/shard_map/ppermute | solution.py:29
  103.6 7.4 %collective-permute-start.29 = (f32[320,128]{1,0:T(8,128)S(1)}, f32[320,128]{1,0:T(8,128)S(1)}, u32[]{:S(2)}, u32[]{:S(2)}) collective-permute-start(f32[320,128]{1,0:T(8,128)S(1)} %bitcast.195), channel_id=1, source_target_pairs={{0,6},{1,3},{2,4},{3,1},{4,2},{5,7},{6,0},{7,5},{8,14},{9,11},{10,... | collective-permute-start | bytes 491528 | tf_op jit(solution)/shard_map/ppermute | solution.py:29
  111.6 12.2 %collective-permute-start.31 = (f32[320,128]{1,0:T(8,128)S(1)}, f32[320,128]{1,0:T(8,128)S(1)}, u32[]{:S(2)}, u32[]{:S(2)}) collective-permute-start(f32[320,128]{1,0:T(8,128)S(1)} %bitcast.130), channel_id=1, source_target_pairs={{0,16},{8,0},{32,8},{40,32},{64,40},{72,64},{96,72},{104,96},{120,... | collective-permute-start | bytes 491528 | tf_op jit(solution)/shard_map/ppermute | solution.py:29
  111.8 12.0 %collective-permute-start.30 = (f32[320,128]{1,0:T(8,128)S(1)}, f32[320,128]{1,0:T(8,128)S(1)}, u32[]{:S(2)}, u32[]{:S(2)}) collective-permute-start(f32[320,128]{1,0:T(8,128)S(1)} %bitcast.131), channel_id=1, source_target_pairs={{0,8},{8,32},{32,40},{40,64},{64,72},{72,96},{96,104},{104,120},{1... | collective-permute-start | bytes 491528 | tf_op jit(solution)/shard_map/ppermute | solution.py:29
  113.2 10.7 %collective-permute-start.33 = (f32[256,128]{1,0:T(8,128)S(1)}, f32[256,128]{1,0:T(8,128)S(1)}, u32[]{:S(2)}, u32[]{:S(2)}) collective-permute-start(f32[256,128]{1,0:T(8,128)S(1)} %bitcast.205), channel_id=1, source_target_pairs={{0,24},{8,16},{32,0},{40,8},{64,32},{72,40},{96,64},{104,72},{120,... | collective-permute-start | bytes 393224 | tf_op jit(solution)/shard_map/ppermute | solution.py:29
  113.2 10.7 %collective-permute-start.32 = (f32[256,128]{1,0:T(8,128)S(1)}, f32[256,128]{1,0:T(8,128)S(1)}, u32[]{:S(2)}, u32[]{:S(2)}) collective-permute-start(f32[256,128]{1,0:T(8,128)S(1)} %bitcast.204), channel_id=1, source_target_pairs={{0,32},{8,40},{32,64},{40,72},{64,96},{72,104},{96,120},{104,112},... | collective-permute-start | bytes 393224 | tf_op jit(solution)/shard_map/ppermute | solution.py:29
  131.9 7.4 %collective-permute-start.37 = (f32[352,128]{1,0:T(8,128)S(1)}, f32[352,128]{1,0:T(8,128)S(1)}, u32[]{:S(2)}, u32[]{:S(2)}) collective-permute-start(f32[352,128]{1,0:T(8,128)S(1)} %bitcast.194), channel_id=1, source_target_pairs={{0,4},{1,5},{2,6},{3,7},{4,0},{5,1},{6,2},{7,3},{8,12},{9,13},{10,... | collective-permute-start | bytes 540680 | tf_op jit(solution)/shard_map/ppermute | solution.py:29
  133.6 9.8 %collective-permute-start.38 = (f32[352,128]{1,0:T(8,128)S(1)}, f32[352,128]{1,0:T(8,128)S(1)}, u32[]{:S(2)}, u32[]{:S(2)}) collective-permute-start(f32[352,128]{1,0:T(8,128)S(1)} %bitcast.193), channel_id=1, source_target_pairs={{0,2},{1,7},{2,0},{3,5},{4,6},{5,3},{6,4},{7,1},{8,10},{9,15},{10,... | collective-permute-start | bytes 540680 | tf_op jit(solution)/shard_map/ppermute | solution.py:29
  135.0 8.3 %collective-permute-start.39 = (f32[352,128]{1,0:T(8,128)S(1)}, f32[352,128]{1,0:T(8,128)S(1)}, u32[]{:S(2)}, u32[]{:S(2)}) collective-permute-start(f32[352,128]{1,0:T(8,128)S(1)} %bitcast.192), channel_id=1, source_target_pairs={{0,6},{1,3},{2,4},{3,1},{4,2},{5,7},{6,0},{7,5},{8,14},{9,11},{10,... | collective-permute-start | bytes 540680 | tf_op jit(solution)/shard_map/ppermute | solution.py:29
  155.0 10.5 %collective-permute-start.45 = (f32[1408,128]{1,0:T(8,128)S(1)}, f32[1408,128]{1,0:T(8,128)S(1)}, u32[]{:S(2)}, u32[]{:S(2)}) collective-permute-start(f32[1408,128]{1,0:T(8,128)S(1)} %bitcast.114), channel_id=1, source_target_pairs={{0,24},{1,97},{8,0},{9,105},{16,8},{17,113},{24,16},{25,121},{32,5... | collective-permute-start | bytes 2162696 | tf_op jit(solution)/shard_map/ppermute | solution.py:29
  155.1 12.1 %collective-permute-start.44 = (f32[1408,128]{1,0:T(8,128)S(1)}, f32[1408,128]{1,0:T(8,128)S(1)}, u32[]{:S(2)}, u32[]{:S(2)}) collective-permute-start(f32[1408,128]{1,0:T(8,128)S(1)} %bitcast.115), channel_id=1, source_target_pairs={{0,16},{1,65},{8,24},{9,73},{16,0},{17,81},{24,8},{25,89},{32,48},... | collective-permute-start | bytes 2162696 | tf_op jit(solution)/shard_map/ppermute | solution.py:29
  155.8 19.1 %collective-permute-start.43 = (f32[1408,128]{1,0:T(8,128)S(1)}, f32[1408,128]{1,0:T(8,128)S(1)}, u32[]{:S(2)}, u32[]{:S(2)}) collective-permute-start(f32[1408,128]{1,0:T(8,128)S(1)} %bitcast.116), channel_id=1, source_target_pairs={{0,8},{1,33},{8,16},{9,41},{16,24},{17,49},{24,0},{25,57},{32,40},... | collective-permute-start | bytes 2162696 | tf_op jit(solution)/shard_map/ppermute | solution.py:29
  177.5 6.3 %collective-permute-start.46 = (f32[1536,128]{1,0:T(8,128)S(1)}, f32[1536,128]{1,0:T(8,128)S(1)}, u32[]{:S(2)}, u32[]{:S(2)}) collective-permute-start(f32[1536,128]{1,0:T(8,128)S(1)} %bitcast.182), channel_id=1, source_target_pairs={{0,1},{1,0},{2,3},{3,2},{4,5},{5,4},{6,7},{7,6},{8,9},{9,8},{10,11... | collective-permute-start | bytes 2359304 | tf_op jit(solution)/shard_map/ppermute | solution.py:29
  183.9 7.7 %collective-permute-start.47 = (f32[384,128]{1,0:T(8,128)S(1)}, f32[384,128]{1,0:T(8,128)S(1)}, u32[]{:S(2)}, u32[]{:S(2)}) collective-permute-start(f32[384,128]{1,0:T(8,128)S(1)} %bitcast.191), channel_id=1, source_target_pairs={{0,4},{1,5},{2,6},{3,7},{4,0},{5,1},{6,2},{7,3},{8,12},{9,13},{10,... | collective-permute-start | bytes 589832 | tf_op jit(solution)/shard_map/ppermute | solution.py:29
  185.5 10.7 %collective-permute-start.48 = (f32[384,128]{1,0:T(8,128)S(1)}, f32[384,128]{1,0:T(8,128)S(1)}, u32[]{:S(2)}, u32[]{:S(2)}) collective-permute-start(f32[384,128]{1,0:T(8,128)S(1)} %bitcast.190), channel_id=1, source_target_pairs={{0,2},{1,7},{2,0},{3,5},{4,6},{5,3},{6,4},{7,1},{8,10},{9,15},{10,... | collective-permute-start | bytes 589832 | tf_op jit(solution)/shard_map/ppermute | solution.py:29
  187.0 9.2 %collective-permute-start.49 = (f32[384,128]{1,0:T(8,128)S(1)}, f32[384,128]{1,0:T(8,128)S(1)}, u32[]{:S(2)}, u32[]{:S(2)}) collective-permute-start(f32[384,128]{1,0:T(8,128)S(1)} %bitcast.189), channel_id=1, source_target_pairs={{0,6},{1,3},{2,4},{3,1},{4,2},{5,7},{6,0},{7,5},{8,14},{9,11},{10,... | collective-permute-start | bytes 589832 | tf_op jit(solution)/shard_map/ppermute | solution.py:29
  201.4 7.1 %collective-permute-start.52 = (f32[256,128]{1,0:T(8,128)S(1)}, f32[256,128]{1,0:T(8,128)S(1)}, u32[]{:S(2)}, u32[]{:S(2)}) collective-permute-start(f32[256,128]{1,0:T(8,128)S(1)} %bitcast.209), channel_id=1, source_target_pairs={{0,2},{1,7},{2,0},{3,5},{4,6},{5,3},{6,4},{7,1},{8,10},{9,15},{10,... | collective-permute-start | bytes 393224 | tf_op jit(solution)/shard_map/ppermute | solution.py:29
  (27 other events, 112.5 us)

commit v9 on v8

--- a/solution.py
+++ b/solution.py
@@ -173,6 +173,7 @@
     line = jnp.stack([rows, near[0], near[2], near[1]])
     line = lax.optimization_barrier(line)
     far = [line_shift(line, k, 1) for k in (1, 3, 2)]
+    line, *far = lax.optimization_barrier((line, *far))
     return [line, far[0], far[2], far[1]]
 
 
@@ -188,8 +189,8 @@
     return jnp.where(first, dy, dx), jnp.where(first, dx, dy), e
 
 
-def write_slabs(tab, p_ref, own_ref, oth_ref, e, base, d, tiles):
-    z, h = tab[PLACE + 6], tab[PLACE + 4]
+def write_slabs(p_ref, own_ref, oth_ref, e, base, d, tiles):
+    z, h = lax.axis_index("col"), lax.axis_index("layer")
     low = low_half()
     for zz in range(4):
         for ref, core in ((own_ref, h), (oth_ref, 1 - h)):
@@ -216,7 +217,7 @@
     return left, (left + 4 + w + 1 + 1) // 2
 
 
-def step_body(tab, strips, w, own_ref, oth_ref, hi_ref, lo_ref, p_ref):
+def step_body(strips, w, own_ref, oth_ref, hi_ref, lo_ref, p_ref):
     left, count = geometry(w)
     nk = 4 + 2 * w
     for a in range(0, nk, 2):
@@ -227,7 +228,7 @@
         store_split(hi_ref, lo_ref, a * 8, pair[0], pair[1])
     p_ref[...] = product(hi_ref, lo_ref, left * 64, 256).reshape(32, 8, count * 128)
     for e in range(4):
-        write_slabs(tab, p_ref, own_ref, oth_ref, e, e * 8, left - (w + 1) + e, w + 2)
+        write_slabs(p_ref, own_ref, oth_ref, e, e * 8, left - (w + 1) + e, w + 2)
 
 
 def first_step_kernel(tab, *refs):
@@ -244,10 +245,10 @@
             cur_ref[b - w] = strip
         return [strip[t] for t in range(w + 1)], 0
 
-    step_body(tab, strips, w, own_ref, oth_ref, hi_ref, lo_ref, p_ref)
-
-
-def step_kernel(w, pieces, tab, *refs):
+    step_body(strips, w, own_ref, oth_ref, hi_ref, lo_ref, p_ref)
+
+
+def step_kernel(w, pieces, *refs):
     n = 1 + len(pieces)
     ins, (own_ref, oth_ref, hi_ref, lo_ref, p_ref) = refs[:n], refs[n:]
 
@@ -261,7 +262,7 @@
         row = off + 4 * d - lo
         return [ins[1 + at][row, t] for t in range(last - first)], first
 
-    step_body(tab, strips, w, own_ref, oth_ref, hi_ref, lo_ref, p_ref)
+    step_body(strips, w, own_ref, oth_ref, hi_ref, lo_ref, p_ref)
 
 
 def halo_pieces(w):
@@ -300,7 +301,7 @@
                 two = shifted(strips(a + 1), left - 2 * w + a + 1, count)
             store_split(hi_ref, lo_ref, a * 8, one, two)
         p_ref[...] = product(hi_ref, lo_ref, left * 64, 64).reshape(8, 8, count * 128)
-        write_slabs(tab, p_ref, own_ref, oth_ref, e, 0, 0, count)
+        write_slabs(p_ref, own_ref, oth_ref, e, 0, 0, count)
 
 
 def pair_kernel(own_ref, got_ref, *outs):
@@ -312,12 +313,17 @@
     return (parts[0][e, m] + parts[1][e, m]) + (parts[2][e, m] + parts[3][e, m])
 
 
-def polynomial(tab, step, cur, square):
-    return jnp.where(tab[BRANCH + step] == 1, 2.0 * cur - square, square)
+def polynomial(coef_ref, step, cur, square):
+    return coef_ref[step, 0] * cur + coef_ref[step, 1] * square
 
 
 def keep_kernel(tab, *refs):
     low = low_half()
+    refs, coef_ref = refs[:-1], refs[-1]
+    for s in range(STEPS):
+        twice = tab[BRANCH + s] == 1
+        coef_ref[s, 0] = jnp.full((8, 128), jnp.where(twice, 2.0, 0.0), F32)
+        coef_ref[s, 1] = jnp.full((8, 128), jnp.where(twice, -1.0, 1.0), F32)
     for s, ref in enumerate(refs):
         w = BAND + s
         margin = w + 1 if s == STEPS else w
@@ -330,7 +336,7 @@
                 ref[e, m] = jnp.where(low, sides[0], sides[1]).astype(F32)
 
 
-def close_kernel(step, cuts, tab, p0, p1, p2, p3, cur_ref, keep_ref, *refs):
+def close_kernel(step, cuts, p0, p1, p2, p3, cur_ref, keep_ref, coef_ref, *refs):
     w = BAND + step
     low = low_half()
     for e in range(4):
@@ -341,13 +347,13 @@
             after = turned[m] if m <= w else zero
             cur = jnp.where(low, before, after)
             square = total((p0, p1, p2, p3), e, m)
-            value = polynomial(tab, step, cur, square) * keep_ref[e, m]
+            value = polynomial(coef_ref, step, cur, square) * keep_ref[e, m]
             for ref, (lo, hi, first, last) in zip(refs, cuts):
                 if lo <= e < hi and first <= m < last:
                     ref[e - lo, m - first] = value
 
 
-def finish_kernel(tab, p0, p1, p2, p3, cur_ref, keep_ref, own_ref, oth_ref, y_ref):
+def finish_kernel(tab, p0, p1, p2, p3, cur_ref, keep_ref, coef_ref, own_ref, oth_ref, y_ref):
     w = BAND + STEPS - 1
     low = low_half()
     row0 = tab[PLACE] * 4
@@ -358,7 +364,7 @@
         for m in range(w + 2):
             cur = cur_ref[e, m - 1] if 1 <= m <= w + 1 else jnp.zeros((8, 128), F32)
             square = total((p0, p1, p2, p3), e, m)
-            value = polynomial(tab, STEPS - 1, cur, square) * keep_ref[e, m]
+            value = polynomial(coef_ref, STEPS - 1, cur, square) * keep_ref[e, m]
             turned = swap_halves(value)
             for half in (0, 1):
                 v = 2 * m + half
@@ -419,7 +425,8 @@
     split = spread_group(*call(split_kernel, [slabs] * 2, [density]))
     tab = tables(masks, branch, perm)
     tiles = [BAND + s + 1 for s in range(STEPS)] + [BAND + STEPS + 1]
-    keep = call(keep_kernel, [(4, n, 8, 128) for n in tiles], [], tab=tab)
+    shapes = [(4, n, 8, 128) for n in tiles] + [(STEPS, 2, 8, 128)]
+    *keep, coef = call(keep_kernel, shapes, [], tab=tab)
     (rows,) = call(
         compact_kernel,
         [(4, BAND + 1, 8, 128)],
@@ -445,7 +452,7 @@
             )
         else:
             kernel = lambda *refs, w=w, pieces=pieces: step_kernel(w, pieces, *refs)
-            own, oth = call(kernel, [part, part], [cur] + around, scratch, tab=tab)
+            own, oth = call(kernel, [part, part], [cur] + around, scratch)
         parts = reduce_group(own, oth)
         pieces = halo_pieces(w + 1) if step < STEPS - 2 else []
         cuts = [(0, 4, 0, w + 2)]
@@ -454,7 +461,7 @@
                 cuts.append(cut)
         kernel = lambda *refs, step=step, cuts=cuts: close_kernel(step, cuts, *refs)
         shapes = [(hi - lo, last - first, 8, 128) for lo, hi, first, last in cuts]
-        sent = call(kernel, shapes, parts + [cur, keep[step + 1]], tab=tab)
+        sent = call(kernel, shapes, parts + [cur, keep[step + 1], coef])
         cur = sent[0]
         around = [ring_shift(sent[cuts.index(cut)], d) for d, cut in pieces]
         cur, *around = lax.optimization_barrier((cur, *around))
@@ -472,7 +479,7 @@
     )
     parts = reduce_group(own, oth)
     own, oth = call(
-        finish_kernel, [slabs] * 2, parts + [cur, keep[STEPS]], [pltpu.VMEM((2,) + slabs, F32)], tab=tab
+        finish_kernel, [slabs] * 2, parts + [cur, keep[STEPS], coef], [pltpu.VMEM((2,) + slabs, F32)], tab=tab
     )
     (out,) = call(join_kernel, [(256, 512)], spread_group(own, oth))
     return out

time: 210 us -> 202 us (0.962)
  Pallas kernels: 17.9 us -> 13.7 us
    pallas_call x21, Pallas kernels: 17.9 us -> 13.7 us  [call(): pl.pallas_call(kernel, out_shape=[jax.ShapeDtypeStruct(o, F32) for o in o...]
    ppermute x54, waiting for transfers between devices: 117 us -> 115 us  [permute(): return lax.ppermute(flat, axes, pairs).reshape(value.shape)]
where the time goes in v9:
time: 202 us
  waiting for transfers between devices  115 us (57%)
  starting transfers between devices  69 us (34%)
  Pallas kernels  13.7 us (7%)
  local copies, waits for them, and re-layouts  3.75 us (2%)
    ppermute x54, waiting for transfers between devices, permute(): return lax.ppermute(flat, axes, pairs).reshape(value.shape)  115 us
    ppermute x54, starting transfers between devices, permute(): return lax.ppermute(flat, axes, pairs).reshape(value.shape)  69 us
    pallas_call x21, Pallas kernels, call(): pl.pallas_call(kernel, out_shape=[jax.ShapeDtypeStruct(o, F32) for o in o...  13.7 us
  transfers between devices with their start and end apart: 54, of which 44 were waited for; matrix products, arithmetic and copies ran while one was open for 1% of the time, Pallas kernels for 1%

profile of v9, /device:TPU:1, one launch (start us, length us, event | category | flops | bytes accessed | tf_op | source)
XLA Modules:
  0.0 202.3 jit_solution(10723125022682598944)
XLA Ops:
  3.8 3.8 %collective-permute-start.1 = (f32[256,128]{1,0:T(8,128)S(1)}, f32[256,128]{1,0:T(8,128)S(1)}, u32[]{:S(2)}, u32[]{:S(2)}) collective-permute-start(f32[256,128]{1,0:T(8,128)S(1)} %bitcast.203), channel_id=1, source_target_pairs={{0,4},{1,5},{2,6},{3,7},{4,0},{5,1},{6,2},{7,3},{8,12},{9,13},{10,... | collective-permute-start | bytes 393224 | tf_op jit(solution)/shard_map/ppermute | solution.py:29
  15.5 3.0 %collective-permute-start.6 = (f32[224,128]{1,0:T(8,128)S(1)}, f32[224,128]{1,0:T(8,128)S(1)}, u32[]{:S(2)}, u32[]{:S(2)}) collective-permute-start(f32[224,128]{1,0:T(8,128)S(1)} %bitcast.141), channel_id=1, source_target_pairs={{0,64},{1,17},{8,72},{9,25},{16,80},{17,1},{24,88},{25,9},{32,96},... | collective-permute-start | bytes 344072 | tf_op jit(solution)/shard_map/ppermute | solution.py:29
  24.1 2.8 %collective-permute-start.9 = (f32[896,128]{1,0:T(8,128)S(1)}, f32[896,128]{1,0:T(8,128)S(1)}, u32[]{:S(2)}, u32[]{:S(2)}) collective-permute-start(f32[896,128]{1,0:T(8,128)S(1)} %bitcast.117), channel_id=1, source_target_pairs={{0,16},{1,65},{8,24},{9,73},{16,0},{17,81},{24,8},{25,89},{32,48},... | collective-permute-start | bytes 1376264 | tf_op jit(solution)/shard_map/ppermute | solution.py:29
  28.4 4.9 %collective-permute-done.9 = f32[896,128]{1,0:T(8,128)S(1)} collective-permute-done((f32[896,128]{1,0:T(8,128)S(1)}, f32[896,128]{1,0:T(8,128)S(1)}, u32[]{:S(2)}, u32[]{:S(2)}) %collective-permute-start.9) | collective-permute-done | bytes 458784 | tf_op jit(solution)/shard_map/ppermute | solution.py:29
  33.4 5.0 %collective-permute-done.8 = f32[896,128]{1,0:T(8,128)S(1)} collective-permute-done((f32[896,128]{1,0:T(8,128)S(1)}, f32[896,128]{1,0:T(8,128)S(1)}, u32[]{:S(2)}, u32[]{:S(2)}) %collective-permute-start.8) | collective-permute-done | bytes 458784 | tf_op jit(solution)/shard_map/ppermute | solution.py:29
  40.2 4.0 %collective-permute-start.10 = (f32[1024,128]{1,0:T(8,128)S(1)}, f32[1024,128]{1,0:T(8,128)S(1)}, u32[]{:S(2)}, u32[]{:S(2)}) collective-permute-start(f32[1024,128]{1,0:T(8,128)S(1)} %bitcast.186), channel_id=1, source_target_pairs={{0,1},{1,0},{2,3},{3,2},{4,5},{5,4},{6,7},{7,6},{8,9},{9,8},{10,11... | collective-permute-start | bytes 1572872 | tf_op jit(solution)/shard_map/ppermute | solution.py:29
  49.0 3.1 %collective-permute-done.11 = f32[256,128]{1,0:T(8,128)S(1)} collective-permute-done((f32[256,128]{1,0:T(8,128)S(1)}, f32[256,128]{1,0:T(8,128)S(1)}, u32[]{:S(2)}, u32[]{:S(2)}) %collective-permute-start.11) | collective-permute-done | bytes 131104 | tf_op jit(solution)/shard_map/ppermute | solution.py:29
  52.1 2.4 %collective-permute-done.12 = f32[256,128]{1,0:T(8,128)S(1)} collective-permute-done((f32[256,128]{1,0:T(8,128)S(1)}, f32[256,128]{1,0:T(8,128)S(1)}, u32[]{:S(2)}, u32[]{:S(2)}) %collective-permute-start.12) | collective-permute-done | bytes 131104 | tf_op jit(solution)/shard_map/ppermute | solution.py:29
  54.9 2.6 %collective-permute-start.15 = (f32[256,128]{1,0:T(8,128)S(1)}, f32[256,128]{1,0:T(8,128)S(1)}, u32[]{:S(2)}, u32[]{:S(2)}) collective-permute-start(f32[256,128]{1,0:T(8,128)S(1)} %bitcast.136), channel_id=1, source_target_pairs={{0,16},{8,0},{32,8},{40,32},{64,40},{72,64},{96,72},{104,96},{120,... | collective-permute-start | bytes 393224 | tf_op jit(solution)/shard_map/ppermute | solution.py:29
  59.0 2.5 %collective-permute-done.17 = f32[144,128]{1,0:T(8,128)S(1)} collective-permute-done((f32[144,128]{1,0:T(8,128)S(1)}, f32[144,128]{1,0:T(8,128)S(1)}, u32[]{:S(2)}, u32[]{:S(2)}) %collective-permute-start.17) | collective-permute-done | bytes 73760 | tf_op jit(solution)/shard_map/ppermute | solution.py:29
  63.2 3.8 %collective-permute-done.14 = f32[256,128]{1,0:T(8,128)S(1)} collective-permute-done((f32[256,128]{1,0:T(8,128)S(1)}, f32[256,128]{1,0:T(8,128)S(1)}, u32[]{:S(2)}, u32[]{:S(2)}) %collective-permute-start.14) | collective-permute-done | bytes 131104 | tf_op jit(solution)/shard_map/ppermute | solution.py:29
  75.4 2.9 %collective-permute-done.19 = f32[288,128]{1,0:T(8,128)S(1)} collective-permute-done((f32[288,128]{1,0:T(8,128)S(1)}, f32[288,128]{1,0:T(8,128)S(1)}, u32[]{:S(2)}, u32[]{:S(2)}) %collective-permute-start.19) | collective-permute-done | bytes 147488 | tf_op jit(solution)/shard_map/ppermute | solution.py:29
  78.3 3.4 %collective-permute-done.20 = f32[288,128]{1,0:T(8,128)S(1)} collective-permute-done((f32[288,128]{1,0:T(8,128)S(1)}, f32[288,128]{1,0:T(8,128)S(1)}, u32[]{:S(2)}, u32[]{:S(2)}) %collective-permute-start.20) | collective-permute-done | bytes 147488 | tf_op jit(solution)/shard_map/ppermute | solution.py:29
  85.1 3.4 %collective-permute-done.25 = f32[224,128]{1,0:T(8,128)S(1)} collective-permute-done((f32[224,128]{1,0:T(8,128)S(1)}, f32[224,128]{1,0:T(8,128)S(1)}, u32[]{:S(2)}, u32[]{:S(2)}) %collective-permute-start.25) | collective-permute-done | bytes 114720 | tf_op jit(solution)/shard_map/ppermute | solution.py:29
  92.6 2.5 %collective-permute-start.26 = (f32[1280,128]{1,0:T(8,128)S(1)}, f32[1280,128]{1,0:T(8,128)S(1)}, u32[]{:S(2)}, u32[]{:S(2)}) collective-permute-start(f32[1280,128]{1,0:T(8,128)S(1)} %bitcast.184), channel_id=1, source_target_pairs={{0,1},{1,0},{2,3},{3,2},{4,5},{5,4},{6,7},{7,6},{8,9},{9,8},{10,11... | collective-permute-start | bytes 1966088 | tf_op jit(solution)/shard_map/ppermute | solution.py:29
  100.6 3.3 %collective-permute-done.27 = f32[320,128]{1,0:T(8,128)S(1)} collective-permute-done((f32[320,128]{1,0:T(8,128)S(1)}, f32[320,128]{1,0:T(8,128)S(1)}, u32[]{:S(2)}, u32[]{:S(2)}) %collective-permute-start.27) | collective-permute-done | bytes 163872 | tf_op jit(solution)/shard_map/ppermute | solution.py:29
  103.9 3.7 %collective-permute-done.28 = f32[320,128]{1,0:T(8,128)S(1)} collective-permute-done((f32[320,128]{1,0:T(8,128)S(1)}, f32[320,128]{1,0:T(8,128)S(1)}, u32[]{:S(2)}, u32[]{:S(2)}) %collective-permute-start.28) | collective-permute-done | bytes 163872 | tf_op jit(solution)/shard_map/ppermute | solution.py:29
  112.9 3.5 %collective-permute-done.34 = f32[48,128]{1,0:T(8,128)S(1)} collective-permute-done((f32[48,128]{1,0:T(8,128)S(1)}, f32[48,128]{1,0:T(8,128)S(1)}, u32[]{:S(2)}, u32[]{:S(2)}) %collective-permute-start.34) | collective-permute-done | bytes 24608 | tf_op jit(solution)/shard_map/ppermute | solution.py:29
  116.4 3.9 %collective-permute-done.35 = f32[48,128]{1,0:T(8,128)S(1)} collective-permute-done((f32[48,128]{1,0:T(8,128)S(1)}, f32[48,128]{1,0:T(8,128)S(1)}, u32[]{:S(2)}, u32[]{:S(2)}) %collective-permute-start.35) | collective-permute-done | bytes 24608 | tf_op jit(solution)/shard_map/ppermute | solution.py:29
  121.6 4.3 %collective-permute-start.36 = (f32[1408,128]{1,0:T(8,128)S(1)}, f32[1408,128]{1,0:T(8,128)S(1)}, u32[]{:S(2)}, u32[]{:S(2)}) collective-permute-start(f32[1408,128]{1,0:T(8,128)S(1)} %bitcast.183), channel_id=1, source_target_pairs={{0,1},{1,0},{2,3},{3,2},{4,5},{5,4},{6,7},{7,6},{8,9},{9,8},{10,11... | collective-permute-start | bytes 2162696 | tf_op jit(solution)/shard_map/ppermute | solution.py:29
  130.9 4.2 %collective-permute-done.37 = f32[352,128]{1,0:T(8,128)S(1)} collective-permute-done((f32[352,128]{1,0:T(8,128)S(1)}, f32[352,128]{1,0:T(8,128)S(1)}, u32[]{:S(2)}, u32[]{:S(2)}) %collective-permute-start.37) | collective-permute-done | bytes 180256 | tf_op jit(solution)/shard_map/ppermute | solution.py:29
  135.1 4.1 %collective-permute-done.38 = f32[352,128]{1,0:T(8,128)S(1)} collective-permute-done((f32[352,128]{1,0:T(8,128)S(1)}, f32[352,128]{1,0:T(8,128)S(1)}, u32[]{:S(2)}, u32[]{:S(2)}) %collective-permute-start.38) | collective-permute-done | bytes 180256 | tf_op jit(solution)/shard_map/ppermute | solution.py:29
  141.4 3.0 %collective-permute-start.41 = (f32[352,128]{1,0:T(8,128)S(1)}, f32[352,128]{1,0:T(8,128)S(1)}, u32[]{:S(2)}, u32[]{:S(2)}) collective-permute-start(f32[352,128]{1,0:T(8,128)S(1)} %bitcast.122), channel_id=1, source_target_pairs={{0,96},{1,25},{8,104},{9,1},{16,112},{17,9},{24,120},{25,17},{32,0... | collective-permute-start | bytes 540680 | tf_op jit(solution)/shard_map/ppermute | solution.py:29
  147.1 3.1 %collective-permute-done.40 = f32[352,128]{1,0:T(8,128)S(1)} collective-permute-done((f32[352,128]{1,0:T(8,128)S(1)}, f32[352,128]{1,0:T(8,128)S(1)}, u32[]{:S(2)}, u32[]{:S(2)}) %collective-permute-start.40) | collective-permute-done | bytes 180256 | tf_op jit(solution)/shard_map/ppermute | solution.py:29
  152.4 9.9 %collective-permute-done.45 = f32[1408,128]{1,0:T(8,128)S(1)} collective-permute-done((f32[1408,128]{1,0:T(8,128)S(1)}, f32[1408,128]{1,0:T(8,128)S(1)}, u32[]{:S(2)}, u32[]{:S(2)}) %collective-permute-start.45) | collective-permute-done | bytes 720928 | tf_op jit(solution)/shard_map/ppermute | solution.py:29
  162.3 4.9 %collective-permute-done.44 = f32[1408,128]{1,0:T(8,128)S(1)} collective-permute-done((f32[1408,128]{1,0:T(8,128)S(1)}, f32[1408,128]{1,0:T(8,128)S(1)}, u32[]{:S(2)}, u32[]{:S(2)}) %collective-permute-start.44) | collective-permute-done | bytes 720928 | tf_op jit(solution)/shard_map/ppermute | solution.py:29
  167.2 2.8 %collective-permute-done.43 = f32[1408,128]{1,0:T(8,128)S(1)} collective-permute-done((f32[1408,128]{1,0:T(8,128)S(1)}, f32[1408,128]{1,0:T(8,128)S(1)}, u32[]{:S(2)}, u32[]{:S(2)}) %collective-permute-start.43) | collective-permute-done | bytes 720928 | tf_op jit(solution)/shard_map/ppermute | solution.py:29
  170.0 2.6 %shard_map.71 = (f32[4,4,12,8,128]{4,3,2,1,0:T(8,128)S(1)}, f32[4,4,12,8,128]{4,3,2,1,0:T(8,128)S(1)}, f32[4,11,8,128]{3,2,1,0:T(8,128)S(1)}) custom-call(s32[912]{0:T(1024)S(1)} %concatenate.3.tab, f32[4,4,11,8,128]{4,3,2,1,0:T(8,128)S(1)} %pad_maximum_fusion.refs_0_, f32[4,4,11,8,128]{4,3,2,1,0:T(8,128)S(1)} %bitcast.128, ...), custom_call_target="tpu_custom_call" | custom-call | tf_op jit(solution)/shard_map/pallas_call | solution.py:121
  179.7 4.6 %collective-permute-done.47 = f32[384,128]{1,0:T(8,128)S(1)} collective-permute-done((f32[384,128]{1,0:T(8,128)S(1)}, f32[384,128]{1,0:T(8,128)S(1)}, u32[]{:S(2)}, u32[]{:S(2)}) %collective-permute-start.47) | collective-permute-done | bytes 196640 | tf_op jit(solution)/shard_map/ppermute | solution.py:29
  184.3 4.6 %collective-permute-done.48 = f32[384,128]{1,0:T(8,128)S(1)} collective-permute-done((f32[384,128]{1,0:T(8,128)S(1)}, f32[384,128]{1,0:T(8,128)S(1)}, u32[]{:S(2)}, u32[]{:S(2)}) %collective-permute-start.48) | collective-permute-done | bytes 196640 | tf_op jit(solution)/shard_map/ppermute | solution.py:29
  195.5 3.2 %collective-permute-done.51 = f32[256,128]{1,0:T(8,128)S(1)} collective-permute-done((f32[256,128]{1,0:T(8,128)S(1)}, f32[256,128]{1,0:T(8,128)S(1)}, u32[]{:S(2)}, u32[]{:S(2)}) %collective-permute-start.51) | collective-permute-done | bytes 131104 | tf_op jit(solution)/shard_map/ppermute | solution.py:29
  198.7 2.4 %collective-permute-done.52 = f32[256,128]{1,0:T(8,128)S(1)} collective-permute-done((f32[256,128]{1,0:T(8,128)S(1)}, f32[256,128]{1,0:T(8,128)S(1)}, u32[]{:S(2)}, u32[]{:S(2)}) %collective-permute-start.52) | collective-permute-done | bytes 131104 | tf_op jit(solution)/shard_map/ppermute | solution.py:29
  (117 shorter events, 83.6 us)
Async XLA Ops:
  3.8 9.4 %collective-permute-start.1 = (f32[256,128]{1,0:T(8,128)S(1)}, f32[256,128]{1,0:T(8,128)S(1)}, u32[]{:S(2)}, u32[]{:S(2)}) collective-permute-start(f32[256,128]{1,0:T(8,128)S(1)} %bitcast.203), channel_id=1, source_target_pairs={{0,4},{1,5},{2,6},{3,7},{4,0},{5,1},{6,2},{7,3},{8,12},{9,13},{10,... | collective-permute-start | bytes 393224 | tf_op jit(solution)/shard_map/ppermute | solution.py:29
  7.6 6.4 %collective-permute-start.2 = (f32[256,128]{1,0:T(8,128)S(1)}, f32[256,128]{1,0:T(8,128)S(1)}, u32[]{:S(2)}, u32[]{:S(2)}) collective-permute-start(f32[256,128]{1,0:T(8,128)S(1)} %bitcast.202), channel_id=1, source_target_pairs={{0,2},{1,7},{2,0},{3,5},{4,6},{5,3},{6,4},{7,1},{8,10},{9,15},{10,... | collective-permute-start | bytes 393224 | tf_op jit(solution)/shard_map/ppermute | solution.py:29
  8.0 6.4 %collective-permute-start.3 = (f32[256,128]{1,0:T(8,128)S(1)}, f32[256,128]{1,0:T(8,128)S(1)}, u32[]{:S(2)}, u32[]{:S(2)}) collective-permute-start(f32[256,128]{1,0:T(8,128)S(1)} %bitcast.201), channel_id=1, source_target_pairs={{0,6},{1,3},{2,4},{3,1},{4,2},{5,7},{6,0},{7,5},{8,14},{9,11},{10,... | collective-permute-start | bytes 393224 | tf_op jit(solution)/shard_map/ppermute | solution.py:29
  24.1 9.2 %collective-permute-start.9 = (f32[896,128]{1,0:T(8,128)S(1)}, f32[896,128]{1,0:T(8,128)S(1)}, u32[]{:S(2)}, u32[]{:S(2)}) collective-permute-start(f32[896,128]{1,0:T(8,128)S(1)} %bitcast.117), channel_id=1, source_target_pairs={{0,16},{1,65},{8,24},{9,73},{16,0},{17,81},{24,8},{25,89},{32,48},... | collective-permute-start | bytes 1376264 | tf_op jit(solution)/shard_map/ppermute | solution.py:29
  27.0 11.4 %collective-permute-start.8 = (f32[896,128]{1,0:T(8,128)S(1)}, f32[896,128]{1,0:T(8,128)S(1)}, u32[]{:S(2)}, u32[]{:S(2)}) collective-permute-start(f32[896,128]{1,0:T(8,128)S(1)} %bitcast.118), channel_id=1, source_target_pairs={{0,24},{1,97},{8,0},{9,105},{16,8},{17,113},{24,16},{25,121},{32,5... | collective-permute-start | bytes 1376264 | tf_op jit(solution)/shard_map/ppermute | solution.py:29
  27.8 10.6 %collective-permute-start.7 = (f32[896,128]{1,0:T(8,128)S(1)}, f32[896,128]{1,0:T(8,128)S(1)}, u32[]{:S(2)}, u32[]{:S(2)}) collective-permute-start(f32[896,128]{1,0:T(8,128)S(1)} %bitcast.119), channel_id=1, source_target_pairs={{0,8},{1,33},{8,16},{9,41},{16,24},{17,49},{24,0},{25,57},{32,40},... | collective-permute-start | bytes 1376264 | tf_op jit(solution)/shard_map/ppermute | solution.py:29
  45.8 6.3 %collective-permute-start.11 = (f32[256,128]{1,0:T(8,128)S(1)}, f32[256,128]{1,0:T(8,128)S(1)}, u32[]{:S(2)}, u32[]{:S(2)}) collective-permute-start(f32[256,128]{1,0:T(8,128)S(1)} %bitcast.210), channel_id=1, source_target_pairs={{0,4},{1,5},{2,6},{3,7},{4,0},{5,1},{6,2},{7,3},{8,12},{9,13},{10,... | collective-permute-start | bytes 393224 | tf_op jit(solution)/shard_map/ppermute | solution.py:29
  47.6 6.9 %collective-permute-start.12 = (f32[256,128]{1,0:T(8,128)S(1)}, f32[256,128]{1,0:T(8,128)S(1)}, u32[]{:S(2)}, u32[]{:S(2)}) collective-permute-start(f32[256,128]{1,0:T(8,128)S(1)} %bitcast.208), channel_id=1, source_target_pairs={{0,2},{1,7},{2,0},{3,5},{4,6},{5,3},{6,4},{7,1},{8,10},{9,15},{10,... | collective-permute-start | bytes 393224 | tf_op jit(solution)/shard_map/ppermute | solution.py:29
  54.9 8.3 %collective-permute-start.15 = (f32[256,128]{1,0:T(8,128)S(1)}, f32[256,128]{1,0:T(8,128)S(1)}, u32[]{:S(2)}, u32[]{:S(2)}) collective-permute-start(f32[256,128]{1,0:T(8,128)S(1)} %bitcast.136), channel_id=1, source_target_pairs={{0,16},{8,0},{32,8},{40,32},{64,40},{72,64},{96,72},{104,96},{120,... | collective-permute-start | bytes 393224 | tf_op jit(solution)/shard_map/ppermute | solution.py:29
  57.5 9.5 %collective-permute-start.14 = (f32[256,128]{1,0:T(8,128)S(1)}, f32[256,128]{1,0:T(8,128)S(1)}, u32[]{:S(2)}, u32[]{:S(2)}) collective-permute-start(f32[256,128]{1,0:T(8,128)S(1)} %bitcast.137), channel_id=1, source_target_pairs={{0,8},{8,32},{32,40},{40,64},{64,72},{72,96},{96,104},{104,120},{1... | collective-permute-start | bytes 393224 | tf_op jit(solution)/shard_map/ppermute | solution.py:29
  71.6 6.6 %collective-permute-start.19 = (f32[288,128]{1,0:T(8,128)S(1)}, f32[288,128]{1,0:T(8,128)S(1)}, u32[]{:S(2)}, u32[]{:S(2)}) collective-permute-start(f32[288,128]{1,0:T(8,128)S(1)} %bitcast.200), channel_id=1, source_target_pairs={{0,4},{1,5},{2,6},{3,7},{4,0},{5,1},{6,2},{7,3},{8,12},{9,13},{10,... | collective-permute-start | bytes 442376 | tf_op jit(solution)/shard_map/ppermute | solution.py:29
  73.9 7.8 %collective-permute-start.20 = (f32[288,128]{1,0:T(8,128)S(1)}, f32[288,128]{1,0:T(8,128)S(1)}, u32[]{:S(2)}, u32[]{:S(2)}) collective-permute-start(f32[288,128]{1,0:T(8,128)S(1)} %bitcast.199), channel_id=1, source_target_pairs={{0,2},{1,7},{2,0},{3,5},{4,6},{5,3},{6,4},{7,1},{8,10},{9,15},{10,... | collective-permute-start | bytes 442376 | tf_op jit(solution)/shard_map/ppermute | solution.py:29
  75.4 6.7 %collective-permute-start.21 = (f32[288,128]{1,0:T(8,128)S(1)}, f32[288,128]{1,0:T(8,128)S(1)}, u32[]{:S(2)}, u32[]{:S(2)}) collective-permute-start(f32[288,128]{1,0:T(8,128)S(1)} %bitcast.198), channel_id=1, source_target_pairs={{0,6},{1,3},{2,4},{3,1},{4,2},{5,7},{6,0},{7,5},{8,14},{9,11},{10,... | collective-permute-start | bytes 442376 | tf_op jit(solution)/shard_map/ppermute | solution.py:29
  82.1 7.0 %collective-permute-start.23 = (f32[288,128]{1,0:T(8,128)S(1)}, f32[288,128]{1,0:T(8,128)S(1)}, u32[]{:S(2)}, u32[]{:S(2)}) collective-permute-start(f32[288,128]{1,0:T(8,128)S(1)} %bitcast.133), channel_id=1, source_target_pairs={{0,16},{8,0},{32,8},{40,32},{64,40},{72,64},{96,72},{104,96},{120,... | collective-permute-start | bytes 442376 | tf_op jit(solution)/shard_map/ppermute | solution.py:29
  82.2 9.2 %collective-permute-start.22 = (f32[288,128]{1,0:T(8,128)S(1)}, f32[288,128]{1,0:T(8,128)S(1)}, u32[]{:S(2)}, u32[]{:S(2)}) collective-permute-start(f32[288,128]{1,0:T(8,128)S(1)} %bitcast.134), channel_id=1, source_target_pairs={{0,8},{8,32},{32,40},{40,64},{64,72},{72,96},{96,104},{104,120},{1... | collective-permute-start | bytes 442376 | tf_op jit(solution)/shard_map/ppermute | solution.py:29
  96.9 7.0 %collective-permute-start.27 = (f32[320,128]{1,0:T(8,128)S(1)}, f32[320,128]{1,0:T(8,128)S(1)}, u32[]{:S(2)}, u32[]{:S(2)}) collective-permute-start(f32[320,128]{1,0:T(8,128)S(1)} %bitcast.197), channel_id=1, source_target_pairs={{0,4},{1,5},{2,6},{3,7},{4,0},{5,1},{6,2},{7,3},{8,12},{9,13},{10,... | collective-permute-start | bytes 491528 | tf_op jit(solution)/shard_map/ppermute | solution.py:29
  99.1 8.5 %collective-permute-start.28 = (f32[320,128]{1,0:T(8,128)S(1)}, f32[320,128]{1,0:T(8,128)S(1)}, u32[]{:S(2)}, u32[]{:S(2)}) collective-permute-start(f32[320,128]{1,0:T(8,128)S(1)} %bitcast.196), channel_id=1, source_target_pairs={{0,2},{1,7},{2,0},{3,5},{4,6},{5,3},{6,4},{7,1},{8,10},{9,15},{10,... | collective-permute-start | bytes 491528 | tf_op jit(solution)/shard_map/ppermute | solution.py:29
  100.6 7.4 %collective-permute-start.29 = (f32[320,128]{1,0:T(8,128)S(1)}, f32[320,128]{1,0:T(8,128)S(1)}, u32[]{:S(2)}, u32[]{:S(2)}) collective-permute-start(f32[320,128]{1,0:T(8,128)S(1)} %bitcast.195), channel_id=1, source_target_pairs={{0,6},{1,3},{2,4},{3,1},{4,2},{5,7},{6,0},{7,5},{8,14},{9,11},{10,... | collective-permute-start | bytes 491528 | tf_op jit(solution)/shard_map/ppermute | solution.py:29
  108.1 12.2 %collective-permute-start.31 = (f32[320,128]{1,0:T(8,128)S(1)}, f32[320,128]{1,0:T(8,128)S(1)}, u32[]{:S(2)}, u32[]{:S(2)}) collective-permute-start(f32[320,128]{1,0:T(8,128)S(1)} %bitcast.130), channel_id=1, source_target_pairs={{0,16},{8,0},{32,8},{40,32},{64,40},{72,64},{96,72},{104,96},{120,... | collective-permute-start | bytes 491528 | tf_op jit(solution)/shard_map/ppermute | solution.py:29
  108.3 12.0 %collective-permute-start.30 = (f32[320,128]{1,0:T(8,128)S(1)}, f32[320,128]{1,0:T(8,128)S(1)}, u32[]{:S(2)}, u32[]{:S(2)}) collective-permute-start(f32[320,128]{1,0:T(8,128)S(1)} %bitcast.131), channel_id=1, source_target_pairs={{0,8},{8,32},{32,40},{40,64},{64,72},{72,96},{96,104},{104,120},{1... | collective-permute-start | bytes 491528 | tf_op jit(solution)/shard_map/ppermute | solution.py:29
  109.6 10.7 %collective-permute-start.33 = (f32[256,128]{1,0:T(8,128)S(1)}, f32[256,128]{1,0:T(8,128)S(1)}, u32[]{:S(2)}, u32[]{:S(2)}) collective-permute-start(f32[256,128]{1,0:T(8,128)S(1)} %bitcast.205), channel_id=1, source_target_pairs={{0,24},{8,16},{32,0},{40,8},{64,32},{72,40},{96,64},{104,72},{120,... | collective-permute-start | bytes 393224 | tf_op jit(solution)/shard_map/ppermute | solution.py:29
  109.6 10.7 %collective-permute-start.32 = (f32[256,128]{1,0:T(8,128)S(1)}, f32[256,128]{1,0:T(8,128)S(1)}, u32[]{:S(2)}, u32[]{:S(2)}) collective-permute-start(f32[256,128]{1,0:T(8,128)S(1)} %bitcast.204), channel_id=1, source_target_pairs={{0,32},{8,40},{32,64},{40,72},{64,96},{72,104},{96,120},{104,112},... | collective-permute-start | bytes 393224 | tf_op jit(solution)/shard_map/ppermute | solution.py:29
  127.7 7.4 %collective-permute-start.37 = (f32[352,128]{1,0:T(8,128)S(1)}, f32[352,128]{1,0:T(8,128)S(1)}, u32[]{:S(2)}, u32[]{:S(2)}) collective-permute-start(f32[352,128]{1,0:T(8,128)S(1)} %bitcast.194), channel_id=1, source_target_pairs={{0,4},{1,5},{2,6},{3,7},{4,0},{5,1},{6,2},{7,3},{8,12},{9,13},{10,... | collective-permute-start | bytes 540680 | tf_op jit(solution)/shard_map/ppermute | solution.py:29
  129.4 9.8 %collective-permute-start.38 = (f32[352,128]{1,0:T(8,128)S(1)}, f32[352,128]{1,0:T(8,128)S(1)}, u32[]{:S(2)}, u32[]{:S(2)}) collective-permute-start(f32[352,128]{1,0:T(8,128)S(1)} %bitcast.193), channel_id=1, source_target_pairs={{0,2},{1,7},{2,0},{3,5},{4,6},{5,3},{6,4},{7,1},{8,10},{9,15},{10,... | collective-permute-start | bytes 540680 | tf_op jit(solution)/shard_map/ppermute | solution.py:29
  130.9 8.3 %collective-permute-start.39 = (f32[352,128]{1,0:T(8,128)S(1)}, f32[352,128]{1,0:T(8,128)S(1)}, u32[]{:S(2)}, u32[]{:S(2)}) collective-permute-start(f32[352,128]{1,0:T(8,128)S(1)} %bitcast.192), channel_id=1, source_target_pairs={{0,6},{1,3},{2,4},{3,1},{4,2},{5,7},{6,0},{7,5},{8,14},{9,11},{10,... | collective-permute-start | bytes 540680 | tf_op jit(solution)/shard_map/ppermute | solution.py:29
  150.3 12.1 %collective-permute-start.45 = (f32[1408,128]{1,0:T(8,128)S(1)}, f32[1408,128]{1,0:T(8,128)S(1)}, u32[]{:S(2)}, u32[]{:S(2)}) collective-permute-start(f32[1408,128]{1,0:T(8,128)S(1)} %bitcast.114), channel_id=1, source_target_pairs={{0,16},{1,65},{8,24},{9,73},{16,0},{17,81},{24,8},{25,89},{32,48},... | collective-permute-start | bytes 2162696 | tf_op jit(solution)/shard_map/ppermute | solution.py:29
  150.9 16.3 %collective-permute-start.44 = (f32[1408,128]{1,0:T(8,128)S(1)}, f32[1408,128]{1,0:T(8,128)S(1)}, u32[]{:S(2)}, u32[]{:S(2)}) collective-permute-start(f32[1408,128]{1,0:T(8,128)S(1)} %bitcast.115), channel_id=1, source_target_pairs={{0,24},{1,97},{8,0},{9,105},{16,8},{17,113},{24,16},{25,121},{32,5... | collective-permute-start | bytes 2162696 | tf_op jit(solution)/shard_map/ppermute | solution.py:29
  151.5 18.5 %collective-permute-start.43 = (f32[1408,128]{1,0:T(8,128)S(1)}, f32[1408,128]{1,0:T(8,128)S(1)}, u32[]{:S(2)}, u32[]{:S(2)}) collective-permute-start(f32[1408,128]{1,0:T(8,128)S(1)} %bitcast.116), channel_id=1, source_target_pairs={{0,8},{1,33},{8,16},{9,41},{16,24},{17,49},{24,0},{25,57},{32,40},... | collective-permute-start | bytes 2162696 | tf_op jit(solution)/shard_map/ppermute | solution.py:29
  176.5 7.7 %collective-permute-start.47 = (f32[384,128]{1,0:T(8,128)S(1)}, f32[384,128]{1,0:T(8,128)S(1)}, u32[]{:S(2)}, u32[]{:S(2)}) collective-permute-start(f32[384,128]{1,0:T(8,128)S(1)} %bitcast.191), channel_id=1, source_target_pairs={{0,4},{1,5},{2,6},{3,7},{4,0},{5,1},{6,2},{7,3},{8,12},{9,13},{10,... | collective-permute-start | bytes 589832 | tf_op jit(solution)/shard_map/ppermute | solution.py:29
  178.2 10.8 %collective-permute-start.48 = (f32[384,128]{1,0:T(8,128)S(1)}, f32[384,128]{1,0:T(8,128)S(1)}, u32[]{:S(2)}, u32[]{:S(2)}) collective-permute-start(f32[384,128]{1,0:T(8,128)S(1)} %bitcast.190), channel_id=1, source_target_pairs={{0,2},{1,7},{2,0},{3,5},{4,6},{5,3},{6,4},{7,1},{8,10},{9,15},{10,... | collective-permute-start | bytes 589832 | tf_op jit(solution)/shard_map/ppermute | solution.py:29
  179.7 9.3 %collective-permute-start.49 = (f32[384,128]{1,0:T(8,128)S(1)}, f32[384,128]{1,0:T(8,128)S(1)}, u32[]{:S(2)}, u32[]{:S(2)}) collective-permute-start(f32[384,128]{1,0:T(8,128)S(1)} %bitcast.189), channel_id=1, source_target_pairs={{0,6},{1,3},{2,4},{3,1},{4,2},{5,7},{6,0},{7,5},{8,14},{9,11},{10,... | collective-permute-start | bytes 589832 | tf_op jit(solution)/shard_map/ppermute | solution.py:29
  194.0 7.1 %collective-permute-start.52 = (f32[256,128]{1,0:T(8,128)S(1)}, f32[256,128]{1,0:T(8,128)S(1)}, u32[]{:S(2)}, u32[]{:S(2)}) collective-permute-start(f32[256,128]{1,0:T(8,128)S(1)} %bitcast.209), channel_id=1, source_target_pairs={{0,2},{1,7},{2,0},{3,5},{4,6},{5,3},{6,4},{7,1},{8,10},{9,15},{10,... | collective-permute-start | bytes 393224 | tf_op jit(solution)/shard_map/ppermute | solution.py:29
  (27 other events, 109.9 us)

commit v10 on v9

--- a/solution.py
+++ b/solution.py
@@ -31,6 +31,14 @@
 
 def ring_shift(value, k):
     return permute(value, "row", [(RING[p], RING[(p + k) % 16]) for p in range(16)])
+
+
+def outward(value, d):
+    pairs = []
+    for p in range(16):
+        pairs.append((RING[p] * 2, RING[(p + d) % 16] * 2))
+        pairs.append((RING[p] * 2 + 1, RING[(p - d) % 16] * 2 + 1))
+    return permute(value, ("row", "layer"), pairs)
 
 
 def line_shift(value, k, swapped):
@@ -219,11 +227,10 @@
 
 def step_body(strips, w, own_ref, oth_ref, hi_ref, lo_ref, p_ref):
     left, count = geometry(w)
-    nk = 4 + 2 * w
-    for a in range(0, nk, 2):
+    for a in range(0, len(strips), 2):
         pair = []
-        for b in (a, a + 1):
-            tiles, first = strips(b)
+        for strip in strips[a : a + 2]:
+            b, tiles, first = strip()
             pair.append(shifted(tiles, left - 2 * w + b + 2 * first, count))
         store_split(hi_ref, lo_ref, a * 8, pair[0], pair[1])
     p_ref[...] = product(hi_ref, lo_ref, left * 64, 256).reshape(32, 8, count * 128)
@@ -237,38 +244,61 @@
     w = BAND
     base = tab[PLACE + 5] * 4 + 64 - w
 
-    def strips(b):
+    def strip_of(b):
         sk = tab[INV + ((base + b) & 63)]
         u, v, e = seat(tab, sk >> 2, sk & 3)
         strip = g_ref[u, v, e]
         if w <= b < w + 4:
             cur_ref[b - w] = strip
-        return [strip[t] for t in range(w + 1)], 0
-
+        return b, [strip[t] for t in range(w + 1)], 0
+
+    strips = [lambda b=b: strip_of(b) for b in range(4 + 2 * w)]
     step_body(strips, w, own_ref, oth_ref, hi_ref, lo_ref, p_ref)
 
 
 def step_kernel(w, pieces, *refs):
-    n = 1 + len(pieces)
+    far = outermost(w) is not None
+    n = 1 + len(pieces) + far
     ins, (own_ref, oth_ref, hi_ref, lo_ref, p_ref) = refs[:n], refs[n:]
 
-    def strips(b):
+    def strip_of(b):
         off = b - w
         if 0 <= off < 4:
-            return [ins[0][off, t] for t in range(w + 1)], 0
+            return b, [ins[0][off, t] for t in range(w + 1)], 0
         d = (-off + 3) // 4 if off < 0 else -(off // 4)
         at = [piece[0] for piece in pieces].index(d)
         _, (lo, hi, first, last) = pieces[at]
         row = off + 4 * d - lo
-        return [ins[1 + at][row, t] for t in range(last - first)], first
-
+        return b, [ins[1 + at][row, t] for t in range(last - first)], first
+
+    def far_strip(b, core, slab):
+        mine = jnp.where(lax.axis_index("layer") == core, 1.0, 0.0)
+        first = 0 if core else w + 1 - far_tiles(w)
+        return b, [ins[-1][slab, t] * mine for t in range(far_tiles(w))], first
+
+    last = 4 + 2 * w - 1
+    strips = [lambda b=b: strip_of(b) for b in range(far, last + 1 - far)]
+    if far:
+        for slab in (0, 1):
+            strips.append(lambda slab=slab: far_strip(0, 0, slab))
+            strips.append(lambda slab=slab: far_strip(last, 1, slab))
     step_body(strips, w, own_ref, oth_ref, hi_ref, lo_ref, p_ref)
+
+
+def far_tiles(w):
+    return w + 1 - 2 * (outermost(w) - 1)
+
+
+def outermost(w):
+    return (w + 3) // 4 if w % 4 == 1 else None
 
 
 def halo_pieces(w):
     out = []
     for d in range(1, (w + 3) // 4 + 1):
         n = min(4, w - 4 * (d - 1))
+        if outermost(w) == d:
+            break
         out.append((d, (4 - n, 4, 2 * (d - 1), w + 1)))
         out.append((-d, (0, n, 0, w + 1 - 2 * (d - 1))))
     return out
@@ -336,7 +366,7 @@
                 ref[e, m] = jnp.where(low, sides[0], sides[1]).astype(F32)
 
 
-def close_kernel(step, cuts, p0, p1, p2, p3, cur_ref, keep_ref, coef_ref, *refs):
+def close_kernel(step, cuts, far, p0, p1, p2, p3, cur_ref, keep_ref, coef_ref, *refs):
     w = BAND + step
     low = low_half()
     for e in range(4):
@@ -351,6 +381,14 @@
             for ref, (lo, hi, first, last) in zip(refs, cuts):
                 if lo <= e < hi and first <= m < last:
                     ref[e - lo, m - first] = value
+            if far and e == 3 and m >= w + 2 - far:
+                refs[-1][0, m - (w + 2 - far)] = value
+            if far and e == 0 and m < far:
+                refs[-1][1, m] = value
+    if far:
+        own_ref, oth_ref, far_ref = refs[-3:]
+        own_ref[...] = far_ref[lax.axis_index("layer")]
+        oth_ref[...] = far_ref[1 - lax.axis_index("layer")]
 
 
 def finish_kernel(tab, p0, p1, p2, p3, cur_ref, keep_ref, coef_ref, own_ref, oth_ref, y_ref):
@@ -438,7 +476,7 @@
     for step in range(STEPS - 1):
         w = BAND + step
         left, count = geometry(w)
-        depth = (4 + 2 * w) * 8
+        depth = (4 + 2 * w + (2 if step and outermost(w) else 0)) * 8
         part = (4, 4, w + 2, 8, 128)
         scratch = [
             pltpu.VMEM((depth, count * 128), BF16),
@@ -459,11 +497,17 @@
         for _, cut in pieces:
             if cut not in cuts:
                 cuts.append(cut)
-        kernel = lambda *refs, step=step, cuts=cuts: close_kernel(step, cuts, *refs)
+        far = far_tiles(w + 1) if pieces and outermost(w + 1) else 0
+        kernel = lambda *refs, step=step, cuts=cuts, far=far: close_kernel(step, cuts, far, *refs)
         shapes = [(hi - lo, last - first, 8, 128) for lo, hi, first, last in cuts]
-        sent = call(kernel, shapes, parts + [cur, keep[step + 1], coef])
+        scratch = [pltpu.VMEM((2, far, 8, 128), F32)] if far else []
+        shapes += [(far, 8, 128)] * 2 if far else []
+        sent = call(kernel, shapes, parts + [cur, keep[step + 1], coef], scratch)
         cur = sent[0]
         around = [ring_shift(sent[cuts.index(cut)], d) for d, cut in pieces]
+        if far:
+            both = jnp.stack([sent[-2], core_swap(sent[-1])])
+            around.append(outward(both, outermost(w + 1)))
         cur, *around = lax.optimization_barrier((cur, *around))
     gathered = gather_rows(cur)
     w = BAND + STEPS - 1

time: 202 us -> 199 us (0.985)
  starting transfers between devices: 69 us -> 64.2 us
    ppermute x54, starting transfers between devices: 69 us -> 64.2 us  [permute(): return lax.ppermute(flat, axes, pairs).reshape(value.shape)]
  transfers between devices with their start and end apart: 54 -> 54, of which waited for: 44 -> 45; matrix products, arithmetic and copies ran while one was open for 1% -> 1% of each run, Pallas kernels for 1% -> 1%
where the time goes in v10:
time: 199 us
  waiting for transfers between devices  116 us (58%)
  starting transfers between devices  64.2 us (32%)
  Pallas kernels  13.7 us (7%)
  local copies, waits for them, and re-layouts  3.75 us (2%)
    ppermute x54, waiting for transfers between devices, permute(): return lax.ppermute(flat, axes, pairs).reshape(value.shape)  116 us
    ppermute x54, starting transfers between devices, permute(): return lax.ppermute(flat, axes, pairs).reshape(value.shape)  64.2 us
    pallas_call x21, Pallas kernels, call(): pl.pallas_call(kernel, out_shape=[jax.ShapeDtypeStruct(o, F32) for o in o...  13.7 us
  transfers between devices with their start and end apart: 54, of which 45 were waited for; matrix products, arithmetic and copies ran while one was open for 1% of the time, Pallas kernels for 1%

profile of v10, /device:TPU:1, one launch (start us, length us, event | category | flops | bytes accessed | tf_op | source)
XLA Modules:
  0.0 199.0 jit_solution(13705700113124151121)
XLA Ops:
  3.8 3.8 %collective-permute-start.1 = (f32[256,128]{1,0:T(8,128)S(1)}, f32[256,128]{1,0:T(8,128)S(1)}, u32[]{:S(2)}, u32[]{:S(2)}) collective-permute-start(f32[256,128]{1,0:T(8,128)S(1)} %bitcast.204), channel_id=1, source_target_pairs={{0,4},{1,5},{2,6},{3,7},{4,0},{5,1},{6,2},{7,3},{8,12},{9,13},{10,... | collective-permute-start | bytes 393224 | tf_op jit(solution)/shard_map/ppermute | solution.py:29
  15.5 3.0 %collective-permute-start.6 = (f32[224,128]{1,0:T(8,128)S(1)}, f32[224,128]{1,0:T(8,128)S(1)}, u32[]{:S(2)}, u32[]{:S(2)}) collective-permute-start(f32[224,128]{1,0:T(8,128)S(1)} %bitcast.142), channel_id=1, source_target_pairs={{0,64},{1,17},{8,72},{9,25},{16,80},{17,1},{24,88},{25,9},{32,96},... | collective-permute-start | bytes 344072 | tf_op jit(solution)/shard_map/ppermute | solution.py:29
  24.1 2.8 %collective-permute-start.9 = (f32[896,128]{1,0:T(8,128)S(1)}, f32[896,128]{1,0:T(8,128)S(1)}, u32[]{:S(2)}, u32[]{:S(2)}) collective-permute-start(f32[896,128]{1,0:T(8,128)S(1)} %bitcast.118), channel_id=1, source_target_pairs={{0,16},{1,65},{8,24},{9,73},{16,0},{17,81},{24,8},{25,89},{32,48},... | collective-permute-start | bytes 1376264 | tf_op jit(solution)/shard_map/ppermute | solution.py:29
  28.4 4.9 %collective-permute-done.9 = f32[896,128]{1,0:T(8,128)S(1)} collective-permute-done((f32[896,128]{1,0:T(8,128)S(1)}, f32[896,128]{1,0:T(8,128)S(1)}, u32[]{:S(2)}, u32[]{:S(2)}) %collective-permute-start.9) | collective-permute-done | bytes 458784 | tf_op jit(solution)/shard_map/ppermute | solution.py:29
  33.4 5.0 %collective-permute-done.8 = f32[896,128]{1,0:T(8,128)S(1)} collective-permute-done((f32[896,128]{1,0:T(8,128)S(1)}, f32[896,128]{1,0:T(8,128)S(1)}, u32[]{:S(2)}, u32[]{:S(2)}) %collective-permute-start.8) | collective-permute-done | bytes 458784 | tf_op jit(solution)/shard_map/ppermute | solution.py:29
  40.2 4.0 %collective-permute-start.10 = (f32[1024,128]{1,0:T(8,128)S(1)}, f32[1024,128]{1,0:T(8,128)S(1)}, u32[]{:S(2)}, u32[]{:S(2)}) collective-permute-start(f32[1024,128]{1,0:T(8,128)S(1)} %bitcast.187), channel_id=1, source_target_pairs={{0,1},{1,0},{2,3},{3,2},{4,5},{5,4},{6,7},{7,6},{8,9},{9,8},{10,11... | collective-permute-start | bytes 1572872 | tf_op jit(solution)/shard_map/ppermute | solution.py:29
  49.0 3.1 %collective-permute-done.11 = f32[256,128]{1,0:T(8,128)S(1)} collective-permute-done((f32[256,128]{1,0:T(8,128)S(1)}, f32[256,128]{1,0:T(8,128)S(1)}, u32[]{:S(2)}, u32[]{:S(2)}) %collective-permute-start.11) | collective-permute-done | bytes 131104 | tf_op jit(solution)/shard_map/ppermute | solution.py:29
  52.1 2.4 %collective-permute-done.12 = f32[256,128]{1,0:T(8,128)S(1)} collective-permute-done((f32[256,128]{1,0:T(8,128)S(1)}, f32[256,128]{1,0:T(8,128)S(1)}, u32[]{:S(2)}, u32[]{:S(2)}) %collective-permute-start.12) | collective-permute-done | bytes 131104 | tf_op jit(solution)/shard_map/ppermute | solution.py:29
  54.9 2.6 %collective-permute-start.15 = (f32[256,128]{1,0:T(8,128)S(1)}, f32[256,128]{1,0:T(8,128)S(1)}, u32[]{:S(2)}, u32[]{:S(2)}) collective-permute-start(f32[256,128]{1,0:T(8,128)S(1)} %bitcast.137), channel_id=1, source_target_pairs={{0,16},{8,0},{32,8},{40,32},{64,40},{72,64},{96,72},{104,96},{120,... | collective-permute-start | bytes 393224 | tf_op jit(solution)/shard_map/ppermute | solution.py:29
  59.0 2.5 %collective-permute-done.17 = f32[144,128]{1,0:T(8,128)S(1)} collective-permute-done((f32[144,128]{1,0:T(8,128)S(1)}, f32[144,128]{1,0:T(8,128)S(1)}, u32[]{:S(2)}, u32[]{:S(2)}) %collective-permute-start.17) | collective-permute-done | bytes 73760 | tf_op jit(solution)/shard_map/ppermute | solution.py:29
  63.2 3.8 %collective-permute-done.14 = f32[256,128]{1,0:T(8,128)S(1)} collective-permute-done((f32[256,128]{1,0:T(8,128)S(1)}, f32[256,128]{1,0:T(8,128)S(1)}, u32[]{:S(2)}, u32[]{:S(2)}) %collective-permute-start.14) | collective-permute-done | bytes 131104 | tf_op jit(solution)/shard_map/ppermute | solution.py:29
  75.4 2.9 %collective-permute-done.19 = f32[288,128]{1,0:T(8,128)S(1)} collective-permute-done((f32[288,128]{1,0:T(8,128)S(1)}, f32[288,128]{1,0:T(8,128)S(1)}, u32[]{:S(2)}, u32[]{:S(2)}) %collective-permute-start.19) | collective-permute-done | bytes 147488 | tf_op jit(solution)/shard_map/ppermute | solution.py:29
  78.3 3.4 %collective-permute-done.20 = f32[288,128]{1,0:T(8,128)S(1)} collective-permute-done((f32[288,128]{1,0:T(8,128)S(1)}, f32[288,128]{1,0:T(8,128)S(1)}, u32[]{:S(2)}, u32[]{:S(2)}) %collective-permute-start.20) | collective-permute-done | bytes 147488 | tf_op jit(solution)/shard_map/ppermute | solution.py:29
  85.1 3.4 %collective-permute-done.25 = f32[224,128]{1,0:T(8,128)S(1)} collective-permute-done((f32[224,128]{1,0:T(8,128)S(1)}, f32[224,128]{1,0:T(8,128)S(1)}, u32[]{:S(2)}, u32[]{:S(2)}) %collective-permute-start.25) | collective-permute-done | bytes 114720 | tf_op jit(solution)/shard_map/ppermute | solution.py:29
  92.6 2.5 %collective-permute-start.26 = (f32[1280,128]{1,0:T(8,128)S(1)}, f32[1280,128]{1,0:T(8,128)S(1)}, u32[]{:S(2)}, u32[]{:S(2)}) collective-permute-start(f32[1280,128]{1,0:T(8,128)S(1)} %bitcast.185), channel_id=1, source_target_pairs={{0,1},{1,0},{2,3},{3,2},{4,5},{5,4},{6,7},{7,6},{8,9},{9,8},{10,11... | collective-permute-start | bytes 1966088 | tf_op jit(solution)/shard_map/ppermute | solution.py:29
  100.6 3.3 %collective-permute-done.27 = f32[320,128]{1,0:T(8,128)S(1)} collective-permute-done((f32[320,128]{1,0:T(8,128)S(1)}, f32[320,128]{1,0:T(8,128)S(1)}, u32[]{:S(2)}, u32[]{:S(2)}) %collective-permute-start.27) | collective-permute-done | bytes 163872 | tf_op jit(solution)/shard_map/ppermute | solution.py:29
  103.9 3.7 %collective-permute-done.28 = f32[320,128]{1,0:T(8,128)S(1)} collective-permute-done((f32[320,128]{1,0:T(8,128)S(1)}, f32[320,128]{1,0:T(8,128)S(1)}, u32[]{:S(2)}, u32[]{:S(2)}) %collective-permute-start.28) | collective-permute-done | bytes 163872 | tf_op jit(solution)/shard_map/ppermute | solution.py:29
  113.8 4.1 %collective-permute-done.35 = f32[96,128]{1,0:T(8,128)S(1)} collective-permute-done((f32[96,128]{1,0:T(8,128)S(1)}, f32[96,128]{1,0:T(8,128)S(1)}, u32[]{:S(2)}, u32[]{:S(2)}) %collective-permute-start.35) | collective-permute-done | bytes 49184 | tf_op jit(solution)/shard_map/ppermute | solution.py:29
  118.9 3.3 %collective-permute-done.30 = f32[320,128]{1,0:T(8,128)S(1)} collective-permute-done((f32[320,128]{1,0:T(8,128)S(1)}, f32[320,128]{1,0:T(8,128)S(1)}, u32[]{:S(2)}, u32[]{:S(2)}) %collective-permute-start.30) | collective-permute-done | bytes 163872 | tf_op jit(solution)/shard_map/ppermute | solution.py:29
  129.5 4.2 %collective-permute-done.37 = f32[352,128]{1,0:T(8,128)S(1)} collective-permute-done((f32[352,128]{1,0:T(8,128)S(1)}, f32[352,128]{1,0:T(8,128)S(1)}, u32[]{:S(2)}, u32[]{:S(2)}) %collective-permute-start.37) | collective-permute-done | bytes 180256 | tf_op jit(solution)/shard_map/ppermute | solution.py:29
  133.8 4.1 %collective-permute-done.38 = f32[352,128]{1,0:T(8,128)S(1)} collective-permute-done((f32[352,128]{1,0:T(8,128)S(1)}, f32[352,128]{1,0:T(8,128)S(1)}, u32[]{:S(2)}, u32[]{:S(2)}) %collective-permute-start.38) | collective-permute-done | bytes 180256 | tf_op jit(solution)/shard_map/ppermute | solution.py:29
  138.0 3.5 %collective-permute-start.41 = (f32[352,128]{1,0:T(8,128)S(1)}, f32[352,128]{1,0:T(8,128)S(1)}, u32[]{:S(2)}, u32[]{:S(2)}) collective-permute-start(f32[352,128]{1,0:T(8,128)S(1)} %bitcast.123), channel_id=1, source_target_pairs={{0,96},{1,25},{8,104},{9,1},{16,112},{17,9},{24,120},{25,17},{32,0... | collective-permute-start | bytes 540680 | tf_op jit(solution)/shard_map/ppermute | solution.py:29
  141.6 2.6 %collective-permute-done.42 = f32[352,128]{1,0:T(8,128)S(1)} collective-permute-done((f32[352,128]{1,0:T(8,128)S(1)}, f32[352,128]{1,0:T(8,128)S(1)}, u32[]{:S(2)}, u32[]{:S(2)}) %collective-permute-start.42) | collective-permute-done | bytes 180256 | tf_op jit(solution)/shard_map/ppermute | solution.py:29
  144.3 3.1 %collective-permute-done.40 = f32[352,128]{1,0:T(8,128)S(1)} collective-permute-done((f32[352,128]{1,0:T(8,128)S(1)}, f32[352,128]{1,0:T(8,128)S(1)}, u32[]{:S(2)}, u32[]{:S(2)}) %collective-permute-start.40) | collective-permute-done | bytes 180256 | tf_op jit(solution)/shard_map/ppermute | solution.py:29
  149.1 10.4 %collective-permute-done.45 = f32[1408,128]{1,0:T(8,128)S(1)} collective-permute-done((f32[1408,128]{1,0:T(8,128)S(1)}, f32[1408,128]{1,0:T(8,128)S(1)}, u32[]{:S(2)}, u32[]{:S(2)}) %collective-permute-start.45) | collective-permute-done | bytes 720928 | tf_op jit(solution)/shard_map/ppermute | solution.py:29
  159.5 3.3 %collective-permute-done.44 = f32[1408,128]{1,0:T(8,128)S(1)} collective-permute-done((f32[1408,128]{1,0:T(8,128)S(1)}, f32[1408,128]{1,0:T(8,128)S(1)}, u32[]{:S(2)}, u32[]{:S(2)}) %collective-permute-start.44) | collective-permute-done | bytes 720928 | tf_op jit(solution)/shard_map/ppermute | solution.py:29
  162.8 4.4 %collective-permute-done.43 = f32[1408,128]{1,0:T(8,128)S(1)} collective-permute-done((f32[1408,128]{1,0:T(8,128)S(1)}, f32[1408,128]{1,0:T(8,128)S(1)}, u32[]{:S(2)}, u32[]{:S(2)}) %collective-permute-start.43) | collective-permute-done | bytes 720928 | tf_op jit(solution)/shard_map/ppermute | solution.py:29
  167.2 2.6 %shard_map.71 = (f32[4,4,12,8,128]{4,3,2,1,0:T(8,128)S(1)}, f32[4,4,12,8,128]{4,3,2,1,0:T(8,128)S(1)}, f32[4,11,8,128]{3,2,1,0:T(8,128)S(1)}) custom-call(s32[912]{0:T(1024)S(1)} %concatenate.3.tab, f32[4,4,11,8,128]{4,3,2,1,0:T(8,128)S(1)} %pad_maximum_fusion.refs_0_, f32[4,4,11,8,128]{4,3,2,1,0:T(8,128)S(1)} %bitcast.129, ...), custom_call_target="tpu_custom_call" | custom-call | tf_op jit(solution)/shard_map/pallas_call | solution.py:129
  176.4 4.6 %collective-permute-done.47 = f32[384,128]{1,0:T(8,128)S(1)} collective-permute-done((f32[384,128]{1,0:T(8,128)S(1)}, f32[384,128]{1,0:T(8,128)S(1)}, u32[]{:S(2)}, u32[]{:S(2)}) %collective-permute-start.47) | collective-permute-done | bytes 196640 | tf_op jit(solution)/shard_map/ppermute | solution.py:29
  181.0 4.6 %collective-permute-done.48 = f32[384,128]{1,0:T(8,128)S(1)} collective-permute-done((f32[384,128]{1,0:T(8,128)S(1)}, f32[384,128]{1,0:T(8,128)S(1)}, u32[]{:S(2)}, u32[]{:S(2)}) %collective-permute-start.48) | collective-permute-done | bytes 196640 | tf_op jit(solution)/shard_map/ppermute | solution.py:29
  192.2 3.2 %collective-permute-done.51 = f32[256,128]{1,0:T(8,128)S(1)} collective-permute-done((f32[256,128]{1,0:T(8,128)S(1)}, f32[256,128]{1,0:T(8,128)S(1)}, u32[]{:S(2)}, u32[]{:S(2)}) %collective-permute-start.51) | collective-permute-done | bytes 131104 | tf_op jit(solution)/shard_map/ppermute | solution.py:29
  195.4 2.5 %collective-permute-done.52 = f32[256,128]{1,0:T(8,128)S(1)} collective-permute-done((f32[256,128]{1,0:T(8,128)S(1)}, f32[256,128]{1,0:T(8,128)S(1)}, u32[]{:S(2)}, u32[]{:S(2)}) %collective-permute-start.52) | collective-permute-done | bytes 131104 | tf_op jit(solution)/shard_map/ppermute | solution.py:29
  (118 shorter events, 80.9 us)
Async XLA Ops:
  3.8 9.4 %collective-permute-start.1 = (f32[256,128]{1,0:T(8,128)S(1)}, f32[256,128]{1,0:T(8,128)S(1)}, u32[]{:S(2)}, u32[]{:S(2)}) collective-permute-start(f32[256,128]{1,0:T(8,128)S(1)} %bitcast.204), channel_id=1, source_target_pairs={{0,4},{1,5},{2,6},{3,7},{4,0},{5,1},{6,2},{7,3},{8,12},{9,13},{10,... | collective-permute-start | bytes 393224 | tf_op jit(solution)/shard_map/ppermute | solution.py:29
  7.6 6.4 %collective-permute-start.2 = (f32[256,128]{1,0:T(8,128)S(1)}, f32[256,128]{1,0:T(8,128)S(1)}, u32[]{:S(2)}, u32[]{:S(2)}) collective-permute-start(f32[256,128]{1,0:T(8,128)S(1)} %bitcast.203), channel_id=1, source_target_pairs={{0,2},{1,7},{2,0},{3,5},{4,6},{5,3},{6,4},{7,1},{8,10},{9,15},{10,... | collective-permute-start | bytes 393224 | tf_op jit(solution)/shard_map/ppermute | solution.py:29
  8.0 6.4 %collective-permute-start.3 = (f32[256,128]{1,0:T(8,128)S(1)}, f32[256,128]{1,0:T(8,128)S(1)}, u32[]{:S(2)}, u32[]{:S(2)}) collective-permute-start(f32[256,128]{1,0:T(8,128)S(1)} %bitcast.202), channel_id=1, source_target_pairs={{0,6},{1,3},{2,4},{3,1},{4,2},{5,7},{6,0},{7,5},{8,14},{9,11},{10,... | collective-permute-start | bytes 393224 | tf_op jit(solution)/shard_map/ppermute | solution.py:29
  24.1 9.2 %collective-permute-start.9 = (f32[896,128]{1,0:T(8,128)S(1)}, f32[896,128]{1,0:T(8,128)S(1)}, u32[]{:S(2)}, u32[]{:S(2)}) collective-permute-start(f32[896,128]{1,0:T(8,128)S(1)} %bitcast.118), channel_id=1, source_target_pairs={{0,16},{1,65},{8,24},{9,73},{16,0},{17,81},{24,8},{25,89},{32,48},... | collective-permute-start | bytes 1376264 | tf_op jit(solution)/shard_map/ppermute | solution.py:29
  27.0 11.4 %collective-permute-start.8 = (f32[896,128]{1,0:T(8,128)S(1)}, f32[896,128]{1,0:T(8,128)S(1)}, u32[]{:S(2)}, u32[]{:S(2)}) collective-permute-start(f32[896,128]{1,0:T(8,128)S(1)} %bitcast.119), channel_id=1, source_target_pairs={{0,24},{1,97},{8,0},{9,105},{16,8},{17,113},{24,16},{25,121},{32,5... | collective-permute-start | bytes 1376264 | tf_op jit(solution)/shard_map/ppermute | solution.py:29
  27.8 10.6 %collective-permute-start.7 = (f32[896,128]{1,0:T(8,128)S(1)}, f32[896,128]{1,0:T(8,128)S(1)}, u32[]{:S(2)}, u32[]{:S(2)}) collective-permute-start(f32[896,128]{1,0:T(8,128)S(1)} %bitcast.120), channel_id=1, source_target_pairs={{0,8},{1,33},{8,16},{9,41},{16,24},{17,49},{24,0},{25,57},{32,40},... | collective-permute-start | bytes 1376264 | tf_op jit(solution)/shard_map/ppermute | solution.py:29
  45.8 6.3 %collective-permute-start.11 = (f32[256,128]{1,0:T(8,128)S(1)}, f32[256,128]{1,0:T(8,128)S(1)}, u32[]{:S(2)}, u32[]{:S(2)}) collective-permute-start(f32[256,128]{1,0:T(8,128)S(1)} %bitcast.211), channel_id=1, source_target_pairs={{0,4},{1,5},{2,6},{3,7},{4,0},{5,1},{6,2},{7,3},{8,12},{9,13},{10,... | collective-permute-start | bytes 393224 | tf_op jit(solution)/shard_map/ppermute | solution.py:29
  47.6 6.9 %collective-permute-start.12 = (f32[256,128]{1,0:T(8,128)S(1)}, f32[256,128]{1,0:T(8,128)S(1)}, u32[]{:S(2)}, u32[]{:S(2)}) collective-permute-start(f32[256,128]{1,0:T(8,128)S(1)} %bitcast.209), channel_id=1, source_target_pairs={{0,2},{1,7},{2,0},{3,5},{4,6},{5,3},{6,4},{7,1},{8,10},{9,15},{10,... | collective-permute-start | bytes 393224 | tf_op jit(solution)/shard_map/ppermute | solution.py:29
  54.9 8.3 %collective-permute-start.15 = (f32[256,128]{1,0:T(8,128)S(1)}, f32[256,128]{1,0:T(8,128)S(1)}, u32[]{:S(2)}, u32[]{:S(2)}) collective-permute-start(f32[256,128]{1,0:T(8,128)S(1)} %bitcast.137), channel_id=1, source_target_pairs={{0,16},{8,0},{32,8},{40,32},{64,40},{72,64},{96,72},{104,96},{120,... | collective-permute-start | bytes 393224 | tf_op jit(solution)/shard_map/ppermute | solution.py:29
  57.5 9.5 %collective-permute-start.14 = (f32[256,128]{1,0:T(8,128)S(1)}, f32[256,128]{1,0:T(8,128)S(1)}, u32[]{:S(2)}, u32[]{:S(2)}) collective-permute-start(f32[256,128]{1,0:T(8,128)S(1)} %bitcast.138), channel_id=1, source_target_pairs={{0,8},{8,32},{32,40},{40,64},{64,72},{72,96},{96,104},{104,120},{1... | collective-permute-start | bytes 393224 | tf_op jit(solution)/shard_map/ppermute | solution.py:29
  71.6 6.6 %collective-permute-start.19 = (f32[288,128]{1,0:T(8,128)S(1)}, f32[288,128]{1,0:T(8,128)S(1)}, u32[]{:S(2)}, u32[]{:S(2)}) collective-permute-start(f32[288,128]{1,0:T(8,128)S(1)} %bitcast.201), channel_id=1, source_target_pairs={{0,4},{1,5},{2,6},{3,7},{4,0},{5,1},{6,2},{7,3},{8,12},{9,13},{10,... | collective-permute-start | bytes 442376 | tf_op jit(solution)/shard_map/ppermute | solution.py:29
  73.9 7.8 %collective-permute-start.20 = (f32[288,128]{1,0:T(8,128)S(1)}, f32[288,128]{1,0:T(8,128)S(1)}, u32[]{:S(2)}, u32[]{:S(2)}) collective-permute-start(f32[288,128]{1,0:T(8,128)S(1)} %bitcast.200), channel_id=1, source_target_pairs={{0,2},{1,7},{2,0},{3,5},{4,6},{5,3},{6,4},{7,1},{8,10},{9,15},{10,... | collective-permute-start | bytes 442376 | tf_op jit(solution)/shard_map/ppermute | solution.py:29
  75.3 6.7 %collective-permute-start.21 = (f32[288,128]{1,0:T(8,128)S(1)}, f32[288,128]{1,0:T(8,128)S(1)}, u32[]{:S(2)}, u32[]{:S(2)}) collective-permute-start(f32[288,128]{1,0:T(8,128)S(1)} %bitcast.199), channel_id=1, source_target_pairs={{0,6},{1,3},{2,4},{3,1},{4,2},{5,7},{6,0},{7,5},{8,14},{9,11},{10,... | collective-permute-start | bytes 442376 | tf_op jit(solution)/shard_map/ppermute | solution.py:29
  82.1 7.0 %collective-permute-start.23 = (f32[288,128]{1,0:T(8,128)S(1)}, f32[288,128]{1,0:T(8,128)S(1)}, u32[]{:S(2)}, u32[]{:S(2)}) collective-permute-start(f32[288,128]{1,0:T(8,128)S(1)} %bitcast.134), channel_id=1, source_target_pairs={{0,16},{8,0},{32,8},{40,32},{64,40},{72,64},{96,72},{104,96},{120,... | collective-permute-start | bytes 442376 | tf_op jit(solution)/shard_map/ppermute | solution.py:29
  82.2 9.2 %collective-permute-start.22 = (f32[288,128]{1,0:T(8,128)S(1)}, f32[288,128]{1,0:T(8,128)S(1)}, u32[]{:S(2)}, u32[]{:S(2)}) collective-permute-start(f32[288,128]{1,0:T(8,128)S(1)} %bitcast.135), channel_id=1, source_target_pairs={{0,8},{8,32},{32,40},{40,64},{64,72},{72,96},{96,104},{104,120},{1... | collective-permute-start | bytes 442376 | tf_op jit(solution)/shard_map/ppermute | solution.py:29
  96.9 7.0 %collective-permute-start.27 = (f32[320,128]{1,0:T(8,128)S(1)}, f32[320,128]{1,0:T(8,128)S(1)}, u32[]{:S(2)}, u32[]{:S(2)}) collective-permute-start(f32[320,128]{1,0:T(8,128)S(1)} %bitcast.198), channel_id=1, source_target_pairs={{0,4},{1,5},{2,6},{3,7},{4,0},{5,1},{6,2},{7,3},{8,12},{9,13},{10,... | collective-permute-start | bytes 491528 | tf_op jit(solution)/shard_map/ppermute | solution.py:29
  99.1 8.5 %collective-permute-start.28 = (f32[320,128]{1,0:T(8,128)S(1)}, f32[320,128]{1,0:T(8,128)S(1)}, u32[]{:S(2)}, u32[]{:S(2)}) collective-permute-start(f32[320,128]{1,0:T(8,128)S(1)} %bitcast.197), channel_id=1, source_target_pairs={{0,2},{1,7},{2,0},{3,5},{4,6},{5,3},{6,4},{7,1},{8,10},{9,15},{10,... | collective-permute-start | bytes 491528 | tf_op jit(solution)/shard_map/ppermute | solution.py:29
  100.6 7.4 %collective-permute-start.29 = (f32[320,128]{1,0:T(8,128)S(1)}, f32[320,128]{1,0:T(8,128)S(1)}, u32[]{:S(2)}, u32[]{:S(2)}) collective-permute-start(f32[320,128]{1,0:T(8,128)S(1)} %bitcast.196), channel_id=1, source_target_pairs={{0,6},{1,3},{2,4},{3,1},{4,2},{5,7},{6,0},{7,5},{8,14},{9,11},{10,... | collective-permute-start | bytes 491528 | tf_op jit(solution)/shard_map/ppermute | solution.py:29
  109.4 9.5 %collective-permute-start.31 = (f32[320,128]{1,0:T(8,128)S(1)}, f32[320,128]{1,0:T(8,128)S(1)}, u32[]{:S(2)}, u32[]{:S(2)}) collective-permute-start(f32[320,128]{1,0:T(8,128)S(1)} %bitcast.131), channel_id=1, source_target_pairs={{0,16},{8,0},{32,8},{40,32},{64,40},{72,64},{96,72},{104,96},{120,... | collective-permute-start | bytes 491528 | tf_op jit(solution)/shard_map/ppermute | solution.py:29
  109.5 12.7 %collective-permute-start.30 = (f32[320,128]{1,0:T(8,128)S(1)}, f32[320,128]{1,0:T(8,128)S(1)}, u32[]{:S(2)}, u32[]{:S(2)}) collective-permute-start(f32[320,128]{1,0:T(8,128)S(1)} %bitcast.132), channel_id=1, source_target_pairs={{0,8},{8,32},{32,40},{40,64},{64,72},{72,96},{96,104},{104,120},{1... | collective-permute-start | bytes 491528 | tf_op jit(solution)/shard_map/ppermute | solution.py:29
  110.9 8.0 %collective-permute-start.33 = (f32[256,128]{1,0:T(8,128)S(1)}, f32[256,128]{1,0:T(8,128)S(1)}, u32[]{:S(2)}, u32[]{:S(2)}) collective-permute-start(f32[256,128]{1,0:T(8,128)S(1)} %bitcast.206), channel_id=1, source_target_pairs={{0,24},{8,16},{32,0},{40,8},{64,32},{72,40},{96,64},{104,72},{120,... | collective-permute-start | bytes 393224 | tf_op jit(solution)/shard_map/ppermute | solution.py:29
  110.9 8.0 %collective-permute-start.32 = (f32[256,128]{1,0:T(8,128)S(1)}, f32[256,128]{1,0:T(8,128)S(1)}, u32[]{:S(2)}, u32[]{:S(2)}) collective-permute-start(f32[256,128]{1,0:T(8,128)S(1)} %bitcast.205), channel_id=1, source_target_pairs={{0,32},{8,40},{32,64},{40,72},{64,96},{72,104},{96,120},{104,112},... | collective-permute-start | bytes 393224 | tf_op jit(solution)/shard_map/ppermute | solution.py:29
  126.4 7.4 %collective-permute-start.37 = (f32[352,128]{1,0:T(8,128)S(1)}, f32[352,128]{1,0:T(8,128)S(1)}, u32[]{:S(2)}, u32[]{:S(2)}) collective-permute-start(f32[352,128]{1,0:T(8,128)S(1)} %bitcast.195), channel_id=1, source_target_pairs={{0,4},{1,5},{2,6},{3,7},{4,0},{5,1},{6,2},{7,3},{8,12},{9,13},{10,... | collective-permute-start | bytes 540680 | tf_op jit(solution)/shard_map/ppermute | solution.py:29
  128.0 9.8 %collective-permute-start.38 = (f32[352,128]{1,0:T(8,128)S(1)}, f32[352,128]{1,0:T(8,128)S(1)}, u32[]{:S(2)}, u32[]{:S(2)}) collective-permute-start(f32[352,128]{1,0:T(8,128)S(1)} %bitcast.194), channel_id=1, source_target_pairs={{0,2},{1,7},{2,0},{3,5},{4,6},{5,3},{6,4},{7,1},{8,10},{9,15},{10,... | collective-permute-start | bytes 540680 | tf_op jit(solution)/shard_map/ppermute | solution.py:29
  129.5 8.3 %collective-permute-start.39 = (f32[352,128]{1,0:T(8,128)S(1)}, f32[352,128]{1,0:T(8,128)S(1)}, u32[]{:S(2)}, u32[]{:S(2)}) collective-permute-start(f32[352,128]{1,0:T(8,128)S(1)} %bitcast.193), channel_id=1, source_target_pairs={{0,6},{1,3},{2,4},{3,1},{4,2},{5,7},{6,0},{7,5},{8,14},{9,11},{10,... | collective-permute-start | bytes 540680 | tf_op jit(solution)/shard_map/ppermute | solution.py:29
  147.5 12.1 %collective-permute-start.45 = (f32[1408,128]{1,0:T(8,128)S(1)}, f32[1408,128]{1,0:T(8,128)S(1)}, u32[]{:S(2)}, u32[]{:S(2)}) collective-permute-start(f32[1408,128]{1,0:T(8,128)S(1)} %bitcast.115), channel_id=1, source_target_pairs={{0,16},{1,65},{8,24},{9,73},{16,0},{17,81},{24,8},{25,89},{32,48},... | collective-permute-start | bytes 2162696 | tf_op jit(solution)/shard_map/ppermute | solution.py:29
  147.6 15.2 %collective-permute-start.44 = (f32[1408,128]{1,0:T(8,128)S(1)}, f32[1408,128]{1,0:T(8,128)S(1)}, u32[]{:S(2)}, u32[]{:S(2)}) collective-permute-start(f32[1408,128]{1,0:T(8,128)S(1)} %bitcast.116), channel_id=1, source_target_pairs={{0,24},{1,97},{8,0},{9,105},{16,8},{17,113},{24,16},{25,121},{32,5... | collective-permute-start | bytes 2162696 | tf_op jit(solution)/shard_map/ppermute | solution.py:29
  148.0 19.2 %collective-permute-start.43 = (f32[1408,128]{1,0:T(8,128)S(1)}, f32[1408,128]{1,0:T(8,128)S(1)}, u32[]{:S(2)}, u32[]{:S(2)}) collective-permute-start(f32[1408,128]{1,0:T(8,128)S(1)} %bitcast.117), channel_id=1, source_target_pairs={{0,8},{1,33},{8,16},{9,41},{16,24},{17,49},{24,0},{25,57},{32,40},... | collective-permute-start | bytes 2162696 | tf_op jit(solution)/shard_map/ppermute | solution.py:29
  173.3 7.7 %collective-permute-start.47 = (f32[384,128]{1,0:T(8,128)S(1)}, f32[384,128]{1,0:T(8,128)S(1)}, u32[]{:S(2)}, u32[]{:S(2)}) collective-permute-start(f32[384,128]{1,0:T(8,128)S(1)} %bitcast.192), channel_id=1, source_target_pairs={{0,4},{1,5},{2,6},{3,7},{4,0},{5,1},{6,2},{7,3},{8,12},{9,13},{10,... | collective-permute-start | bytes 589832 | tf_op jit(solution)/shard_map/ppermute | solution.py:29
  174.9 10.7 %collective-permute-start.48 = (f32[384,128]{1,0:T(8,128)S(1)}, f32[384,128]{1,0:T(8,128)S(1)}, u32[]{:S(2)}, u32[]{:S(2)}) collective-permute-start(f32[384,128]{1,0:T(8,128)S(1)} %bitcast.191), channel_id=1, source_target_pairs={{0,2},{1,7},{2,0},{3,5},{4,6},{5,3},{6,4},{7,1},{8,10},{9,15},{10,... | collective-permute-start | bytes 589832 | tf_op jit(solution)/shard_map/ppermute | solution.py:29
  176.4 9.2 %collective-permute-start.49 = (f32[384,128]{1,0:T(8,128)S(1)}, f32[384,128]{1,0:T(8,128)S(1)}, u32[]{:S(2)}, u32[]{:S(2)}) collective-permute-start(f32[384,128]{1,0:T(8,128)S(1)} %bitcast.190), channel_id=1, source_target_pairs={{0,6},{1,3},{2,4},{3,1},{4,2},{5,7},{6,0},{7,5},{8,14},{9,11},{10,... | collective-permute-start | bytes 589832 | tf_op jit(solution)/shard_map/ppermute | solution.py:29
  190.8 7.1 %collective-permute-start.52 = (f32[256,128]{1,0:T(8,128)S(1)}, f32[256,128]{1,0:T(8,128)S(1)}, u32[]{:S(2)}, u32[]{:S(2)}) collective-permute-start(f32[256,128]{1,0:T(8,128)S(1)} %bitcast.210), channel_id=1, source_target_pairs={{0,2},{1,7},{2,0},{3,5},{4,6},{5,3},{6,4},{7,1},{8,10},{9,15},{10,... | collective-permute-start | bytes 393224 | tf_op jit(solution)/shard_map/ppermute | solution.py:29
  (27 other events, 107.5 us)

commit v11 on v10

--- a/solution.py
+++ b/solution.py
@@ -136,21 +136,26 @@
     )(*([] if tab is None else [tab]), *args)
 
 
-def split_kernel(d_ref, own_ref, oth_ref):
+def slot_view(pair, slot):
+    return pair[0].at[0] if slot == 1 else pair[1].at[(0, None, 1, 2)[slot]]
+
+
+def split_kernel(d_ref, *refs):
     z, h = lax.axis_index("col"), lax.axis_index("layer")
     for k in range(4):
-        for ref, core in ((own_ref, h), (oth_ref, 1 - h)):
+        for pair, core in ((refs[:2], h), (refs[2:], 1 - h)):
+            ref = slot_view(pair, k)
             for e in range(4):
                 start = pl.multiple_of(e * 64 + (2 * slot_of(z, core, k) + core) * 8, 8)
                 rows = d_ref[pl.ds(start, 8), :]
                 for t in range(4):
-                    ref[k, e, t] = rows[:, t * 128 : (t + 1) * 128]
+                    ref[e, t] = rows[:, t * 128 : (t + 1) * 128]
 
 
 def pack_kernel(own_ref, got_ref, *outs):
-    for k in range(4):
-        outs[k][0] = own_ref[k]
-        outs[k][1] = got_ref[k]
+    for k, out_ref in enumerate(outs):
+        out_ref[0] = own_ref[k]
+        out_ref[1] = got_ref[k]
 
 
 def compact_kernel(tab, *refs):
@@ -197,16 +202,17 @@
     return jnp.where(first, dy, dx), jnp.where(first, dx, dy), e
 
 
-def write_slabs(p_ref, own_ref, oth_ref, e, base, d, tiles):
+def write_slabs(p_ref, own, oth, e, base, d, tiles):
     z, h = lax.axis_index("col"), lax.axis_index("layer")
     low = low_half()
     for zz in range(4):
-        for ref, core in ((own_ref, h), (oth_ref, 1 - h)):
+        for pair, core in ((own, h), (oth, 1 - h)):
+            ref = slot_view(pair, zz)
             rows = p_ref[base + 2 * slot_of(z, core, zz) + core]
             if d % 2 == 0:
                 for m in range(tiles):
                     at = (d // 2 + m) * 128
-                    ref[zz, e, m] = rows[:, at : at + 128]
+                    ref[e, m] = rows[:, at : at + 128]
             else:
                 q = d // 2
                 turned = []
@@ -217,7 +223,7 @@
                     else:
                         turned.append(jnp.zeros((8, 128), F32))
                 for m in range(tiles):
-                    ref[zz, e, m] = jnp.where(low, turned[m], turned[m + 1])
+                    ref[e, m] = jnp.where(low, turned[m], turned[m + 1])
 
 
 def geometry(w):
@@ -225,7 +231,7 @@
     return left, (left + 4 + w + 1 + 1) // 2
 
 
-def step_body(strips, w, own_ref, oth_ref, hi_ref, lo_ref, p_ref):
+def step_body(strips, w, own, oth, hi_ref, lo_ref, p_ref):
     left, count = geometry(w)
     for a in range(0, len(strips), 2):
         pair = []
@@ -235,11 +241,12 @@
         store_split(hi_ref, lo_ref, a * 8, pair[0], pair[1])
     p_ref[...] = product(hi_ref, lo_ref, left * 64, 256).reshape(32, 8, count * 128)
     for e in range(4):
-        write_slabs(p_ref, own_ref, oth_ref, e, e * 8, left - (w + 1) + e, w + 2)
+        write_slabs(p_ref, own, oth, e, e * 8, left - (w + 1) + e, w + 2)
 
 
 def first_step_kernel(tab, *refs):
-    ins, (own_ref, oth_ref, cur_ref, hi_ref, lo_ref, p_ref, g_ref) = refs[:4], refs[4:]
+    ins, own, oth = refs[:4], refs[4:6], refs[6:8]
+    cur_ref, hi_ref, lo_ref, p_ref, g_ref = refs[8:]
     collect(ins, g_ref)
     w = BAND
     base = tab[PLACE + 5] * 4 + 64 - w
@@ -253,13 +260,14 @@
         return b, [strip[t] for t in range(w + 1)], 0
 
     strips = [lambda b=b: strip_of(b) for b in range(4 + 2 * w)]
-    step_body(strips, w, own_ref, oth_ref, hi_ref, lo_ref, p_ref)
+    step_body(strips, w, own, oth, hi_ref, lo_ref, p_ref)
 
 
 def step_kernel(w, pieces, *refs):
     far = outermost(w) is not None
     n = 1 + len(pieces) + far
-    ins, (own_ref, oth_ref, hi_ref, lo_ref, p_ref) = refs[:n], refs[n:]
+    ins, own, oth = refs[:n], refs[n : n + 2], refs[n + 2 : n + 4]
+    hi_ref, lo_ref, p_ref = refs[n + 4 :]
 
     def strip_of(b):
         off = b - w
@@ -282,7 +290,7 @@
         for slab in (0, 1):
             strips.append(lambda slab=slab: far_strip(0, 0, slab))
             strips.append(lambda slab=slab: far_strip(last, 1, slab))
-    step_body(strips, w, own_ref, oth_ref, hi_ref, lo_ref, p_ref)
+    step_body(strips, w, own, oth, hi_ref, lo_ref, p_ref)
 
 
 def far_tiles(w):
@@ -305,7 +313,8 @@
 
 
 def last_step_kernel(tab, *refs):
-    ins, (own_ref, oth_ref, cur_ref, hi_ref, lo_ref, p_ref, g_ref) = refs[:4], refs[4:]
+    ins, own, oth = refs[:4], refs[4:6], refs[6:8]
+    cur_ref, hi_ref, lo_ref, p_ref, g_ref = refs[8:]
     collect(ins, g_ref)
     w = BAND + STEPS - 1
     row0 = tab[PLACE] * 4
@@ -331,12 +340,12 @@
                 two = shifted(strips(a + 1), left - 2 * w + a + 1, count)
             store_split(hi_ref, lo_ref, a * 8, one, two)
         p_ref[...] = product(hi_ref, lo_ref, left * 64, 64).reshape(8, 8, count * 128)
-        write_slabs(p_ref, own_ref, oth_ref, e, 0, 0, count)
+        write_slabs(p_ref, own, oth, e, 0, 0, count)
 
 
 def pair_kernel(own_ref, got_ref, *outs):
-    for k in range(4):
-        outs[k][...] = own_ref[k] + got_ref[k]
+    for k, out_ref in enumerate(outs):
+        out_ref[...] = own_ref[k] + got_ref[k]
 
 
 def total(parts, e, m):
@@ -391,11 +400,12 @@
         oth_ref[...] = far_ref[1 - lax.axis_index("layer")]
 
 
-def finish_kernel(tab, p0, p1, p2, p3, cur_ref, keep_ref, coef_ref, own_ref, oth_ref, y_ref):
+def finish_kernel(tab, p0, p1, p2, p3, cur_ref, keep_ref, coef_ref, *refs):
     w = BAND + STEPS - 1
     low = low_half()
     row0 = tab[PLACE] * 4
     z, h = tab[PLACE + 6], tab[PLACE + 4]
+    own, oth, y_ref = refs[:2], refs[2:4], refs[4]
     y_ref[...] = jnp.zeros_like(y_ref)
     for e in range(4):
         i = tab[PERM + row0 + e]
@@ -416,8 +426,9 @@
                 core = (sj >> 3) & 1
                 at = core ^ h, slot_with((sj >> 4) ^ z, core), e, (sj & 7) >> 1
                 y_ref[at] = jnp.where(side, piece, y_ref[at])
-    own_ref[...] = y_ref[0]
-    oth_ref[...] = y_ref[1]
+    for slot in range(4):
+        slot_view(own, slot)[...] = y_ref[0, slot]
+        slot_view(oth, slot)[...] = y_ref[1, slot]
 
 
 def join_kernel(y0, y1, y2, y3, out_ref):
@@ -445,22 +456,30 @@
     )
 
 
-def z_exchange(parts):
-    return [parts[0]] + [z_swap(parts[k], k) for k in (1, 2, 3)]
-
-
-def reduce_group(own, oth):
-    return z_exchange(call(pair_kernel, [own.shape[1:]] * 4, [own, core_swap(oth)]))
-
-
-def spread_group(own, oth):
-    shape = (2,) + own.shape[1:]
-    return z_exchange(call(pack_kernel, [shape] * 4, [own, core_swap(oth)]))
+def z_exchange(kernel, shape, parts):
+    first, rest, other_first, other_rest = parts
+    other_first, other_rest = core_swap(other_first), core_swap(other_rest)
+    (far,) = call(kernel, [shape], [first, other_first])
+    far = z_swap(far, 1)
+    stay, near, last = call(kernel, [shape] * 3, [rest, other_rest])
+    return [stay, far, z_swap(near, 2), z_swap(last, 3)]
+
+
+def reduce_group(parts):
+    return z_exchange(pair_kernel, parts[0].shape[1:], parts)
+
+
+def spread_group(parts):
+    return z_exchange(pack_kernel, (2,) + parts[0].shape[1:], parts)
+
+
+def in_parts(shape):
+    return [(1,) + shape, (3,) + shape] * 2
 
 
 def shards(density, masks, branch, perm):
-    slabs = (4, 4, 4, 8, 128)
-    split = spread_group(*call(split_kernel, [slabs] * 2, [density]))
+    slabs = (4, 4, 8, 128)
+    split = spread_group(call(split_kernel, in_parts(slabs), [density]))
     tab = tables(masks, branch, perm)
     tiles = [BAND + s + 1 for s in range(STEPS)] + [BAND + STEPS + 1]
     shapes = [(4, n, 8, 128) for n in tiles] + [(STEPS, 2, 8, 128)]
@@ -477,7 +496,7 @@
         w = BAND + step
         left, count = geometry(w)
         depth = (4 + 2 * w + (2 if step and outermost(w) else 0)) * 8
-        part = (4, 4, w + 2, 8, 128)
+        part = in_parts((4, w + 2, 8, 128))
         scratch = [
             pltpu.VMEM((depth, count * 128), BF16),
             pltpu.VMEM((depth, count * 128), BF16),
@@ -485,13 +504,13 @@
         ]
         if step == 0:
             scratch.append(pltpu.VMEM((4, 4, 4, w + 1, 8, 128), F32))
-            own, oth, cur = call(
-                first_step_kernel, [part, part, (4, w + 1, 8, 128)], gathered, scratch, tab=tab
+            *sums, cur = call(
+                first_step_kernel, part + [(4, w + 1, 8, 128)], gathered, scratch, tab=tab
             )
         else:
             kernel = lambda *refs, w=w, pieces=pieces: step_kernel(w, pieces, *refs)
-            own, oth = call(kernel, [part, part], [cur] + around, scratch)
-        parts = reduce_group(own, oth)
+            sums = call(kernel, part, [cur] + around, scratch)
+        parts = reduce_group(sums)
         pieces = halo_pieces(w + 1) if step < STEPS - 2 else []
         cuts = [(0, 4, 0, w + 2)]
         for _, cut in pieces:
@@ -511,21 +530,25 @@
         cur, *around = lax.optimization_barrier((cur, *around))
     gathered = gather_rows(cur)
     w = BAND + STEPS - 1
-    part = (4, 4, w + 2, 8, 128)
+    part = in_parts((4, w + 2, 8, 128))
     scratch = [
         pltpu.VMEM(((2 * w + 2) * 8, (w + 2) * 128), BF16),
         pltpu.VMEM(((2 * w + 2) * 8, (w + 2) * 128), BF16),
         pltpu.VMEM((8, 8, (w + 2) * 128), F32),
         pltpu.VMEM((4, 4, 4, w + 1, 8, 128), F32),
     ]
-    own, oth, cur = call(
-        last_step_kernel, [part, part, (4, w + 1, 8, 128)], gathered, scratch, tab=tab
+    *sums, cur = call(
+        last_step_kernel, part + [(4, w + 1, 8, 128)], gathered, scratch, tab=tab
     )
-    parts = reduce_group(own, oth)
-    own, oth = call(
-        finish_kernel, [slabs] * 2, parts + [cur, keep[STEPS], coef], [pltpu.VMEM((2,) + slabs, F32)], tab=tab
+    parts = reduce_group(sums)
+    tiles = call(
+        finish_kernel,
+        in_parts(slabs),
+        parts + [cur, keep[STEPS], coef],
+        [pltpu.VMEM((2, 4) + slabs, F32)],
+        tab=tab,
     )
-    (out,) = call(join_kernel, [(256, 512)], spread_group(own, oth))
+    (out,) = call(join_kernel, [(256, 512)], spread_group(tiles))
     return out
 
 

time: 199 us -> 199 us (level)
    ppermute x54 -> x61, starting transfers between devices: 64.2 us -> 65.6 us  [permute(): return lax.ppermute(flat, axes, pairs).reshape(value.shape)]
    ppermute x54 -> x61, waiting for transfers between devices: 116 us -> 115 us  [permute(): return lax.ppermute(flat, axes, pairs).reshape(value.shape)]
    pallas_call x21 -> x28, Pallas kernels: 13.7 us -> 13.7 us  [call(): pl.pallas_call(kernel, out_shape=[jax.ShapeDtypeStruct(o, F32) for o in o...]
  transfers between devices with their start and end apart: 54 -> 61, of which waited for: 45 -> 45; matrix products, arithmetic and copies ran while one was open for 1% -> 1% of each run, Pallas kernels for 1% -> 1%
where the time goes in v11:
time: 199 us
  waiting for transfers between devices  115 us (58%)
  starting transfers between devices  65.6 us (33%)
  Pallas kernels  13.7 us (7%)
  local copies, waits for them, and re-layouts  3.67 us (2%)
    ppermute x61, waiting for transfers between devices, permute(): return lax.ppermute(flat, axes, pairs).reshape(value.shape)  115 us
    ppermute x61, starting transfers between devices, permute(): return lax.ppermute(flat, axes, pairs).reshape(value.shape)  65.6 us
    pallas_call x28, Pallas kernels, call(): pl.pallas_call(kernel, out_shape=[jax.ShapeDtypeStruct(o, F32) for o in o...  13.7 us
  transfers between devices with their start and end apart: 61, of which 45 were waited for; matrix products, arithmetic and copies ran while one was open for 1% of the time, Pallas kernels for 1%

profile of v11, /device:TPU:1, one launch (start us, length us, event | category | flops | bytes accessed | tf_op | source)
XLA Modules:
  0.0 199.0 jit_solution(363250691502185691)
XLA Ops:
  3.9 3.8 %collective-permute-start.2 = (f32[256,128]{1,0:T(8,128)S(1)}, f32[256,128]{1,0:T(8,128)S(1)}, u32[]{:S(2)}, u32[]{:S(2)}) collective-permute-start(f32[256,128]{1,0:T(8,128)S(1)} %bitcast.193), channel_id=1, source_target_pairs={{0,4},{1,5},{2,6},{3,7},{4,0},{5,1},{6,2},{7,3},{8,12},{9,13},{10,... | collective-permute-start | bytes 393224 | tf_op jit(solution)/shard_map/ppermute | solution.py:29
  15.7 3.0 %collective-permute-start.7 = (f32[224,128]{1,0:T(8,128)S(1)}, f32[224,128]{1,0:T(8,128)S(1)}, u32[]{:S(2)}, u32[]{:S(2)}) collective-permute-start(f32[224,128]{1,0:T(8,128)S(1)} %bitcast.154), channel_id=1, source_target_pairs={{0,64},{1,17},{8,72},{9,25},{16,80},{17,1},{24,88},{25,9},{32,96},... | collective-permute-start | bytes 344072 | tf_op jit(solution)/shard_map/ppermute | solution.py:29
  24.3 2.8 %collective-permute-start.10 = (f32[896,128]{1,0:T(8,128)S(1)}, f32[896,128]{1,0:T(8,128)S(1)}, u32[]{:S(2)}, u32[]{:S(2)}) collective-permute-start(f32[896,128]{1,0:T(8,128)S(1)} %bitcast.132), channel_id=1, source_target_pairs={{0,16},{1,65},{8,24},{9,73},{16,0},{17,81},{24,8},{25,89},{32,48},... | collective-permute-start | bytes 1376264 | tf_op jit(solution)/shard_map/ppermute | solution.py:29
  28.6 4.9 %collective-permute-done.10 = f32[896,128]{1,0:T(8,128)S(1)} collective-permute-done((f32[896,128]{1,0:T(8,128)S(1)}, f32[896,128]{1,0:T(8,128)S(1)}, u32[]{:S(2)}, u32[]{:S(2)}) %collective-permute-start.10) | collective-permute-done | bytes 458784 | tf_op jit(solution)/shard_map/ppermute | solution.py:29
  33.5 5.0 %collective-permute-done.9 = f32[896,128]{1,0:T(8,128)S(1)} collective-permute-done((f32[896,128]{1,0:T(8,128)S(1)}, f32[896,128]{1,0:T(8,128)S(1)}, u32[]{:S(2)}, u32[]{:S(2)}) %collective-permute-start.9) | collective-permute-done | bytes 458784 | tf_op jit(solution)/shard_map/ppermute | solution.py:29
  40.3 3.9 %collective-permute-start.11 = (f32[768,128]{1,0:T(8,128)S(1)}, f32[768,128]{1,0:T(8,128)S(1)}, u32[]{:S(2)}, u32[]{:S(2)}) collective-permute-start(f32[768,128]{1,0:T(8,128)S(1)} %bitcast.215), channel_id=1, source_target_pairs={{0,1},{1,0},{2,3},{3,2},{4,5},{5,4},{6,7},{7,6},{8,9},{9,8},{10,11... | collective-permute-start | bytes 1179656 | tf_op jit(solution)/shard_map/ppermute | solution.py:29
  49.1 3.0 %collective-permute-done.13 = f32[256,128]{1,0:T(8,128)S(1)} collective-permute-done((f32[256,128]{1,0:T(8,128)S(1)}, f32[256,128]{1,0:T(8,128)S(1)}, u32[]{:S(2)}, u32[]{:S(2)}) %collective-permute-start.13) | collective-permute-done | bytes 131104 | tf_op jit(solution)/shard_map/ppermute | solution.py:29
  52.1 2.4 %collective-permute-done.14 = f32[256,128]{1,0:T(8,128)S(1)} collective-permute-done((f32[256,128]{1,0:T(8,128)S(1)}, f32[256,128]{1,0:T(8,128)S(1)}, u32[]{:S(2)}, u32[]{:S(2)}) %collective-permute-start.14) | collective-permute-done | bytes 131104 | tf_op jit(solution)/shard_map/ppermute | solution.py:29
  55.0 2.6 %collective-permute-start.17 = (f32[256,128]{1,0:T(8,128)S(1)}, f32[256,128]{1,0:T(8,128)S(1)}, u32[]{:S(2)}, u32[]{:S(2)}) collective-permute-start(f32[256,128]{1,0:T(8,128)S(1)} %bitcast.148), channel_id=1, source_target_pairs={{0,16},{8,0},{32,8},{40,32},{64,40},{72,64},{96,72},{104,96},{120,... | collective-permute-start | bytes 393224 | tf_op jit(solution)/shard_map/ppermute | solution.py:29
  59.0 2.5 %collective-permute-done.19 = f32[144,128]{1,0:T(8,128)S(1)} collective-permute-done((f32[144,128]{1,0:T(8,128)S(1)}, f32[144,128]{1,0:T(8,128)S(1)}, u32[]{:S(2)}, u32[]{:S(2)}) %collective-permute-start.19) | collective-permute-done | bytes 73760 | tf_op jit(solution)/shard_map/ppermute | solution.py:29
  63.3 3.8 %collective-permute-done.16 = f32[256,128]{1,0:T(8,128)S(1)} collective-permute-done((f32[256,128]{1,0:T(8,128)S(1)}, f32[256,128]{1,0:T(8,128)S(1)}, u32[]{:S(2)}, u32[]{:S(2)}) %collective-permute-start.16) | collective-permute-done | bytes 131104 | tf_op jit(solution)/shard_map/ppermute | solution.py:29
  71.6 2.4 %collective-permute-start.22 = (f32[288,128]{1,0:T(8,128)S(1)}, f32[288,128]{1,0:T(8,128)S(1)}, u32[]{:S(2)}, u32[]{:S(2)}) collective-permute-start(f32[288,128]{1,0:T(8,128)S(1)} %bitcast.180), channel_id=1, source_target_pairs={{0,4},{1,5},{2,6},{3,7},{4,0},{5,1},{6,2},{7,3},{8,12},{9,13},{10,... | collective-permute-start | bytes 442376 | tf_op jit(solution)/shard_map/ppermute | solution.py:29
  75.6 2.6 %collective-permute-done.22 = f32[288,128]{1,0:T(8,128)S(1)} collective-permute-done((f32[288,128]{1,0:T(8,128)S(1)}, f32[288,128]{1,0:T(8,128)S(1)}, u32[]{:S(2)}, u32[]{:S(2)}) %collective-permute-start.22) | collective-permute-done | bytes 147488 | tf_op jit(solution)/shard_map/ppermute | solution.py:29
  78.3 3.4 %collective-permute-done.23 = f32[288,128]{1,0:T(8,128)S(1)} collective-permute-done((f32[288,128]{1,0:T(8,128)S(1)}, f32[288,128]{1,0:T(8,128)S(1)}, u32[]{:S(2)}, u32[]{:S(2)}) %collective-permute-start.23) | collective-permute-done | bytes 147488 | tf_op jit(solution)/shard_map/ppermute | solution.py:29
  85.1 3.4 %collective-permute-done.28 = f32[224,128]{1,0:T(8,128)S(1)} collective-permute-done((f32[224,128]{1,0:T(8,128)S(1)}, f32[224,128]{1,0:T(8,128)S(1)}, u32[]{:S(2)}, u32[]{:S(2)}) %collective-permute-start.28) | collective-permute-done | bytes 114720 | tf_op jit(solution)/shard_map/ppermute | solution.py:29
  92.6 2.5 %collective-permute-start.29 = (f32[960,128]{1,0:T(8,128)S(1)}, f32[960,128]{1,0:T(8,128)S(1)}, u32[]{:S(2)}, u32[]{:S(2)}) collective-permute-start(f32[960,128]{1,0:T(8,128)S(1)} %bitcast.213), channel_id=1, source_target_pairs={{0,1},{1,0},{2,3},{3,2},{4,5},{5,4},{6,7},{7,6},{8,9},{9,8},{10,11... | collective-permute-start | bytes 1474568 | tf_op jit(solution)/shard_map/ppermute | solution.py:29
  100.6 3.2 %collective-permute-done.31 = f32[320,128]{1,0:T(8,128)S(1)} collective-permute-done((f32[320,128]{1,0:T(8,128)S(1)}, f32[320,128]{1,0:T(8,128)S(1)}, u32[]{:S(2)}, u32[]{:S(2)}) %collective-permute-start.31) | collective-permute-done | bytes 163872 | tf_op jit(solution)/shard_map/ppermute | solution.py:29
  103.9 3.7 %collective-permute-done.32 = f32[320,128]{1,0:T(8,128)S(1)} collective-permute-done((f32[320,128]{1,0:T(8,128)S(1)}, f32[320,128]{1,0:T(8,128)S(1)}, u32[]{:S(2)}, u32[]{:S(2)}) %collective-permute-start.32) | collective-permute-done | bytes 163872 | tf_op jit(solution)/shard_map/ppermute | solution.py:29
  113.7 4.1 %collective-permute-done.39 = f32[96,128]{1,0:T(8,128)S(1)} collective-permute-done((f32[96,128]{1,0:T(8,128)S(1)}, f32[96,128]{1,0:T(8,128)S(1)}, u32[]{:S(2)}, u32[]{:S(2)}) %collective-permute-start.39) | collective-permute-done | bytes 49184 | tf_op jit(solution)/shard_map/ppermute | solution.py:29
  118.8 3.3 %collective-permute-done.34 = f32[320,128]{1,0:T(8,128)S(1)} collective-permute-done((f32[320,128]{1,0:T(8,128)S(1)}, f32[320,128]{1,0:T(8,128)S(1)}, u32[]{:S(2)}, u32[]{:S(2)}) %collective-permute-start.34) | collective-permute-done | bytes 163872 | tf_op jit(solution)/shard_map/ppermute | solution.py:29
  129.5 4.1 %collective-permute-done.42 = f32[352,128]{1,0:T(8,128)S(1)} collective-permute-done((f32[352,128]{1,0:T(8,128)S(1)}, f32[352,128]{1,0:T(8,128)S(1)}, u32[]{:S(2)}, u32[]{:S(2)}) %collective-permute-start.42) | collective-permute-done | bytes 180256 | tf_op jit(solution)/shard_map/ppermute | solution.py:29
  133.6 4.0 %collective-permute-done.43 = f32[352,128]{1,0:T(8,128)S(1)} collective-permute-done((f32[352,128]{1,0:T(8,128)S(1)}, f32[352,128]{1,0:T(8,128)S(1)}, u32[]{:S(2)}, u32[]{:S(2)}) %collective-permute-start.43) | collective-permute-done | bytes 180256 | tf_op jit(solution)/shard_map/ppermute | solution.py:29
  137.9 3.5 %collective-permute-start.46 = (f32[352,128]{1,0:T(8,128)S(1)}, f32[352,128]{1,0:T(8,128)S(1)}, u32[]{:S(2)}, u32[]{:S(2)}) collective-permute-start(f32[352,128]{1,0:T(8,128)S(1)} %bitcast.136), channel_id=1, source_target_pairs={{0,96},{1,25},{8,104},{9,1},{16,112},{17,9},{24,120},{25,17},{32,0... | collective-permute-start | bytes 540680 | tf_op jit(solution)/shard_map/ppermute | solution.py:29
  141.4 2.6 %collective-permute-done.47 = f32[352,128]{1,0:T(8,128)S(1)} collective-permute-done((f32[352,128]{1,0:T(8,128)S(1)}, f32[352,128]{1,0:T(8,128)S(1)}, u32[]{:S(2)}, u32[]{:S(2)}) %collective-permute-start.47) | collective-permute-done | bytes 180256 | tf_op jit(solution)/shard_map/ppermute | solution.py:29
  144.1 3.1 %collective-permute-done.45 = f32[352,128]{1,0:T(8,128)S(1)} collective-permute-done((f32[352,128]{1,0:T(8,128)S(1)}, f32[352,128]{1,0:T(8,128)S(1)}, u32[]{:S(2)}, u32[]{:S(2)}) %collective-permute-start.45) | collective-permute-done | bytes 180256 | tf_op jit(solution)/shard_map/ppermute | solution.py:29
  148.9 10.4 %collective-permute-done.50 = f32[1408,128]{1,0:T(8,128)S(1)} collective-permute-done((f32[1408,128]{1,0:T(8,128)S(1)}, f32[1408,128]{1,0:T(8,128)S(1)}, u32[]{:S(2)}, u32[]{:S(2)}) %collective-permute-start.50) | collective-permute-done | bytes 720928 | tf_op jit(solution)/shard_map/ppermute | solution.py:29
  159.3 3.3 %collective-permute-done.49 = f32[1408,128]{1,0:T(8,128)S(1)} collective-permute-done((f32[1408,128]{1,0:T(8,128)S(1)}, f32[1408,128]{1,0:T(8,128)S(1)}, u32[]{:S(2)}, u32[]{:S(2)}) %collective-permute-start.49) | collective-permute-done | bytes 720928 | tf_op jit(solution)/shard_map/ppermute | solution.py:29
  162.6 4.4 %collective-permute-done.48 = f32[1408,128]{1,0:T(8,128)S(1)} collective-permute-done((f32[1408,128]{1,0:T(8,128)S(1)}, f32[1408,128]{1,0:T(8,128)S(1)}, u32[]{:S(2)}, u32[]{:S(2)}) %collective-permute-start.48) | collective-permute-done | bytes 720928 | tf_op jit(solution)/shard_map/ppermute | solution.py:29
  167.0 2.6 %shard_map.76 = (f32[1,4,12,8,128]{4,3,2,1,0:T(8,128)S(1)}, f32[3,4,12,8,128]{4,3,2,1,0:T(8,128)S(1)}, f32[1,4,12,8,128]{4,3,2,1,0:T(8,128)S(1)}, f32[3,4,12,8,128]{4,3,2,1,0:T(8,128)S(1)}, f32[4,11,8,128]{3,2,1,0:T(8,128)S(1)}) custom-call(s32[912]{0:T(1024)S(1)} %concatenate.3.tab, f32[4,4,11,8,128]{4,3,2,1,0:T(8,128)S(1)} %pad_maximum_fusion.refs_0_, ...), custom_call_target="tpu_custom_call" | custom-call | tf_op jit(solution)/shard_map/pallas_call | solution.py:129
  176.3 4.5 %collective-permute-done.53 = f32[384,128]{1,0:T(8,128)S(1)} collective-permute-done((f32[384,128]{1,0:T(8,128)S(1)}, f32[384,128]{1,0:T(8,128)S(1)}, u32[]{:S(2)}, u32[]{:S(2)}) %collective-permute-start.53) | collective-permute-done | bytes 196640 | tf_op jit(solution)/shard_map/ppermute | solution.py:29
  180.8 4.5 %collective-permute-done.54 = f32[384,128]{1,0:T(8,128)S(1)} collective-permute-done((f32[384,128]{1,0:T(8,128)S(1)}, f32[384,128]{1,0:T(8,128)S(1)}, u32[]{:S(2)}, u32[]{:S(2)}) %collective-permute-start.54) | collective-permute-done | bytes 196640 | tf_op jit(solution)/shard_map/ppermute | solution.py:29
  192.2 3.2 %collective-permute-done.58 = f32[256,128]{1,0:T(8,128)S(1)} collective-permute-done((f32[256,128]{1,0:T(8,128)S(1)}, f32[256,128]{1,0:T(8,128)S(1)}, u32[]{:S(2)}, u32[]{:S(2)}) %collective-permute-start.58) | collective-permute-done | bytes 131104 | tf_op jit(solution)/shard_map/ppermute | solution.py:29
  (139 shorter events, 81.9 us)
Async XLA Ops:
  1.1 6.5 %collective-permute-start = (f32[384,128]{1,0:T(8,128)S(1)}, f32[384,128]{1,0:T(8,128)S(1)}, u32[]{:S(2)}, u32[]{:S(2)}) collective-permute-start(f32[384,128]{1,0:T(8,128)S(1)} %bitcast.216), channel_id=1, source_target_pairs={{0,1},{1,0},{2,3},{3,2},{4,5},{5,4},{6,7},{7,6},{8,9},{9,8},{10,11... | collective-permute-start | bytes 589832 | tf_op jit(solution)/shard_map/ppermute | solution.py:29
  3.9 9.5 %collective-permute-start.2 = (f32[256,128]{1,0:T(8,128)S(1)}, f32[256,128]{1,0:T(8,128)S(1)}, u32[]{:S(2)}, u32[]{:S(2)}) collective-permute-start(f32[256,128]{1,0:T(8,128)S(1)} %bitcast.193), channel_id=1, source_target_pairs={{0,4},{1,5},{2,6},{3,7},{4,0},{5,1},{6,2},{7,3},{8,12},{9,13},{10,... | collective-permute-start | bytes 393224 | tf_op jit(solution)/shard_map/ppermute | solution.py:29
  24.3 9.2 %collective-permute-start.10 = (f32[896,128]{1,0:T(8,128)S(1)}, f32[896,128]{1,0:T(8,128)S(1)}, u32[]{:S(2)}, u32[]{:S(2)}) collective-permute-start(f32[896,128]{1,0:T(8,128)S(1)} %bitcast.132), channel_id=1, source_target_pairs={{0,16},{1,65},{8,24},{9,73},{16,0},{17,81},{24,8},{25,89},{32,48},... | collective-permute-start | bytes 1376264 | tf_op jit(solution)/shard_map/ppermute | solution.py:29
  27.1 11.4 %collective-permute-start.9 = (f32[896,128]{1,0:T(8,128)S(1)}, f32[896,128]{1,0:T(8,128)S(1)}, u32[]{:S(2)}, u32[]{:S(2)}) collective-permute-start(f32[896,128]{1,0:T(8,128)S(1)} %bitcast.133), channel_id=1, source_target_pairs={{0,24},{1,97},{8,0},{9,105},{16,8},{17,113},{24,16},{25,121},{32,5... | collective-permute-start | bytes 1376264 | tf_op jit(solution)/shard_map/ppermute | solution.py:29
  28.0 10.6 %collective-permute-start.8 = (f32[896,128]{1,0:T(8,128)S(1)}, f32[896,128]{1,0:T(8,128)S(1)}, u32[]{:S(2)}, u32[]{:S(2)}) collective-permute-start(f32[896,128]{1,0:T(8,128)S(1)} %bitcast.134), channel_id=1, source_target_pairs={{0,8},{1,33},{8,16},{9,41},{16,24},{17,49},{24,0},{25,57},{32,40},... | collective-permute-start | bytes 1376264 | tf_op jit(solution)/shard_map/ppermute | solution.py:29
  40.3 7.4 %collective-permute-start.11 = (f32[768,128]{1,0:T(8,128)S(1)}, f32[768,128]{1,0:T(8,128)S(1)}, u32[]{:S(2)}, u32[]{:S(2)}) collective-permute-start(f32[768,128]{1,0:T(8,128)S(1)} %bitcast.215), channel_id=1, source_target_pairs={{0,1},{1,0},{2,3},{3,2},{4,5},{5,4},{6,7},{7,6},{8,9},{9,8},{10,11... | collective-permute-start | bytes 1179656 | tf_op jit(solution)/shard_map/ppermute | solution.py:29
  47.8 6.8 %collective-permute-start.14 = (f32[256,128]{1,0:T(8,128)S(1)}, f32[256,128]{1,0:T(8,128)S(1)}, u32[]{:S(2)}, u32[]{:S(2)}) collective-permute-start(f32[256,128]{1,0:T(8,128)S(1)} %bitcast.237), channel_id=1, source_target_pairs={{0,2},{1,7},{2,0},{3,5},{4,6},{5,3},{6,4},{7,1},{8,10},{9,15},{10,... | collective-permute-start | bytes 393224 | tf_op jit(solution)/shard_map/ppermute | solution.py:29
  55.0 8.3 %collective-permute-start.17 = (f32[256,128]{1,0:T(8,128)S(1)}, f32[256,128]{1,0:T(8,128)S(1)}, u32[]{:S(2)}, u32[]{:S(2)}) collective-permute-start(f32[256,128]{1,0:T(8,128)S(1)} %bitcast.148), channel_id=1, source_target_pairs={{0,16},{8,0},{32,8},{40,32},{64,40},{72,64},{96,72},{104,96},{120,... | collective-permute-start | bytes 393224 | tf_op jit(solution)/shard_map/ppermute | solution.py:29
  57.6 9.5 %collective-permute-start.16 = (f32[256,128]{1,0:T(8,128)S(1)}, f32[256,128]{1,0:T(8,128)S(1)}, u32[]{:S(2)}, u32[]{:S(2)}) collective-permute-start(f32[256,128]{1,0:T(8,128)S(1)} %bitcast.149), channel_id=1, source_target_pairs={{0,8},{8,32},{32,40},{40,64},{64,72},{72,96},{96,104},{104,120},{1... | collective-permute-start | bytes 393224 | tf_op jit(solution)/shard_map/ppermute | solution.py:29
  71.6 6.6 %collective-permute-start.22 = (f32[288,128]{1,0:T(8,128)S(1)}, f32[288,128]{1,0:T(8,128)S(1)}, u32[]{:S(2)}, u32[]{:S(2)}) collective-permute-start(f32[288,128]{1,0:T(8,128)S(1)} %bitcast.180), channel_id=1, source_target_pairs={{0,4},{1,5},{2,6},{3,7},{4,0},{5,1},{6,2},{7,3},{8,12},{9,13},{10,... | collective-permute-start | bytes 442376 | tf_op jit(solution)/shard_map/ppermute | solution.py:29
  74.1 7.6 %collective-permute-start.23 = (f32[288,128]{1,0:T(8,128)S(1)}, f32[288,128]{1,0:T(8,128)S(1)}, u32[]{:S(2)}, u32[]{:S(2)}) collective-permute-start(f32[288,128]{1,0:T(8,128)S(1)} %bitcast.228), channel_id=1, source_target_pairs={{0,2},{1,7},{2,0},{3,5},{4,6},{5,3},{6,4},{7,1},{8,10},{9,15},{10,... | collective-permute-start | bytes 442376 | tf_op jit(solution)/shard_map/ppermute | solution.py:29
  75.3 6.7 %collective-permute-start.24 = (f32[288,128]{1,0:T(8,128)S(1)}, f32[288,128]{1,0:T(8,128)S(1)}, u32[]{:S(2)}, u32[]{:S(2)}) collective-permute-start(f32[288,128]{1,0:T(8,128)S(1)} %bitcast.227), channel_id=1, source_target_pairs={{0,6},{1,3},{2,4},{3,1},{4,2},{5,7},{6,0},{7,5},{8,14},{9,11},{10,... | collective-permute-start | bytes 442376 | tf_op jit(solution)/shard_map/ppermute | solution.py:29
  82.1 7.0 %collective-permute-start.26 = (f32[288,128]{1,0:T(8,128)S(1)}, f32[288,128]{1,0:T(8,128)S(1)}, u32[]{:S(2)}, u32[]{:S(2)}) collective-permute-start(f32[288,128]{1,0:T(8,128)S(1)} %bitcast.145), channel_id=1, source_target_pairs={{0,16},{8,0},{32,8},{40,32},{64,40},{72,64},{96,72},{104,96},{120,... | collective-permute-start | bytes 442376 | tf_op jit(solution)/shard_map/ppermute | solution.py:29
  82.2 9.2 %collective-permute-start.25 = (f32[288,128]{1,0:T(8,128)S(1)}, f32[288,128]{1,0:T(8,128)S(1)}, u32[]{:S(2)}, u32[]{:S(2)}) collective-permute-start(f32[288,128]{1,0:T(8,128)S(1)} %bitcast.146), channel_id=1, source_target_pairs={{0,8},{8,32},{32,40},{40,64},{64,72},{72,96},{96,104},{104,120},{1... | collective-permute-start | bytes 442376 | tf_op jit(solution)/shard_map/ppermute | solution.py:29
  92.6 6.6 %collective-permute-start.29 = (f32[960,128]{1,0:T(8,128)S(1)}, f32[960,128]{1,0:T(8,128)S(1)}, u32[]{:S(2)}, u32[]{:S(2)}) collective-permute-start(f32[960,128]{1,0:T(8,128)S(1)} %bitcast.213), channel_id=1, source_target_pairs={{0,1},{1,0},{2,3},{3,2},{4,5},{5,4},{6,7},{7,6},{8,9},{9,8},{10,11... | collective-permute-start | bytes 1474568 | tf_op jit(solution)/shard_map/ppermute | solution.py:29
  96.9 7.0 %collective-permute-start.31 = (f32[320,128]{1,0:T(8,128)S(1)}, f32[320,128]{1,0:T(8,128)S(1)}, u32[]{:S(2)}, u32[]{:S(2)}) collective-permute-start(f32[320,128]{1,0:T(8,128)S(1)} %bitcast.174), channel_id=1, source_target_pairs={{0,4},{1,5},{2,6},{3,7},{4,0},{5,1},{6,2},{7,3},{8,12},{9,13},{10,... | collective-permute-start | bytes 491528 | tf_op jit(solution)/shard_map/ppermute | solution.py:29
  99.3 8.3 %collective-permute-start.32 = (f32[320,128]{1,0:T(8,128)S(1)}, f32[320,128]{1,0:T(8,128)S(1)}, u32[]{:S(2)}, u32[]{:S(2)}) collective-permute-start(f32[320,128]{1,0:T(8,128)S(1)} %bitcast.225), channel_id=1, source_target_pairs={{0,2},{1,7},{2,0},{3,5},{4,6},{5,3},{6,4},{7,1},{8,10},{9,15},{10,... | collective-permute-start | bytes 491528 | tf_op jit(solution)/shard_map/ppermute | solution.py:29
  100.5 7.4 %collective-permute-start.33 = (f32[320,128]{1,0:T(8,128)S(1)}, f32[320,128]{1,0:T(8,128)S(1)}, u32[]{:S(2)}, u32[]{:S(2)}) collective-permute-start(f32[320,128]{1,0:T(8,128)S(1)} %bitcast.224), channel_id=1, source_target_pairs={{0,6},{1,3},{2,4},{3,1},{4,2},{5,7},{6,0},{7,5},{8,14},{9,11},{10,... | collective-permute-start | bytes 491528 | tf_op jit(solution)/shard_map/ppermute | solution.py:29
  109.3 9.5 %collective-permute-start.35 = (f32[320,128]{1,0:T(8,128)S(1)}, f32[320,128]{1,0:T(8,128)S(1)}, u32[]{:S(2)}, u32[]{:S(2)}) collective-permute-start(f32[320,128]{1,0:T(8,128)S(1)} %bitcast.142), channel_id=1, source_target_pairs={{0,16},{8,0},{32,8},{40,32},{64,40},{72,64},{96,72},{104,96},{120,... | collective-permute-start | bytes 491528 | tf_op jit(solution)/shard_map/ppermute | solution.py:29
  109.5 12.7 %collective-permute-start.34 = (f32[320,128]{1,0:T(8,128)S(1)}, f32[320,128]{1,0:T(8,128)S(1)}, u32[]{:S(2)}, u32[]{:S(2)}) collective-permute-start(f32[320,128]{1,0:T(8,128)S(1)} %bitcast.143), channel_id=1, source_target_pairs={{0,8},{8,32},{32,40},{40,64},{64,72},{72,96},{96,104},{104,120},{1... | collective-permute-start | bytes 491528 | tf_op jit(solution)/shard_map/ppermute | solution.py:29
  110.8 8.0 %collective-permute-start.37 = (f32[256,128]{1,0:T(8,128)S(1)}, f32[256,128]{1,0:T(8,128)S(1)}, u32[]{:S(2)}, u32[]{:S(2)}) collective-permute-start(f32[256,128]{1,0:T(8,128)S(1)} %bitcast.233), channel_id=1, source_target_pairs={{0,24},{8,16},{32,0},{40,8},{64,32},{72,40},{96,64},{104,72},{120,... | collective-permute-start | bytes 393224 | tf_op jit(solution)/shard_map/ppermute | solution.py:29
  110.8 8.0 %collective-permute-start.36 = (f32[256,128]{1,0:T(8,128)S(1)}, f32[256,128]{1,0:T(8,128)S(1)}, u32[]{:S(2)}, u32[]{:S(2)}) collective-permute-start(f32[256,128]{1,0:T(8,128)S(1)} %bitcast.232), channel_id=1, source_target_pairs={{0,32},{8,40},{32,64},{40,72},{64,96},{72,104},{96,120},{104,112},... | collective-permute-start | bytes 393224 | tf_op jit(solution)/shard_map/ppermute | solution.py:29
  126.3 7.3 %collective-permute-start.42 = (f32[352,128]{1,0:T(8,128)S(1)}, f32[352,128]{1,0:T(8,128)S(1)}, u32[]{:S(2)}, u32[]{:S(2)}) collective-permute-start(f32[352,128]{1,0:T(8,128)S(1)} %bitcast.170), channel_id=1, source_target_pairs={{0,4},{1,5},{2,6},{3,7},{4,0},{5,1},{6,2},{7,3},{8,12},{9,13},{10,... | collective-permute-start | bytes 540680 | tf_op jit(solution)/shard_map/ppermute | solution.py:29
  128.1 9.5 %collective-permute-start.43 = (f32[352,128]{1,0:T(8,128)S(1)}, f32[352,128]{1,0:T(8,128)S(1)}, u32[]{:S(2)}, u32[]{:S(2)}) collective-permute-start(f32[352,128]{1,0:T(8,128)S(1)} %bitcast.223), channel_id=1, source_target_pairs={{0,2},{1,7},{2,0},{3,5},{4,6},{5,3},{6,4},{7,1},{8,10},{9,15},{10,... | collective-permute-start | bytes 540680 | tf_op jit(solution)/shard_map/ppermute | solution.py:29
  129.4 8.3 %collective-permute-start.44 = (f32[352,128]{1,0:T(8,128)S(1)}, f32[352,128]{1,0:T(8,128)S(1)}, u32[]{:S(2)}, u32[]{:S(2)}) collective-permute-start(f32[352,128]{1,0:T(8,128)S(1)} %bitcast.221), channel_id=1, source_target_pairs={{0,6},{1,3},{2,4},{3,1},{4,2},{5,7},{6,0},{7,5},{8,14},{9,11},{10,... | collective-permute-start | bytes 540680 | tf_op jit(solution)/shard_map/ppermute | solution.py:29
  147.3 12.1 %collective-permute-start.50 = (f32[1408,128]{1,0:T(8,128)S(1)}, f32[1408,128]{1,0:T(8,128)S(1)}, u32[]{:S(2)}, u32[]{:S(2)}) collective-permute-start(f32[1408,128]{1,0:T(8,128)S(1)} %bitcast.129), channel_id=1, source_target_pairs={{0,16},{1,65},{8,24},{9,73},{16,0},{17,81},{24,8},{25,89},{32,48},... | collective-permute-start | bytes 2162696 | tf_op jit(solution)/shard_map/ppermute | solution.py:29
  147.4 15.3 %collective-permute-start.49 = (f32[1408,128]{1,0:T(8,128)S(1)}, f32[1408,128]{1,0:T(8,128)S(1)}, u32[]{:S(2)}, u32[]{:S(2)}) collective-permute-start(f32[1408,128]{1,0:T(8,128)S(1)} %bitcast.130), channel_id=1, source_target_pairs={{0,24},{1,97},{8,0},{9,105},{16,8},{17,113},{24,16},{25,121},{32,5... | collective-permute-start | bytes 2162696 | tf_op jit(solution)/shard_map/ppermute | solution.py:29
  147.8 19.2 %collective-permute-start.48 = (f32[1408,128]{1,0:T(8,128)S(1)}, f32[1408,128]{1,0:T(8,128)S(1)}, u32[]{:S(2)}, u32[]{:S(2)}) collective-permute-start(f32[1408,128]{1,0:T(8,128)S(1)} %bitcast.131), channel_id=1, source_target_pairs={{0,8},{1,33},{8,16},{9,41},{16,24},{17,49},{24,0},{25,57},{32,40},... | collective-permute-start | bytes 2162696 | tf_op jit(solution)/shard_map/ppermute | solution.py:29
  173.1 7.7 %collective-permute-start.53 = (f32[384,128]{1,0:T(8,128)S(1)}, f32[384,128]{1,0:T(8,128)S(1)}, u32[]{:S(2)}, u32[]{:S(2)}) collective-permute-start(f32[384,128]{1,0:T(8,128)S(1)} %bitcast.165), channel_id=1, source_target_pairs={{0,4},{1,5},{2,6},{3,7},{4,0},{5,1},{6,2},{7,3},{8,12},{9,13},{10,... | collective-permute-start | bytes 589832 | tf_op jit(solution)/shard_map/ppermute | solution.py:29
  175.0 10.4 %collective-permute-start.54 = (f32[384,128]{1,0:T(8,128)S(1)}, f32[384,128]{1,0:T(8,128)S(1)}, u32[]{:S(2)}, u32[]{:S(2)}) collective-permute-start(f32[384,128]{1,0:T(8,128)S(1)} %bitcast.220), channel_id=1, source_target_pairs={{0,2},{1,7},{2,0},{3,5},{4,6},{5,3},{6,4},{7,1},{8,10},{9,15},{10,... | collective-permute-start | bytes 589832 | tf_op jit(solution)/shard_map/ppermute | solution.py:29
  176.2 9.2 %collective-permute-start.55 = (f32[384,128]{1,0:T(8,128)S(1)}, f32[384,128]{1,0:T(8,128)S(1)}, u32[]{:S(2)}, u32[]{:S(2)}) collective-permute-start(f32[384,128]{1,0:T(8,128)S(1)} %bitcast.218), channel_id=1, source_target_pairs={{0,6},{1,3},{2,4},{3,1},{4,2},{5,7},{6,0},{7,5},{8,14},{9,11},{10,... | collective-permute-start | bytes 589832 | tf_op jit(solution)/shard_map/ppermute | solution.py:29
  190.8 6.9 %collective-permute-start.59 = (f32[256,128]{1,0:T(8,128)S(1)}, f32[256,128]{1,0:T(8,128)S(1)}, u32[]{:S(2)}, u32[]{:S(2)}) collective-permute-start(f32[256,128]{1,0:T(8,128)S(1)} %bitcast.238), channel_id=1, source_target_pairs={{0,2},{1,7},{2,0},{3,5},{4,6},{5,3},{6,4},{7,1},{8,10},{9,15},{10,... | collective-permute-start | bytes 393224 | tf_op jit(solution)/shard_map/ppermute | solution.py:29
  (34 other events, 133.8 us)

commit v12 on v11

--- a/solution.py
+++ b/solution.py
@@ -27,10 +27,6 @@
 def permute(value, axes, pairs):
     flat = value.reshape(-1, 128)
     return lax.ppermute(flat, axes, pairs).reshape(value.shape)
-
-
-def ring_shift(value, k):
-    return permute(value, "row", [(RING[p], RING[(p + k) % 16]) for p in range(16)])
 
 
 def outward(value, d):
@@ -267,7 +263,11 @@
     far = outermost(w) is not None
     n = 1 + len(pieces) + far
     ins, own, oth = refs[:n], refs[n : n + 2], refs[n + 2 : n + 4]
-    hi_ref, lo_ref, p_ref = refs[n + 4 :]
+    (hi_ref, lo_ref, p_ref), sides = refs[n + 4 : n + 7], refs[n + 7 :]
+    h = lax.axis_index("layer")
+    for k, side in enumerate(sides):
+        side[h] = ins[1 + 2 * k][...]
+        side[1 - h] = ins[2 + 2 * k][...]
 
     def strip_of(b):
         off = b - w
@@ -277,7 +277,7 @@
         at = [piece[0] for piece in pieces].index(d)
         _, (lo, hi, first, last) = pieces[at]
         row = off + 4 * d - lo
-        return b, [ins[1 + at][row, t] for t in range(last - first)], first
+        return b, [sides[at // 2][at % 2, row, t] for t in range(last - first)], first
 
     def far_strip(b, core, slab):
         mine = jnp.where(lax.axis_index("layer") == core, 1.0, 0.0)
@@ -377,7 +377,12 @@
 
 def close_kernel(step, cuts, far, p0, p1, p2, p3, cur_ref, keep_ref, coef_ref, *refs):
     w = BAND + step
+    h = lax.axis_index("layer")
     low = low_half()
+    n = len(cuts) + (far > 0)
+    out_ref, sent, kept = refs[0], refs[1 : 1 + 2 * n], refs[1 + 2 * n :]
+    if far:
+        cuts = cuts + [((3, 4, w + 2 - far, w + 2), (0, 1, 0, far))]
     for e in range(4):
         turned = [swap_halves(cur_ref[e, t]) for t in range(w + 1)]
         zero = jnp.zeros((8, 128), F32)
@@ -387,17 +392,14 @@
             cur = jnp.where(low, before, after)
             square = total((p0, p1, p2, p3), e, m)
             value = polynomial(coef_ref, step, cur, square) * keep_ref[e, m]
-            for ref, (lo, hi, first, last) in zip(refs, cuts):
-                if lo <= e < hi and first <= m < last:
-                    ref[e - lo, m - first] = value
-            if far and e == 3 and m >= w + 2 - far:
-                refs[-1][0, m - (w + 2 - far)] = value
-            if far and e == 0 and m < far:
-                refs[-1][1, m] = value
-    if far:
-        own_ref, oth_ref, far_ref = refs[-3:]
-        own_ref[...] = far_ref[lax.axis_index("layer")]
-        oth_ref[...] = far_ref[1 - lax.axis_index("layer")]
+            out_ref[e, m] = value
+            for ref, pair in zip(kept, cuts):
+                for side, (lo, hi, first, last) in enumerate(pair):
+                    if lo <= e < hi and first <= m < last:
+                        ref[side, e - lo, m - first] = value
+    for k, ref in enumerate(kept):
+        sent[2 * k][...] = ref[h]
+        sent[2 * k + 1][...] = ref[1 - h]
 
 
 def finish_kernel(tab, p0, p1, p2, p3, cur_ref, keep_ref, coef_ref, *refs):
@@ -509,25 +511,27 @@
             )
         else:
             kernel = lambda *refs, w=w, pieces=pieces: step_kernel(w, pieces, *refs)
+            for _, (lo, hi, first, last) in pieces[::2]:
+                scratch.append(pltpu.VMEM((2, hi - lo, last - first, 8, 128), F32))
             sums = call(kernel, part, [cur] + around, scratch)
         parts = reduce_group(sums)
         pieces = halo_pieces(w + 1) if step < STEPS - 2 else []
-        cuts = [(0, 4, 0, w + 2)]
-        for _, cut in pieces:
-            if cut not in cuts:
-                cuts.append(cut)
+        cuts = [(pieces[k][1], pieces[k + 1][1]) for k in range(2, len(pieces), 2)]
         far = far_tiles(w + 1) if pieces and outermost(w + 1) else 0
         kernel = lambda *refs, step=step, cuts=cuts, far=far: close_kernel(step, cuts, far, *refs)
-        shapes = [(hi - lo, last - first, 8, 128) for lo, hi, first, last in cuts]
-        scratch = [pltpu.VMEM((2, far, 8, 128), F32)] if far else []
-        shapes += [(far, 8, 128)] * 2 if far else []
-        sent = call(kernel, shapes, parts + [cur, keep[step + 1], coef], scratch)
-        cur = sent[0]
-        around = [ring_shift(sent[cuts.index(cut)], d) for d, cut in pieces]
-        if far:
-            both = jnp.stack([sent[-2], core_swap(sent[-1])])
-            around.append(outward(both, outermost(w + 1)))
-        cur, *around = lax.optimization_barrier((cur, *around))
+        shapes = [(hi - lo, last - first, 8, 128) for (lo, hi, first, last), _ in cuts]
+        shapes += [(1, far, 8, 128)] if far else []
+        outs = [(4, w + 2, 8, 128)] + [shape for shape in shapes for _ in (0, 1)]
+        scratch = [pltpu.VMEM((2,) + shape, F32) for shape in shapes]
+        cur, *sent = call(kernel, outs, parts + [cur, keep[step + 1], coef], scratch)
+        if pieces:
+            around = [outward(cur, 1), outward(cur, -1)]
+            for k in range(len(cuts)):
+                around += [outward(sent[2 * k], k + 2), outward(sent[2 * k + 1], -k - 2)]
+            if far:
+                both = jnp.stack([sent[-2][0], core_swap(sent[-1])[0]])
+                around.append(outward(both, outermost(w + 1)))
+            cur, *around = lax.optimization_barrier((cur, *around))
     gathered = gather_rows(cur)
     w = BAND + STEPS - 1
     part = in_parts((4, w + 2, 8, 128))

time: 199 us -> 200 us (level)
  starting transfers between devices: 65.6 us -> 73.1 us
  waiting for transfers between devices: 115 us -> 108 us
    ppermute x61, starting transfers between devices: 65.6 us -> 73.1 us  [permute(): return lax.ppermute(flat, axes, pairs).reshape(value.shape)]
    ppermute x61, waiting for transfers between devices: 115 us -> 108 us  [permute(): return lax.ppermute(flat, axes, pairs).reshape(value.shape)]
  transfers between devices with their start and end apart: 61 -> 61, of which waited for: 45 -> 41; matrix products, arithmetic and copies ran while one was open for 1% -> 1% of each run, Pallas kernels for 1% -> 1%
where the time goes in v12:
time: 200 us
  waiting for transfers between devices  108 us (54%)
  starting transfers between devices  73.1 us (37%)
  Pallas kernels  14 us (7%)
  local copies, waits for them, and re-layouts  3.67 us (2%)
    ppermute x61, waiting for transfers between devices, permute(): return lax.ppermute(flat, axes, pairs).reshape(value.shape)  108 us
    ppermute x61, starting transfers between devices, permute(): return lax.ppermute(flat, axes, pairs).reshape(value.shape)  73.1 us
    pallas_call x28, Pallas kernels, call(): pl.pallas_call(kernel, out_shape=[jax.ShapeDtypeStruct(o, F32) for o in o...  14 us
  transfers between devices with their start and end apart: 61, of which 41 were waited for; matrix products, arithmetic and copies ran while one was open for 1% of the time, Pallas kernels for 1%

profile of v12, /device:TPU:1, one launch (start us, length us, event | category | flops | bytes accessed | tf_op | source)
XLA Modules:
  0.0 200.1 jit_solution(11324502071763575586)
XLA Ops:
  3.9 3.8 %collective-permute-start.2 = (f32[256,128]{1,0:T(8,128)S(1)}, f32[256,128]{1,0:T(8,128)S(1)}, u32[]{:S(2)}, u32[]{:S(2)}) collective-permute-start(f32[256,128]{1,0:T(8,128)S(1)} %bitcast.192), channel_id=1, source_target_pairs={{0,4},{1,5},{2,6},{3,7},{4,0},{5,1},{6,2},{7,3},{8,12},{9,13},{10,... | collective-permute-start | bytes 393224 | tf_op jit(solution)/shard_map/ppermute | solution.py:29
  15.7 3.0 %collective-permute-start.7 = (f32[224,128]{1,0:T(8,128)S(1)}, f32[224,128]{1,0:T(8,128)S(1)}, u32[]{:S(2)}, u32[]{:S(2)}) collective-permute-start(f32[224,128]{1,0:T(8,128)S(1)} %bitcast.153), channel_id=1, source_target_pairs={{0,64},{1,17},{8,72},{9,25},{16,80},{17,1},{24,88},{25,9},{32,96},... | collective-permute-start | bytes 344072 | tf_op jit(solution)/shard_map/ppermute | solution.py:29
  24.3 2.8 %collective-permute-start.10 = (f32[896,128]{1,0:T(8,128)S(1)}, f32[896,128]{1,0:T(8,128)S(1)}, u32[]{:S(2)}, u32[]{:S(2)}) collective-permute-start(f32[896,128]{1,0:T(8,128)S(1)} %bitcast.131), channel_id=1, source_target_pairs={{0,16},{1,65},{8,24},{9,73},{16,0},{17,81},{24,8},{25,89},{32,48},... | collective-permute-start | bytes 1376264 | tf_op jit(solution)/shard_map/ppermute | solution.py:29
  28.6 4.9 %collective-permute-done.10 = f32[896,128]{1,0:T(8,128)S(1)} collective-permute-done((f32[896,128]{1,0:T(8,128)S(1)}, f32[896,128]{1,0:T(8,128)S(1)}, u32[]{:S(2)}, u32[]{:S(2)}) %collective-permute-start.10) | collective-permute-done | bytes 458784 | tf_op jit(solution)/shard_map/ppermute | solution.py:29
  33.5 5.0 %collective-permute-done.9 = f32[896,128]{1,0:T(8,128)S(1)} collective-permute-done((f32[896,128]{1,0:T(8,128)S(1)}, f32[896,128]{1,0:T(8,128)S(1)}, u32[]{:S(2)}, u32[]{:S(2)}) %collective-permute-start.9) | collective-permute-done | bytes 458784 | tf_op jit(solution)/shard_map/ppermute | solution.py:29
  40.3 3.9 %collective-permute-start.11 = (f32[768,128]{1,0:T(8,128)S(1)}, f32[768,128]{1,0:T(8,128)S(1)}, u32[]{:S(2)}, u32[]{:S(2)}) collective-permute-start(f32[768,128]{1,0:T(8,128)S(1)} %bitcast.213), channel_id=1, source_target_pairs={{0,1},{1,0},{2,3},{3,2},{4,5},{5,4},{6,7},{7,6},{8,9},{9,8},{10,11... | collective-permute-start | bytes 1179656 | tf_op jit(solution)/shard_map/ppermute | solution.py:29
  49.1 3.0 %collective-permute-done.13 = f32[256,128]{1,0:T(8,128)S(1)} collective-permute-done((f32[256,128]{1,0:T(8,128)S(1)}, f32[256,128]{1,0:T(8,128)S(1)}, u32[]{:S(2)}, u32[]{:S(2)}) %collective-permute-start.13) | collective-permute-done | bytes 131104 | tf_op jit(solution)/shard_map/ppermute | solution.py:29
  58.0 2.7 %collective-permute-start.18 = (f32[144,128]{1,0:T(8,128)S(1)}, f32[144,128]{1,0:T(8,128)S(1)}, u32[]{:S(2)}, u32[]{:S(2)}) collective-permute-start(f32[144,128]{1,0:T(8,128)S(1)} %bitcast.239), channel_id=1, source_target_pairs={{0,32},{1,25},{8,40},{9,17},{32,64},{33,1},{40,72},{41,9},{64,96},... | collective-permute-start | bytes 221192 | tf_op jit(solution)/shard_map/ppermute | solution.py:29
  64.9 4.4 %collective-permute-start.20 = (f32[864,128]{1,0:T(8,128)S(1)}, f32[864,128]{1,0:T(8,128)S(1)}, u32[]{:S(2)}, u32[]{:S(2)}) collective-permute-start(f32[864,128]{1,0:T(8,128)S(1)} %bitcast.212), channel_id=1, source_target_pairs={{0,1},{1,0},{2,3},{3,2},{4,5},{5,4},{6,7},{7,6},{8,9},{9,8},{10,11... | collective-permute-start | bytes 1327112 | tf_op jit(solution)/shard_map/ppermute | solution.py:29
  70.9 2.5 %collective-permute-start.22 = (f32[288,128]{1,0:T(8,128)S(1)}, f32[288,128]{1,0:T(8,128)S(1)}, u32[]{:S(2)}, u32[]{:S(2)}) collective-permute-start(f32[288,128]{1,0:T(8,128)S(1)} %bitcast.179), channel_id=1, source_target_pairs={{0,4},{1,5},{2,6},{3,7},{4,0},{5,1},{6,2},{7,3},{8,12},{9,13},{10,... | collective-permute-start | bytes 442376 | tf_op jit(solution)/shard_map/ppermute | solution.py:29
  75.1 2.5 %collective-permute-done.22 = f32[288,128]{1,0:T(8,128)S(1)} collective-permute-done((f32[288,128]{1,0:T(8,128)S(1)}, f32[288,128]{1,0:T(8,128)S(1)}, u32[]{:S(2)}, u32[]{:S(2)}) %collective-permute-start.22) | collective-permute-done | bytes 147488 | tf_op jit(solution)/shard_map/ppermute | solution.py:29
  77.6 3.6 %collective-permute-done.23 = f32[288,128]{1,0:T(8,128)S(1)} collective-permute-done((f32[288,128]{1,0:T(8,128)S(1)}, f32[288,128]{1,0:T(8,128)S(1)}, u32[]{:S(2)}, u32[]{:S(2)}) %collective-permute-start.23) | collective-permute-done | bytes 147488 | tf_op jit(solution)/shard_map/ppermute | solution.py:29
  81.7 3.0 %collective-permute-start.25 = (f32[288,128]{1,0:T(8,128)S(1)}, f32[288,128]{1,0:T(8,128)S(1)}, u32[]{:S(2)}, u32[]{:S(2)}) collective-permute-start(f32[288,128]{1,0:T(8,128)S(1)} %bitcast.145), channel_id=1, source_target_pairs={{0,8},{1,17},{8,32},{9,1},{32,40},{33,9},{40,64},{41,33},{64,72},{... | collective-permute-start | bytes 442376 | tf_op jit(solution)/shard_map/ppermute | solution.py:29
  84.7 2.7 %collective-permute-start.27 = (f32[224,128]{1,0:T(8,128)S(1)}, f32[224,128]{1,0:T(8,128)S(1)}, u32[]{:S(2)}, u32[]{:S(2)}) collective-permute-start(f32[224,128]{1,0:T(8,128)S(1)} %bitcast.237), channel_id=1, source_target_pairs={{0,32},{1,25},{8,40},{9,17},{32,64},{33,1},{40,72},{41,9},{64,96},... | collective-permute-start | bytes 344072 | tf_op jit(solution)/shard_map/ppermute | solution.py:29
  87.4 5.9 %collective-permute-done.28 = f32[224,128]{1,0:T(8,128)S(1)} collective-permute-done((f32[224,128]{1,0:T(8,128)S(1)}, f32[224,128]{1,0:T(8,128)S(1)}, u32[]{:S(2)}, u32[]{:S(2)}) %collective-permute-start.28) | collective-permute-done | bytes 114720 | tf_op jit(solution)/shard_map/ppermute | solution.py:29
  97.1 2.5 %collective-permute-start.31 = (f32[320,128]{1,0:T(8,128)S(1)}, f32[320,128]{1,0:T(8,128)S(1)}, u32[]{:S(2)}, u32[]{:S(2)}) collective-permute-start(f32[320,128]{1,0:T(8,128)S(1)} %bitcast.173), channel_id=1, source_target_pairs={{0,4},{1,5},{2,6},{3,7},{4,0},{5,1},{6,2},{7,3},{8,12},{9,13},{10,... | collective-permute-start | bytes 491528 | tf_op jit(solution)/shard_map/ppermute | solution.py:29
  101.0 3.1 %collective-permute-done.31 = f32[320,128]{1,0:T(8,128)S(1)} collective-permute-done((f32[320,128]{1,0:T(8,128)S(1)}, f32[320,128]{1,0:T(8,128)S(1)}, u32[]{:S(2)}, u32[]{:S(2)}) %collective-permute-start.31) | collective-permute-done | bytes 163872 | tf_op jit(solution)/shard_map/ppermute | solution.py:29
  104.1 3.8 %collective-permute-done.32 = f32[320,128]{1,0:T(8,128)S(1)} collective-permute-done((f32[320,128]{1,0:T(8,128)S(1)}, f32[320,128]{1,0:T(8,128)S(1)}, u32[]{:S(2)}, u32[]{:S(2)}) %collective-permute-start.32) | collective-permute-done | bytes 163872 | tf_op jit(solution)/shard_map/ppermute | solution.py:29
  110.1 2.6 %collective-permute-start.34 = (f32[320,128]{1,0:T(8,128)S(1)}, f32[320,128]{1,0:T(8,128)S(1)}, u32[]{:S(2)}, u32[]{:S(2)}) collective-permute-start(f32[320,128]{1,0:T(8,128)S(1)} %bitcast.142), channel_id=1, source_target_pairs={{0,8},{1,17},{8,32},{9,1},{32,40},{33,9},{40,64},{41,33},{64,72},{... | collective-permute-start | bytes 491528 | tf_op jit(solution)/shard_map/ppermute | solution.py:29
  112.7 2.7 %collective-permute-start.36 = (f32[256,128]{1,0:T(8,128)S(1)}, f32[256,128]{1,0:T(8,128)S(1)}, u32[]{:S(2)}, u32[]{:S(2)}) collective-permute-start(f32[256,128]{1,0:T(8,128)S(1)} %bitcast.230), channel_id=1, source_target_pairs={{0,32},{1,25},{8,40},{9,17},{32,64},{33,1},{40,72},{41,9},{64,96},... | collective-permute-start | bytes 393224 | tf_op jit(solution)/shard_map/ppermute | solution.py:29
  115.5 4.1 %collective-permute-done.39 = f32[96,128]{1,0:T(8,128)S(1)} collective-permute-done((f32[96,128]{1,0:T(8,128)S(1)}, f32[96,128]{1,0:T(8,128)S(1)}, u32[]{:S(2)}, u32[]{:S(2)}) %collective-permute-start.39) | collective-permute-done | bytes 49184 | tf_op jit(solution)/shard_map/ppermute | solution.py:29
  119.6 3.0 %collective-permute-done.37 = f32[256,128]{1,0:T(8,128)S(1)} collective-permute-done((f32[256,128]{1,0:T(8,128)S(1)}, f32[256,128]{1,0:T(8,128)S(1)}, u32[]{:S(2)}, u32[]{:S(2)}) %collective-permute-start.37) | collective-permute-done | bytes 131104 | tf_op jit(solution)/shard_map/ppermute | solution.py:29
  130.6 4.1 %collective-permute-done.42 = f32[352,128]{1,0:T(8,128)S(1)} collective-permute-done((f32[352,128]{1,0:T(8,128)S(1)}, f32[352,128]{1,0:T(8,128)S(1)}, u32[]{:S(2)}, u32[]{:S(2)}) %collective-permute-start.42) | collective-permute-done | bytes 180256 | tf_op jit(solution)/shard_map/ppermute | solution.py:29
  134.7 4.0 %collective-permute-done.43 = f32[352,128]{1,0:T(8,128)S(1)} collective-permute-done((f32[352,128]{1,0:T(8,128)S(1)}, f32[352,128]{1,0:T(8,128)S(1)}, u32[]{:S(2)}, u32[]{:S(2)}) %collective-permute-start.43) | collective-permute-done | bytes 180256 | tf_op jit(solution)/shard_map/ppermute | solution.py:29
  142.1 3.0 %collective-permute-done.47 = f32[352,128]{1,0:T(8,128)S(1)} collective-permute-done((f32[352,128]{1,0:T(8,128)S(1)}, f32[352,128]{1,0:T(8,128)S(1)}, u32[]{:S(2)}, u32[]{:S(2)}) %collective-permute-start.47) | collective-permute-done | bytes 180256 | tf_op jit(solution)/shard_map/ppermute | solution.py:29
  145.4 2.5 %collective-permute-done.45 = f32[352,128]{1,0:T(8,128)S(1)} collective-permute-done((f32[352,128]{1,0:T(8,128)S(1)}, f32[352,128]{1,0:T(8,128)S(1)}, u32[]{:S(2)}, u32[]{:S(2)}) %collective-permute-start.45) | collective-permute-done | bytes 180256 | tf_op jit(solution)/shard_map/ppermute | solution.py:29
  149.6 10.4 %collective-permute-done.50 = f32[1408,128]{1,0:T(8,128)S(1)} collective-permute-done((f32[1408,128]{1,0:T(8,128)S(1)}, f32[1408,128]{1,0:T(8,128)S(1)}, u32[]{:S(2)}, u32[]{:S(2)}) %collective-permute-start.50) | collective-permute-done | bytes 720928 | tf_op jit(solution)/shard_map/ppermute | solution.py:29
  160.1 6.2 %collective-permute-done.49 = f32[1408,128]{1,0:T(8,128)S(1)} collective-permute-done((f32[1408,128]{1,0:T(8,128)S(1)}, f32[1408,128]{1,0:T(8,128)S(1)}, u32[]{:S(2)}, u32[]{:S(2)}) %collective-permute-start.49) | collective-permute-done | bytes 720928 | tf_op jit(solution)/shard_map/ppermute | solution.py:29
  167.8 2.6 %shard_map.76 = (f32[1,4,12,8,128]{4,3,2,1,0:T(8,128)S(1)}, f32[3,4,12,8,128]{4,3,2,1,0:T(8,128)S(1)}, f32[1,4,12,8,128]{4,3,2,1,0:T(8,128)S(1)}, f32[3,4,12,8,128]{4,3,2,1,0:T(8,128)S(1)}, f32[4,11,8,128]{3,2,1,0:T(8,128)S(1)}) custom-call(s32[912]{0:T(1024)S(1)} %concatenate.3.tab, f32[4,4,11,8,128]{4,3,2,1,0:T(8,128)S(1)} %pad_maximum_fusion.refs_0_, ...), custom_call_target="tpu_custom_call" | custom-call | tf_op jit(solution)/shard_map/pallas_call | solution.py:125
  177.4 4.5 %collective-permute-done.53 = f32[384,128]{1,0:T(8,128)S(1)} collective-permute-done((f32[384,128]{1,0:T(8,128)S(1)}, f32[384,128]{1,0:T(8,128)S(1)}, u32[]{:S(2)}, u32[]{:S(2)}) %collective-permute-start.53) | collective-permute-done | bytes 196640 | tf_op jit(solution)/shard_map/ppermute | solution.py:29
  181.9 4.5 %collective-permute-done.54 = f32[384,128]{1,0:T(8,128)S(1)} collective-permute-done((f32[384,128]{1,0:T(8,128)S(1)}, f32[384,128]{1,0:T(8,128)S(1)}, u32[]{:S(2)}, u32[]{:S(2)}) %collective-permute-start.54) | collective-permute-done | bytes 196640 | tf_op jit(solution)/shard_map/ppermute | solution.py:29
  193.3 3.2 %collective-permute-done.58 = f32[256,128]{1,0:T(8,128)S(1)} collective-permute-done((f32[256,128]{1,0:T(8,128)S(1)}, f32[256,128]{1,0:T(8,128)S(1)}, u32[]{:S(2)}, u32[]{:S(2)}) %collective-permute-start.58) | collective-permute-done | bytes 131104 | tf_op jit(solution)/shard_map/ppermute | solution.py:29
  (139 shorter events, 79.3 us)
Async XLA Ops:
  3.9 9.5 %collective-permute-start.2 = (f32[256,128]{1,0:T(8,128)S(1)}, f32[256,128]{1,0:T(8,128)S(1)}, u32[]{:S(2)}, u32[]{:S(2)}) collective-permute-start(f32[256,128]{1,0:T(8,128)S(1)} %bitcast.192), channel_id=1, source_target_pairs={{0,4},{1,5},{2,6},{3,7},{4,0},{5,1},{6,2},{7,3},{8,12},{9,13},{10,... | collective-permute-start | bytes 393224 | tf_op jit(solution)/shard_map/ppermute | solution.py:29
  24.3 9.2 %collective-permute-start.10 = (f32[896,128]{1,0:T(8,128)S(1)}, f32[896,128]{1,0:T(8,128)S(1)}, u32[]{:S(2)}, u32[]{:S(2)}) collective-permute-start(f32[896,128]{1,0:T(8,128)S(1)} %bitcast.131), channel_id=1, source_target_pairs={{0,16},{1,65},{8,24},{9,73},{16,0},{17,81},{24,8},{25,89},{32,48},... | collective-permute-start | bytes 1376264 | tf_op jit(solution)/shard_map/ppermute | solution.py:29
  27.1 11.4 %collective-permute-start.9 = (f32[896,128]{1,0:T(8,128)S(1)}, f32[896,128]{1,0:T(8,128)S(1)}, u32[]{:S(2)}, u32[]{:S(2)}) collective-permute-start(f32[896,128]{1,0:T(8,128)S(1)} %bitcast.132), channel_id=1, source_target_pairs={{0,24},{1,97},{8,0},{9,105},{16,8},{17,113},{24,16},{25,121},{32,5... | collective-permute-start | bytes 1376264 | tf_op jit(solution)/shard_map/ppermute | solution.py:29
  28.0 10.6 %collective-permute-start.8 = (f32[896,128]{1,0:T(8,128)S(1)}, f32[896,128]{1,0:T(8,128)S(1)}, u32[]{:S(2)}, u32[]{:S(2)}) collective-permute-start(f32[896,128]{1,0:T(8,128)S(1)} %bitcast.133), channel_id=1, source_target_pairs={{0,8},{1,33},{8,16},{9,41},{16,24},{17,49},{24,0},{25,57},{32,40},... | collective-permute-start | bytes 1376264 | tf_op jit(solution)/shard_map/ppermute | solution.py:29
  40.3 7.4 %collective-permute-start.11 = (f32[768,128]{1,0:T(8,128)S(1)}, f32[768,128]{1,0:T(8,128)S(1)}, u32[]{:S(2)}, u32[]{:S(2)}) collective-permute-start(f32[768,128]{1,0:T(8,128)S(1)} %bitcast.213), channel_id=1, source_target_pairs={{0,1},{1,0},{2,3},{3,2},{4,5},{5,4},{6,7},{7,6},{8,9},{9,8},{10,11... | collective-permute-start | bytes 1179656 | tf_op jit(solution)/shard_map/ppermute | solution.py:29
  47.8 6.8 %collective-permute-start.14 = (f32[256,128]{1,0:T(8,128)S(1)}, f32[256,128]{1,0:T(8,128)S(1)}, u32[]{:S(2)}, u32[]{:S(2)}) collective-permute-start(f32[256,128]{1,0:T(8,128)S(1)} %bitcast.235), channel_id=1, source_target_pairs={{0,2},{1,7},{2,0},{3,5},{4,6},{5,3},{6,4},{7,1},{8,10},{9,15},{10,... | collective-permute-start | bytes 393224 | tf_op jit(solution)/shard_map/ppermute | solution.py:29
  55.0 7.5 %collective-permute-start.17 = (f32[256,128]{1,0:T(8,128)S(1)}, f32[256,128]{1,0:T(8,128)S(1)}, u32[]{:S(2)}, u32[]{:S(2)}) collective-permute-start(f32[256,128]{1,0:T(8,128)S(1)} %bitcast.147), channel_id=1, source_target_pairs={{0,16},{1,9},{8,0},{9,33},{32,8},{33,41},{40,32},{41,65},{64,40},{... | collective-permute-start | bytes 393224 | tf_op jit(solution)/shard_map/ppermute | solution.py:29
  56.1 7.6 %collective-permute-start.16 = (f32[256,128]{1,0:T(8,128)S(1)}, f32[256,128]{1,0:T(8,128)S(1)}, u32[]{:S(2)}, u32[]{:S(2)}) collective-permute-start(f32[256,128]{1,0:T(8,128)S(1)} %bitcast.148), channel_id=1, source_target_pairs={{0,8},{1,17},{8,32},{9,1},{32,40},{33,9},{40,64},{41,33},{64,72},{... | collective-permute-start | bytes 393224 | tf_op jit(solution)/shard_map/ppermute | solution.py:29
  64.9 8.6 %collective-permute-start.20 = (f32[864,128]{1,0:T(8,128)S(1)}, f32[864,128]{1,0:T(8,128)S(1)}, u32[]{:S(2)}, u32[]{:S(2)}) collective-permute-start(f32[864,128]{1,0:T(8,128)S(1)} %bitcast.212), channel_id=1, source_target_pairs={{0,1},{1,0},{2,3},{3,2},{4,5},{5,4},{6,7},{7,6},{8,9},{9,8},{10,11... | collective-permute-start | bytes 1327112 | tf_op jit(solution)/shard_map/ppermute | solution.py:29
  73.5 7.6 %collective-permute-start.23 = (f32[288,128]{1,0:T(8,128)S(1)}, f32[288,128]{1,0:T(8,128)S(1)}, u32[]{:S(2)}, u32[]{:S(2)}) collective-permute-start(f32[288,128]{1,0:T(8,128)S(1)} %bitcast.226), channel_id=1, source_target_pairs={{0,2},{1,7},{2,0},{3,5},{4,6},{5,3},{6,4},{7,1},{8,10},{9,15},{10,... | collective-permute-start | bytes 442376 | tf_op jit(solution)/shard_map/ppermute | solution.py:29
  81.6 11.6 %collective-permute-start.26 = (f32[288,128]{1,0:T(8,128)S(1)}, f32[288,128]{1,0:T(8,128)S(1)}, u32[]{:S(2)}, u32[]{:S(2)}) collective-permute-start(f32[288,128]{1,0:T(8,128)S(1)} %bitcast.144), channel_id=1, source_target_pairs={{0,16},{1,9},{8,0},{9,33},{32,8},{33,41},{40,32},{41,65},{64,40},{... | collective-permute-start | bytes 442376 | tf_op jit(solution)/shard_map/ppermute | solution.py:29
  81.7 11.5 %collective-permute-start.25 = (f32[288,128]{1,0:T(8,128)S(1)}, f32[288,128]{1,0:T(8,128)S(1)}, u32[]{:S(2)}, u32[]{:S(2)}) collective-permute-start(f32[288,128]{1,0:T(8,128)S(1)} %bitcast.145), channel_id=1, source_target_pairs={{0,8},{1,17},{8,32},{9,1},{32,40},{33,9},{40,64},{41,33},{64,72},{... | collective-permute-start | bytes 442376 | tf_op jit(solution)/shard_map/ppermute | solution.py:29
  84.7 8.5 %collective-permute-start.28 = (f32[224,128]{1,0:T(8,128)S(1)}, f32[224,128]{1,0:T(8,128)S(1)}, u32[]{:S(2)}, u32[]{:S(2)}) collective-permute-start(f32[224,128]{1,0:T(8,128)S(1)} %bitcast.238), channel_id=1, source_target_pairs={{0,24},{1,33},{8,16},{9,41},{32,0},{33,65},{40,8},{41,73},{64,32},... | collective-permute-start | bytes 344072 | tf_op jit(solution)/shard_map/ppermute | solution.py:29
  84.7 8.5 %collective-permute-start.27 = (f32[224,128]{1,0:T(8,128)S(1)}, f32[224,128]{1,0:T(8,128)S(1)}, u32[]{:S(2)}, u32[]{:S(2)}) collective-permute-start(f32[224,128]{1,0:T(8,128)S(1)} %bitcast.237), channel_id=1, source_target_pairs={{0,32},{1,25},{8,40},{9,17},{32,64},{33,1},{40,72},{41,9},{64,96},... | collective-permute-start | bytes 344072 | tf_op jit(solution)/shard_map/ppermute | solution.py:29
  97.1 7.0 %collective-permute-start.31 = (f32[320,128]{1,0:T(8,128)S(1)}, f32[320,128]{1,0:T(8,128)S(1)}, u32[]{:S(2)}, u32[]{:S(2)}) collective-permute-start(f32[320,128]{1,0:T(8,128)S(1)} %bitcast.173), channel_id=1, source_target_pairs={{0,4},{1,5},{2,6},{3,7},{4,0},{5,1},{6,2},{7,3},{8,12},{9,13},{10,... | collective-permute-start | bytes 491528 | tf_op jit(solution)/shard_map/ppermute | solution.py:29
  99.6 8.3 %collective-permute-start.32 = (f32[320,128]{1,0:T(8,128)S(1)}, f32[320,128]{1,0:T(8,128)S(1)}, u32[]{:S(2)}, u32[]{:S(2)}) collective-permute-start(f32[320,128]{1,0:T(8,128)S(1)} %bitcast.223), channel_id=1, source_target_pairs={{0,2},{1,7},{2,0},{3,5},{4,6},{5,3},{6,4},{7,1},{8,10},{9,15},{10,... | collective-permute-start | bytes 491528 | tf_op jit(solution)/shard_map/ppermute | solution.py:29
  100.9 7.4 %collective-permute-start.33 = (f32[320,128]{1,0:T(8,128)S(1)}, f32[320,128]{1,0:T(8,128)S(1)}, u32[]{:S(2)}, u32[]{:S(2)}) collective-permute-start(f32[320,128]{1,0:T(8,128)S(1)} %bitcast.222), channel_id=1, source_target_pairs={{0,6},{1,3},{2,4},{3,1},{4,2},{5,7},{6,0},{7,5},{8,14},{9,11},{10,... | collective-permute-start | bytes 491528 | tf_op jit(solution)/shard_map/ppermute | solution.py:29
  108.5 6.9 %collective-permute-start.38 = (f32[48,128]{1,0:T(8,128)S(1)}, f32[48,128]{1,0:T(8,128)S(1)}, u32[]{:S(2)}, u32[]{:S(2)}) collective-permute-start(f32[48,128]{1,0:T(8,128)S(1)} %bitcast.243), channel_id=1, source_target_pairs={{0,1},{1,0},{2,3},{3,2},{4,5},{5,4},{6,7},{7,6},{8,9},{9,8},{10,11... | collective-permute-start | bytes 73736 | tf_op jit(solution)/shard_map/ppermute | solution.py:29
  109.7 12.9 %collective-permute-start.35 = (f32[320,128]{1,0:T(8,128)S(1)}, f32[320,128]{1,0:T(8,128)S(1)}, u32[]{:S(2)}, u32[]{:S(2)}) collective-permute-start(f32[320,128]{1,0:T(8,128)S(1)} %bitcast.141), channel_id=1, source_target_pairs={{0,16},{1,9},{8,0},{9,33},{32,8},{33,41},{40,32},{41,65},{64,40},{... | collective-permute-start | bytes 491528 | tf_op jit(solution)/shard_map/ppermute | solution.py:29
  110.1 12.5 %collective-permute-start.34 = (f32[320,128]{1,0:T(8,128)S(1)}, f32[320,128]{1,0:T(8,128)S(1)}, u32[]{:S(2)}, u32[]{:S(2)}) collective-permute-start(f32[320,128]{1,0:T(8,128)S(1)} %bitcast.142), channel_id=1, source_target_pairs={{0,8},{1,17},{8,32},{9,1},{32,40},{33,9},{40,64},{41,33},{64,72},{... | collective-permute-start | bytes 491528 | tf_op jit(solution)/shard_map/ppermute | solution.py:29
  112.7 9.9 %collective-permute-start.37 = (f32[256,128]{1,0:T(8,128)S(1)}, f32[256,128]{1,0:T(8,128)S(1)}, u32[]{:S(2)}, u32[]{:S(2)}) collective-permute-start(f32[256,128]{1,0:T(8,128)S(1)} %bitcast.231), channel_id=1, source_target_pairs={{0,24},{1,33},{8,16},{9,41},{32,0},{33,65},{40,8},{41,73},{64,32},... | collective-permute-start | bytes 393224 | tf_op jit(solution)/shard_map/ppermute | solution.py:29
  112.7 9.9 %collective-permute-start.36 = (f32[256,128]{1,0:T(8,128)S(1)}, f32[256,128]{1,0:T(8,128)S(1)}, u32[]{:S(2)}, u32[]{:S(2)}) collective-permute-start(f32[256,128]{1,0:T(8,128)S(1)} %bitcast.230), channel_id=1, source_target_pairs={{0,32},{1,25},{8,40},{9,17},{32,64},{33,1},{40,72},{41,9},{64,96},... | collective-permute-start | bytes 393224 | tf_op jit(solution)/shard_map/ppermute | solution.py:29
  127.4 7.3 %collective-permute-start.42 = (f32[352,128]{1,0:T(8,128)S(1)}, f32[352,128]{1,0:T(8,128)S(1)}, u32[]{:S(2)}, u32[]{:S(2)}) collective-permute-start(f32[352,128]{1,0:T(8,128)S(1)} %bitcast.169), channel_id=1, source_target_pairs={{0,4},{1,5},{2,6},{3,7},{4,0},{5,1},{6,2},{7,3},{8,12},{9,13},{10,... | collective-permute-start | bytes 540680 | tf_op jit(solution)/shard_map/ppermute | solution.py:29
  129.2 9.5 %collective-permute-start.43 = (f32[352,128]{1,0:T(8,128)S(1)}, f32[352,128]{1,0:T(8,128)S(1)}, u32[]{:S(2)}, u32[]{:S(2)}) collective-permute-start(f32[352,128]{1,0:T(8,128)S(1)} %bitcast.221), channel_id=1, source_target_pairs={{0,2},{1,7},{2,0},{3,5},{4,6},{5,3},{6,4},{7,1},{8,10},{9,15},{10,... | collective-permute-start | bytes 540680 | tf_op jit(solution)/shard_map/ppermute | solution.py:29
  130.4 8.3 %collective-permute-start.44 = (f32[352,128]{1,0:T(8,128)S(1)}, f32[352,128]{1,0:T(8,128)S(1)}, u32[]{:S(2)}, u32[]{:S(2)}) collective-permute-start(f32[352,128]{1,0:T(8,128)S(1)} %bitcast.219), channel_id=1, source_target_pairs={{0,6},{1,3},{2,4},{3,1},{4,2},{5,7},{6,0},{7,5},{8,14},{9,11},{10,... | collective-permute-start | bytes 540680 | tf_op jit(solution)/shard_map/ppermute | solution.py:29
  148.0 12.1 %collective-permute-start.50 = (f32[1408,128]{1,0:T(8,128)S(1)}, f32[1408,128]{1,0:T(8,128)S(1)}, u32[]{:S(2)}, u32[]{:S(2)}) collective-permute-start(f32[1408,128]{1,0:T(8,128)S(1)} %bitcast.128), channel_id=1, source_target_pairs={{0,16},{1,65},{8,24},{9,73},{16,0},{17,81},{24,8},{25,89},{32,48},... | collective-permute-start | bytes 2162696 | tf_op jit(solution)/shard_map/ppermute | solution.py:29
  148.1 18.2 %collective-permute-start.49 = (f32[1408,128]{1,0:T(8,128)S(1)}, f32[1408,128]{1,0:T(8,128)S(1)}, u32[]{:S(2)}, u32[]{:S(2)}) collective-permute-start(f32[1408,128]{1,0:T(8,128)S(1)} %bitcast.129), channel_id=1, source_target_pairs={{0,24},{1,97},{8,0},{9,105},{16,8},{17,113},{24,16},{25,121},{32,5... | collective-permute-start | bytes 2162696 | tf_op jit(solution)/shard_map/ppermute | solution.py:29
  149.0 18.7 %collective-permute-start.48 = (f32[1408,128]{1,0:T(8,128)S(1)}, f32[1408,128]{1,0:T(8,128)S(1)}, u32[]{:S(2)}, u32[]{:S(2)}) collective-permute-start(f32[1408,128]{1,0:T(8,128)S(1)} %bitcast.130), channel_id=1, source_target_pairs={{0,8},{1,33},{8,16},{9,41},{16,24},{17,49},{24,0},{25,57},{32,40},... | collective-permute-start | bytes 2162696 | tf_op jit(solution)/shard_map/ppermute | solution.py:29
  174.2 7.7 %collective-permute-start.53 = (f32[384,128]{1,0:T(8,128)S(1)}, f32[384,128]{1,0:T(8,128)S(1)}, u32[]{:S(2)}, u32[]{:S(2)}) collective-permute-start(f32[384,128]{1,0:T(8,128)S(1)} %bitcast.164), channel_id=1, source_target_pairs={{0,4},{1,5},{2,6},{3,7},{4,0},{5,1},{6,2},{7,3},{8,12},{9,13},{10,... | collective-permute-start | bytes 589832 | tf_op jit(solution)/shard_map/ppermute | solution.py:29
  176.0 10.4 %collective-permute-start.54 = (f32[384,128]{1,0:T(8,128)S(1)}, f32[384,128]{1,0:T(8,128)S(1)}, u32[]{:S(2)}, u32[]{:S(2)}) collective-permute-start(f32[384,128]{1,0:T(8,128)S(1)} %bitcast.218), channel_id=1, source_target_pairs={{0,2},{1,7},{2,0},{3,5},{4,6},{5,3},{6,4},{7,1},{8,10},{9,15},{10,... | collective-permute-start | bytes 589832 | tf_op jit(solution)/shard_map/ppermute | solution.py:29
  177.3 9.2 %collective-permute-start.55 = (f32[384,128]{1,0:T(8,128)S(1)}, f32[384,128]{1,0:T(8,128)S(1)}, u32[]{:S(2)}, u32[]{:S(2)}) collective-permute-start(f32[384,128]{1,0:T(8,128)S(1)} %bitcast.216), channel_id=1, source_target_pairs={{0,6},{1,3},{2,4},{3,1},{4,2},{5,7},{6,0},{7,5},{8,14},{9,11},{10,... | collective-permute-start | bytes 589832 | tf_op jit(solution)/shard_map/ppermute | solution.py:29
  191.9 6.9 %collective-permute-start.59 = (f32[256,128]{1,0:T(8,128)S(1)}, f32[256,128]{1,0:T(8,128)S(1)}, u32[]{:S(2)}, u32[]{:S(2)}) collective-permute-start(f32[256,128]{1,0:T(8,128)S(1)} %bitcast.236), channel_id=1, source_target_pairs={{0,2},{1,7},{2,0},{3,5},{4,6},{5,3},{6,4},{7,1},{8,10},{9,15},{10,... | collective-permute-start | bytes 393224 | tf_op jit(solution)/shard_map/ppermute | solution.py:29
  (34 other events, 137.3 us)

commit v13 on v11

--- a/solution.py
+++ b/solution.py
@@ -125,13 +125,29 @@
 
 def call(kernel, outs, args, scratch=(), tab=None):
     vmem = pl.BlockSpec(memory_space=pltpu.VMEM)
-    table = [] if tab is None else [pl.BlockSpec(memory_space=pltpu.SMEM)]
+    table, body = [], kernel
+    scratch = list(scratch)
+    if tab is not None:
+        table = [pl.BlockSpec(memory_space=pl.ANY)]
+        scratch += [pltpu.SMEM(tab.shape, jnp.int32), pltpu.SemaphoreType.DMA]
+
+        def body(tab_ref, *refs):
+            refs, (here, sem) = refs[:-2], refs[-2:]
+            copy = pltpu.make_async_copy(tab_ref, here, sem)
+            copy.start()
+
+            def arrived():
+                copy.wait()
+                return here
+
+            kernel(arrived, *refs)
+
     return pl.pallas_call(
-        kernel,
+        body,
         out_shape=[jax.ShapeDtypeStruct(o, F32) for o in outs],
         in_specs=table + [vmem] * len(args),
         out_specs=[vmem] * len(outs),
-        scratch_shapes=list(scratch),
+        scratch_shapes=scratch,
         compiler_params=pltpu.CompilerParams(vmem_limit_bytes=48 * 1024 * 1024),
     )(*([] if tab is None else [tab]), *args)
 
@@ -158,10 +174,11 @@
         out_ref[1] = got_ref[k]
 
 
-def compact_kernel(tab, *refs):
+def compact_kernel(arrived, *refs):
     ins, (keep_ref, out_ref, x_ref) = refs[:4], refs[4:]
     for k in range(4):
         x_ref[k] = ins[k][...]
+    tab = arrived()
     low = low_half()
     row0 = tab[PLACE] * 4
     z, h = tab[PLACE + 6], tab[PLACE + 4]
@@ -244,10 +261,11 @@
         write_slabs(p_ref, own, oth, e, e * 8, left - (w + 1) + e, w + 2)
 
 
-def first_step_kernel(tab, *refs):
+def first_step_kernel(arrived, *refs):
     ins, own, oth = refs[:4], refs[4:6], refs[6:8]
     cur_ref, hi_ref, lo_ref, p_ref, g_ref = refs[8:]
     collect(ins, g_ref)
+    tab = arrived()
     w = BAND
     base = tab[PLACE + 5] * 4 + 64 - w
 
@@ -312,10 +330,11 @@
     return out
 
 
-def last_step_kernel(tab, *refs):
+def last_step_kernel(arrived, *refs):
     ins, own, oth = refs[:4], refs[4:6], refs[6:8]
     cur_ref, hi_ref, lo_ref, p_ref, g_ref = refs[8:]
     collect(ins, g_ref)
+    tab = arrived()
     w = BAND + STEPS - 1
     row0 = tab[PLACE] * 4
     left, count = w + 2, w + 2
@@ -356,9 +375,10 @@
     return coef_ref[step, 0] * cur + coef_ref[step, 1] * square
 
 
-def keep_kernel(tab, *refs):
+def keep_kernel(arrived, *refs):
     low = low_half()
     refs, coef_ref = refs[:-1], refs[-1]
+    tab = arrived()
     for s in range(STEPS):
         twice = tab[BRANCH + s] == 1
         coef_ref[s, 0] = jnp.full((8, 128), jnp.where(twice, 2.0, 0.0), F32)
@@ -400,32 +420,31 @@
         oth_ref[...] = far_ref[1 - lax.axis_index("layer")]
 
 
-def finish_kernel(tab, p0, p1, p2, p3, cur_ref, keep_ref, coef_ref, *refs):
+def finish_kernel(arrived, p0, p1, p2, p3, cur_ref, keep_ref, coef_ref, *refs):
     w = BAND + STEPS - 1
     low = low_half()
-    row0 = tab[PLACE] * 4
-    z, h = tab[PLACE + 6], tab[PLACE + 4]
-    own, oth, y_ref = refs[:2], refs[2:4], refs[4]
+    own, oth, y_ref, v_ref = refs[:2], refs[2:4], refs[4], refs[5]
     y_ref[...] = jnp.zeros_like(y_ref)
     for e in range(4):
-        i = tab[PERM + row0 + e]
         for m in range(w + 2):
             cur = cur_ref[e, m - 1] if 1 <= m <= w + 1 else jnp.zeros((8, 128), F32)
             square = total((p0, p1, p2, p3), e, m)
             value = polynomial(coef_ref, STEPS - 1, cur, square) * keep_ref[e, m]
-            turned = swap_halves(value)
-            for half in (0, 1):
-                v = 2 * m + half
-                if v == 0:
-                    continue
-                j = (i + v + 64 - (w + 2)) & 63
-                sj = tab[INV + j]
-                odd = sj & 1
-                piece = jnp.where(odd == half, value, turned)
-                side = jnp.where(low, 0, 1) == odd
-                core = (sj >> 3) & 1
-                at = core ^ h, slot_with((sj >> 4) ^ z, core), e, (sj & 7) >> 1
-                y_ref[at] = jnp.where(side, piece, y_ref[at])
+            v_ref[0, e, m] = value
+            v_ref[1, e, m] = swap_halves(value)
+    tab = arrived()
+    row0 = tab[PLACE] * 4
+    z, h = tab[PLACE + 6], tab[PLACE + 4]
+    for e in range(4):
+        i = tab[PERM + row0 + e]
+        for v in range(1, 2 * w + 4):
+            j = (i + v + 64 - (w + 2)) & 63
+            sj = tab[INV + j]
+            odd, core = sj & 1, (sj >> 3) & 1
+            piece = v_ref[odd ^ (v & 1), e, v // 2]
+            side = jnp.where(low, 0, 1) == odd
+            at = core ^ h, slot_with((sj >> 4) ^ z, core), e, (sj & 7) >> 1
+            y_ref[at] = jnp.where(side, piece, y_ref[at])
     for slot in range(4):
         slot_view(own, slot)[...] = y_ref[0, slot]
         slot_view(oth, slot)[...] = y_ref[1, slot]
@@ -452,7 +471,15 @@
     pos = jnp.sum(jnp.where(jnp.asarray(RING) == r, jnp.arange(16), 0))
     place = jnp.stack([r, z * 2 + h, r // 4, r % 4, h, pos, z, z]).astype(jnp.int32)
     return jnp.concatenate(
-        [perm, inverse.astype(jnp.int32), branch, jnp.zeros((3,), jnp.int32), bits.reshape(-1), place]
+        [
+            perm,
+            inverse.astype(jnp.int32),
+            branch,
+            jnp.zeros((3,), jnp.int32),
+            bits.reshape(-1),
+            place,
+            jnp.zeros((1024 - PLACE - 8,), jnp.int32),
+        ]
     )
 
 
@@ -545,7 +572,7 @@
         finish_kernel,
         in_parts(slabs),
         parts + [cur, keep[STEPS], coef],
-        [pltpu.VMEM((2, 4) + slabs, F32)],
+        [pltpu.VMEM((2, 4) + slabs, F32), pltpu.VMEM((2, 4, w + 2, 8, 128), F32)],
         tab=tab,
     )
     (out,) = call(join_kernel, [(256, 512)], spread_group(tiles))

time: 199 us -> 199 us (level)
  no operation moved by 1% of the time
where the time goes in v13:
time: 199 us
  waiting for transfers between devices  115 us (58%)
  starting transfers between devices  65.6 us (33%)
  Pallas kernels  13.6 us (7%)
  local copies, waits for them, and re-layouts  3.67 us (2%)
    ppermute x61, waiting for transfers between devices, permute(): return lax.ppermute(flat, axes, pairs).reshape(value.shape)  115 us
    ppermute x61, starting transfers between devices, permute(): return lax.ppermute(flat, axes, pairs).reshape(value.shape)  65.6 us
    pallas_call x28, Pallas kernels, call(): pl.pallas_call(body, out_shape=[jax.ShapeDtypeStruct(o, F32) for o in out...  13.6 us
  transfers between devices with their start and end apart: 61, of which 45 were waited for; matrix products, arithmetic and copies ran while one was open for 1% of the time, Pallas kernels for 1%

profile of v13, /device:TPU:1, one launch (start us, length us, event | category | flops | bytes accessed | tf_op | source)
XLA Modules:
  0.0 198.9 jit_solution(6114471026359196668)
XLA Ops:
  3.9 3.8 %collective-permute-start.2 = (f32[256,128]{1,0:T(8,128)S(1)}, f32[256,128]{1,0:T(8,128)S(1)}, u32[]{:S(2)}, u32[]{:S(2)}) collective-permute-start(f32[256,128]{1,0:T(8,128)S(1)} %bitcast.193), channel_id=1, source_target_pairs={{0,4},{1,5},{2,6},{3,7},{4,0},{5,1},{6,2},{7,3},{8,12},{9,13},{10,... | collective-permute-start | bytes 393224 | tf_op jit(solution)/shard_map/ppermute | solution.py:29
  15.7 3.0 %collective-permute-start.7 = (f32[224,128]{1,0:T(8,128)S(1)}, f32[224,128]{1,0:T(8,128)S(1)}, u32[]{:S(2)}, u32[]{:S(2)}) collective-permute-start(f32[224,128]{1,0:T(8,128)S(1)} %bitcast.154), channel_id=1, source_target_pairs={{0,64},{1,17},{8,72},{9,25},{16,80},{17,1},{24,88},{25,9},{32,96},... | collective-permute-start | bytes 344072 | tf_op jit(solution)/shard_map/ppermute | solution.py:29
  24.3 2.8 %collective-permute-start.10 = (f32[896,128]{1,0:T(8,128)S(1)}, f32[896,128]{1,0:T(8,128)S(1)}, u32[]{:S(2)}, u32[]{:S(2)}) collective-permute-start(f32[896,128]{1,0:T(8,128)S(1)} %bitcast.132), channel_id=1, source_target_pairs={{0,16},{1,65},{8,24},{9,73},{16,0},{17,81},{24,8},{25,89},{32,48},... | collective-permute-start | bytes 1376264 | tf_op jit(solution)/shard_map/ppermute | solution.py:29
  28.6 4.9 %collective-permute-done.10 = f32[896,128]{1,0:T(8,128)S(1)} collective-permute-done((f32[896,128]{1,0:T(8,128)S(1)}, f32[896,128]{1,0:T(8,128)S(1)}, u32[]{:S(2)}, u32[]{:S(2)}) %collective-permute-start.10) | collective-permute-done | bytes 458784 | tf_op jit(solution)/shard_map/ppermute | solution.py:29
  33.6 5.0 %collective-permute-done.9 = f32[896,128]{1,0:T(8,128)S(1)} collective-permute-done((f32[896,128]{1,0:T(8,128)S(1)}, f32[896,128]{1,0:T(8,128)S(1)}, u32[]{:S(2)}, u32[]{:S(2)}) %collective-permute-start.9) | collective-permute-done | bytes 458784 | tf_op jit(solution)/shard_map/ppermute | solution.py:29
  40.3 3.9 %collective-permute-start.11 = (f32[768,128]{1,0:T(8,128)S(1)}, f32[768,128]{1,0:T(8,128)S(1)}, u32[]{:S(2)}, u32[]{:S(2)}) collective-permute-start(f32[768,128]{1,0:T(8,128)S(1)} %bitcast.215), channel_id=1, source_target_pairs={{0,1},{1,0},{2,3},{3,2},{4,5},{5,4},{6,7},{7,6},{8,9},{9,8},{10,11... | collective-permute-start | bytes 1179656 | tf_op jit(solution)/shard_map/ppermute | solution.py:29
  49.1 3.0 %collective-permute-done.13 = f32[256,128]{1,0:T(8,128)S(1)} collective-permute-done((f32[256,128]{1,0:T(8,128)S(1)}, f32[256,128]{1,0:T(8,128)S(1)}, u32[]{:S(2)}, u32[]{:S(2)}) %collective-permute-start.13) | collective-permute-done | bytes 131104 | tf_op jit(solution)/shard_map/ppermute | solution.py:29
  52.1 2.4 %collective-permute-done.14 = f32[256,128]{1,0:T(8,128)S(1)} collective-permute-done((f32[256,128]{1,0:T(8,128)S(1)}, f32[256,128]{1,0:T(8,128)S(1)}, u32[]{:S(2)}, u32[]{:S(2)}) %collective-permute-start.14) | collective-permute-done | bytes 131104 | tf_op jit(solution)/shard_map/ppermute | solution.py:29
  54.9 2.6 %collective-permute-start.17 = (f32[256,128]{1,0:T(8,128)S(1)}, f32[256,128]{1,0:T(8,128)S(1)}, u32[]{:S(2)}, u32[]{:S(2)}) collective-permute-start(f32[256,128]{1,0:T(8,128)S(1)} %bitcast.148), channel_id=1, source_target_pairs={{0,16},{8,0},{32,8},{40,32},{64,40},{72,64},{96,72},{104,96},{120,... | collective-permute-start | bytes 393224 | tf_op jit(solution)/shard_map/ppermute | solution.py:29
  59.0 2.5 %collective-permute-done.19 = f32[144,128]{1,0:T(8,128)S(1)} collective-permute-done((f32[144,128]{1,0:T(8,128)S(1)}, f32[144,128]{1,0:T(8,128)S(1)}, u32[]{:S(2)}, u32[]{:S(2)}) %collective-permute-start.19) | collective-permute-done | bytes 73760 | tf_op jit(solution)/shard_map/ppermute | solution.py:29
  63.2 3.8 %collective-permute-done.16 = f32[256,128]{1,0:T(8,128)S(1)} collective-permute-done((f32[256,128]{1,0:T(8,128)S(1)}, f32[256,128]{1,0:T(8,128)S(1)}, u32[]{:S(2)}, u32[]{:S(2)}) %collective-permute-start.16) | collective-permute-done | bytes 131104 | tf_op jit(solution)/shard_map/ppermute | solution.py:29
  71.6 2.4 %collective-permute-start.22 = (f32[288,128]{1,0:T(8,128)S(1)}, f32[288,128]{1,0:T(8,128)S(1)}, u32[]{:S(2)}, u32[]{:S(2)}) collective-permute-start(f32[288,128]{1,0:T(8,128)S(1)} %bitcast.180), channel_id=1, source_target_pairs={{0,4},{1,5},{2,6},{3,7},{4,0},{5,1},{6,2},{7,3},{8,12},{9,13},{10,... | collective-permute-start | bytes 442376 | tf_op jit(solution)/shard_map/ppermute | solution.py:29
  75.6 2.7 %collective-permute-done.22 = f32[288,128]{1,0:T(8,128)S(1)} collective-permute-done((f32[288,128]{1,0:T(8,128)S(1)}, f32[288,128]{1,0:T(8,128)S(1)}, u32[]{:S(2)}, u32[]{:S(2)}) %collective-permute-start.22) | collective-permute-done | bytes 147488 | tf_op jit(solution)/shard_map/ppermute | solution.py:29
  78.2 3.4 %collective-permute-done.23 = f32[288,128]{1,0:T(8,128)S(1)} collective-permute-done((f32[288,128]{1,0:T(8,128)S(1)}, f32[288,128]{1,0:T(8,128)S(1)}, u32[]{:S(2)}, u32[]{:S(2)}) %collective-permute-start.23) | collective-permute-done | bytes 147488 | tf_op jit(solution)/shard_map/ppermute | solution.py:29
  85.1 3.4 %collective-permute-done.28 = f32[224,128]{1,0:T(8,128)S(1)} collective-permute-done((f32[224,128]{1,0:T(8,128)S(1)}, f32[224,128]{1,0:T(8,128)S(1)}, u32[]{:S(2)}, u32[]{:S(2)}) %collective-permute-start.28) | collective-permute-done | bytes 114720 | tf_op jit(solution)/shard_map/ppermute | solution.py:29
  92.6 2.5 %collective-permute-start.29 = (f32[960,128]{1,0:T(8,128)S(1)}, f32[960,128]{1,0:T(8,128)S(1)}, u32[]{:S(2)}, u32[]{:S(2)}) collective-permute-start(f32[960,128]{1,0:T(8,128)S(1)} %bitcast.213), channel_id=1, source_target_pairs={{0,1},{1,0},{2,3},{3,2},{4,5},{5,4},{6,7},{7,6},{8,9},{9,8},{10,11... | collective-permute-start | bytes 1474568 | tf_op jit(solution)/shard_map/ppermute | solution.py:29
  100.6 3.2 %collective-permute-done.31 = f32[320,128]{1,0:T(8,128)S(1)} collective-permute-done((f32[320,128]{1,0:T(8,128)S(1)}, f32[320,128]{1,0:T(8,128)S(1)}, u32[]{:S(2)}, u32[]{:S(2)}) %collective-permute-start.31) | collective-permute-done | bytes 163872 | tf_op jit(solution)/shard_map/ppermute | solution.py:29
  103.8 3.7 %collective-permute-done.32 = f32[320,128]{1,0:T(8,128)S(1)} collective-permute-done((f32[320,128]{1,0:T(8,128)S(1)}, f32[320,128]{1,0:T(8,128)S(1)}, u32[]{:S(2)}, u32[]{:S(2)}) %collective-permute-start.32) | collective-permute-done | bytes 163872 | tf_op jit(solution)/shard_map/ppermute | solution.py:29
  113.7 4.1 %collective-permute-done.39 = f32[96,128]{1,0:T(8,128)S(1)} collective-permute-done((f32[96,128]{1,0:T(8,128)S(1)}, f32[96,128]{1,0:T(8,128)S(1)}, u32[]{:S(2)}, u32[]{:S(2)}) %collective-permute-start.39) | collective-permute-done | bytes 49184 | tf_op jit(solution)/shard_map/ppermute | solution.py:29
  118.8 3.3 %collective-permute-done.34 = f32[320,128]{1,0:T(8,128)S(1)} collective-permute-done((f32[320,128]{1,0:T(8,128)S(1)}, f32[320,128]{1,0:T(8,128)S(1)}, u32[]{:S(2)}, u32[]{:S(2)}) %collective-permute-start.34) | collective-permute-done | bytes 163872 | tf_op jit(solution)/shard_map/ppermute | solution.py:29
  129.4 4.1 %collective-permute-done.42 = f32[352,128]{1,0:T(8,128)S(1)} collective-permute-done((f32[352,128]{1,0:T(8,128)S(1)}, f32[352,128]{1,0:T(8,128)S(1)}, u32[]{:S(2)}, u32[]{:S(2)}) %collective-permute-start.42) | collective-permute-done | bytes 180256 | tf_op jit(solution)/shard_map/ppermute | solution.py:29
  133.6 4.0 %collective-permute-done.43 = f32[352,128]{1,0:T(8,128)S(1)} collective-permute-done((f32[352,128]{1,0:T(8,128)S(1)}, f32[352,128]{1,0:T(8,128)S(1)}, u32[]{:S(2)}, u32[]{:S(2)}) %collective-permute-start.43) | collective-permute-done | bytes 180256 | tf_op jit(solution)/shard_map/ppermute | solution.py:29
  137.8 3.5 %collective-permute-start.46 = (f32[352,128]{1,0:T(8,128)S(1)}, f32[352,128]{1,0:T(8,128)S(1)}, u32[]{:S(2)}, u32[]{:S(2)}) collective-permute-start(f32[352,128]{1,0:T(8,128)S(1)} %bitcast.136), channel_id=1, source_target_pairs={{0,96},{1,25},{8,104},{9,1},{16,112},{17,9},{24,120},{25,17},{32,0... | collective-permute-start | bytes 540680 | tf_op jit(solution)/shard_map/ppermute | solution.py:29
  141.3 2.6 %collective-permute-done.47 = f32[352,128]{1,0:T(8,128)S(1)} collective-permute-done((f32[352,128]{1,0:T(8,128)S(1)}, f32[352,128]{1,0:T(8,128)S(1)}, u32[]{:S(2)}, u32[]{:S(2)}) %collective-permute-start.47) | collective-permute-done | bytes 180256 | tf_op jit(solution)/shard_map/ppermute | solution.py:29
  144.0 3.1 %collective-permute-done.45 = f32[352,128]{1,0:T(8,128)S(1)} collective-permute-done((f32[352,128]{1,0:T(8,128)S(1)}, f32[352,128]{1,0:T(8,128)S(1)}, u32[]{:S(2)}, u32[]{:S(2)}) %collective-permute-start.45) | collective-permute-done | bytes 180256 | tf_op jit(solution)/shard_map/ppermute | solution.py:29
  148.9 10.4 %collective-permute-done.50 = f32[1408,128]{1,0:T(8,128)S(1)} collective-permute-done((f32[1408,128]{1,0:T(8,128)S(1)}, f32[1408,128]{1,0:T(8,128)S(1)}, u32[]{:S(2)}, u32[]{:S(2)}) %collective-permute-start.50) | collective-permute-done | bytes 720928 | tf_op jit(solution)/shard_map/ppermute | solution.py:29
  159.3 3.3 %collective-permute-done.49 = f32[1408,128]{1,0:T(8,128)S(1)} collective-permute-done((f32[1408,128]{1,0:T(8,128)S(1)}, f32[1408,128]{1,0:T(8,128)S(1)}, u32[]{:S(2)}, u32[]{:S(2)}) %collective-permute-start.49) | collective-permute-done | bytes 720928 | tf_op jit(solution)/shard_map/ppermute | solution.py:29
  162.6 4.4 %collective-permute-done.48 = f32[1408,128]{1,0:T(8,128)S(1)} collective-permute-done((f32[1408,128]{1,0:T(8,128)S(1)}, f32[1408,128]{1,0:T(8,128)S(1)}, u32[]{:S(2)}, u32[]{:S(2)}) %collective-permute-start.48) | collective-permute-done | bytes 720928 | tf_op jit(solution)/shard_map/ppermute | solution.py:29
  167.0 2.5 %shard_map.76 = (f32[1,4,12,8,128]{4,3,2,1,0:T(8,128)S(1)}, f32[3,4,12,8,128]{4,3,2,1,0:T(8,128)S(1)}, f32[1,4,12,8,128]{4,3,2,1,0:T(8,128)S(1)}, f32[3,4,12,8,128]{4,3,2,1,0:T(8,128)S(1)}, f32[4,11,8,128]{3,2,1,0:T(8,128)S(1)}) custom-call(s32[1024]{0:T(1024)S(1)} %concatenate.3.tab_ref, f32[4,4,11,8,128]{4,3,2,1,0:T(8,128)S(1)} %pad_maximum_fusion.refs_0_, ...), custom_call_target="tpu_custom_call" | custom-call | tf_op jit(solution)/shard_map/pallas_call | solution.py:145
  176.2 4.5 %collective-permute-done.53 = f32[384,128]{1,0:T(8,128)S(1)} collective-permute-done((f32[384,128]{1,0:T(8,128)S(1)}, f32[384,128]{1,0:T(8,128)S(1)}, u32[]{:S(2)}, u32[]{:S(2)}) %collective-permute-start.53) | collective-permute-done | bytes 196640 | tf_op jit(solution)/shard_map/ppermute | solution.py:29
  180.6 4.5 %collective-permute-done.54 = f32[384,128]{1,0:T(8,128)S(1)} collective-permute-done((f32[384,128]{1,0:T(8,128)S(1)}, f32[384,128]{1,0:T(8,128)S(1)}, u32[]{:S(2)}, u32[]{:S(2)}) %collective-permute-start.54) | collective-permute-done | bytes 196640 | tf_op jit(solution)/shard_map/ppermute | solution.py:29
  192.1 3.2 %collective-permute-done.58 = f32[256,128]{1,0:T(8,128)S(1)} collective-permute-done((f32[256,128]{1,0:T(8,128)S(1)}, f32[256,128]{1,0:T(8,128)S(1)}, u32[]{:S(2)}, u32[]{:S(2)}) %collective-permute-start.58) | collective-permute-done | bytes 131104 | tf_op jit(solution)/shard_map/ppermute | solution.py:29
  (140 shorter events, 81.9 us)
Async XLA Ops:
  1.1 6.5 %collective-permute-start = (f32[384,128]{1,0:T(8,128)S(1)}, f32[384,128]{1,0:T(8,128)S(1)}, u32[]{:S(2)}, u32[]{:S(2)}) collective-permute-start(f32[384,128]{1,0:T(8,128)S(1)} %bitcast.216), channel_id=1, source_target_pairs={{0,1},{1,0},{2,3},{3,2},{4,5},{5,4},{6,7},{7,6},{8,9},{9,8},{10,11... | collective-permute-start | bytes 589832 | tf_op jit(solution)/shard_map/ppermute | solution.py:29
  3.9 9.6 %collective-permute-start.2 = (f32[256,128]{1,0:T(8,128)S(1)}, f32[256,128]{1,0:T(8,128)S(1)}, u32[]{:S(2)}, u32[]{:S(2)}) collective-permute-start(f32[256,128]{1,0:T(8,128)S(1)} %bitcast.193), channel_id=1, source_target_pairs={{0,4},{1,5},{2,6},{3,7},{4,0},{5,1},{6,2},{7,3},{8,12},{9,13},{10,... | collective-permute-start | bytes 393224 | tf_op jit(solution)/shard_map/ppermute | solution.py:29
  24.3 9.2 %collective-permute-start.10 = (f32[896,128]{1,0:T(8,128)S(1)}, f32[896,128]{1,0:T(8,128)S(1)}, u32[]{:S(2)}, u32[]{:S(2)}) collective-permute-start(f32[896,128]{1,0:T(8,128)S(1)} %bitcast.132), channel_id=1, source_target_pairs={{0,16},{1,65},{8,24},{9,73},{16,0},{17,81},{24,8},{25,89},{32,48},... | collective-permute-start | bytes 1376264 | tf_op jit(solution)/shard_map/ppermute | solution.py:29
  27.2 11.4 %collective-permute-start.9 = (f32[896,128]{1,0:T(8,128)S(1)}, f32[896,128]{1,0:T(8,128)S(1)}, u32[]{:S(2)}, u32[]{:S(2)}) collective-permute-start(f32[896,128]{1,0:T(8,128)S(1)} %bitcast.133), channel_id=1, source_target_pairs={{0,24},{1,97},{8,0},{9,105},{16,8},{17,113},{24,16},{25,121},{32,5... | collective-permute-start | bytes 1376264 | tf_op jit(solution)/shard_map/ppermute | solution.py:29
  28.0 10.6 %collective-permute-start.8 = (f32[896,128]{1,0:T(8,128)S(1)}, f32[896,128]{1,0:T(8,128)S(1)}, u32[]{:S(2)}, u32[]{:S(2)}) collective-permute-start(f32[896,128]{1,0:T(8,128)S(1)} %bitcast.134), channel_id=1, source_target_pairs={{0,8},{1,33},{8,16},{9,41},{16,24},{17,49},{24,0},{25,57},{32,40},... | collective-permute-start | bytes 1376264 | tf_op jit(solution)/shard_map/ppermute | solution.py:29
  40.3 7.4 %collective-permute-start.11 = (f32[768,128]{1,0:T(8,128)S(1)}, f32[768,128]{1,0:T(8,128)S(1)}, u32[]{:S(2)}, u32[]{:S(2)}) collective-permute-start(f32[768,128]{1,0:T(8,128)S(1)} %bitcast.215), channel_id=1, source_target_pairs={{0,1},{1,0},{2,3},{3,2},{4,5},{5,4},{6,7},{7,6},{8,9},{9,8},{10,11... | collective-permute-start | bytes 1179656 | tf_op jit(solution)/shard_map/ppermute | solution.py:29
  47.7 6.8 %collective-permute-start.14 = (f32[256,128]{1,0:T(8,128)S(1)}, f32[256,128]{1,0:T(8,128)S(1)}, u32[]{:S(2)}, u32[]{:S(2)}) collective-permute-start(f32[256,128]{1,0:T(8,128)S(1)} %bitcast.237), channel_id=1, source_target_pairs={{0,2},{1,7},{2,0},{3,5},{4,6},{5,3},{6,4},{7,1},{8,10},{9,15},{10,... | collective-permute-start | bytes 393224 | tf_op jit(solution)/shard_map/ppermute | solution.py:29
  54.9 8.3 %collective-permute-start.17 = (f32[256,128]{1,0:T(8,128)S(1)}, f32[256,128]{1,0:T(8,128)S(1)}, u32[]{:S(2)}, u32[]{:S(2)}) collective-permute-start(f32[256,128]{1,0:T(8,128)S(1)} %bitcast.148), channel_id=1, source_target_pairs={{0,16},{8,0},{32,8},{40,32},{64,40},{72,64},{96,72},{104,96},{120,... | collective-permute-start | bytes 393224 | tf_op jit(solution)/shard_map/ppermute | solution.py:29
  57.5 9.5 %collective-permute-start.16 = (f32[256,128]{1,0:T(8,128)S(1)}, f32[256,128]{1,0:T(8,128)S(1)}, u32[]{:S(2)}, u32[]{:S(2)}) collective-permute-start(f32[256,128]{1,0:T(8,128)S(1)} %bitcast.149), channel_id=1, source_target_pairs={{0,8},{8,32},{32,40},{40,64},{64,72},{72,96},{96,104},{104,120},{1... | collective-permute-start | bytes 393224 | tf_op jit(solution)/shard_map/ppermute | solution.py:29
  71.6 6.6 %collective-permute-start.22 = (f32[288,128]{1,0:T(8,128)S(1)}, f32[288,128]{1,0:T(8,128)S(1)}, u32[]{:S(2)}, u32[]{:S(2)}) collective-permute-start(f32[288,128]{1,0:T(8,128)S(1)} %bitcast.180), channel_id=1, source_target_pairs={{0,4},{1,5},{2,6},{3,7},{4,0},{5,1},{6,2},{7,3},{8,12},{9,13},{10,... | collective-permute-start | bytes 442376 | tf_op jit(solution)/shard_map/ppermute | solution.py:29
  74.0 7.6 %collective-permute-start.23 = (f32[288,128]{1,0:T(8,128)S(1)}, f32[288,128]{1,0:T(8,128)S(1)}, u32[]{:S(2)}, u32[]{:S(2)}) collective-permute-start(f32[288,128]{1,0:T(8,128)S(1)} %bitcast.228), channel_id=1, source_target_pairs={{0,2},{1,7},{2,0},{3,5},{4,6},{5,3},{6,4},{7,1},{8,10},{9,15},{10,... | collective-permute-start | bytes 442376 | tf_op jit(solution)/shard_map/ppermute | solution.py:29
  75.3 6.6 %collective-permute-start.24 = (f32[288,128]{1,0:T(8,128)S(1)}, f32[288,128]{1,0:T(8,128)S(1)}, u32[]{:S(2)}, u32[]{:S(2)}) collective-permute-start(f32[288,128]{1,0:T(8,128)S(1)} %bitcast.227), channel_id=1, source_target_pairs={{0,6},{1,3},{2,4},{3,1},{4,2},{5,7},{6,0},{7,5},{8,14},{9,11},{10,... | collective-permute-start | bytes 442376 | tf_op jit(solution)/shard_map/ppermute | solution.py:29
  82.1 7.0 %collective-permute-start.26 = (f32[288,128]{1,0:T(8,128)S(1)}, f32[288,128]{1,0:T(8,128)S(1)}, u32[]{:S(2)}, u32[]{:S(2)}) collective-permute-start(f32[288,128]{1,0:T(8,128)S(1)} %bitcast.145), channel_id=1, source_target_pairs={{0,16},{8,0},{32,8},{40,32},{64,40},{72,64},{96,72},{104,96},{120,... | collective-permute-start | bytes 442376 | tf_op jit(solution)/shard_map/ppermute | solution.py:29
  82.2 9.2 %collective-permute-start.25 = (f32[288,128]{1,0:T(8,128)S(1)}, f32[288,128]{1,0:T(8,128)S(1)}, u32[]{:S(2)}, u32[]{:S(2)}) collective-permute-start(f32[288,128]{1,0:T(8,128)S(1)} %bitcast.146), channel_id=1, source_target_pairs={{0,8},{8,32},{32,40},{40,64},{64,72},{72,96},{96,104},{104,120},{1... | collective-permute-start | bytes 442376 | tf_op jit(solution)/shard_map/ppermute | solution.py:29
  92.6 6.6 %collective-permute-start.29 = (f32[960,128]{1,0:T(8,128)S(1)}, f32[960,128]{1,0:T(8,128)S(1)}, u32[]{:S(2)}, u32[]{:S(2)}) collective-permute-start(f32[960,128]{1,0:T(8,128)S(1)} %bitcast.213), channel_id=1, source_target_pairs={{0,1},{1,0},{2,3},{3,2},{4,5},{5,4},{6,7},{7,6},{8,9},{9,8},{10,11... | collective-permute-start | bytes 1474568 | tf_op jit(solution)/shard_map/ppermute | solution.py:29
  96.8 7.0 %collective-permute-start.31 = (f32[320,128]{1,0:T(8,128)S(1)}, f32[320,128]{1,0:T(8,128)S(1)}, u32[]{:S(2)}, u32[]{:S(2)}) collective-permute-start(f32[320,128]{1,0:T(8,128)S(1)} %bitcast.174), channel_id=1, source_target_pairs={{0,4},{1,5},{2,6},{3,7},{4,0},{5,1},{6,2},{7,3},{8,12},{9,13},{10,... | collective-permute-start | bytes 491528 | tf_op jit(solution)/shard_map/ppermute | solution.py:29
  99.2 8.3 %collective-permute-start.32 = (f32[320,128]{1,0:T(8,128)S(1)}, f32[320,128]{1,0:T(8,128)S(1)}, u32[]{:S(2)}, u32[]{:S(2)}) collective-permute-start(f32[320,128]{1,0:T(8,128)S(1)} %bitcast.225), channel_id=1, source_target_pairs={{0,2},{1,7},{2,0},{3,5},{4,6},{5,3},{6,4},{7,1},{8,10},{9,15},{10,... | collective-permute-start | bytes 491528 | tf_op jit(solution)/shard_map/ppermute | solution.py:29
  100.5 7.4 %collective-permute-start.33 = (f32[320,128]{1,0:T(8,128)S(1)}, f32[320,128]{1,0:T(8,128)S(1)}, u32[]{:S(2)}, u32[]{:S(2)}) collective-permute-start(f32[320,128]{1,0:T(8,128)S(1)} %bitcast.224), channel_id=1, source_target_pairs={{0,6},{1,3},{2,4},{3,1},{4,2},{5,7},{6,0},{7,5},{8,14},{9,11},{10,... | collective-permute-start | bytes 491528 | tf_op jit(solution)/shard_map/ppermute | solution.py:29
  109.3 9.5 %collective-permute-start.35 = (f32[320,128]{1,0:T(8,128)S(1)}, f32[320,128]{1,0:T(8,128)S(1)}, u32[]{:S(2)}, u32[]{:S(2)}) collective-permute-start(f32[320,128]{1,0:T(8,128)S(1)} %bitcast.142), channel_id=1, source_target_pairs={{0,16},{8,0},{32,8},{40,32},{64,40},{72,64},{96,72},{104,96},{120,... | collective-permute-start | bytes 491528 | tf_op jit(solution)/shard_map/ppermute | solution.py:29
  109.4 12.7 %collective-permute-start.34 = (f32[320,128]{1,0:T(8,128)S(1)}, f32[320,128]{1,0:T(8,128)S(1)}, u32[]{:S(2)}, u32[]{:S(2)}) collective-permute-start(f32[320,128]{1,0:T(8,128)S(1)} %bitcast.143), channel_id=1, source_target_pairs={{0,8},{8,32},{32,40},{40,64},{64,72},{72,96},{96,104},{104,120},{1... | collective-permute-start | bytes 491528 | tf_op jit(solution)/shard_map/ppermute | solution.py:29
  110.8 8.0 %collective-permute-start.37 = (f32[256,128]{1,0:T(8,128)S(1)}, f32[256,128]{1,0:T(8,128)S(1)}, u32[]{:S(2)}, u32[]{:S(2)}) collective-permute-start(f32[256,128]{1,0:T(8,128)S(1)} %bitcast.233), channel_id=1, source_target_pairs={{0,24},{8,16},{32,0},{40,8},{64,32},{72,40},{96,64},{104,72},{120,... | collective-permute-start | bytes 393224 | tf_op jit(solution)/shard_map/ppermute | solution.py:29
  110.8 8.0 %collective-permute-start.36 = (f32[256,128]{1,0:T(8,128)S(1)}, f32[256,128]{1,0:T(8,128)S(1)}, u32[]{:S(2)}, u32[]{:S(2)}) collective-permute-start(f32[256,128]{1,0:T(8,128)S(1)} %bitcast.232), channel_id=1, source_target_pairs={{0,32},{8,40},{32,64},{40,72},{64,96},{72,104},{96,120},{104,112},... | collective-permute-start | bytes 393224 | tf_op jit(solution)/shard_map/ppermute | solution.py:29
  126.2 7.3 %collective-permute-start.42 = (f32[352,128]{1,0:T(8,128)S(1)}, f32[352,128]{1,0:T(8,128)S(1)}, u32[]{:S(2)}, u32[]{:S(2)}) collective-permute-start(f32[352,128]{1,0:T(8,128)S(1)} %bitcast.170), channel_id=1, source_target_pairs={{0,4},{1,5},{2,6},{3,7},{4,0},{5,1},{6,2},{7,3},{8,12},{9,13},{10,... | collective-permute-start | bytes 540680 | tf_op jit(solution)/shard_map/ppermute | solution.py:29
  128.1 9.5 %collective-permute-start.43 = (f32[352,128]{1,0:T(8,128)S(1)}, f32[352,128]{1,0:T(8,128)S(1)}, u32[]{:S(2)}, u32[]{:S(2)}) collective-permute-start(f32[352,128]{1,0:T(8,128)S(1)} %bitcast.223), channel_id=1, source_target_pairs={{0,2},{1,7},{2,0},{3,5},{4,6},{5,3},{6,4},{7,1},{8,10},{9,15},{10,... | collective-permute-start | bytes 540680 | tf_op jit(solution)/shard_map/ppermute | solution.py:29
  129.3 8.3 %collective-permute-start.44 = (f32[352,128]{1,0:T(8,128)S(1)}, f32[352,128]{1,0:T(8,128)S(1)}, u32[]{:S(2)}, u32[]{:S(2)}) collective-permute-start(f32[352,128]{1,0:T(8,128)S(1)} %bitcast.221), channel_id=1, source_target_pairs={{0,6},{1,3},{2,4},{3,1},{4,2},{5,7},{6,0},{7,5},{8,14},{9,11},{10,... | collective-permute-start | bytes 540680 | tf_op jit(solution)/shard_map/ppermute | solution.py:29
  147.2 12.1 %collective-permute-start.50 = (f32[1408,128]{1,0:T(8,128)S(1)}, f32[1408,128]{1,0:T(8,128)S(1)}, u32[]{:S(2)}, u32[]{:S(2)}) collective-permute-start(f32[1408,128]{1,0:T(8,128)S(1)} %bitcast.129), channel_id=1, source_target_pairs={{0,16},{1,65},{8,24},{9,73},{16,0},{17,81},{24,8},{25,89},{32,48},... | collective-permute-start | bytes 2162696 | tf_op jit(solution)/shard_map/ppermute | solution.py:29
  147.3 15.2 %collective-permute-start.49 = (f32[1408,128]{1,0:T(8,128)S(1)}, f32[1408,128]{1,0:T(8,128)S(1)}, u32[]{:S(2)}, u32[]{:S(2)}) collective-permute-start(f32[1408,128]{1,0:T(8,128)S(1)} %bitcast.130), channel_id=1, source_target_pairs={{0,24},{1,97},{8,0},{9,105},{16,8},{17,113},{24,16},{25,121},{32,5... | collective-permute-start | bytes 2162696 | tf_op jit(solution)/shard_map/ppermute | solution.py:29
  147.7 19.2 %collective-permute-start.48 = (f32[1408,128]{1,0:T(8,128)S(1)}, f32[1408,128]{1,0:T(8,128)S(1)}, u32[]{:S(2)}, u32[]{:S(2)}) collective-permute-start(f32[1408,128]{1,0:T(8,128)S(1)} %bitcast.131), channel_id=1, source_target_pairs={{0,8},{1,33},{8,16},{9,41},{16,24},{17,49},{24,0},{25,57},{32,40},... | collective-permute-start | bytes 2162696 | tf_op jit(solution)/shard_map/ppermute | solution.py:29
  172.9 7.7 %collective-permute-start.53 = (f32[384,128]{1,0:T(8,128)S(1)}, f32[384,128]{1,0:T(8,128)S(1)}, u32[]{:S(2)}, u32[]{:S(2)}) collective-permute-start(f32[384,128]{1,0:T(8,128)S(1)} %bitcast.165), channel_id=1, source_target_pairs={{0,4},{1,5},{2,6},{3,7},{4,0},{5,1},{6,2},{7,3},{8,12},{9,13},{10,... | collective-permute-start | bytes 589832 | tf_op jit(solution)/shard_map/ppermute | solution.py:29
  174.8 10.4 %collective-permute-start.54 = (f32[384,128]{1,0:T(8,128)S(1)}, f32[384,128]{1,0:T(8,128)S(1)}, u32[]{:S(2)}, u32[]{:S(2)}) collective-permute-start(f32[384,128]{1,0:T(8,128)S(1)} %bitcast.220), channel_id=1, source_target_pairs={{0,2},{1,7},{2,0},{3,5},{4,6},{5,3},{6,4},{7,1},{8,10},{9,15},{10,... | collective-permute-start | bytes 589832 | tf_op jit(solution)/shard_map/ppermute | solution.py:29
  176.0 9.1 %collective-permute-start.55 = (f32[384,128]{1,0:T(8,128)S(1)}, f32[384,128]{1,0:T(8,128)S(1)}, u32[]{:S(2)}, u32[]{:S(2)}) collective-permute-start(f32[384,128]{1,0:T(8,128)S(1)} %bitcast.218), channel_id=1, source_target_pairs={{0,6},{1,3},{2,4},{3,1},{4,2},{5,7},{6,0},{7,5},{8,14},{9,11},{10,... | collective-permute-start | bytes 589832 | tf_op jit(solution)/shard_map/ppermute | solution.py:29
  190.7 6.9 %collective-permute-start.59 = (f32[256,128]{1,0:T(8,128)S(1)}, f32[256,128]{1,0:T(8,128)S(1)}, u32[]{:S(2)}, u32[]{:S(2)}) collective-permute-start(f32[256,128]{1,0:T(8,128)S(1)} %bitcast.238), channel_id=1, source_target_pairs={{0,2},{1,7},{2,0},{3,5},{4,6},{5,3},{6,4},{7,1},{8,10},{9,15},{10,... | collective-permute-start | bytes 393224 | tf_op jit(solution)/shard_map/ppermute | solution.py:29
  (34 other events, 133.7 us)

commit v14 on v11

--- a/solution.py
+++ b/solution.py
@@ -181,13 +181,13 @@
 
 
 def gather_rows(rows):
-    near = [line_shift(rows, k, 0) for k in (1, 3, 2)]
+    near = [line_shift(rows, k, 0) for k in (3, 1, 2)]
     rows, *near = lax.optimization_barrier((rows, *near))
-    line = jnp.stack([rows, near[0], near[2], near[1]])
+    line = jnp.stack([rows, near[1], near[2], near[0]])
     line = lax.optimization_barrier(line)
-    far = [line_shift(line, k, 1) for k in (1, 3, 2)]
+    far = [line_shift(line, k, 1) for k in (3, 1, 2)]
     line, *far = lax.optimization_barrier((line, *far))
-    return [line, far[0], far[2], far[1]]
+    return [line, far[1], far[2], far[0]]
 
 
 def collect(ins, g_ref):

time: 199 us -> 198 us (level)
  waiting for transfers between devices: 115 us -> 108 us
  starting transfers between devices: 65.6 us -> 71.3 us
    ppermute x61, waiting for transfers between devices: 115 us -> 108 us  [permute(): return lax.ppermute(flat, axes, pairs).reshape(value.shape)]
    ppermute x61, starting transfers between devices: 65.6 us -> 71.3 us  [permute(): return lax.ppermute(flat, axes, pairs).reshape(value.shape)]
  transfers between devices with their start and end apart: 61 -> 61, of which waited for: 45 -> 42; matrix products, arithmetic and copies ran while one was open for 1% -> 1% of each run, Pallas kernels for 1% -> 1%
where the time goes in v14:
time: 198 us
  waiting for transfers between devices  108 us (55%)
  starting transfers between devices  71.3 us (36%)
  Pallas kernels  13.7 us (7%)
  local copies, waits for them, and re-layouts  3.67 us (2%)
    ppermute x61, waiting for transfers between devices, permute(): return lax.ppermute(flat, axes, pairs).reshape(value.shape)  108 us
    ppermute x61, starting transfers between devices, permute(): return lax.ppermute(flat, axes, pairs).reshape(value.shape)  71.3 us
    pallas_call x28, Pallas kernels, call(): pl.pallas_call(kernel, out_shape=[jax.ShapeDtypeStruct(o, F32) for o in o...  13.7 us
  transfers between devices with their start and end apart: 61, of which 42 were waited for; matrix products, arithmetic and copies ran while one was open for 1% of the time, Pallas kernels for 1%

profile of v14, /device:TPU:1, one launch (start us, length us, event | category | flops | bytes accessed | tf_op | source)
XLA Modules:
  0.0 197.9 jit_solution(12641074224827744658)
XLA Ops:
  3.9 3.8 %collective-permute-start.2 = (f32[256,128]{1,0:T(8,128)S(1)}, f32[256,128]{1,0:T(8,128)S(1)}, u32[]{:S(2)}, u32[]{:S(2)}) collective-permute-start(f32[256,128]{1,0:T(8,128)S(1)} %bitcast.193), channel_id=1, source_target_pairs={{0,4},{1,5},{2,6},{3,7},{4,0},{5,1},{6,2},{7,3},{8,12},{9,13},{10,... | collective-permute-start | bytes 393224 | tf_op jit(solution)/shard_map/ppermute | solution.py:29
  15.7 3.0 %collective-permute-start.7 = (f32[224,128]{1,0:T(8,128)S(1)}, f32[224,128]{1,0:T(8,128)S(1)}, u32[]{:S(2)}, u32[]{:S(2)}) collective-permute-start(f32[224,128]{1,0:T(8,128)S(1)} %bitcast.154), channel_id=1, source_target_pairs={{0,64},{1,17},{8,72},{9,25},{16,80},{17,1},{24,88},{25,9},{32,96},... | collective-permute-start | bytes 344072 | tf_op jit(solution)/shard_map/ppermute | solution.py:29
  23.5 2.8 %collective-permute-start.10 = (f32[896,128]{1,0:T(8,128)S(1)}, f32[896,128]{1,0:T(8,128)S(1)}, u32[]{:S(2)}, u32[]{:S(2)}) collective-permute-start(f32[896,128]{1,0:T(8,128)S(1)} %bitcast.132), channel_id=1, source_target_pairs={{0,16},{1,65},{8,24},{9,73},{16,0},{17,81},{24,8},{25,89},{32,48},... | collective-permute-start | bytes 1376264 | tf_op jit(solution)/shard_map/ppermute | solution.py:29
  26.7 2.4 %collective-permute-start.8 = (f32[896,128]{1,0:T(8,128)S(1)}, f32[896,128]{1,0:T(8,128)S(1)}, u32[]{:S(2)}, u32[]{:S(2)}) collective-permute-start(f32[896,128]{1,0:T(8,128)S(1)} %bitcast.134), channel_id=1, source_target_pairs={{0,24},{1,97},{8,0},{9,105},{16,8},{17,113},{24,16},{25,121},{32,5... | collective-permute-start | bytes 1376264 | tf_op jit(solution)/shard_map/ppermute | solution.py:29
  29.0 3.8 %collective-permute-done.10 = f32[896,128]{1,0:T(8,128)S(1)} collective-permute-done((f32[896,128]{1,0:T(8,128)S(1)}, f32[896,128]{1,0:T(8,128)S(1)}, u32[]{:S(2)}, u32[]{:S(2)}) %collective-permute-start.10) | collective-permute-done | bytes 458784 | tf_op jit(solution)/shard_map/ppermute | solution.py:29
  32.8 4.9 %collective-permute-done.9 = f32[896,128]{1,0:T(8,128)S(1)} collective-permute-done((f32[896,128]{1,0:T(8,128)S(1)}, f32[896,128]{1,0:T(8,128)S(1)}, u32[]{:S(2)}, u32[]{:S(2)}) %collective-permute-start.9) | collective-permute-done | bytes 458784 | tf_op jit(solution)/shard_map/ppermute | solution.py:29
  39.6 3.5 %collective-permute-start.11 = (f32[768,128]{1,0:T(8,128)S(1)}, f32[768,128]{1,0:T(8,128)S(1)}, u32[]{:S(2)}, u32[]{:S(2)}) collective-permute-start(f32[768,128]{1,0:T(8,128)S(1)} %bitcast.215), channel_id=1, source_target_pairs={{0,1},{1,0},{2,3},{3,2},{4,5},{5,4},{6,7},{7,6},{8,9},{9,8},{10,11... | collective-permute-start | bytes 1179656 | tf_op jit(solution)/shard_map/ppermute | solution.py:29
  48.0 3.0 %collective-permute-done.13 = f32[256,128]{1,0:T(8,128)S(1)} collective-permute-done((f32[256,128]{1,0:T(8,128)S(1)}, f32[256,128]{1,0:T(8,128)S(1)}, u32[]{:S(2)}, u32[]{:S(2)}) %collective-permute-start.13) | collective-permute-done | bytes 131104 | tf_op jit(solution)/shard_map/ppermute | solution.py:29
  50.9 2.5 %collective-permute-done.14 = f32[256,128]{1,0:T(8,128)S(1)} collective-permute-done((f32[256,128]{1,0:T(8,128)S(1)}, f32[256,128]{1,0:T(8,128)S(1)}, u32[]{:S(2)}, u32[]{:S(2)}) %collective-permute-start.14) | collective-permute-done | bytes 131104 | tf_op jit(solution)/shard_map/ppermute | solution.py:29
  59.8 2.4 %collective-permute-done.18 = f32[144,128]{1,0:T(8,128)S(1)} collective-permute-done((f32[144,128]{1,0:T(8,128)S(1)}, f32[144,128]{1,0:T(8,128)S(1)}, u32[]{:S(2)}, u32[]{:S(2)}) %collective-permute-start.18) | collective-permute-done | bytes 73760 | tf_op jit(solution)/shard_map/ppermute | solution.py:29
  62.2 3.7 %collective-permute-done.16 = f32[256,128]{1,0:T(8,128)S(1)} collective-permute-done((f32[256,128]{1,0:T(8,128)S(1)}, f32[256,128]{1,0:T(8,128)S(1)}, u32[]{:S(2)}, u32[]{:S(2)}) %collective-permute-start.16) | collective-permute-done | bytes 131104 | tf_op jit(solution)/shard_map/ppermute | solution.py:29
  70.5 2.4 %collective-permute-start.22 = (f32[288,128]{1,0:T(8,128)S(1)}, f32[288,128]{1,0:T(8,128)S(1)}, u32[]{:S(2)}, u32[]{:S(2)}) collective-permute-start(f32[288,128]{1,0:T(8,128)S(1)} %bitcast.180), channel_id=1, source_target_pairs={{0,4},{1,5},{2,6},{3,7},{4,0},{5,1},{6,2},{7,3},{8,12},{9,13},{10,... | collective-permute-start | bytes 442376 | tf_op jit(solution)/shard_map/ppermute | solution.py:29
  74.5 2.7 %collective-permute-done.22 = f32[288,128]{1,0:T(8,128)S(1)} collective-permute-done((f32[288,128]{1,0:T(8,128)S(1)}, f32[288,128]{1,0:T(8,128)S(1)}, u32[]{:S(2)}, u32[]{:S(2)}) %collective-permute-start.22) | collective-permute-done | bytes 147488 | tf_op jit(solution)/shard_map/ppermute | solution.py:29
  77.1 3.4 %collective-permute-done.23 = f32[288,128]{1,0:T(8,128)S(1)} collective-permute-done((f32[288,128]{1,0:T(8,128)S(1)}, f32[288,128]{1,0:T(8,128)S(1)}, u32[]{:S(2)}, u32[]{:S(2)}) %collective-permute-start.23) | collective-permute-done | bytes 147488 | tf_op jit(solution)/shard_map/ppermute | solution.py:29
  84.0 3.3 %collective-permute-done.28 = f32[224,128]{1,0:T(8,128)S(1)} collective-permute-done((f32[224,128]{1,0:T(8,128)S(1)}, f32[224,128]{1,0:T(8,128)S(1)}, u32[]{:S(2)}, u32[]{:S(2)}) %collective-permute-start.28) | collective-permute-done | bytes 114720 | tf_op jit(solution)/shard_map/ppermute | solution.py:29
  91.5 2.5 %collective-permute-start.29 = (f32[960,128]{1,0:T(8,128)S(1)}, f32[960,128]{1,0:T(8,128)S(1)}, u32[]{:S(2)}, u32[]{:S(2)}) collective-permute-start(f32[960,128]{1,0:T(8,128)S(1)} %bitcast.213), channel_id=1, source_target_pairs={{0,1},{1,0},{2,3},{3,2},{4,5},{5,4},{6,7},{7,6},{8,9},{9,8},{10,11... | collective-permute-start | bytes 1474568 | tf_op jit(solution)/shard_map/ppermute | solution.py:29
  95.7 2.3 %collective-permute-start.31 = (f32[320,128]{1,0:T(8,128)S(1)}, f32[320,128]{1,0:T(8,128)S(1)}, u32[]{:S(2)}, u32[]{:S(2)}) collective-permute-start(f32[320,128]{1,0:T(8,128)S(1)} %bitcast.174), channel_id=1, source_target_pairs={{0,4},{1,5},{2,6},{3,7},{4,0},{5,1},{6,2},{7,3},{8,12},{9,13},{10,... | collective-permute-start | bytes 491528 | tf_op jit(solution)/shard_map/ppermute | solution.py:29
  99.5 3.2 %collective-permute-done.31 = f32[320,128]{1,0:T(8,128)S(1)} collective-permute-done((f32[320,128]{1,0:T(8,128)S(1)}, f32[320,128]{1,0:T(8,128)S(1)}, u32[]{:S(2)}, u32[]{:S(2)}) %collective-permute-start.31) | collective-permute-done | bytes 163872 | tf_op jit(solution)/shard_map/ppermute | solution.py:29
  102.7 3.7 %collective-permute-done.32 = f32[320,128]{1,0:T(8,128)S(1)} collective-permute-done((f32[320,128]{1,0:T(8,128)S(1)}, f32[320,128]{1,0:T(8,128)S(1)}, u32[]{:S(2)}, u32[]{:S(2)}) %collective-permute-start.32) | collective-permute-done | bytes 163872 | tf_op jit(solution)/shard_map/ppermute | solution.py:29
  113.0 3.6 %collective-permute-done.39 = f32[96,128]{1,0:T(8,128)S(1)} collective-permute-done((f32[96,128]{1,0:T(8,128)S(1)}, f32[96,128]{1,0:T(8,128)S(1)}, u32[]{:S(2)}, u32[]{:S(2)}) %collective-permute-start.39) | collective-permute-done | bytes 49184 | tf_op jit(solution)/shard_map/ppermute | solution.py:29
  117.7 3.3 %collective-permute-done.34 = f32[320,128]{1,0:T(8,128)S(1)} collective-permute-done((f32[320,128]{1,0:T(8,128)S(1)}, f32[320,128]{1,0:T(8,128)S(1)}, u32[]{:S(2)}, u32[]{:S(2)}) %collective-permute-start.34) | collective-permute-done | bytes 163872 | tf_op jit(solution)/shard_map/ppermute | solution.py:29
  128.4 4.1 %collective-permute-done.42 = f32[352,128]{1,0:T(8,128)S(1)} collective-permute-done((f32[352,128]{1,0:T(8,128)S(1)}, f32[352,128]{1,0:T(8,128)S(1)}, u32[]{:S(2)}, u32[]{:S(2)}) %collective-permute-start.42) | collective-permute-done | bytes 180256 | tf_op jit(solution)/shard_map/ppermute | solution.py:29
  132.5 4.0 %collective-permute-done.43 = f32[352,128]{1,0:T(8,128)S(1)} collective-permute-done((f32[352,128]{1,0:T(8,128)S(1)}, f32[352,128]{1,0:T(8,128)S(1)}, u32[]{:S(2)}, u32[]{:S(2)}) %collective-permute-start.43) | collective-permute-done | bytes 180256 | tf_op jit(solution)/shard_map/ppermute | solution.py:29
  140.3 2.6 %collective-permute-done.47 = f32[352,128]{1,0:T(8,128)S(1)} collective-permute-done((f32[352,128]{1,0:T(8,128)S(1)}, f32[352,128]{1,0:T(8,128)S(1)}, u32[]{:S(2)}, u32[]{:S(2)}) %collective-permute-start.47) | collective-permute-done | bytes 180256 | tf_op jit(solution)/shard_map/ppermute | solution.py:29
  148.5 8.4 %collective-permute-done.50 = f32[1408,128]{1,0:T(8,128)S(1)} collective-permute-done((f32[1408,128]{1,0:T(8,128)S(1)}, f32[1408,128]{1,0:T(8,128)S(1)}, u32[]{:S(2)}, u32[]{:S(2)}) %collective-permute-start.50) | collective-permute-done | bytes 720928 | tf_op jit(solution)/shard_map/ppermute | solution.py:29
  156.9 7.7 %collective-permute-done.49 = f32[1408,128]{1,0:T(8,128)S(1)} collective-permute-done((f32[1408,128]{1,0:T(8,128)S(1)}, f32[1408,128]{1,0:T(8,128)S(1)}, u32[]{:S(2)}, u32[]{:S(2)}) %collective-permute-start.49) | collective-permute-done | bytes 720928 | tf_op jit(solution)/shard_map/ppermute | solution.py:29
  164.6 2.6 %shard_map.76 = (f32[1,4,12,8,128]{4,3,2,1,0:T(8,128)S(1)}, f32[3,4,12,8,128]{4,3,2,1,0:T(8,128)S(1)}, f32[1,4,12,8,128]{4,3,2,1,0:T(8,128)S(1)}, f32[3,4,12,8,128]{4,3,2,1,0:T(8,128)S(1)}, f32[4,11,8,128]{3,2,1,0:T(8,128)S(1)}) custom-call(s32[912]{0:T(1024)S(1)} %concatenate.3.tab, f32[4,4,11,8,128]{4,3,2,1,0:T(8,128)S(1)} %pad_maximum_fusion.refs_0_, ...), custom_call_target="tpu_custom_call" | custom-call | tf_op jit(solution)/shard_map/pallas_call | solution.py:129
  167.2 2.8 %collective-permute-start.51 = (f32[1152,128]{1,0:T(8,128)S(1)}, f32[1152,128]{1,0:T(8,128)S(1)}, u32[]{:S(2)}, u32[]{:S(2)}) collective-permute-start(f32[1152,128]{1,0:T(8,128)S(1)} %bitcast.211), channel_id=1, source_target_pairs={{0,1},{1,0},{2,3},{3,2},{4,5},{5,4},{6,7},{7,6},{8,9},{9,8},{10,11... | collective-permute-start | bytes 1769480 | tf_op jit(solution)/shard_map/ppermute | solution.py:29
  175.2 4.5 %collective-permute-done.53 = f32[384,128]{1,0:T(8,128)S(1)} collective-permute-done((f32[384,128]{1,0:T(8,128)S(1)}, f32[384,128]{1,0:T(8,128)S(1)}, u32[]{:S(2)}, u32[]{:S(2)}) %collective-permute-start.53) | collective-permute-done | bytes 196640 | tf_op jit(solution)/shard_map/ppermute | solution.py:29
  179.7 4.5 %collective-permute-done.54 = f32[384,128]{1,0:T(8,128)S(1)} collective-permute-done((f32[384,128]{1,0:T(8,128)S(1)}, f32[384,128]{1,0:T(8,128)S(1)}, u32[]{:S(2)}, u32[]{:S(2)}) %collective-permute-start.54) | collective-permute-done | bytes 196640 | tf_op jit(solution)/shard_map/ppermute | solution.py:29
  191.1 3.2 %collective-permute-done.58 = f32[256,128]{1,0:T(8,128)S(1)} collective-permute-done((f32[256,128]{1,0:T(8,128)S(1)}, f32[256,128]{1,0:T(8,128)S(1)}, u32[]{:S(2)}, u32[]{:S(2)}) %collective-permute-start.58) | collective-permute-done | bytes 131104 | tf_op jit(solution)/shard_map/ppermute | solution.py:29
  194.2 2.3 %collective-permute-done.59 = f32[256,128]{1,0:T(8,128)S(1)} collective-permute-done((f32[256,128]{1,0:T(8,128)S(1)}, f32[256,128]{1,0:T(8,128)S(1)}, u32[]{:S(2)}, u32[]{:S(2)}) %collective-permute-start.59) | collective-permute-done | bytes 131104 | tf_op jit(solution)/shard_map/ppermute | solution.py:29
  (139 shorter events, 84.8 us)
Async XLA Ops:
  3.9 9.5 %collective-permute-start.2 = (f32[256,128]{1,0:T(8,128)S(1)}, f32[256,128]{1,0:T(8,128)S(1)}, u32[]{:S(2)}, u32[]{:S(2)}) collective-permute-start(f32[256,128]{1,0:T(8,128)S(1)} %bitcast.193), channel_id=1, source_target_pairs={{0,4},{1,5},{2,6},{3,7},{4,0},{5,1},{6,2},{7,3},{8,12},{9,13},{10,... | collective-permute-start | bytes 393224 | tf_op jit(solution)/shard_map/ppermute | solution.py:29
  23.5 9.3 %collective-permute-start.10 = (f32[896,128]{1,0:T(8,128)S(1)}, f32[896,128]{1,0:T(8,128)S(1)}, u32[]{:S(2)}, u32[]{:S(2)}) collective-permute-start(f32[896,128]{1,0:T(8,128)S(1)} %bitcast.132), channel_id=1, source_target_pairs={{0,16},{1,65},{8,24},{9,73},{16,0},{17,81},{24,8},{25,89},{32,48},... | collective-permute-start | bytes 1376264 | tf_op jit(solution)/shard_map/ppermute | solution.py:29
  26.4 11.3 %collective-permute-start.9 = (f32[896,128]{1,0:T(8,128)S(1)}, f32[896,128]{1,0:T(8,128)S(1)}, u32[]{:S(2)}, u32[]{:S(2)}) collective-permute-start(f32[896,128]{1,0:T(8,128)S(1)} %bitcast.133), channel_id=1, source_target_pairs={{0,8},{1,33},{8,16},{9,41},{16,24},{17,49},{24,0},{25,57},{32,40},... | collective-permute-start | bytes 1376264 | tf_op jit(solution)/shard_map/ppermute | solution.py:29
  26.7 11.1 %collective-permute-start.8 = (f32[896,128]{1,0:T(8,128)S(1)}, f32[896,128]{1,0:T(8,128)S(1)}, u32[]{:S(2)}, u32[]{:S(2)}) collective-permute-start(f32[896,128]{1,0:T(8,128)S(1)} %bitcast.134), channel_id=1, source_target_pairs={{0,24},{1,97},{8,0},{9,105},{16,8},{17,113},{24,16},{25,121},{32,5... | collective-permute-start | bytes 1376264 | tf_op jit(solution)/shard_map/ppermute | solution.py:29
  39.6 7.0 %collective-permute-start.11 = (f32[768,128]{1,0:T(8,128)S(1)}, f32[768,128]{1,0:T(8,128)S(1)}, u32[]{:S(2)}, u32[]{:S(2)}) collective-permute-start(f32[768,128]{1,0:T(8,128)S(1)} %bitcast.215), channel_id=1, source_target_pairs={{0,1},{1,0},{2,3},{3,2},{4,5},{5,4},{6,7},{7,6},{8,9},{9,8},{10,11... | collective-permute-start | bytes 1179656 | tf_op jit(solution)/shard_map/ppermute | solution.py:29
  46.6 6.8 %collective-permute-start.14 = (f32[256,128]{1,0:T(8,128)S(1)}, f32[256,128]{1,0:T(8,128)S(1)}, u32[]{:S(2)}, u32[]{:S(2)}) collective-permute-start(f32[256,128]{1,0:T(8,128)S(1)} %bitcast.237), channel_id=1, source_target_pairs={{0,2},{1,7},{2,0},{3,5},{4,6},{5,3},{6,4},{7,1},{8,10},{9,15},{10,... | collective-permute-start | bytes 393224 | tf_op jit(solution)/shard_map/ppermute | solution.py:29
  53.8 8.4 %collective-permute-start.17 = (f32[256,128]{1,0:T(8,128)S(1)}, f32[256,128]{1,0:T(8,128)S(1)}, u32[]{:S(2)}, u32[]{:S(2)}) collective-permute-start(f32[256,128]{1,0:T(8,128)S(1)} %bitcast.148), channel_id=1, source_target_pairs={{0,16},{8,0},{32,8},{40,32},{64,40},{72,64},{96,72},{104,96},{120,... | collective-permute-start | bytes 393224 | tf_op jit(solution)/shard_map/ppermute | solution.py:29
  55.6 10.3 %collective-permute-start.16 = (f32[256,128]{1,0:T(8,128)S(1)}, f32[256,128]{1,0:T(8,128)S(1)}, u32[]{:S(2)}, u32[]{:S(2)}) collective-permute-start(f32[256,128]{1,0:T(8,128)S(1)} %bitcast.149), channel_id=1, source_target_pairs={{0,8},{8,32},{32,40},{40,64},{64,72},{72,96},{96,104},{104,120},{1... | collective-permute-start | bytes 393224 | tf_op jit(solution)/shard_map/ppermute | solution.py:29
  70.5 6.6 %collective-permute-start.22 = (f32[288,128]{1,0:T(8,128)S(1)}, f32[288,128]{1,0:T(8,128)S(1)}, u32[]{:S(2)}, u32[]{:S(2)}) collective-permute-start(f32[288,128]{1,0:T(8,128)S(1)} %bitcast.180), channel_id=1, source_target_pairs={{0,4},{1,5},{2,6},{3,7},{4,0},{5,1},{6,2},{7,3},{8,12},{9,13},{10,... | collective-permute-start | bytes 442376 | tf_op jit(solution)/shard_map/ppermute | solution.py:29
  72.9 7.6 %collective-permute-start.23 = (f32[288,128]{1,0:T(8,128)S(1)}, f32[288,128]{1,0:T(8,128)S(1)}, u32[]{:S(2)}, u32[]{:S(2)}) collective-permute-start(f32[288,128]{1,0:T(8,128)S(1)} %bitcast.228), channel_id=1, source_target_pairs={{0,2},{1,7},{2,0},{3,5},{4,6},{5,3},{6,4},{7,1},{8,10},{9,15},{10,... | collective-permute-start | bytes 442376 | tf_op jit(solution)/shard_map/ppermute | solution.py:29
  74.2 6.7 %collective-permute-start.24 = (f32[288,128]{1,0:T(8,128)S(1)}, f32[288,128]{1,0:T(8,128)S(1)}, u32[]{:S(2)}, u32[]{:S(2)}) collective-permute-start(f32[288,128]{1,0:T(8,128)S(1)} %bitcast.227), channel_id=1, source_target_pairs={{0,6},{1,3},{2,4},{3,1},{4,2},{5,7},{6,0},{7,5},{8,14},{9,11},{10,... | collective-permute-start | bytes 442376 | tf_op jit(solution)/shard_map/ppermute | solution.py:29
  81.0 7.0 %collective-permute-start.26 = (f32[288,128]{1,0:T(8,128)S(1)}, f32[288,128]{1,0:T(8,128)S(1)}, u32[]{:S(2)}, u32[]{:S(2)}) collective-permute-start(f32[288,128]{1,0:T(8,128)S(1)} %bitcast.145), channel_id=1, source_target_pairs={{0,16},{8,0},{32,8},{40,32},{64,40},{72,64},{96,72},{104,96},{120,... | collective-permute-start | bytes 442376 | tf_op jit(solution)/shard_map/ppermute | solution.py:29
  81.1 9.2 %collective-permute-start.25 = (f32[288,128]{1,0:T(8,128)S(1)}, f32[288,128]{1,0:T(8,128)S(1)}, u32[]{:S(2)}, u32[]{:S(2)}) collective-permute-start(f32[288,128]{1,0:T(8,128)S(1)} %bitcast.146), channel_id=1, source_target_pairs={{0,8},{8,32},{32,40},{40,64},{64,72},{72,96},{96,104},{104,120},{1... | collective-permute-start | bytes 442376 | tf_op jit(solution)/shard_map/ppermute | solution.py:29
  95.7 7.0 %collective-permute-start.31 = (f32[320,128]{1,0:T(8,128)S(1)}, f32[320,128]{1,0:T(8,128)S(1)}, u32[]{:S(2)}, u32[]{:S(2)}) collective-permute-start(f32[320,128]{1,0:T(8,128)S(1)} %bitcast.174), channel_id=1, source_target_pairs={{0,4},{1,5},{2,6},{3,7},{4,0},{5,1},{6,2},{7,3},{8,12},{9,13},{10,... | collective-permute-start | bytes 491528 | tf_op jit(solution)/shard_map/ppermute | solution.py:29
  98.1 8.3 %collective-permute-start.32 = (f32[320,128]{1,0:T(8,128)S(1)}, f32[320,128]{1,0:T(8,128)S(1)}, u32[]{:S(2)}, u32[]{:S(2)}) collective-permute-start(f32[320,128]{1,0:T(8,128)S(1)} %bitcast.225), channel_id=1, source_target_pairs={{0,2},{1,7},{2,0},{3,5},{4,6},{5,3},{6,4},{7,1},{8,10},{9,15},{10,... | collective-permute-start | bytes 491528 | tf_op jit(solution)/shard_map/ppermute | solution.py:29
  99.4 7.4 %collective-permute-start.33 = (f32[320,128]{1,0:T(8,128)S(1)}, f32[320,128]{1,0:T(8,128)S(1)}, u32[]{:S(2)}, u32[]{:S(2)}) collective-permute-start(f32[320,128]{1,0:T(8,128)S(1)} %bitcast.224), channel_id=1, source_target_pairs={{0,6},{1,3},{2,4},{3,1},{4,2},{5,7},{6,0},{7,5},{8,14},{9,11},{10,... | collective-permute-start | bytes 491528 | tf_op jit(solution)/shard_map/ppermute | solution.py:29
  108.2 9.6 %collective-permute-start.35 = (f32[320,128]{1,0:T(8,128)S(1)}, f32[320,128]{1,0:T(8,128)S(1)}, u32[]{:S(2)}, u32[]{:S(2)}) collective-permute-start(f32[320,128]{1,0:T(8,128)S(1)} %bitcast.142), channel_id=1, source_target_pairs={{0,16},{8,0},{32,8},{40,32},{64,40},{72,64},{96,72},{104,96},{120,... | collective-permute-start | bytes 491528 | tf_op jit(solution)/shard_map/ppermute | solution.py:29
  108.4 12.7 %collective-permute-start.34 = (f32[320,128]{1,0:T(8,128)S(1)}, f32[320,128]{1,0:T(8,128)S(1)}, u32[]{:S(2)}, u32[]{:S(2)}) collective-permute-start(f32[320,128]{1,0:T(8,128)S(1)} %bitcast.143), channel_id=1, source_target_pairs={{0,8},{8,32},{32,40},{40,64},{64,72},{72,96},{96,104},{104,120},{1... | collective-permute-start | bytes 491528 | tf_op jit(solution)/shard_map/ppermute | solution.py:29
  109.7 8.1 %collective-permute-start.37 = (f32[256,128]{1,0:T(8,128)S(1)}, f32[256,128]{1,0:T(8,128)S(1)}, u32[]{:S(2)}, u32[]{:S(2)}) collective-permute-start(f32[256,128]{1,0:T(8,128)S(1)} %bitcast.233), channel_id=1, source_target_pairs={{0,24},{8,16},{32,0},{40,8},{64,32},{72,40},{96,64},{104,72},{120,... | collective-permute-start | bytes 393224 | tf_op jit(solution)/shard_map/ppermute | solution.py:29
  109.7 8.1 %collective-permute-start.36 = (f32[256,128]{1,0:T(8,128)S(1)}, f32[256,128]{1,0:T(8,128)S(1)}, u32[]{:S(2)}, u32[]{:S(2)}) collective-permute-start(f32[256,128]{1,0:T(8,128)S(1)} %bitcast.232), channel_id=1, source_target_pairs={{0,32},{8,40},{32,64},{40,72},{64,96},{72,104},{96,120},{104,112},... | collective-permute-start | bytes 393224 | tf_op jit(solution)/shard_map/ppermute | solution.py:29
  125.1 7.3 %collective-permute-start.42 = (f32[352,128]{1,0:T(8,128)S(1)}, f32[352,128]{1,0:T(8,128)S(1)}, u32[]{:S(2)}, u32[]{:S(2)}) collective-permute-start(f32[352,128]{1,0:T(8,128)S(1)} %bitcast.170), channel_id=1, source_target_pairs={{0,4},{1,5},{2,6},{3,7},{4,0},{5,1},{6,2},{7,3},{8,12},{9,13},{10,... | collective-permute-start | bytes 540680 | tf_op jit(solution)/shard_map/ppermute | solution.py:29
  127.0 9.5 %collective-permute-start.43 = (f32[352,128]{1,0:T(8,128)S(1)}, f32[352,128]{1,0:T(8,128)S(1)}, u32[]{:S(2)}, u32[]{:S(2)}) collective-permute-start(f32[352,128]{1,0:T(8,128)S(1)} %bitcast.223), channel_id=1, source_target_pairs={{0,2},{1,7},{2,0},{3,5},{4,6},{5,3},{6,4},{7,1},{8,10},{9,15},{10,... | collective-permute-start | bytes 540680 | tf_op jit(solution)/shard_map/ppermute | solution.py:29
  128.2 8.3 %collective-permute-start.44 = (f32[352,128]{1,0:T(8,128)S(1)}, f32[352,128]{1,0:T(8,128)S(1)}, u32[]{:S(2)}, u32[]{:S(2)}) collective-permute-start(f32[352,128]{1,0:T(8,128)S(1)} %bitcast.221), channel_id=1, source_target_pairs={{0,6},{1,3},{2,4},{3,1},{4,2},{5,7},{6,0},{7,5},{8,14},{9,11},{10,... | collective-permute-start | bytes 540680 | tf_op jit(solution)/shard_map/ppermute | solution.py:29
  136.7 8.1 %collective-permute-start.46 = (f32[352,128]{1,0:T(8,128)S(1)}, f32[352,128]{1,0:T(8,128)S(1)}, u32[]{:S(2)}, u32[]{:S(2)}) collective-permute-start(f32[352,128]{1,0:T(8,128)S(1)} %bitcast.136), channel_id=1, source_target_pairs={{0,32},{1,9},{8,40},{9,17},{16,48},{17,25},{24,56},{25,1},{32,64},... | collective-permute-start | bytes 540680 | tf_op jit(solution)/shard_map/ppermute | solution.py:29
  137.9 6.8 %collective-permute-start.45 = (f32[352,128]{1,0:T(8,128)S(1)}, f32[352,128]{1,0:T(8,128)S(1)}, u32[]{:S(2)}, u32[]{:S(2)}) collective-permute-start(f32[352,128]{1,0:T(8,128)S(1)} %bitcast.137), channel_id=1, source_target_pairs={{0,96},{1,25},{8,104},{9,1},{16,112},{17,9},{24,120},{25,17},{32,0... | collective-permute-start | bytes 540680 | tf_op jit(solution)/shard_map/ppermute | solution.py:29
  144.8 12.1 %collective-permute-start.50 = (f32[1408,128]{1,0:T(8,128)S(1)}, f32[1408,128]{1,0:T(8,128)S(1)}, u32[]{:S(2)}, u32[]{:S(2)}) collective-permute-start(f32[1408,128]{1,0:T(8,128)S(1)} %bitcast.129), channel_id=1, source_target_pairs={{0,16},{1,65},{8,24},{9,73},{16,0},{17,81},{24,8},{25,89},{32,48},... | collective-permute-start | bytes 2162696 | tf_op jit(solution)/shard_map/ppermute | solution.py:29
  145.9 18.7 %collective-permute-start.49 = (f32[1408,128]{1,0:T(8,128)S(1)}, f32[1408,128]{1,0:T(8,128)S(1)}, u32[]{:S(2)}, u32[]{:S(2)}) collective-permute-start(f32[1408,128]{1,0:T(8,128)S(1)} %bitcast.130), channel_id=1, source_target_pairs={{0,8},{1,33},{8,16},{9,41},{16,24},{17,49},{24,0},{25,57},{32,40},... | collective-permute-start | bytes 2162696 | tf_op jit(solution)/shard_map/ppermute | solution.py:29
  147.7 16.8 %collective-permute-start.48 = (f32[1408,128]{1,0:T(8,128)S(1)}, f32[1408,128]{1,0:T(8,128)S(1)}, u32[]{:S(2)}, u32[]{:S(2)}) collective-permute-start(f32[1408,128]{1,0:T(8,128)S(1)} %bitcast.131), channel_id=1, source_target_pairs={{0,24},{1,97},{8,0},{9,105},{16,8},{17,113},{24,16},{25,121},{32,5... | collective-permute-start | bytes 2162696 | tf_op jit(solution)/shard_map/ppermute | solution.py:29
  171.9 7.7 %collective-permute-start.53 = (f32[384,128]{1,0:T(8,128)S(1)}, f32[384,128]{1,0:T(8,128)S(1)}, u32[]{:S(2)}, u32[]{:S(2)}) collective-permute-start(f32[384,128]{1,0:T(8,128)S(1)} %bitcast.165), channel_id=1, source_target_pairs={{0,4},{1,5},{2,6},{3,7},{4,0},{5,1},{6,2},{7,3},{8,12},{9,13},{10,... | collective-permute-start | bytes 589832 | tf_op jit(solution)/shard_map/ppermute | solution.py:29
  173.8 10.4 %collective-permute-start.54 = (f32[384,128]{1,0:T(8,128)S(1)}, f32[384,128]{1,0:T(8,128)S(1)}, u32[]{:S(2)}, u32[]{:S(2)}) collective-permute-start(f32[384,128]{1,0:T(8,128)S(1)} %bitcast.220), channel_id=1, source_target_pairs={{0,2},{1,7},{2,0},{3,5},{4,6},{5,3},{6,4},{7,1},{8,10},{9,15},{10,... | collective-permute-start | bytes 589832 | tf_op jit(solution)/shard_map/ppermute | solution.py:29
  175.0 9.2 %collective-permute-start.55 = (f32[384,128]{1,0:T(8,128)S(1)}, f32[384,128]{1,0:T(8,128)S(1)}, u32[]{:S(2)}, u32[]{:S(2)}) collective-permute-start(f32[384,128]{1,0:T(8,128)S(1)} %bitcast.218), channel_id=1, source_target_pairs={{0,6},{1,3},{2,4},{3,1},{4,2},{5,7},{6,0},{7,5},{8,14},{9,11},{10,... | collective-permute-start | bytes 589832 | tf_op jit(solution)/shard_map/ppermute | solution.py:29
  189.7 6.9 %collective-permute-start.59 = (f32[256,128]{1,0:T(8,128)S(1)}, f32[256,128]{1,0:T(8,128)S(1)}, u32[]{:S(2)}, u32[]{:S(2)}) collective-permute-start(f32[256,128]{1,0:T(8,128)S(1)} %bitcast.238), channel_id=1, source_target_pairs={{0,2},{1,7},{2,0},{3,5},{4,6},{5,3},{6,4},{7,1},{8,10},{9,15},{10,... | collective-permute-start | bytes 393224 | tf_op jit(solution)/shard_map/ppermute | solution.py:29
  (34 other events, 137.1 us)
